TPU v7x, 32 devices: a whole 2x2x4 slice. The times are simulated.
32 devices in a mesh: dom: 16 (over z, y, x), blk: 2 (over core).
Axes of the slice: x: 2, y: 2, z: 4, core: 2. Of those that a mesh axis runs over, the one named last changes fastest.
Arguments:
- self_block: float32 [96, 96, 4096], P(None, None, ('dom', 'blk')), may hold values from -1 to 8
- couple: float32 [64, 96, 4096], P(None, None, ('dom', 'blk')), may hold values from -0.625 to 0.625
- inverse: float32 [64, 64, 4096], P(None, None, ('dom', 'blk')), may hold values from -1 to 8
- body_force: float32 [3, 64, 4096], P(None, None, ('dom', 'blk')), may hold values from -6 to 6
- face_mortar: int32 [24576], P(('dom', 'blk')), may hold values from 0 to 8191, as said below
- face_kind: int32 [24576], P(('dom', 'blk')), may hold values from 0 to 4
Outputs:
- trace_field: float32 [48, 8192], P(None, ('dom', 'blk'))
- interior: float32 [3, 64, 4096], P(None, None, ('dom', 'blk'))
Inputs may be any that keep to these rules, and one draw needn't show every extreme that they name: `face_mortar`: mortar m is owned by device m // 256 along the curve. The 768 slots of device r come in five runs in this order: mortars owned by r - 2, r - 1, r, r + 1, r + 32 // 2 (modulo 32); each of the four other runs holds 1 to 32 slots and one of them holds exactly 32; the first 256 slots of the run owned by r name each of r's mortars once.
All inputs are finite; a program needn't handle non-finite values.
Results may differ from a plain program's by a relative error of at most 0.0003.
Values sent between devices are 32-bit elements; how exact they have to be, the bound alone decides.
No kernel may reach another device: no remote copies, remote signals or barrier semaphores. Data moves between devices by JAX's collectives and lax.ppermute only.
A program may use at most 128 MiB of HBM per device.

v0:
```python
import functools

import jax
import jax.numpy as jnp
import numpy as np
from jax import lax
from jax.experimental import pallas as pl
from jax.experimental.pallas import tpu as pltpu
from jax.sharding import PartitionSpec as P

AXES = ("dom", "blk")
COMP = 3
NODES = 16
FACES = 6
RUNS = 4
F32 = jnp.float32
BF16 = jnp.bfloat16


def interp_tables():
    abscissae = -np.cos(np.pi * np.arange(4) / 3.0)

    def lagrange(points):
        columns = [
            np.prod(
                [
                    (points - abscissae[other_node])
                    / (abscissae[basis_node] - abscissae[other_node])
                    for other_node in range(4)
                    if other_node != basis_node
                ],
                axis=0,
            )
            for basis_node in range(4)
        ]
        return np.stack(columns, axis=1)

    lower_map = lagrange((abscissae - 1.0) / 2.0)
    upper_map = lagrange((abscissae + 1.0) / 2.0)
    return np.stack(
        [
            np.kron(lower_map, lower_map),
            np.kron(lower_map, upper_map),
            np.kron(upper_map, lower_map),
            np.kron(upper_map, upper_map),
        ]
    ).astype(np.float32)


def block_tables():
    tables = interp_tables()
    eye = np.eye(COMP, dtype=np.float32)
    forward = np.concatenate([np.kron(eye, t) for t in tables])
    backward = np.concatenate([np.kron(eye, t.T) for t in tables])
    return forward, backward


def split(x):
    hi = x.astype(BF16)
    return hi, (x - hi.astype(F32)).astype(BF16)


def dot(a, b, rhs_dim=0):
    return lax.dot_general(a, b, (((1,), (rhs_dim,)), ((), ())), preferred_element_type=F32)


def exact_dot(x, onehot, rhs_dim=0):
    hi, lo = split(x)
    both = dot(jnp.concatenate([hi, lo], axis=0), onehot, rhs_dim)
    return both[: x.shape[0]] + both[x.shape[0] :]


def by_kind(x, table_ref, kind):
    rows = x.shape[0]
    t_hi, t_lo = split(table_ref[...])
    x_hi, x_lo = split(x)
    mapped = dot(
        jnp.concatenate([t_hi, t_hi, t_lo], axis=1), jnp.concatenate([x_hi, x_lo, x_hi], axis=0)
    )
    for number in range(4):
        x = jnp.where(kind == number + 1, mapped[number * rows : (number + 1) * rows], x)
    return x


def lanes(rows_ref, start, count=FACES):
    return jnp.concatenate([rows_ref[start + f : start + f + 1, :] for f in range(count)], axis=1)


def contract(acc, mat_ref, vec_ref, outs, terms, across, unroll=8):
    blocks = outs // 8

    def body(t, acc):
        acc = [list(a) for a in acc]
        vecs = [
            jnp.broadcast_to(vec_ref[pl.ds(c * terms + t, 1), :], (8, vec_ref.shape[1]))
            for c in range(COMP)
        ]
        for j in range(blocks):
            if across:
                tile = mat_ref[pl.ds(j * 8 * terms + t, 8, stride=terms), :]
            else:
                tile = mat_ref[pl.ds(pl.multiple_of(t * outs + j * 8, 8), 8), :]
            for c in range(COMP):
                acc[c][j] = acc[c][j] + tile * vecs[c]
        return acc

    return lax.fori_loop(0, terms, body, acc, unroll=unroll)


def zeros(outs, width):
    return [[jnp.zeros((8, width), F32) for _ in range(outs // 8)] for _ in range(COMP)]


def put(ref, acc):
    outs = 8 * len(acc[0])
    for c in range(COMP):
        for j, tile in enumerate(acc[c]):
            ref[c * outs + 8 * j : c * outs + 8 * j + 8, :] = tile


def face_columns(acc):
    half = NODES // 8
    return jnp.concatenate(
        [
            jnp.concatenate(
                [acc[c][f * half + h] for c in range(COMP) for h in range(half)], axis=0
            )
            for f in range(FACES)
        ],
        axis=1,
    )


def start_kernel(
    ranks, inner, trace, owned, cap,
    mortar_ref, kind_ref, inverse_ref, couple_ref, force_ref, back_ref,
    own_ref, out_ref, onehot_ref, meta_ref, load_ref,
):
    width = mortar_ref.shape[1]
    mortar = mortar_ref[...]
    owner = lax.div(mortar, owned)
    index = lax.rem(mortar, owned)
    me = lax.rem(owner[0:1, 0:1] + 2, ranks)
    distance = lax.rem(owner - me + ranks, ranks)
    slot = lax.broadcasted_iota(jnp.int32, mortar.shape, 1) * FACES + lax.broadcasted_iota(
        jnp.int32, mortar.shape, 0
    )
    column = index
    begin = jnp.zeros((1, 1), jnp.int32)
    for number, away in enumerate((ranks - 2, ranks - 1, 0, 1, ranks // 2)):
        inside = distance == away
        count = jnp.sum(inside.astype(F32), keepdims=True).astype(jnp.int32)
        if away:
            run = number - (number > 2)
            column = jnp.where(inside, owned + run * cap + slot - begin, column)
        begin = begin + count
    meta_ref[0:FACES, :] = kind_ref[...]
    meta_ref[FACES : FACES + 1, :] = jnp.broadcast_to(lax.rem(me, 2), (1, width))
    meta_ref[FACES + 1 : FACES + 2, :] = jnp.zeros((1, width), jnp.int32)
    rows = owned + RUNS * cap
    for f in range(FACES):
        onehot_ref[:, f * width : (f + 1) * width] = jnp.where(
            lax.broadcasted_iota(jnp.int32, (rows, width), 0) == column[f : f + 1, :], 1.0, 0.0
        ).astype(BF16)
    load = contract(zeros(inner, width), inverse_ref, force_ref, inner, inner, True)
    put(load_ref, load)
    y = contract(zeros(trace, width), couple_ref, load_ref, trace, inner, False)
    z = by_kind(face_columns(y), back_ref, lanes(kind_ref, 0))
    label = jnp.concatenate([index[f : f + 1, :] for f in range(FACES)], axis=1) + 1
    label = jnp.where(
        lax.broadcasted_iota(jnp.int32, (8, z.shape[1]), 0) == 0, label, 0
    ).astype(F32)
    sums = exact_dot(jnp.concatenate([z, label], axis=0), onehot_ref[...], 1)
    own_ref[...] = sums[: COMP * NODES, :owned]
    out_ref[...] = sums[:, owned:]


def merged(meta_ref, first, second, third, fourth, cap, to_owner):
    lane = lax.broadcasted_iota(jnp.int32, (1, RUNS * cap), 1)
    odd = meta_ref[FACES : FACES + 1, :] == 1
    low = lane < 2 * cap
    take_first = (low != odd) if to_owner else (low == odd)
    middle = jnp.where(take_first, first, second)
    return jnp.where(lane < cap, fourth, jnp.where(lane < 3 * cap, middle, third))


def owner_kernel(owned, cap, initial, meta_ref, label_ref, own_ref, a_ref, b_ref, c_ref, d_ref, *outs):
    received = merged(meta_ref, a_ref[...], b_ref[...], c_ref[...], d_ref[...], cap, True)
    rows = COMP * NODES
    if initial:
        field_ref, out_ref, label_out_ref = outs
        label = received[rows : rows + 8]
        label_out_ref[...] = label
    else:
        field_ref, out_ref = outs
        label = label_ref[...]
    wanted = (
        lax.broadcasted_iota(jnp.int32, (owned, RUNS * cap), 0)
        == label[0:1, :].astype(jnp.int32) - 1
    )
    wanted = jnp.where(wanted, 1.0, 0.0).astype(BF16)
    field = own_ref[...] + exact_dot(received[:rows], wanted, 1)
    field_ref[...] = field
    out_ref[...] = exact_dot(field, wanted)


def element_values(cap, meta_ref, onehot_ref, forth_ref, field_ref, blocks, spread_ref):
    received = merged(meta_ref, *[b[...] for b in blocks], cap, False)
    source = jnp.concatenate([field_ref[...], received], axis=1)
    kind = lanes(meta_ref, 0)
    faces = by_kind(exact_dot(source, onehot_ref[...]), forth_ref, kind)
    width = spread_ref.shape[1]
    for c in range(COMP):
        for f in range(FACES):
            spread_ref[(c * FACES + f) * NODES : (c * FACES + f + 1) * NODES, :] = faces[
                c * NODES : (c + 1) * NODES, f * width : (f + 1) * width
            ]
    return kind


def apply_kernel(
    inner, trace, owned, cap,
    meta_ref, onehot_ref, forth_ref, back_ref, inverse_ref, couple_ref, self_ref,
    field_ref, a_ref, b_ref, c_ref, d_ref,
    own_ref, out_ref, spread_ref, mid_ref, weight_ref,
):
    width = spread_ref.shape[1]
    kind = element_values(
        cap, meta_ref, onehot_ref, forth_ref, field_ref, (a_ref, b_ref, c_ref, d_ref), spread_ref
    )
    put(mid_ref, contract(zeros(inner, width), couple_ref, spread_ref, inner, trace, True))
    put(weight_ref, contract(zeros(inner, width), inverse_ref, mid_ref, inner, inner, True))
    y = contract(zeros(trace, width), self_ref, spread_ref, trace, trace, True)
    y = contract(y, couple_ref, weight_ref, trace, inner, False)
    z = by_kind(face_columns(y), back_ref, kind)
    sums = exact_dot(z, onehot_ref[...], 1)
    own_ref[...] = sums[:, :owned]
    out_ref[...] = sums[:, owned:]


def total(x):
    return jnp.sum(jnp.sum(x, axis=0, keepdims=True), axis=1, keepdims=True)


def last_kernel(
    inner, trace, cap,
    meta_ref, onehot_ref, forth_ref, inverse_ref, couple_ref, self_ref,
    k0_ref, k1_ref, k2_ref, a_ref, b_ref, c_ref, d_ref, s0_ref, s1_ref, u0_ref, u1_ref,
    weight_ref, moment_ref, spread_ref, mid_ref, image_ref,
):
    width = spread_ref.shape[1]
    element_values(
        cap, meta_ref, onehot_ref, forth_ref, k2_ref, (a_ref, b_ref, c_ref, d_ref), spread_ref
    )
    put(mid_ref, contract(zeros(inner, width), couple_ref, spread_ref, inner, trace, True))
    put(weight_ref, contract(zeros(inner, width), inverse_ref, mid_ref, inner, inner, True))
    put(image_ref, contract(zeros(trace, width), self_ref, spread_ref, trace, trace, True))
    image, weight = image_ref[...], weight_ref[...]
    ks = (k0_ref[...], k1_ref[...], k2_ref[...])
    values = [total(ks[i] * ks[j]) for i in range(3) for j in range(i, 3)]
    for s_ref, u_ref in ((s0_ref, u0_ref), (s1_ref, u1_ref), (spread_ref, mid_ref)):
        values.append(total(s_ref[...] * image) + total(u_ref[...] * weight))
    lane = lax.broadcasted_iota(jnp.int32, (1, width), 1)
    row = jnp.zeros((1, width), F32)
    for number, value in enumerate(values):
        row = jnp.where(lane == number, value, row)
    moment_ref[...] = jnp.broadcast_to(row[None], moment_ref.shape)


def finish_kernel(
    moment_ref, k0_ref, k1_ref, k2_ref, w0_ref, w1_ref, w2_ref, load_ref, field_ref, interior_ref
):
    sums = jnp.sum(moment_ref[...], axis=0)
    m = [sums[:, n : n + 1] for n in range(9)]
    gram = [[m[0], m[1], m[2]], [m[1], m[3], m[4]], [m[2], m[4], m[5]]]
    energy = [[gram[i][1], gram[i][2], m[6 + i]] for i in range(3)]

    def form(x, matrix):
        return sum(x[i] * sum(matrix[i][j] * x[j] for j in range(3)) for i in range(3))

    zero, one = jnp.zeros((1, 1), F32), jnp.ones((1, 1), F32)
    x = [zero, zero, zero]
    r = [one, zero, zero]
    d = [one, zero, zero]
    current = gram[0][0]
    for iteration in range(3):
        step = current / form(d, energy)
        x = [x[i] + step * d[i] for i in range(3)]
        if iteration < 2:
            r = [r[0], r[1] - step * d[0], r[2] - step * d[1]]
            following = form(r, gram)
            d = [r[i] + following / current * d[i] for i in range(3)]
            current = following
    field_ref[...] = x[0] * k0_ref[...] + x[1] * k1_ref[...] + x[2] * k2_ref[...]
    interior_ref[...] = load_ref[...] - (
        x[0] * w0_ref[...] + x[1] * w1_ref[...] + x[2] * w2_ref[...]
    )


def call(kernel, outs, *args):
    return pl.pallas_call(
        kernel,
        out_shape=[jax.ShapeDtypeStruct(shape, dtype) for shape, dtype in outs],
        in_specs=[pl.BlockSpec(memory_space=pltpu.VMEM)] * len(args),
        out_specs=[pl.BlockSpec(memory_space=pltpu.VMEM)] * len(outs),
        compiler_params=pltpu.CompilerParams(vmem_limit_bytes=40 * 1024 * 1024),
    )(*args)


def call_scratch(kernel, outs, scratch, *args):
    return pl.pallas_call(
        kernel,
        out_shape=[jax.ShapeDtypeStruct(shape, dtype) for shape, dtype in outs],
        in_specs=[pl.BlockSpec(memory_space=pltpu.VMEM)] * len(args),
        out_specs=[pl.BlockSpec(memory_space=pltpu.VMEM)] * len(outs),
        scratch_shapes=[pltpu.VMEM(shape, F32) for shape in scratch],
        compiler_params=pltpu.CompilerParams(vmem_limit_bytes=40 * 1024 * 1024),
    )(*args)


def exchange(block, ranks, to_owner):
    away = ranks - 2 if to_owner else 2
    pairs = [
        [(r, r ^ 1) for r in range(ranks)],
        [(r, (r + (1 if r % 2 else ranks - 1)) % ranks) for r in range(ranks)],
        [(r, (r + ranks // 2) % ranks) for r in range(ranks)],
        [(r, (r + away) % ranks) for r in range(ranks)],
    ]
    return [lax.ppermute(block, AXES, p) for p in pairs]


def local(self_block, couple, inverse, body_force, face_mortar, face_kind, *, ranks):
    trace, _, elements = self_block.shape
    inner = inverse.shape[0]
    owned = 2 * elements
    cap = max(2, elements // 4)
    width = elements
    rows = COMP * NODES
    forward, backward = block_tables()
    mortar = face_mortar.reshape(elements, FACES).T
    kind = face_kind.reshape(elements, FACES).T
    self_block = self_block.reshape(trace * trace, width)
    couple = couple.reshape(inner * trace, width)
    inverse = inverse.reshape(inner * inner, width)
    force = body_force.reshape(COMP * inner, width)

    own, out, onehot, meta, load = call(
        functools.partial(start_kernel, ranks, inner, trace, owned, cap),
        [
            ((rows, owned), F32),
            ((rows + 8, RUNS * cap), F32),
            ((owned + RUNS * cap, FACES * width), BF16),
            ((8, width), jnp.int32),
            ((COMP * inner, width), F32),
        ],
        mortar, kind, inverse, couple, force, backward,
    )
    blocks = exchange(out, ranks, True)
    field, out, label = call(
        functools.partial(owner_kernel, owned, cap, True),
        [((rows, owned), F32), ((rows, RUNS * cap), F32), ((8, RUNS * cap), F32)],
        meta, meta, own, *blocks,
    )
    fields, spreads, mids, weights = [field], [], [], []
    for _ in range(2):
        blocks = exchange(out, ranks, False)
        own, out, spread, mid, weight = call(
            functools.partial(apply_kernel, inner, trace, owned, cap),
            [
                ((rows, owned), F32),
                ((rows, RUNS * cap), F32),
                ((COMP * trace, width), F32),
                ((COMP * inner, width), F32),
                ((COMP * inner, width), F32),
            ],
            meta, onehot, forward, backward, inverse, couple, self_block, field, *blocks,
        )
        spreads.append(spread)
        mids.append(mid)
        weights.append(weight)
        blocks = exchange(out, ranks, True)
        field, out = call(
            functools.partial(owner_kernel, owned, cap, False),
            [((rows, owned), F32), ((rows, RUNS * cap), F32)],
            meta, label, own, *blocks,
        )
        fields.append(field)
    blocks = exchange(out, ranks, False)
    weight, moments = call_scratch(
        functools.partial(last_kernel, inner, trace, cap),
        [((COMP * inner, width), F32), ((ranks, 1, width), F32)],
        [(COMP * trace, width), (COMP * inner, width), (COMP * trace, width)],
        meta, onehot, forward, inverse, couple, self_block, *fields, *blocks, *spreads, *mids,
    )
    weights.append(weight)
    moments = lax.all_to_all(moments, AXES, split_axis=0, concat_axis=0, tiled=True)
    trace_field, interior = call(
        finish_kernel,
        [((rows, owned), F32), ((COMP * inner, width), F32)],
        moments, *fields, *weights, load,
    )
    return trace_field, interior.reshape(COMP, inner, elements)


def solution(mesh):
    placed = (
        P(None, None, AXES),
        P(None, None, AXES),
        P(None, None, AXES),
        P(None, None, AXES),
        P(AXES),
        P(AXES),
    )
    ranks = int(np.prod([mesh.shape[a] for a in AXES]))
    return jax.shard_map(
        functools.partial(local, ranks=ranks),
        mesh=mesh,
        in_specs=placed,
        out_specs=(P(None, AXES), P(None, None, AXES)),
        check_vma=False,
    )
```

profile of v0, /device:TPU:0, one launch (start us, length us, event | category | flops | bytes accessed | tf_op | source)
XLA Modules:
  0.0 111.5 jit_solution(11612400701264456675)
XLA Ops:
  0.6 0.8 reshape.25
  1.6 0.8 reshape.26
  2.5 1.9 %copy-done = f32[64,96,128]{2,1,0:T(8,128)S(1)} copy-done((f32[64,96,128]{2,1,0:T(8,128)S(1)}, f32[64,96,128]{2,1,0:T(8,128)}, u32[]{:S(2)}) %copy-start) | copy-done | bytes 3145752
  4.4 1.6 %copy-done.4 = f32[64,64,128]{2,1,0:T(8,128)S(1)} copy-done((f32[64,64,128]{2,1,0:T(8,128)S(1)}, f32[64,64,128]{2,1,0:T(8,128)}, u32[]{:S(2)}) %copy-start.4) | copy-done | bytes 2097176
  6.0 0.9 copy-done.6
  6.9 0.9 copy-done.8
  7.8 3.2 %shard_map.95 = (f32[48,256]{1,0:T(8,128)S(1)}, f32[56,128]{1,0:T(8,128)S(1)}, bf16[384,768]{1,0:T(8,128)(2,1)S(1)}, s32[8,128]{1,0:T(8,128)S(1)}, f32[192,128]{1,0:T(8,128)S(1)}) custom-call(s32[6,128]{1,0:T(8,128)S(1)} %bitcast.19, s32[6,128]{1,0:T(8,128)S(1)} %bitcast.20, f32[4096,128]{1,0:T(8,128)S(1)} %bitcast.14, f32[6144,128]{1,0:T(8,128)S(1)} %bitcast.7, ...), custom_call_target="tpu_custom_call" | custom-call | tf_op jit(solution)/shard_map/pallas_call | solution.py:301
  10.9 7.0 %collective-permute-start.3 = (f32[56,128]{1,0:T(8,128)S(1)}, f32[56,128]{1,0:T(8,128)S(1)}, u32[]{:S(2)}, u32[]{:S(2)}) collective-permute-start(f32[56,128]{1,0:T(8,128)S(1)} %get-tuple-element.31), channel_id=1, source_target_pairs={{0,30},{1,31},{2,0},{3,1},{4,2},{5,3},{6,4},{7,5},{8,6},{9,7},{10,... | collective-permute-start | bytes 86024 | tf_op jit(solution)/shard_map/ppermute | solution.py:329
  18.0 1.5 %collective-permute-done.3.d_ref = f32[56,128]{1,0:T(8,128)S(1)} collective-permute-done((f32[56,128]{1,0:T(8,128)S(1)}, f32[56,128]{1,0:T(8,128)S(1)}, u32[]{:S(2)}, u32[]{:S(2)}) %collective-permute-start.3) | collective-permute-done | bytes 28704 | tf_op jit(solution)/shard_map/ppermute | solution.py:329
  19.5 3.2 %collective-permute-done.2.c_ref = f32[56,128]{1,0:T(8,128)S(1)} collective-permute-done((f32[56,128]{1,0:T(8,128)S(1)}, f32[56,128]{1,0:T(8,128)S(1)}, u32[]{:S(2)}, u32[]{:S(2)}) %collective-permute-start.2) | collective-permute-done | bytes 28704 | tf_op jit(solution)/shard_map/ppermute | solution.py:329
  22.7 2.1 %collective-permute-done.1.b_ref = f32[56,128]{1,0:T(8,128)S(1)} collective-permute-done((f32[56,128]{1,0:T(8,128)S(1)}, f32[56,128]{1,0:T(8,128)S(1)}, u32[]{:S(2)}, u32[]{:S(2)}) %collective-permute-start.1) | collective-permute-done | bytes 28704 | tf_op jit(solution)/shard_map/ppermute | solution.py:329
  25.2 1.2 %collective-permute-start.6 = (f32[48,128]{1,0:T(8,128)S(1)}, f32[48,128]{1,0:T(8,128)S(1)}, u32[]{:S(2)}, u32[]{:S(2)}) collective-permute-start(f32[48,128]{1,0:T(8,128)S(1)} %get-tuple-element.34), channel_id=1, source_target_pairs={{0,16},{1,17},{2,18},{3,19},{4,20},{5,21},{6,22},{7,23},{8,24},{9,... | collective-permute-start | bytes 73736 | tf_op jit(solution)/shard_map/ppermute | solution.py:329
  26.4 1.2 %collective-permute-start.5 = (f32[48,128]{1,0:T(8,128)S(1)}, f32[48,128]{1,0:T(8,128)S(1)}, u32[]{:S(2)}, u32[]{:S(2)}) collective-permute-start(f32[48,128]{1,0:T(8,128)S(1)} %get-tuple-element.34), channel_id=1, source_target_pairs={{0,31},{1,2},{2,1},{3,4},{4,3},{5,6},{6,5},{7,8},{8,7},{9,10},{10,... | collective-permute-start | bytes 73736 | tf_op jit(solution)/shard_map/ppermute | solution.py:329
  27.6 5.1 %collective-permute-done.7.d_ref = f32[48,128]{1,0:T(8,128)S(1)} collective-permute-done((f32[48,128]{1,0:T(8,128)S(1)}, f32[48,128]{1,0:T(8,128)S(1)}, u32[]{:S(2)}, u32[]{:S(2)}) %collective-permute-start.7) | collective-permute-done | bytes 24608 | tf_op jit(solution)/shard_map/ppermute | solution.py:329
  33.3 2.3 %copy-done.2 = f32[96,96,128]{2,1,0:T(8,128)S(1)} copy-done((f32[96,96,128]{2,1,0:T(8,128)S(1)}, f32[96,96,128]{2,1,0:T(8,128)}, u32[]{:S(2)}) %copy-start.2) | copy-done | bytes 4718616
  35.6 9.7 %shard_map.97 = (f32[48,256]{1,0:T(8,128)S(1)}, f32[48,128]{1,0:T(8,128)S(1)}, f32[288,128]{1,0:T(8,128)S(1)}, f32[192,128]{1,0:T(8,128)S(1)}, f32[192,128]{1,0:T(8,128)S(1)}) custom-call(s32[8,128]{1,0:T(8,128)S(1)} %get-tuple-element.28.meta_ref.label_ref, bf16[384,768]{1,0:T(8,128)(2,1)S(1)} %get-tuple-element.29.onehot_ref, f32[192,48]{1,0:T(8,128)S(1)} %copy-done.7, ...), custom_call_target="tpu_custom_call" | custom-call | tf_op jit(solution)/shard_map/pallas_call | solution.py:301
  45.3 2.4 %collective-permute-start.11 = (f32[48,128]{1,0:T(8,128)S(1)}, f32[48,128]{1,0:T(8,128)S(1)}, u32[]{:S(2)}, u32[]{:S(2)}) collective-permute-start(f32[48,128]{1,0:T(8,128)S(1)} %get-tuple-element.36), channel_id=1, source_target_pairs={{0,30},{1,31},{2,0},{3,1},{4,2},{5,3},{6,4},{7,5},{8,6},{9,7},{10,... | collective-permute-start | bytes 73736 | tf_op jit(solution)/shard_map/ppermute | solution.py:329
  48.5 0.6 collective-permute-done.11.d_ref
  49.2 3.5 %collective-permute-done.10.c_ref = f32[48,128]{1,0:T(8,128)S(1)} collective-permute-done((f32[48,128]{1,0:T(8,128)S(1)}, f32[48,128]{1,0:T(8,128)S(1)}, u32[]{:S(2)}, u32[]{:S(2)}) %collective-permute-start.10) | collective-permute-done | bytes 24608 | tf_op jit(solution)/shard_map/ppermute | solution.py:329
  52.6 2.4 %collective-permute-done.9.b_ref = f32[48,128]{1,0:T(8,128)S(1)} collective-permute-done((f32[48,128]{1,0:T(8,128)S(1)}, f32[48,128]{1,0:T(8,128)S(1)}, u32[]{:S(2)}, u32[]{:S(2)}) %collective-permute-start.9) | collective-permute-done | bytes 24608 | tf_op jit(solution)/shard_map/ppermute | solution.py:329
  55.4 0.7 collective-permute-start.14
  56.1 1.1 %collective-permute-start.13 = (f32[48,128]{1,0:T(8,128)S(1)}, f32[48,128]{1,0:T(8,128)S(1)}, u32[]{:S(2)}, u32[]{:S(2)}) collective-permute-start(f32[48,128]{1,0:T(8,128)S(1)} %get-tuple-element.38), channel_id=1, source_target_pairs={{0,31},{1,2},{2,1},{3,4},{4,3},{5,6},{6,5},{7,8},{8,7},{9,10},{10,... | collective-permute-start | bytes 73736 | tf_op jit(solution)/shard_map/ppermute | solution.py:329
  57.2 5.8 %collective-permute-done.15.d_ref = f32[48,128]{1,0:T(8,128)S(1)} collective-permute-done((f32[48,128]{1,0:T(8,128)S(1)}, f32[48,128]{1,0:T(8,128)S(1)}, u32[]{:S(2)}, u32[]{:S(2)}) %collective-permute-start.15) | collective-permute-done | bytes 24608 | tf_op jit(solution)/shard_map/ppermute | solution.py:329
  63.2 9.7 %shard_map.99 = (f32[48,256]{1,0:T(8,128)S(1)}, f32[48,128]{1,0:T(8,128)S(1)}, f32[288,128]{1,0:T(8,128)S(1)}, f32[192,128]{1,0:T(8,128)S(1)}, f32[192,128]{1,0:T(8,128)S(1)}) custom-call(s32[8,128]{1,0:T(8,128)S(1)} %get-tuple-element.28.meta_ref.label_ref, bf16[384,768]{1,0:T(8,128)(2,1)S(1)} %get-tuple-element.29.onehot_ref, f32[192,48]{1,0:T(8,128)S(1)} %copy-done.7, ...), custom_call_target="tpu_custom_call" | custom-call | tf_op jit(solution)/shard_map/pallas_call | solution.py:301
  72.8 2.6 %collective-permute-start.19 = (f32[48,128]{1,0:T(8,128)S(1)}, f32[48,128]{1,0:T(8,128)S(1)}, u32[]{:S(2)}, u32[]{:S(2)}) collective-permute-start(f32[48,128]{1,0:T(8,128)S(1)} %get-tuple-element.40), channel_id=1, source_target_pairs={{0,30},{1,31},{2,0},{3,1},{4,2},{5,3},{6,4},{7,5},{8,6},{9,7},{10,... | collective-permute-start | bytes 73736 | tf_op jit(solution)/shard_map/ppermute | solution.py:329
  77.0 3.5 %collective-permute-done.18.c_ref = f32[48,128]{1,0:T(8,128)S(1)} collective-permute-done((f32[48,128]{1,0:T(8,128)S(1)}, f32[48,128]{1,0:T(8,128)S(1)}, u32[]{:S(2)}, u32[]{:S(2)}) %collective-permute-start.18) | collective-permute-done | bytes 24608 | tf_op jit(solution)/shard_map/ppermute | solution.py:329
  80.5 2.4 %collective-permute-done.17.b_ref = f32[48,128]{1,0:T(8,128)S(1)} collective-permute-done((f32[48,128]{1,0:T(8,128)S(1)}, f32[48,128]{1,0:T(8,128)S(1)}, u32[]{:S(2)}, u32[]{:S(2)}) %collective-permute-start.17) | collective-permute-done | bytes 24608 | tf_op jit(solution)/shard_map/ppermute | solution.py:329
  83.9 1.1 %collective-permute-start.21 = (f32[48,128]{1,0:T(8,128)S(1)}, f32[48,128]{1,0:T(8,128)S(1)}, u32[]{:S(2)}, u32[]{:S(2)}) collective-permute-start(f32[48,128]{1,0:T(8,128)S(1)} %get-tuple-element.42), channel_id=1, source_target_pairs={{0,31},{1,2},{2,1},{3,4},{4,3},{5,6},{6,5},{7,8},{8,7},{9,10},{10,... | collective-permute-start | bytes 73736 | tf_op jit(solution)/shard_map/ppermute | solution.py:329
  85.0 5.8 %collective-permute-done.23.d_ref = f32[48,128]{1,0:T(8,128)S(1)} collective-permute-done((f32[48,128]{1,0:T(8,128)S(1)}, f32[48,128]{1,0:T(8,128)S(1)}, u32[]{:S(2)}, u32[]{:S(2)}) %collective-permute-start.23) | collective-permute-done | bytes 24608 | tf_op jit(solution)/shard_map/ppermute | solution.py:329
  91.0 8.7 %shard_map.101 = (f32[192,128]{1,0:T(8,128)S(1)}, f32[32,1,128]{2,1,0:T(1,128)S(1)}) custom-call(s32[8,128]{1,0:T(8,128)S(1)} %get-tuple-element.28.meta_ref.label_ref, bf16[384,768]{1,0:T(8,128)(2,1)S(1)} %get-tuple-element.29.onehot_ref, f32[192,48]{1,0:T(8,128)S(1)} %copy-done.7, f32[4096,128]{1,0:T(8,128)S(1)} %bitcast.17, f32[6144,128]{1,0:T(8,128)S(1)} %bitcast.10, ...), custom_call_target="tpu_custom_call" | custom-call | tf_op jit(solution)/shard_map/pallas_call | solution.py:311
  99.7 9.9 %all_to_all.5.moment_ref = f32[32,1,128]{2,1,0:T(1,128)S(1)} all-to-all(f32[32,1,128]{2,1,0:T(1,128)S(1)} %get-tuple-element.47), channel_id=1, replica_groups=mesh['dom'=16,'blk'=2] {'dom','blk'}, dimensions={0} | all-to-all | bytes 32768 | tf_op jit(solution)/shard_map/all_to_all | solution.py:396
  109.6 1.8 %shard_map.102 = (f32[48,256]{1,0:T(8,128)}, f32[192,128]{1,0:T(8,128)}) custom-call(f32[32,1,128]{2,1,0:T(1,128)S(1)} %all_to_all.5.moment_ref, f32[48,256]{1,0:T(8,128)S(1)} %get-tuple-element.32.field_ref.k0_ref, f32[48,256]{1,0:T(8,128)S(1)} %get-tuple-element.37.field_ref.k1_ref, f32[48,256]{1,0:T(8,128)S(1)} %get-tuple-element.41.k2_ref, ...), custom_call_target="tpu_custom_call" | custom-call | tf_op jit(solution)/shard_map/pallas_call | solution.py:301
  (47 shorter events, 5.3 us)
Async XLA Ops:
  0.6 32.6 %copy-start.7 = (f32[192,48]{1,0:T(8,128)S(1)}, f32[192,48]{1,0:T(8,128)}, u32[]{:S(2)}) copy-start(f32[192,48]{1,0:T(8,128)} %constant.5.clone.forth_ref) | copy-start | bytes 110596
  2.5 1.9 %copy-start = (f32[64,96,128]{2,1,0:T(8,128)S(1)}, f32[64,96,128]{2,1,0:T(8,128)}, u32[]{:S(2)}) copy-start(f32[64,96,128]{2,1,0:T(8,128)} %param.9) | copy-start | bytes 9437188
  4.4 1.6 %copy-start.4 = (f32[64,64,128]{2,1,0:T(8,128)S(1)}, f32[64,64,128]{2,1,0:T(8,128)}, u32[]{:S(2)}) copy-start(f32[64,64,128]{2,1,0:T(8,128)} %param.10) | copy-start | bytes 6291460
  6.0 0.9 copy-start.6
  7.8 25.5 %copy-start.1 = (f32[64,96,128]{2,1,0:T(8,128)S(1)}, f32[64,96,128]{2,1,0:T(8,128)}, u32[]{:S(2)}) copy-start(f32[64,96,128]{2,1,0:T(8,128)} %param.9) | copy-start | bytes 9437188
  7.8 25.5 %copy-start.5 = (f32[64,64,128]{2,1,0:T(8,128)S(1)}, f32[64,64,128]{2,1,0:T(8,128)}, u32[]{:S(2)}) copy-start(f32[64,64,128]{2,1,0:T(8,128)} %param.10) | copy-start | bytes 6291460
  10.9 8.5 %collective-permute-start.3 = (f32[56,128]{1,0:T(8,128)S(1)}, f32[56,128]{1,0:T(8,128)S(1)}, u32[]{:S(2)}, u32[]{:S(2)}) collective-permute-start(f32[56,128]{1,0:T(8,128)S(1)} %get-tuple-element.31), channel_id=1, source_target_pairs={{0,30},{1,31},{2,0},{3,1},{4,2},{5,3},{6,4},{7,5},{8,6},{9,7},{10,... | collective-permute-start | bytes 86024 | tf_op jit(solution)/shard_map/ppermute | solution.py:329
  17.9 4.8 %collective-permute-start.2 = (f32[56,128]{1,0:T(8,128)S(1)}, f32[56,128]{1,0:T(8,128)S(1)}, u32[]{:S(2)}, u32[]{:S(2)}) collective-permute-start(f32[56,128]{1,0:T(8,128)S(1)} %get-tuple-element.31), channel_id=1, source_target_pairs={{0,16},{1,17},{2,18},{3,19},{4,20},{5,21},{6,22},{7,23},{8,24},{9,... | collective-permute-start | bytes 86024 | tf_op jit(solution)/shard_map/ppermute | solution.py:329
  17.9 6.9 %collective-permute-start.1 = (f32[56,128]{1,0:T(8,128)S(1)}, f32[56,128]{1,0:T(8,128)S(1)}, u32[]{:S(2)}, u32[]{:S(2)}) collective-permute-start(f32[56,128]{1,0:T(8,128)S(1)} %get-tuple-element.31), channel_id=1, source_target_pairs={{0,31},{1,2},{2,1},{3,4},{4,3},{5,6},{6,5},{7,8},{8,7},{9,10},{10,... | collective-permute-start | bytes 86024 | tf_op jit(solution)/shard_map/ppermute | solution.py:329
  17.9 6.9 %collective-permute-start = (f32[56,128]{1,0:T(8,128)S(1)}, f32[56,128]{1,0:T(8,128)S(1)}, u32[]{:S(2)}, u32[]{:S(2)}) collective-permute-start(f32[56,128]{1,0:T(8,128)S(1)} %get-tuple-element.31), channel_id=1, source_target_pairs={{0,1},{1,0},{2,3},{3,2},{4,5},{5,4},{6,7},{7,6},{8,9},{9,8},{10,11... | collective-permute-start | bytes 86024 | tf_op jit(solution)/shard_map/ppermute | solution.py:329
  25.2 7.5 %collective-permute-start.7 = (f32[48,128]{1,0:T(8,128)S(1)}, f32[48,128]{1,0:T(8,128)S(1)}, u32[]{:S(2)}, u32[]{:S(2)}) collective-permute-start(f32[48,128]{1,0:T(8,128)S(1)} %get-tuple-element.34), channel_id=1, source_target_pairs={{0,2},{1,3},{2,4},{3,5},{4,6},{5,7},{6,8},{7,9},{8,10},{9,11},{10,... | collective-permute-start | bytes 73736 | tf_op jit(solution)/shard_map/ppermute | solution.py:329
  25.2 7.4 %collective-permute-start.6 = (f32[48,128]{1,0:T(8,128)S(1)}, f32[48,128]{1,0:T(8,128)S(1)}, u32[]{:S(2)}, u32[]{:S(2)}) collective-permute-start(f32[48,128]{1,0:T(8,128)S(1)} %get-tuple-element.34), channel_id=1, source_target_pairs={{0,16},{1,17},{2,18},{3,19},{4,20},{5,21},{6,22},{7,23},{8,24},{9,... | collective-permute-start | bytes 73736 | tf_op jit(solution)/shard_map/ppermute | solution.py:329
  26.4 6.8 %collective-permute-start.5 = (f32[48,128]{1,0:T(8,128)S(1)}, f32[48,128]{1,0:T(8,128)S(1)}, u32[]{:S(2)}, u32[]{:S(2)}) collective-permute-start(f32[48,128]{1,0:T(8,128)S(1)} %get-tuple-element.34), channel_id=1, source_target_pairs={{0,31},{1,2},{2,1},{3,4},{4,3},{5,6},{6,5},{7,8},{8,7},{9,10},{10,... | collective-permute-start | bytes 73736 | tf_op jit(solution)/shard_map/ppermute | solution.py:329
  27.6 5.7 %collective-permute-start.4 = (f32[48,128]{1,0:T(8,128)S(1)}, f32[48,128]{1,0:T(8,128)S(1)}, u32[]{:S(2)}, u32[]{:S(2)}) collective-permute-start(f32[48,128]{1,0:T(8,128)S(1)} %get-tuple-element.34), channel_id=1, source_target_pairs={{0,1},{1,0},{2,3},{3,2},{4,5},{5,4},{6,7},{7,6},{8,9},{9,8},{10,11... | collective-permute-start | bytes 73736 | tf_op jit(solution)/shard_map/ppermute | solution.py:329
  33.3 2.3 %copy-start.2 = (f32[96,96,128]{2,1,0:T(8,128)S(1)}, f32[96,96,128]{2,1,0:T(8,128)}, u32[]{:S(2)}) copy-start(f32[96,96,128]{2,1,0:T(8,128)} %param.8) | copy-start | bytes 14155780
  35.6 27.6 %copy-start.3 = (f32[96,96,128]{2,1,0:T(8,128)S(1)}, f32[96,96,128]{2,1,0:T(8,128)}, u32[]{:S(2)}) copy-start(f32[96,96,128]{2,1,0:T(8,128)} %param.8) | copy-start | bytes 14155780
  45.3 3.9 %collective-permute-start.11 = (f32[48,128]{1,0:T(8,128)S(1)}, f32[48,128]{1,0:T(8,128)S(1)}, u32[]{:S(2)}, u32[]{:S(2)}) collective-permute-start(f32[48,128]{1,0:T(8,128)S(1)} %get-tuple-element.36), channel_id=1, source_target_pairs={{0,30},{1,31},{2,0},{3,1},{4,2},{5,3},{6,4},{7,5},{8,6},{9,7},{10,... | collective-permute-start | bytes 73736 | tf_op jit(solution)/shard_map/ppermute | solution.py:329
  47.6 5.0 %collective-permute-start.10 = (f32[48,128]{1,0:T(8,128)S(1)}, f32[48,128]{1,0:T(8,128)S(1)}, u32[]{:S(2)}, u32[]{:S(2)}) collective-permute-start(f32[48,128]{1,0:T(8,128)S(1)} %get-tuple-element.36), channel_id=1, source_target_pairs={{0,16},{1,17},{2,18},{3,19},{4,20},{5,21},{6,22},{7,23},{8,24},{9,... | collective-permute-start | bytes 73736 | tf_op jit(solution)/shard_map/ppermute | solution.py:329
  48.2 6.8 %collective-permute-start.9 = (f32[48,128]{1,0:T(8,128)S(1)}, f32[48,128]{1,0:T(8,128)S(1)}, u32[]{:S(2)}, u32[]{:S(2)}) collective-permute-start(f32[48,128]{1,0:T(8,128)S(1)} %get-tuple-element.36), channel_id=1, source_target_pairs={{0,31},{1,2},{2,1},{3,4},{4,3},{5,6},{6,5},{7,8},{8,7},{9,10},{10,... | collective-permute-start | bytes 73736 | tf_op jit(solution)/shard_map/ppermute | solution.py:329
  48.5 6.5 %collective-permute-start.8 = (f32[48,128]{1,0:T(8,128)S(1)}, f32[48,128]{1,0:T(8,128)S(1)}, u32[]{:S(2)}, u32[]{:S(2)}) collective-permute-start(f32[48,128]{1,0:T(8,128)S(1)} %get-tuple-element.36), channel_id=1, source_target_pairs={{0,1},{1,0},{2,3},{3,2},{4,5},{5,4},{6,7},{7,6},{8,9},{9,8},{10,11... | collective-permute-start | bytes 73736 | tf_op jit(solution)/shard_map/ppermute | solution.py:329
  55.3 7.6 %collective-permute-start.15 = (f32[48,128]{1,0:T(8,128)S(1)}, f32[48,128]{1,0:T(8,128)S(1)}, u32[]{:S(2)}, u32[]{:S(2)}) collective-permute-start(f32[48,128]{1,0:T(8,128)S(1)} %get-tuple-element.38), channel_id=1, source_target_pairs={{0,2},{1,3},{2,4},{3,5},{4,6},{5,7},{6,8},{7,9},{8,10},{9,11},{10,... | collective-permute-start | bytes 73736 | tf_op jit(solution)/shard_map/ppermute | solution.py:329
  55.4 7.6 %collective-permute-start.14 = (f32[48,128]{1,0:T(8,128)S(1)}, f32[48,128]{1,0:T(8,128)S(1)}, u32[]{:S(2)}, u32[]{:S(2)}) collective-permute-start(f32[48,128]{1,0:T(8,128)S(1)} %get-tuple-element.38), channel_id=1, source_target_pairs={{0,16},{1,17},{2,18},{3,19},{4,20},{5,21},{6,22},{7,23},{8,24},{9,... | collective-permute-start | bytes 73736 | tf_op jit(solution)/shard_map/ppermute | solution.py:329
  56.1 7.1 %collective-permute-start.13 = (f32[48,128]{1,0:T(8,128)S(1)}, f32[48,128]{1,0:T(8,128)S(1)}, u32[]{:S(2)}, u32[]{:S(2)}) collective-permute-start(f32[48,128]{1,0:T(8,128)S(1)} %get-tuple-element.38), channel_id=1, source_target_pairs={{0,31},{1,2},{2,1},{3,4},{4,3},{5,6},{6,5},{7,8},{8,7},{9,10},{10,... | collective-permute-start | bytes 73736 | tf_op jit(solution)/shard_map/ppermute | solution.py:329
  57.2 6.0 %collective-permute-start.12 = (f32[48,128]{1,0:T(8,128)S(1)}, f32[48,128]{1,0:T(8,128)S(1)}, u32[]{:S(2)}, u32[]{:S(2)}) collective-permute-start(f32[48,128]{1,0:T(8,128)S(1)} %get-tuple-element.38), channel_id=1, source_target_pairs={{0,1},{1,0},{2,3},{3,2},{4,5},{5,4},{6,7},{7,6},{8,9},{9,8},{10,11... | collective-permute-start | bytes 73736 | tf_op jit(solution)/shard_map/ppermute | solution.py:329
  72.8 4.1 %collective-permute-start.19 = (f32[48,128]{1,0:T(8,128)S(1)}, f32[48,128]{1,0:T(8,128)S(1)}, u32[]{:S(2)}, u32[]{:S(2)}) collective-permute-start(f32[48,128]{1,0:T(8,128)S(1)} %get-tuple-element.40), channel_id=1, source_target_pairs={{0,30},{1,31},{2,0},{3,1},{4,2},{5,3},{6,4},{7,5},{8,6},{9,7},{10,... | collective-permute-start | bytes 73736 | tf_op jit(solution)/shard_map/ppermute | solution.py:329
  75.5 5.0 %collective-permute-start.18 = (f32[48,128]{1,0:T(8,128)S(1)}, f32[48,128]{1,0:T(8,128)S(1)}, u32[]{:S(2)}, u32[]{:S(2)}) collective-permute-start(f32[48,128]{1,0:T(8,128)S(1)} %get-tuple-element.40), channel_id=1, source_target_pairs={{0,16},{1,17},{2,18},{3,19},{4,20},{5,21},{6,22},{7,23},{8,24},{9,... | collective-permute-start | bytes 73736 | tf_op jit(solution)/shard_map/ppermute | solution.py:329
  76.0 6.9 %collective-permute-start.17 = (f32[48,128]{1,0:T(8,128)S(1)}, f32[48,128]{1,0:T(8,128)S(1)}, u32[]{:S(2)}, u32[]{:S(2)}) collective-permute-start(f32[48,128]{1,0:T(8,128)S(1)} %get-tuple-element.40), channel_id=1, source_target_pairs={{0,31},{1,2},{2,1},{3,4},{4,3},{5,6},{6,5},{7,8},{8,7},{9,10},{10,... | collective-permute-start | bytes 73736 | tf_op jit(solution)/shard_map/ppermute | solution.py:329
  76.3 6.5 %collective-permute-start.16 = (f32[48,128]{1,0:T(8,128)S(1)}, f32[48,128]{1,0:T(8,128)S(1)}, u32[]{:S(2)}, u32[]{:S(2)}) collective-permute-start(f32[48,128]{1,0:T(8,128)S(1)} %get-tuple-element.40), channel_id=1, source_target_pairs={{0,1},{1,0},{2,3},{3,2},{4,5},{5,4},{6,7},{7,6},{8,9},{9,8},{10,11... | collective-permute-start | bytes 73736 | tf_op jit(solution)/shard_map/ppermute | solution.py:329
  83.2 7.7 %collective-permute-start.23 = (f32[48,128]{1,0:T(8,128)S(1)}, f32[48,128]{1,0:T(8,128)S(1)}, u32[]{:S(2)}, u32[]{:S(2)}) collective-permute-start(f32[48,128]{1,0:T(8,128)S(1)} %get-tuple-element.42), channel_id=1, source_target_pairs={{0,2},{1,3},{2,4},{3,5},{4,6},{5,7},{6,8},{7,9},{8,10},{9,11},{10,... | collective-permute-start | bytes 73736 | tf_op jit(solution)/shard_map/ppermute | solution.py:329
  83.2 7.6 %collective-permute-start.22 = (f32[48,128]{1,0:T(8,128)S(1)}, f32[48,128]{1,0:T(8,128)S(1)}, u32[]{:S(2)}, u32[]{:S(2)}) collective-permute-start(f32[48,128]{1,0:T(8,128)S(1)} %get-tuple-element.42), channel_id=1, source_target_pairs={{0,16},{1,17},{2,18},{3,19},{4,20},{5,21},{6,22},{7,23},{8,24},{9,... | collective-permute-start | bytes 73736 | tf_op jit(solution)/shard_map/ppermute | solution.py:329
  83.9 7.1 %collective-permute-start.21 = (f32[48,128]{1,0:T(8,128)S(1)}, f32[48,128]{1,0:T(8,128)S(1)}, u32[]{:S(2)}, u32[]{:S(2)}) collective-permute-start(f32[48,128]{1,0:T(8,128)S(1)} %get-tuple-element.42), channel_id=1, source_target_pairs={{0,31},{1,2},{2,1},{3,4},{4,3},{5,6},{6,5},{7,8},{8,7},{9,10},{10,... | collective-permute-start | bytes 73736 | tf_op jit(solution)/shard_map/ppermute | solution.py:329
  85.0 6.0 %collective-permute-start.20 = (f32[48,128]{1,0:T(8,128)S(1)}, f32[48,128]{1,0:T(8,128)S(1)}, u32[]{:S(2)}, u32[]{:S(2)}) collective-permute-start(f32[48,128]{1,0:T(8,128)S(1)} %get-tuple-element.42), channel_id=1, source_target_pairs={{0,1},{1,0},{2,3},{3,2},{4,5},{5,4},{6,7},{7,6},{8,9},{9,8},{10,11... | collective-permute-start | bytes 73736 | tf_op jit(solution)/shard_map/ppermute | solution.py:329
  (1 other events, 0.9 us)
where the time goes:
time: 112 us; the launch traced here: 111 us
  waiting for transfers between devices  37.5 us (33%)
  Pallas kernels  33.9 us (30%)
  starting transfers between devices  19.8 us (18%)
  blocking collectives  9.92 us (9%)
  local copies, waits for them, and re-layouts  9.44 us (8%)
    ppermute x24, waiting for transfers between devices, exchange(): return [lax.ppermute(block, AXES, p) for p in pairs]  37.5 us
    pallas_call x7, Pallas kernels, call(): pl.pallas_call(kernel, out_shape=[jax.ShapeDtypeStruct(shape, dtype) for...  25.2 us
    ppermute x24, starting transfers between devices, exchange(): return [lax.ppermute(block, AXES, p) for p in pairs]  19.8 us
    all_to_all x1, blocking collectives, local(): lax.all_to_all(moments, AXES, split_axis=0, concat_axis=0, tiled=True)  9.92 us
    pallas_call x1, Pallas kernels, call_scratch(): pl.pallas_call(kernel, out_shape=[jax.ShapeDtypeStruct(shape, dtype) for...  8.7 us
    unnamed x18, local copies, waits for them, and re-layouts  7.64 us
  transfers between devices with their start and end apart: 24, of which 15 were waited for; matrix products, arithmetic and copies ran while one was open for 0% of the time, Pallas kernels for 0%

commit v1 on v0

--- a/solution.py
+++ b/solution.py
@@ -82,24 +82,64 @@
     return x
 
 
-def lanes(rows_ref, start, count=FACES):
-    return jnp.concatenate([rows_ref[start + f : start + f + 1, :] for f in range(count)], axis=1)
-
-
-def contract(acc, mat_ref, vec_ref, outs, terms, across, unroll=8):
-    blocks = outs // 8
-
+def in_a_row(x):
+    return jnp.concatenate([x[r : r + 1, :] for r in range(x.shape[0])], axis=1)
+
+
+def gather_rows(tiles, sublane):
+    tiles = [tiles[r] for r in (0, 4, 2, 6, 1, 5, 3, 7)]
+    keep = (sublane & 4) == 0
+    tiles = [
+        jnp.where(keep, x, y) + pltpu.roll(jnp.where(keep, y, x), 4, 0)
+        for x, y in zip(tiles[::2], tiles[1::2])
+    ]
+    for shift in (2, 1):
+        keep = (sublane & shift) == 0
+        tiles = [
+            jnp.where(keep, x + pltpu.roll(x, 8 - shift, 0), y + pltpu.roll(y, shift, 0))
+            for x, y in zip(tiles[::2], tiles[1::2])
+        ]
+    return tiles[0]
+
+
+def rows_times(mat_ref, vec_ref, out_ref, outs, terms, group=32):
+    width = vec_ref.shape[1]
+    sublane = lax.broadcasted_iota(jnp.int32, (8, width), 0)
+    vecs = [
+        [vec_ref[c * terms + t : c * terms + t + 8, :] for t in range(0, terms, 8)]
+        for c in range(COMP)
+    ]
+
+    def body(g, carry):
+        for first in range(0, group, 8):
+            sums = [[] for _ in range(COMP)]
+            for r in range(first, first + 8):
+                acc = [None] * COMP
+                for j in range(terms // 8):
+                    start = pl.multiple_of((g * group + r) * terms + 8 * j, 8)
+                    tile = mat_ref[pl.ds(start, 8), :]
+                    for c in range(COMP):
+                        term = tile * vecs[c][j]
+                        acc[c] = term if j == 0 else acc[c] + term
+                for c in range(COMP):
+                    sums[c].append(acc[c])
+            for c in range(COMP):
+                start = pl.multiple_of(c * outs + g * group + first, 8)
+                out_ref[pl.ds(start, 8), :] = gather_rows(sums[c], sublane)
+        return carry
+
+    lax.fori_loop(0, outs // group, body, 0)
+
+
+def columns_times(acc, mat_ref, vec_ref, outs, terms, unroll=16):
     def body(t, acc):
         acc = [list(a) for a in acc]
         vecs = [
             jnp.broadcast_to(vec_ref[pl.ds(c * terms + t, 1), :], (8, vec_ref.shape[1]))
             for c in range(COMP)
         ]
-        for j in range(blocks):
-            if across:
-                tile = mat_ref[pl.ds(j * 8 * terms + t, 8, stride=terms), :]
-            else:
-                tile = mat_ref[pl.ds(pl.multiple_of(t * outs + j * 8, 8), 8), :]
+        for j in range(outs // 8):
+            tile = mat_ref[pl.ds(pl.multiple_of(t * outs + j * 8, 8), 8), :]
             for c in range(COMP):
                 acc[c][j] = acc[c][j] + tile * vecs[c]
         return acc
@@ -107,15 +147,12 @@
     return lax.fori_loop(0, terms, body, acc, unroll=unroll)
 
 
+def tiles_of(ref, outs):
+    return [[ref[c * outs + t : c * outs + t + 8, :] for t in range(0, outs, 8)] for c in range(COMP)]
+
+
 def zeros(outs, width):
     return [[jnp.zeros((8, width), F32) for _ in range(outs // 8)] for _ in range(COMP)]
-
-
-def put(ref, acc):
-    outs = 8 * len(acc[0])
-    for c in range(COMP):
-        for j, tile in enumerate(acc[c]):
-            ref[c * outs + 8 * j : c * outs + 8 * j + 8, :] = tile
 
 
 def face_columns(acc):
@@ -133,17 +170,31 @@
 
 def start_kernel(
     ranks, inner, trace, owned, cap,
-    mortar_ref, kind_ref, inverse_ref, couple_ref, force_ref, back_ref,
-    own_ref, out_ref, onehot_ref, meta_ref, load_ref,
+    mortar_hbm, kind_hbm, force_hbm, back_hbm, inverse_hbm, couple_hbm,
+    own_ref, out_ref, onehot_ref, meta_ref, load_ref, inverse_ref, couple_ref,
+    mortar_ref, kind_ref, force_ref, back_ref, *sems,
 ):
+    copies = [
+        pltpu.make_async_copy(source, target, sem)
+        for source, target, sem in zip(
+            (mortar_hbm, kind_hbm, force_hbm, back_hbm, inverse_hbm, couple_hbm),
+            (mortar_ref, kind_ref, force_ref, back_ref, inverse_ref, couple_ref),
+            sems,
+        )
+    ]
+    for copy in copies:
+        copy.start()
+    copies[0].wait()
+    copies[1].wait()
     width = mortar_ref.shape[1]
+    slots = FACES * width
     mortar = mortar_ref[...]
     owner = lax.div(mortar, owned)
     index = lax.rem(mortar, owned)
     me = lax.rem(owner[0:1, 0:1] + 2, ranks)
     distance = lax.rem(owner - me + ranks, ranks)
-    slot = lax.broadcasted_iota(jnp.int32, mortar.shape, 1) * FACES + lax.broadcasted_iota(
-        jnp.int32, mortar.shape, 0
+    slot = lax.broadcasted_iota(jnp.int32, mortar.shape, 0) * width + lax.broadcasted_iota(
+        jnp.int32, mortar.shape, 1
     )
     column = index
     begin = jnp.zeros((1, 1), jnp.int32)
@@ -154,22 +205,32 @@
             run = number - (number > 2)
             column = jnp.where(inside, owned + run * cap + slot - begin, column)
         begin = begin + count
-    meta_ref[0:FACES, :] = kind_ref[...]
-    meta_ref[FACES : FACES + 1, :] = jnp.broadcast_to(lax.rem(me, 2), (1, width))
-    meta_ref[FACES + 1 : FACES + 2, :] = jnp.zeros((1, width), jnp.int32)
-    rows = owned + RUNS * cap
-    for f in range(FACES):
-        onehot_ref[:, f * width : (f + 1) * width] = jnp.where(
-            lax.broadcasted_iota(jnp.int32, (rows, width), 0) == column[f : f + 1, :], 1.0, 0.0
-        ).astype(BF16)
-    load = contract(zeros(inner, width), inverse_ref, force_ref, inner, inner, True)
-    put(load_ref, load)
-    y = contract(zeros(trace, width), couple_ref, load_ref, trace, inner, False)
-    z = by_kind(face_columns(y), back_ref, lanes(kind_ref, 0))
-    label = jnp.concatenate([index[f : f + 1, :] for f in range(FACES)], axis=1) + 1
+    target = lax.broadcasted_iota(jnp.int32, (1, slots), 1)
+    target = lax.rem(target, width) * FACES + lax.div(target, width)
+    order = jnp.where(
+        lax.broadcasted_iota(jnp.int32, (slots, slots), 0) == target, 1.0, 0.0
+    ).astype(BF16)
+    facts = jnp.concatenate(
+        [in_a_row(column), in_a_row(index + 1), in_a_row(kind_ref[...]), jnp.zeros((5, slots), jnp.int32)],
+        axis=0,
+    ).astype(F32)
+    facts = exact_dot(facts, order)
+    meta_ref[...] = facts
+    meta_ref[3:4, :] = jnp.broadcast_to(lax.rem(me, 2).astype(F32), (1, slots))
+    column = facts[0:1, :].astype(jnp.int32)
+    onehot_ref[...] = jnp.where(
+        lax.broadcasted_iota(jnp.int32, onehot_ref.shape, 0) == column, 1.0, 0.0
+    ).astype(BF16)
+    copies[2].wait()
+    copies[4].wait()
+    rows_times(inverse_ref, force_ref, load_ref, inner, inner)
+    copies[3].wait()
+    copies[5].wait()
+    y = columns_times(zeros(trace, width), couple_ref, load_ref, trace, inner)
+    z = by_kind(face_columns(y), back_ref, facts[2:3, :])
     label = jnp.where(
-        lax.broadcasted_iota(jnp.int32, (8, z.shape[1]), 0) == 0, label, 0
-    ).astype(F32)
+        lax.broadcasted_iota(jnp.int32, (8, slots), 0) == 0, facts[1:2, :], 0.0
+    )
     sums = exact_dot(jnp.concatenate([z, label], axis=0), onehot_ref[...], 1)
     own_ref[...] = sums[: COMP * NODES, :owned]
     out_ref[...] = sums[:, owned:]
@@ -177,7 +238,7 @@
 
 def merged(meta_ref, first, second, third, fourth, cap, to_owner):
     lane = lax.broadcasted_iota(jnp.int32, (1, RUNS * cap), 1)
-    odd = meta_ref[FACES : FACES + 1, :] == 1
+    odd = meta_ref[3:4, : RUNS * cap] == 1.0
     low = lane < 2 * cap
     take_first = (low != odd) if to_owner else (low == odd)
     middle = jnp.where(take_first, first, second)
@@ -207,7 +268,7 @@
 def element_values(cap, meta_ref, onehot_ref, forth_ref, field_ref, blocks, spread_ref):
     received = merged(meta_ref, *[b[...] for b in blocks], cap, False)
     source = jnp.concatenate([field_ref[...], received], axis=1)
-    kind = lanes(meta_ref, 0)
+    kind = meta_ref[2:3, :]
     faces = by_kind(exact_dot(source, onehot_ref[...]), forth_ref, kind)
     width = spread_ref.shape[1]
     for c in range(COMP):
@@ -220,18 +281,21 @@
 
 def apply_kernel(
     inner, trace, owned, cap,
-    meta_ref, onehot_ref, forth_ref, back_ref, inverse_ref, couple_ref, self_ref,
-    field_ref, a_ref, b_ref, c_ref, d_ref,
-    own_ref, out_ref, spread_ref, mid_ref, weight_ref,
+    meta_ref, onehot_ref, forth_ref, back_ref, inverse_ref, couple_ref,
+    field_ref, a_ref, b_ref, c_ref, d_ref, self_hbm,
+    own_ref, out_ref, spread_ref, mid_ref, weight_ref, image_ref, self_ref, sem,
 ):
+    copy = pltpu.make_async_copy(self_hbm, self_ref, sem)
+    copy.start()
     width = spread_ref.shape[1]
     kind = element_values(
         cap, meta_ref, onehot_ref, forth_ref, field_ref, (a_ref, b_ref, c_ref, d_ref), spread_ref
     )
-    put(mid_ref, contract(zeros(inner, width), couple_ref, spread_ref, inner, trace, True))
-    put(weight_ref, contract(zeros(inner, width), inverse_ref, mid_ref, inner, inner, True))
-    y = contract(zeros(trace, width), self_ref, spread_ref, trace, trace, True)
-    y = contract(y, couple_ref, weight_ref, trace, inner, False)
+    rows_times(couple_ref, spread_ref, mid_ref, inner, trace)
+    rows_times(inverse_ref, mid_ref, weight_ref, inner, inner)
+    copy.wait()
+    rows_times(self_ref, spread_ref, image_ref, trace, trace)
+    y = columns_times(tiles_of(image_ref, trace), couple_ref, weight_ref, trace, inner)
     z = by_kind(face_columns(y), back_ref, kind)
     sums = exact_dot(z, onehot_ref[...], 1)
     own_ref[...] = sums[:, :owned]
@@ -244,17 +308,20 @@
 
 def last_kernel(
     inner, trace, cap,
-    meta_ref, onehot_ref, forth_ref, inverse_ref, couple_ref, self_ref,
-    k0_ref, k1_ref, k2_ref, a_ref, b_ref, c_ref, d_ref, s0_ref, s1_ref, u0_ref, u1_ref,
-    weight_ref, moment_ref, spread_ref, mid_ref, image_ref,
+    meta_ref, onehot_ref, forth_ref, inverse_ref, couple_ref,
+    k0_ref, k1_ref, k2_ref, a_ref, b_ref, c_ref, d_ref, s0_ref, s1_ref, u0_ref, u1_ref, self_hbm,
+    weight_ref, moment_ref, spread_ref, mid_ref, image_ref, self_ref, sem,
 ):
+    copy = pltpu.make_async_copy(self_hbm, self_ref, sem)
+    copy.start()
     width = spread_ref.shape[1]
     element_values(
         cap, meta_ref, onehot_ref, forth_ref, k2_ref, (a_ref, b_ref, c_ref, d_ref), spread_ref
     )
-    put(mid_ref, contract(zeros(inner, width), couple_ref, spread_ref, inner, trace, True))
-    put(weight_ref, contract(zeros(inner, width), inverse_ref, mid_ref, inner, inner, True))
-    put(image_ref, contract(zeros(trace, width), self_ref, spread_ref, trace, trace, True))
+    rows_times(couple_ref, spread_ref, mid_ref, inner, trace)
+    rows_times(inverse_ref, mid_ref, weight_ref, inner, inner)
+    copy.wait()
+    rows_times(self_ref, spread_ref, image_ref, trace, trace)
     image, weight = image_ref[...], weight_ref[...]
     ks = (k0_ref[...], k1_ref[...], k2_ref[...])
     values = [total(ks[i] * ks[j]) for i in range(3) for j in range(i, 3)]
@@ -297,24 +364,20 @@
     )
 
 
-def call(kernel, outs, *args):
+def call(kernel, outs, *args, scratch=(), in_hbm=0, vmem=8):
+    inside = len(args) - in_hbm
+    args = args[:inside] + tuple(
+        pltpu.with_memory_space_constraint(x, pltpu.HBM) for x in args[inside:]
+    )
     return pl.pallas_call(
         kernel,
         out_shape=[jax.ShapeDtypeStruct(shape, dtype) for shape, dtype in outs],
-        in_specs=[pl.BlockSpec(memory_space=pltpu.VMEM)] * len(args),
+        in_specs=[pl.BlockSpec(memory_space=pltpu.VMEM)] * inside
+        + [pl.BlockSpec(memory_space=pltpu.HBM)] * in_hbm,
         out_specs=[pl.BlockSpec(memory_space=pltpu.VMEM)] * len(outs),
-        compiler_params=pltpu.CompilerParams(vmem_limit_bytes=40 * 1024 * 1024),
-    )(*args)
-
-
-def call_scratch(kernel, outs, scratch, *args):
-    return pl.pallas_call(
-        kernel,
-        out_shape=[jax.ShapeDtypeStruct(shape, dtype) for shape, dtype in outs],
-        in_specs=[pl.BlockSpec(memory_space=pltpu.VMEM)] * len(args),
-        out_specs=[pl.BlockSpec(memory_space=pltpu.VMEM)] * len(outs),
-        scratch_shapes=[pltpu.VMEM(shape, F32) for shape in scratch],
-        compiler_params=pltpu.CompilerParams(vmem_limit_bytes=40 * 1024 * 1024),
+        scratch_shapes=[pltpu.VMEM(shape, dtype) for shape, dtype in scratch]
+        + [pltpu.SemaphoreType.DMA(())] * in_hbm,
+        compiler_params=pltpu.CompilerParams(vmem_limit_bytes=vmem * 1024 * 1024),
     )(*args)
 
 
@@ -337,23 +400,29 @@
     width = elements
     rows = COMP * NODES
     forward, backward = block_tables()
-    mortar = face_mortar.reshape(elements, FACES).T
-    kind = face_kind.reshape(elements, FACES).T
+    mortar = face_mortar.reshape(FACES, width)
+    kind = face_kind.reshape(FACES, width)
     self_block = self_block.reshape(trace * trace, width)
     couple = couple.reshape(inner * trace, width)
     inverse = inverse.reshape(inner * inner, width)
     force = body_force.reshape(COMP * inner, width)
 
-    own, out, onehot, meta, load = call(
+    own, out, onehot, meta, load, inverse_in, couple_in = call(
         functools.partial(start_kernel, ranks, inner, trace, owned, cap),
         [
             ((rows, owned), F32),
             ((rows + 8, RUNS * cap), F32),
             ((owned + RUNS * cap, FACES * width), BF16),
-            ((8, width), jnp.int32),
+            ((8, FACES * width), F32),
             ((COMP * inner, width), F32),
+            (inverse.shape, F32),
+            (couple.shape, F32),
         ],
-        mortar, kind, inverse, couple, force, backward,
+        mortar, kind, force, backward, inverse, couple,
+        scratch=[
+            (mortar.shape, jnp.int32), (kind.shape, jnp.int32), (force.shape, F32), (backward.shape, F32)
+        ],
+        in_hbm=6, vmem=16,
     )
     blocks = exchange(out, ranks, True)
     field, out, label = call(
@@ -373,7 +442,8 @@
                 ((COMP * inner, width), F32),
                 ((COMP * inner, width), F32),
             ],
-            meta, onehot, forward, backward, inverse, couple, self_block, field, *blocks,
+            meta, onehot, forward, backward, inverse_in, couple_in, field, *blocks, self_block,
+            scratch=[((COMP * trace, width), F32), (self_block.shape, F32)], in_hbm=1, vmem=12,
         )
         spreads.append(spread)
         mids.append(mid)
@@ -386,11 +456,17 @@
         )
         fields.append(field)
     blocks = exchange(out, ranks, False)
-    weight, moments = call_scratch(
+    weight, moments = call(
         functools.partial(last_kernel, inner, trace, cap),
         [((COMP * inner, width), F32), ((ranks, 1, width), F32)],
-        [(COMP * trace, width), (COMP * inner, width), (COMP * trace, width)],
-        meta, onehot, forward, inverse, couple, self_block, *fields, *blocks, *spreads, *mids,
+        meta, onehot, forward, inverse_in, couple_in, *fields, *blocks, *spreads, *mids, self_block,
+        scratch=[
+            ((COMP * trace, width), F32),
+            ((COMP * inner, width), F32),
+            ((COMP * trace, width), F32),
+            (self_block.shape, F32),
+        ],
+        in_hbm=1, vmem=12,
     )
     weights.append(weight)
     moments = lax.all_to_all(moments, AXES, split_axis=0, concat_axis=0, tiled=True)

time: 112 us -> 89 us (0.79)
  Pallas kernels: 33.9 us -> 20.7 us
  local copies, waits for them, and re-layouts: 9.44 us -> 0.01 us
    pallas_call x1 -> x0, Pallas kernels: 8.7 us -> none  [call_scratch(): pl.pallas_call(kernel, out_shape=[jax.ShapeDtypeStruct(shape, dtype) for...]
    unnamed x18 -> x4, local copies, waits for them, and re-layouts: 7.64 us -> 0.01 us
    pallas_call x7 -> x8, Pallas kernels: 25.2 us -> 20.7 us  [call(): pl.pallas_call(kernel, out_shape=[jax.ShapeDtypeStruct(shape, dtype) for...]
    reshape x4 -> x0, local copies, waits for them, and re-layouts: 1.8 us -> none  [the longest x2 0.91 us: local(): mortar = face_mortar.reshape(elements, FACES).T]
where the time goes in v1:
time: 89 us; the launch traced here: 88.7 us
  waiting for transfers between devices  37.5 us (42%)
  Pallas kernels  20.7 us (23%)
  starting transfers between devices  19.9 us (22%)
  blocking collectives  9.91 us (11%)
    ppermute x24, waiting for transfers between devices, exchange(): return [lax.ppermute(block, AXES, p) for p in pairs]  37.5 us
    pallas_call x8, Pallas kernels, call(): pl.pallas_call(kernel, out_shape=[jax.ShapeDtypeStruct(shape, dtype) for...  20.7 us
    ppermute x24, starting transfers between devices, exchange(): return [lax.ppermute(block, AXES, p) for p in pairs]  19.9 us
    all_to_all x1, blocking collectives, local(): lax.all_to_all(moments, AXES, split_axis=0, concat_axis=0, tiled=True)  9.91 us
  transfers between devices with their start and end apart: 24, of which 15 were waited for; matrix products, arithmetic and copies ran while one was open for 0% of the time, Pallas kernels for 0%

profile of v1, /device:TPU:0, one launch (start us, length us, event | category | flops | bytes accessed | tf_op | source)
XLA Modules:
  0.0 88.7 jit_solution(13993541801872645769)
XLA Ops:
  0.7 4.0 %shard_map.95 = (f32[48,256]{1,0:T(8,128)S(1)}, f32[56,128]{1,0:T(8,128)S(1)}, bf16[384,768]{1,0:T(8,128)(2,1)S(1)}, f32[8,768]{1,0:T(8,128)S(1)}, f32[192,128]{...) custom-call(s32[6,128]{1,0:T(8,128)} %bitcast.13, s32[6,128]{1,0:T(8,128)} %bitcast.14, ...), custom_call_target="tpu_custom_call" | custom-call | tf_op jit(solution)/shard_map/pallas_call | solution.py:372
  4.6 7.0 %collective-permute-start.3 = (f32[56,128]{1,0:T(8,128)S(1)}, f32[56,128]{1,0:T(8,128)S(1)}, u32[]{:S(2)}, u32[]{:S(2)}) collective-permute-start(f32[56,128]{1,0:T(8,128)S(1)} %get-tuple-element.35), channel_id=1, source_target_pairs={{0,30},{1,31},{2,0},{3,1},{4,2},{5,3},{6,4},{7,5},{8,6},{9,7},{10,... | collective-permute-start | bytes 86024 | tf_op jit(solution)/shard_map/ppermute | solution.py:392
  11.6 1.5 %collective-permute-done.3.d_ref = f32[56,128]{1,0:T(8,128)S(1)} collective-permute-done((f32[56,128]{1,0:T(8,128)S(1)}, f32[56,128]{1,0:T(8,128)S(1)}, u32[]{:S(2)}, u32[]{:S(2)}) %collective-permute-start.3) | collective-permute-done | bytes 28704 | tf_op jit(solution)/shard_map/ppermute | solution.py:392
  13.2 3.2 %collective-permute-done.2.c_ref = f32[56,128]{1,0:T(8,128)S(1)} collective-permute-done((f32[56,128]{1,0:T(8,128)S(1)}, f32[56,128]{1,0:T(8,128)S(1)}, u32[]{:S(2)}, u32[]{:S(2)}) %collective-permute-start.2) | collective-permute-done | bytes 28704 | tf_op jit(solution)/shard_map/ppermute | solution.py:392
  16.4 2.1 %collective-permute-done.1.b_ref = f32[56,128]{1,0:T(8,128)S(1)} collective-permute-done((f32[56,128]{1,0:T(8,128)S(1)}, f32[56,128]{1,0:T(8,128)S(1)}, u32[]{:S(2)}, u32[]{:S(2)}) %collective-permute-start.1) | collective-permute-done | bytes 28704 | tf_op jit(solution)/shard_map/ppermute | solution.py:392
  18.9 1.2 %collective-permute-start.6 = (f32[48,128]{1,0:T(8,128)S(1)}, f32[48,128]{1,0:T(8,128)S(1)}, u32[]{:S(2)}, u32[]{:S(2)}) collective-permute-start(f32[48,128]{1,0:T(8,128)S(1)} %get-tuple-element.38), channel_id=1, source_target_pairs={{0,16},{1,17},{2,18},{3,19},{4,20},{5,21},{6,22},{7,23},{8,24},{9,... | collective-permute-start | bytes 73736 | tf_op jit(solution)/shard_map/ppermute | solution.py:392
  20.1 1.2 %collective-permute-start.5 = (f32[48,128]{1,0:T(8,128)S(1)}, f32[48,128]{1,0:T(8,128)S(1)}, u32[]{:S(2)}, u32[]{:S(2)}) collective-permute-start(f32[48,128]{1,0:T(8,128)S(1)} %get-tuple-element.38), channel_id=1, source_target_pairs={{0,31},{1,2},{2,1},{3,4},{4,3},{5,6},{6,5},{7,8},{8,7},{9,10},{10,... | collective-permute-start | bytes 73736 | tf_op jit(solution)/shard_map/ppermute | solution.py:392
  21.3 5.0 %collective-permute-done.7.d_ref = f32[48,128]{1,0:T(8,128)S(1)} collective-permute-done((f32[48,128]{1,0:T(8,128)S(1)}, f32[48,128]{1,0:T(8,128)S(1)}, u32[]{:S(2)}, u32[]{:S(2)}) %collective-permute-start.7) | collective-permute-done | bytes 24608 | tf_op jit(solution)/shard_map/ppermute | solution.py:392
  26.3 0.6 collective-permute-done.5.b_ref
  27.0 4.9 %shard_map.97 = (f32[48,256]{1,0:T(8,128)S(1)}, f32[48,128]{1,0:T(8,128)S(1)}, f32[288,128]{1,0:T(8,128)S(1)}, f32[192,128]{1,0:T(8,128)S(1)}, f32[192,128]{1,0:T(8,128)S(1)}) custom-call(f32[8,768]{1,0:T(8,128)S(1)} %get-tuple-element.30.meta_ref.label_ref, bf16[384,768]{1,0:T(8,128)(2,1)S(1)} %get-tuple-element.31.onehot_ref, f32[192,48]{1,0:T(8,128)S(1)} %copy-done, ...), custom_call_target="tpu_custom_call" | custom-call | tf_op jit(solution)/shard_map/pallas_call | solution.py:372
  31.9 2.4 %collective-permute-start.11 = (f32[48,128]{1,0:T(8,128)S(1)}, f32[48,128]{1,0:T(8,128)S(1)}, u32[]{:S(2)}, u32[]{:S(2)}) collective-permute-start(f32[48,128]{1,0:T(8,128)S(1)} %get-tuple-element.40), channel_id=1, source_target_pairs={{0,30},{1,31},{2,0},{3,1},{4,2},{5,3},{6,4},{7,5},{8,6},{9,7},{10,... | collective-permute-start | bytes 73736 | tf_op jit(solution)/shard_map/ppermute | solution.py:392
  34.3 0.5 collective-permute-start.10
  34.8 0.3 collective-permute-start.9
  35.2 0.6 collective-permute-done.11.d_ref
  35.8 3.5 %collective-permute-done.10.c_ref = f32[48,128]{1,0:T(8,128)S(1)} collective-permute-done((f32[48,128]{1,0:T(8,128)S(1)}, f32[48,128]{1,0:T(8,128)S(1)}, u32[]{:S(2)}, u32[]{:S(2)}) %collective-permute-start.10) | collective-permute-done | bytes 24608 | tf_op jit(solution)/shard_map/ppermute | solution.py:392
  39.3 2.4 %collective-permute-done.9.b_ref = f32[48,128]{1,0:T(8,128)S(1)} collective-permute-done((f32[48,128]{1,0:T(8,128)S(1)}, f32[48,128]{1,0:T(8,128)S(1)}, u32[]{:S(2)}, u32[]{:S(2)}) %collective-permute-start.9) | collective-permute-done | bytes 24608 | tf_op jit(solution)/shard_map/ppermute | solution.py:392
  42.0 0.7 collective-permute-start.14
  42.7 1.1 %collective-permute-start.13 = (f32[48,128]{1,0:T(8,128)S(1)}, f32[48,128]{1,0:T(8,128)S(1)}, u32[]{:S(2)}, u32[]{:S(2)}) collective-permute-start(f32[48,128]{1,0:T(8,128)S(1)} %get-tuple-element.42), channel_id=1, source_target_pairs={{0,31},{1,2},{2,1},{3,4},{4,3},{5,6},{6,5},{7,8},{8,7},{9,10},{10,... | collective-permute-start | bytes 73736 | tf_op jit(solution)/shard_map/ppermute | solution.py:392
  43.8 5.8 %collective-permute-done.15.d_ref = f32[48,128]{1,0:T(8,128)S(1)} collective-permute-done((f32[48,128]{1,0:T(8,128)S(1)}, f32[48,128]{1,0:T(8,128)S(1)}, u32[]{:S(2)}, u32[]{:S(2)}) %collective-permute-start.15) | collective-permute-done | bytes 24608 | tf_op jit(solution)/shard_map/ppermute | solution.py:392
  49.8 4.9 %shard_map.99 = (f32[48,256]{1,0:T(8,128)S(1)}, f32[48,128]{1,0:T(8,128)S(1)}, f32[288,128]{1,0:T(8,128)S(1)}, f32[192,128]{1,0:T(8,128)S(1)}, f32[192,128]{1,0:T(8,128)S(1)}) custom-call(f32[8,768]{1,0:T(8,128)S(1)} %get-tuple-element.30.meta_ref.label_ref, bf16[384,768]{1,0:T(8,128)(2,1)S(1)} %get-tuple-element.31.onehot_ref, f32[192,48]{1,0:T(8,128)S(1)} %copy-done, ...), custom_call_target="tpu_custom_call" | custom-call | tf_op jit(solution)/shard_map/pallas_call | solution.py:372
  54.8 2.6 %collective-permute-start.19 = (f32[48,128]{1,0:T(8,128)S(1)}, f32[48,128]{1,0:T(8,128)S(1)}, u32[]{:S(2)}, u32[]{:S(2)}) collective-permute-start(f32[48,128]{1,0:T(8,128)S(1)} %get-tuple-element.44), channel_id=1, source_target_pairs={{0,30},{1,31},{2,0},{3,1},{4,2},{5,3},{6,4},{7,5},{8,6},{9,7},{10,... | collective-permute-start | bytes 73736 | tf_op jit(solution)/shard_map/ppermute | solution.py:392
  57.4 0.5 collective-permute-start.18
  57.9 0.3 collective-permute-start.17
  58.3 0.6 collective-permute-done.19.d_ref
  58.9 3.5 %collective-permute-done.18.c_ref = f32[48,128]{1,0:T(8,128)S(1)} collective-permute-done((f32[48,128]{1,0:T(8,128)S(1)}, f32[48,128]{1,0:T(8,128)S(1)}, u32[]{:S(2)}, u32[]{:S(2)}) %collective-permute-start.18) | collective-permute-done | bytes 24608 | tf_op jit(solution)/shard_map/ppermute | solution.py:392
  62.4 2.4 %collective-permute-done.17.b_ref = f32[48,128]{1,0:T(8,128)S(1)} collective-permute-done((f32[48,128]{1,0:T(8,128)S(1)}, f32[48,128]{1,0:T(8,128)S(1)}, u32[]{:S(2)}, u32[]{:S(2)}) %collective-permute-start.17) | collective-permute-done | bytes 24608 | tf_op jit(solution)/shard_map/ppermute | solution.py:392
  65.2 0.6 collective-permute-start.22
  65.8 1.1 %collective-permute-start.21 = (f32[48,128]{1,0:T(8,128)S(1)}, f32[48,128]{1,0:T(8,128)S(1)}, u32[]{:S(2)}, u32[]{:S(2)}) collective-permute-start(f32[48,128]{1,0:T(8,128)S(1)} %get-tuple-element.46), channel_id=1, source_target_pairs={{0,31},{1,2},{2,1},{3,4},{4,3},{5,6},{6,5},{7,8},{8,7},{9,10},{10,... | collective-permute-start | bytes 73736 | tf_op jit(solution)/shard_map/ppermute | solution.py:392
  67.0 5.8 %collective-permute-done.23.d_ref = f32[48,128]{1,0:T(8,128)S(1)} collective-permute-done((f32[48,128]{1,0:T(8,128)S(1)}, f32[48,128]{1,0:T(8,128)S(1)}, u32[]{:S(2)}, u32[]{:S(2)}) %collective-permute-start.23) | collective-permute-done | bytes 24608 | tf_op jit(solution)/shard_map/ppermute | solution.py:392
  72.9 4.1 %shard_map.101 = (f32[192,128]{1,0:T(8,128)S(1)}, f32[32,1,128]{2,1,0:T(1,128)S(1)}) custom-call(f32[8,768]{1,0:T(8,128)S(1)} %get-tuple-element.30.meta_ref.label_ref, bf16[384,768]{1,0:T(8,128)(2,1)S(1)} %get-tuple-element.31.onehot_ref, f32[192,48]{1,0:T(8,128)S(1)} %copy-done, f32[4096,128]{1,0:T(8,128)S(1)} %get-tuple-element.32.inverse_ref, ...), custom_call_target="tpu_custom_call" | custom-call | tf_op jit(solution)/shard_map/pallas_call | solution.py:372
  77.0 9.9 %all_to_all.5.moment_ref = f32[32,1,128]{2,1,0:T(1,128)S(1)} all-to-all(f32[32,1,128]{2,1,0:T(1,128)S(1)} %get-tuple-element.51), channel_id=1, replica_groups=mesh['dom'=16,'blk'=2] {'dom','blk'}, dimensions={0} | all-to-all | bytes 32768 | tf_op jit(solution)/shard_map/all_to_all | solution.py:472
  86.9 1.8 %shard_map.102 = (f32[48,256]{1,0:T(8,128)}, f32[192,128]{1,0:T(8,128)}) custom-call(f32[32,1,128]{2,1,0:T(1,128)S(1)} %all_to_all.5.moment_ref, f32[48,256]{1,0:T(8,128)S(1)} %get-tuple-element.36.field_ref.k0_ref, f32[48,256]{1,0:T(8,128)S(1)} %get-tuple-element.41.field_ref.k1_ref, f32[48,256]{1,0:T(8,128)S(1)} %get-tuple-element.45.k2_ref, ...), custom_call_target="tpu_custom_call" | custom-call | tf_op jit(solution)/shard_map/pallas_call | solution.py:372
  (29 shorter events, 1.5 us)
Async XLA Ops:
  0.6 26.3 %copy-start.1 = (f32[192,48]{1,0:T(8,128)S(1)}, f32[192,48]{1,0:T(8,128)}, u32[]{:S(2)}) copy-start(f32[192,48]{1,0:T(8,128)} %constant.4.clone.back_hbm.back_ref) | copy-start | bytes 110596
  0.6 26.3 %copy-start = (f32[192,48]{1,0:T(8,128)S(1)}, f32[192,48]{1,0:T(8,128)}, u32[]{:S(2)}) copy-start(f32[192,48]{1,0:T(8,128)} %constant.5.clone.forth_ref) | copy-start | bytes 110596
  4.6 8.5 %collective-permute-start.3 = (f32[56,128]{1,0:T(8,128)S(1)}, f32[56,128]{1,0:T(8,128)S(1)}, u32[]{:S(2)}, u32[]{:S(2)}) collective-permute-start(f32[56,128]{1,0:T(8,128)S(1)} %get-tuple-element.35), channel_id=1, source_target_pairs={{0,30},{1,31},{2,0},{3,1},{4,2},{5,3},{6,4},{7,5},{8,6},{9,7},{10,... | collective-permute-start | bytes 86024 | tf_op jit(solution)/shard_map/ppermute | solution.py:392
  11.6 4.8 %collective-permute-start.2 = (f32[56,128]{1,0:T(8,128)S(1)}, f32[56,128]{1,0:T(8,128)S(1)}, u32[]{:S(2)}, u32[]{:S(2)}) collective-permute-start(f32[56,128]{1,0:T(8,128)S(1)} %get-tuple-element.35), channel_id=1, source_target_pairs={{0,16},{1,17},{2,18},{3,19},{4,20},{5,21},{6,22},{7,23},{8,24},{9,... | collective-permute-start | bytes 86024 | tf_op jit(solution)/shard_map/ppermute | solution.py:392
  11.6 6.9 %collective-permute-start.1 = (f32[56,128]{1,0:T(8,128)S(1)}, f32[56,128]{1,0:T(8,128)S(1)}, u32[]{:S(2)}, u32[]{:S(2)}) collective-permute-start(f32[56,128]{1,0:T(8,128)S(1)} %get-tuple-element.35), channel_id=1, source_target_pairs={{0,31},{1,2},{2,1},{3,4},{4,3},{5,6},{6,5},{7,8},{8,7},{9,10},{10,... | collective-permute-start | bytes 86024 | tf_op jit(solution)/shard_map/ppermute | solution.py:392
  11.6 6.9 %collective-permute-start = (f32[56,128]{1,0:T(8,128)S(1)}, f32[56,128]{1,0:T(8,128)S(1)}, u32[]{:S(2)}, u32[]{:S(2)}) collective-permute-start(f32[56,128]{1,0:T(8,128)S(1)} %get-tuple-element.35), channel_id=1, source_target_pairs={{0,1},{1,0},{2,3},{3,2},{4,5},{5,4},{6,7},{7,6},{8,9},{9,8},{10,11... | collective-permute-start | bytes 86024 | tf_op jit(solution)/shard_map/ppermute | solution.py:392
  18.8 7.5 %collective-permute-start.7 = (f32[48,128]{1,0:T(8,128)S(1)}, f32[48,128]{1,0:T(8,128)S(1)}, u32[]{:S(2)}, u32[]{:S(2)}) collective-permute-start(f32[48,128]{1,0:T(8,128)S(1)} %get-tuple-element.38), channel_id=1, source_target_pairs={{0,2},{1,3},{2,4},{3,5},{4,6},{5,7},{6,8},{7,9},{8,10},{9,11},{10,... | collective-permute-start | bytes 73736 | tf_op jit(solution)/shard_map/ppermute | solution.py:392
  18.9 7.4 %collective-permute-start.6 = (f32[48,128]{1,0:T(8,128)S(1)}, f32[48,128]{1,0:T(8,128)S(1)}, u32[]{:S(2)}, u32[]{:S(2)}) collective-permute-start(f32[48,128]{1,0:T(8,128)S(1)} %get-tuple-element.38), channel_id=1, source_target_pairs={{0,16},{1,17},{2,18},{3,19},{4,20},{5,21},{6,22},{7,23},{8,24},{9,... | collective-permute-start | bytes 73736 | tf_op jit(solution)/shard_map/ppermute | solution.py:392
  20.1 6.8 %collective-permute-start.5 = (f32[48,128]{1,0:T(8,128)S(1)}, f32[48,128]{1,0:T(8,128)S(1)}, u32[]{:S(2)}, u32[]{:S(2)}) collective-permute-start(f32[48,128]{1,0:T(8,128)S(1)} %get-tuple-element.38), channel_id=1, source_target_pairs={{0,31},{1,2},{2,1},{3,4},{4,3},{5,6},{6,5},{7,8},{8,7},{9,10},{10,... | collective-permute-start | bytes 73736 | tf_op jit(solution)/shard_map/ppermute | solution.py:392
  21.3 5.7 %collective-permute-start.4 = (f32[48,128]{1,0:T(8,128)S(1)}, f32[48,128]{1,0:T(8,128)S(1)}, u32[]{:S(2)}, u32[]{:S(2)}) collective-permute-start(f32[48,128]{1,0:T(8,128)S(1)} %get-tuple-element.38), channel_id=1, source_target_pairs={{0,1},{1,0},{2,3},{3,2},{4,5},{5,4},{6,7},{7,6},{8,9},{9,8},{10,11... | collective-permute-start | bytes 73736 | tf_op jit(solution)/shard_map/ppermute | solution.py:392
  31.9 3.9 %collective-permute-start.11 = (f32[48,128]{1,0:T(8,128)S(1)}, f32[48,128]{1,0:T(8,128)S(1)}, u32[]{:S(2)}, u32[]{:S(2)}) collective-permute-start(f32[48,128]{1,0:T(8,128)S(1)} %get-tuple-element.40), channel_id=1, source_target_pairs={{0,30},{1,31},{2,0},{3,1},{4,2},{5,3},{6,4},{7,5},{8,6},{9,7},{10,... | collective-permute-start | bytes 73736 | tf_op jit(solution)/shard_map/ppermute | solution.py:392
  34.3 5.0 %collective-permute-start.10 = (f32[48,128]{1,0:T(8,128)S(1)}, f32[48,128]{1,0:T(8,128)S(1)}, u32[]{:S(2)}, u32[]{:S(2)}) collective-permute-start(f32[48,128]{1,0:T(8,128)S(1)} %get-tuple-element.40), channel_id=1, source_target_pairs={{0,16},{1,17},{2,18},{3,19},{4,20},{5,21},{6,22},{7,23},{8,24},{9,... | collective-permute-start | bytes 73736 | tf_op jit(solution)/shard_map/ppermute | solution.py:392
  34.8 6.8 %collective-permute-start.9 = (f32[48,128]{1,0:T(8,128)S(1)}, f32[48,128]{1,0:T(8,128)S(1)}, u32[]{:S(2)}, u32[]{:S(2)}) collective-permute-start(f32[48,128]{1,0:T(8,128)S(1)} %get-tuple-element.40), channel_id=1, source_target_pairs={{0,31},{1,2},{2,1},{3,4},{4,3},{5,6},{6,5},{7,8},{8,7},{9,10},{10,... | collective-permute-start | bytes 73736 | tf_op jit(solution)/shard_map/ppermute | solution.py:392
  35.1 6.5 %collective-permute-start.8 = (f32[48,128]{1,0:T(8,128)S(1)}, f32[48,128]{1,0:T(8,128)S(1)}, u32[]{:S(2)}, u32[]{:S(2)}) collective-permute-start(f32[48,128]{1,0:T(8,128)S(1)} %get-tuple-element.40), channel_id=1, source_target_pairs={{0,1},{1,0},{2,3},{3,2},{4,5},{5,4},{6,7},{7,6},{8,9},{9,8},{10,11... | collective-permute-start | bytes 73736 | tf_op jit(solution)/shard_map/ppermute | solution.py:392
  42.0 7.6 %collective-permute-start.15 = (f32[48,128]{1,0:T(8,128)S(1)}, f32[48,128]{1,0:T(8,128)S(1)}, u32[]{:S(2)}, u32[]{:S(2)}) collective-permute-start(f32[48,128]{1,0:T(8,128)S(1)} %get-tuple-element.42), channel_id=1, source_target_pairs={{0,2},{1,3},{2,4},{3,5},{4,6},{5,7},{6,8},{7,9},{8,10},{9,11},{10,... | collective-permute-start | bytes 73736 | tf_op jit(solution)/shard_map/ppermute | solution.py:392
  42.0 7.6 %collective-permute-start.14 = (f32[48,128]{1,0:T(8,128)S(1)}, f32[48,128]{1,0:T(8,128)S(1)}, u32[]{:S(2)}, u32[]{:S(2)}) collective-permute-start(f32[48,128]{1,0:T(8,128)S(1)} %get-tuple-element.42), channel_id=1, source_target_pairs={{0,16},{1,17},{2,18},{3,19},{4,20},{5,21},{6,22},{7,23},{8,24},{9,... | collective-permute-start | bytes 73736 | tf_op jit(solution)/shard_map/ppermute | solution.py:392
  42.7 7.1 %collective-permute-start.13 = (f32[48,128]{1,0:T(8,128)S(1)}, f32[48,128]{1,0:T(8,128)S(1)}, u32[]{:S(2)}, u32[]{:S(2)}) collective-permute-start(f32[48,128]{1,0:T(8,128)S(1)} %get-tuple-element.42), channel_id=1, source_target_pairs={{0,31},{1,2},{2,1},{3,4},{4,3},{5,6},{6,5},{7,8},{8,7},{9,10},{10,... | collective-permute-start | bytes 73736 | tf_op jit(solution)/shard_map/ppermute | solution.py:392
  43.8 6.0 %collective-permute-start.12 = (f32[48,128]{1,0:T(8,128)S(1)}, f32[48,128]{1,0:T(8,128)S(1)}, u32[]{:S(2)}, u32[]{:S(2)}) collective-permute-start(f32[48,128]{1,0:T(8,128)S(1)} %get-tuple-element.42), channel_id=1, source_target_pairs={{0,1},{1,0},{2,3},{3,2},{4,5},{5,4},{6,7},{7,6},{8,9},{9,8},{10,11... | collective-permute-start | bytes 73736 | tf_op jit(solution)/shard_map/ppermute | solution.py:392
  54.8 4.1 %collective-permute-start.19 = (f32[48,128]{1,0:T(8,128)S(1)}, f32[48,128]{1,0:T(8,128)S(1)}, u32[]{:S(2)}, u32[]{:S(2)}) collective-permute-start(f32[48,128]{1,0:T(8,128)S(1)} %get-tuple-element.44), channel_id=1, source_target_pairs={{0,30},{1,31},{2,0},{3,1},{4,2},{5,3},{6,4},{7,5},{8,6},{9,7},{10,... | collective-permute-start | bytes 73736 | tf_op jit(solution)/shard_map/ppermute | solution.py:392
  57.4 5.0 %collective-permute-start.18 = (f32[48,128]{1,0:T(8,128)S(1)}, f32[48,128]{1,0:T(8,128)S(1)}, u32[]{:S(2)}, u32[]{:S(2)}) collective-permute-start(f32[48,128]{1,0:T(8,128)S(1)} %get-tuple-element.44), channel_id=1, source_target_pairs={{0,16},{1,17},{2,18},{3,19},{4,20},{5,21},{6,22},{7,23},{8,24},{9,... | collective-permute-start | bytes 73736 | tf_op jit(solution)/shard_map/ppermute | solution.py:392
  57.9 6.9 %collective-permute-start.17 = (f32[48,128]{1,0:T(8,128)S(1)}, f32[48,128]{1,0:T(8,128)S(1)}, u32[]{:S(2)}, u32[]{:S(2)}) collective-permute-start(f32[48,128]{1,0:T(8,128)S(1)} %get-tuple-element.44), channel_id=1, source_target_pairs={{0,31},{1,2},{2,1},{3,4},{4,3},{5,6},{6,5},{7,8},{8,7},{9,10},{10,... | collective-permute-start | bytes 73736 | tf_op jit(solution)/shard_map/ppermute | solution.py:392
  58.3 6.5 %collective-permute-start.16 = (f32[48,128]{1,0:T(8,128)S(1)}, f32[48,128]{1,0:T(8,128)S(1)}, u32[]{:S(2)}, u32[]{:S(2)}) collective-permute-start(f32[48,128]{1,0:T(8,128)S(1)} %get-tuple-element.44), channel_id=1, source_target_pairs={{0,1},{1,0},{2,3},{3,2},{4,5},{5,4},{6,7},{7,6},{8,9},{9,8},{10,11... | collective-permute-start | bytes 73736 | tf_op jit(solution)/shard_map/ppermute | solution.py:392
  65.1 7.7 %collective-permute-start.23 = (f32[48,128]{1,0:T(8,128)S(1)}, f32[48,128]{1,0:T(8,128)S(1)}, u32[]{:S(2)}, u32[]{:S(2)}) collective-permute-start(f32[48,128]{1,0:T(8,128)S(1)} %get-tuple-element.46), channel_id=1, source_target_pairs={{0,2},{1,3},{2,4},{3,5},{4,6},{5,7},{6,8},{7,9},{8,10},{9,11},{10,... | collective-permute-start | bytes 73736 | tf_op jit(solution)/shard_map/ppermute | solution.py:392
  65.2 7.6 %collective-permute-start.22 = (f32[48,128]{1,0:T(8,128)S(1)}, f32[48,128]{1,0:T(8,128)S(1)}, u32[]{:S(2)}, u32[]{:S(2)}) collective-permute-start(f32[48,128]{1,0:T(8,128)S(1)} %get-tuple-element.46), channel_id=1, source_target_pairs={{0,16},{1,17},{2,18},{3,19},{4,20},{5,21},{6,22},{7,23},{8,24},{9,... | collective-permute-start | bytes 73736 | tf_op jit(solution)/shard_map/ppermute | solution.py:392
  65.8 7.1 %collective-permute-start.21 = (f32[48,128]{1,0:T(8,128)S(1)}, f32[48,128]{1,0:T(8,128)S(1)}, u32[]{:S(2)}, u32[]{:S(2)}) collective-permute-start(f32[48,128]{1,0:T(8,128)S(1)} %get-tuple-element.46), channel_id=1, source_target_pairs={{0,31},{1,2},{2,1},{3,4},{4,3},{5,6},{6,5},{7,8},{8,7},{9,10},{10,... | collective-permute-start | bytes 73736 | tf_op jit(solution)/shard_map/ppermute | solution.py:392
  67.0 6.0 %collective-permute-start.20 = (f32[48,128]{1,0:T(8,128)S(1)}, f32[48,128]{1,0:T(8,128)S(1)}, u32[]{:S(2)}, u32[]{:S(2)}) collective-permute-start(f32[48,128]{1,0:T(8,128)S(1)} %get-tuple-element.46), channel_id=1, source_target_pairs={{0,1},{1,0},{2,3},{3,2},{4,5},{5,4},{6,7},{7,6},{8,9},{9,8},{10,11... | collective-permute-start | bytes 73736 | tf_op jit(solution)/shard_map/ppermute | solution.py:392

commit v2 on v1

--- a/solution.py
+++ b/solution.py
@@ -170,15 +170,15 @@
 
 def start_kernel(
     ranks, inner, trace, owned, cap,
-    mortar_hbm, kind_hbm, force_hbm, back_hbm, inverse_hbm, couple_hbm,
-    own_ref, out_ref, onehot_ref, meta_ref, load_ref, inverse_ref, couple_ref,
+    mortar_hbm, kind_hbm, force_hbm, back_hbm, inverse_hbm, couple_hbm, self_hbm,
+    own_ref, out_ref, onehot_ref, meta_ref, load_ref, inverse_ref, couple_ref, self_ref,
     mortar_ref, kind_ref, force_ref, back_ref, *sems,
 ):
     copies = [
         pltpu.make_async_copy(source, target, sem)
         for source, target, sem in zip(
-            (mortar_hbm, kind_hbm, force_hbm, back_hbm, inverse_hbm, couple_hbm),
-            (mortar_ref, kind_ref, force_ref, back_ref, inverse_ref, couple_ref),
+            (mortar_hbm, kind_hbm, force_hbm, back_hbm, inverse_hbm, couple_hbm, self_hbm),
+            (mortar_ref, kind_ref, force_ref, back_ref, inverse_ref, couple_ref, self_ref),
             sems,
         )
     ]
@@ -234,9 +234,10 @@
     sums = exact_dot(jnp.concatenate([z, label], axis=0), onehot_ref[...], 1)
     own_ref[...] = sums[: COMP * NODES, :owned]
     out_ref[...] = sums[:, owned:]
-
-
-def merged(meta_ref, first, second, third, fourth, cap, to_owner):
+    copies[6].wait()
+
+
+def merged(meta_ref, first, third, second, fourth, cap, to_owner):
     lane = lax.broadcasted_iota(jnp.int32, (1, RUNS * cap), 1)
     odd = meta_ref[3:4, : RUNS * cap] == 1.0
     low = lane < 2 * cap
@@ -281,19 +282,16 @@
 
 def apply_kernel(
     inner, trace, owned, cap,
-    meta_ref, onehot_ref, forth_ref, back_ref, inverse_ref, couple_ref,
-    field_ref, a_ref, b_ref, c_ref, d_ref, self_hbm,
-    own_ref, out_ref, spread_ref, mid_ref, weight_ref, image_ref, self_ref, sem,
+    meta_ref, onehot_ref, forth_ref, back_ref, inverse_ref, couple_ref, self_ref,
+    field_ref, a_ref, b_ref, c_ref, d_ref,
+    own_ref, out_ref, spread_ref, mid_ref, weight_ref, image_ref,
 ):
-    copy = pltpu.make_async_copy(self_hbm, self_ref, sem)
-    copy.start()
     width = spread_ref.shape[1]
     kind = element_values(
         cap, meta_ref, onehot_ref, forth_ref, field_ref, (a_ref, b_ref, c_ref, d_ref), spread_ref
     )
     rows_times(couple_ref, spread_ref, mid_ref, inner, trace)
     rows_times(inverse_ref, mid_ref, weight_ref, inner, inner)
-    copy.wait()
     rows_times(self_ref, spread_ref, image_ref, trace, trace)
     y = columns_times(tiles_of(image_ref, trace), couple_ref, weight_ref, trace, inner)
     z = by_kind(face_columns(y), back_ref, kind)
@@ -308,19 +306,16 @@
 
 def last_kernel(
     inner, trace, cap,
-    meta_ref, onehot_ref, forth_ref, inverse_ref, couple_ref,
-    k0_ref, k1_ref, k2_ref, a_ref, b_ref, c_ref, d_ref, s0_ref, s1_ref, u0_ref, u1_ref, self_hbm,
-    weight_ref, moment_ref, spread_ref, mid_ref, image_ref, self_ref, sem,
+    meta_ref, onehot_ref, forth_ref, inverse_ref, couple_ref, self_ref,
+    k0_ref, k1_ref, k2_ref, a_ref, b_ref, c_ref, d_ref, s0_ref, s1_ref, u0_ref, u1_ref,
+    weight_ref, moment_ref, spread_ref, mid_ref, image_ref,
 ):
-    copy = pltpu.make_async_copy(self_hbm, self_ref, sem)
-    copy.start()
     width = spread_ref.shape[1]
     element_values(
         cap, meta_ref, onehot_ref, forth_ref, k2_ref, (a_ref, b_ref, c_ref, d_ref), spread_ref
     )
     rows_times(couple_ref, spread_ref, mid_ref, inner, trace)
     rows_times(inverse_ref, mid_ref, weight_ref, inner, inner)
-    copy.wait()
     rows_times(self_ref, spread_ref, image_ref, trace, trace)
     image, weight = image_ref[...], weight_ref[...]
     ks = (k0_ref[...], k1_ref[...], k2_ref[...])
@@ -389,7 +384,7 @@
         [(r, (r + ranks // 2) % ranks) for r in range(ranks)],
         [(r, (r + away) % ranks) for r in range(ranks)],
     ]
-    return [lax.ppermute(block, AXES, p) for p in pairs]
+    return [lax.ppermute(block, AXES, pairs[n]) for n in (0, 2, 1, 3)]
 
 
 def local(self_block, couple, inverse, body_force, face_mortar, face_kind, *, ranks):
@@ -407,7 +402,7 @@
     inverse = inverse.reshape(inner * inner, width)
     force = body_force.reshape(COMP * inner, width)
 
-    own, out, onehot, meta, load, inverse_in, couple_in = call(
+    own, out, onehot, meta, load, *matrices = call(
         functools.partial(start_kernel, ranks, inner, trace, owned, cap),
         [
             ((rows, owned), F32),
@@ -417,12 +412,13 @@
             ((COMP * inner, width), F32),
             (inverse.shape, F32),
             (couple.shape, F32),
+            (self_block.shape, F32),
         ],
-        mortar, kind, force, backward, inverse, couple,
+        mortar, kind, force, backward, inverse, couple, self_block,
         scratch=[
             (mortar.shape, jnp.int32), (kind.shape, jnp.int32), (force.shape, F32), (backward.shape, F32)
         ],
-        in_hbm=6, vmem=16,
+        in_hbm=7, vmem=16,
     )
     blocks = exchange(out, ranks, True)
     field, out, label = call(
@@ -442,8 +438,8 @@
                 ((COMP * inner, width), F32),
                 ((COMP * inner, width), F32),
             ],
-            meta, onehot, forward, backward, inverse_in, couple_in, field, *blocks, self_block,
-            scratch=[((COMP * trace, width), F32), (self_block.shape, F32)], in_hbm=1, vmem=12,
+            meta, onehot, forward, backward, *matrices, field, *blocks,
+            scratch=[((COMP * trace, width), F32)],
         )
         spreads.append(spread)
         mids.append(mid)
@@ -459,14 +455,12 @@
     weight, moments = call(
         functools.partial(last_kernel, inner, trace, cap),
         [((COMP * inner, width), F32), ((ranks, 1, width), F32)],
-        meta, onehot, forward, inverse_in, couple_in, *fields, *blocks, *spreads, *mids, self_block,
+        meta, onehot, forward, *matrices, *fields, *blocks, *spreads, *mids,
         scratch=[
             ((COMP * trace, width), F32),
             ((COMP * inner, width), F32),
             ((COMP * trace, width), F32),
-            (self_block.shape, F32),
         ],
-        in_hbm=1, vmem=12,
     )
     weights.append(weight)
     moments = lax.all_to_all(moments, AXES, split_axis=0, concat_axis=0, tiled=True)

time: 89 us -> 85.5 us (0.961)
  Pallas kernels: 20.7 us -> 18.4 us
  waiting for transfers between devices: 37.5 us -> 35.9 us
    pallas_call x8, Pallas kernels: 20.7 us -> 18.4 us  [call(): pl.pallas_call(kernel, out_shape=[jax.ShapeDtypeStruct(shape, dtype) for...]
    ppermute x24, waiting for transfers between devices: 37.5 us -> 35.9 us  [exchange(): return [lax.ppermute(block, AXES, pairs[n]) for n in (0, 2, 1, 3)]]
  transfers between devices with their start and end apart: 24 -> 24, of which waited for: 15 -> 9; matrix products, arithmetic and copies ran while one was open for 0% -> 0% of each run, Pallas kernels for 0% -> 0%
where the time goes in v2:
time: 85.5 us; the launch traced here: 85.4 us
  waiting for transfers between devices  35.9 us (42%)
  starting transfers between devices  20.1 us (24%)
  Pallas kernels  18.4 us (22%)
  blocking collectives  10.2 us (12%)
    ppermute x24, waiting for transfers between devices, exchange(): return [lax.ppermute(block, AXES, pairs[n]) for n in (0, 2, 1, 3)]  35.9 us
    ppermute x24, starting transfers between devices, exchange(): return [lax.ppermute(block, AXES, pairs[n]) for n in (0, 2, 1, 3)]  20.1 us
    pallas_call x8, Pallas kernels, call(): pl.pallas_call(kernel, out_shape=[jax.ShapeDtypeStruct(shape, dtype) for...  18.4 us
    all_to_all x1, blocking collectives, local(): lax.all_to_all(moments, AXES, split_axis=0, concat_axis=0, tiled=True)  10.2 us
  transfers between devices with their start and end apart: 24, of which 9 were waited for; matrix products, arithmetic and copies ran while one was open for 0% of the time, Pallas kernels for 0%

profile of v2, /device:TPU:0, one launch (start us, length us, event | category | flops | bytes accessed | tf_op | source)
XLA Modules:
  0.0 85.4 jit_solution(15113172802276391046)
XLA Ops:
  0.6 0.0 copy-start
  0.6 0.0 copy-start.1
  0.7 4.1 %shard_map.95 = (f32[48,256]{1,0:T(8,128)S(1)}, f32[56,128]{1,0:T(8,128)S(1)}, bf16[384,768]{1,0:T(8,128)(2,1)S(1)}, f32[8,768]{1,0:T(8,128)S(1)}, f32[192,128]{...) custom-call(s32[6,128]{1,0:T(8,128)} %bitcast.11, s32[6,128]{1,0:T(8,128)} %bitcast.12, ...), custom_call_target="tpu_custom_call" | custom-call | tf_op jit(solution)/shard_map/pallas_call | solution.py:367
  4.8 7.0 %collective-permute-start.3 = (f32[56,128]{1,0:T(8,128)S(1)}, f32[56,128]{1,0:T(8,128)S(1)}, u32[]{:S(2)}, u32[]{:S(2)}) collective-permute-start(f32[56,128]{1,0:T(8,128)S(1)} %get-tuple-element.37), channel_id=1, source_target_pairs={{0,30},{1,31},{2,0},{3,1},{4,2},{5,3},{6,4},{7,5},{8,6},{9,7},{10,... | collective-permute-start | bytes 86024 | tf_op jit(solution)/shard_map/ppermute | solution.py:387
  11.8 0.0 collective-permute-start.2
  11.8 1.5 %collective-permute-done.3.d_ref = f32[56,128]{1,0:T(8,128)S(1)} collective-permute-done((f32[56,128]{1,0:T(8,128)S(1)}, f32[56,128]{1,0:T(8,128)S(1)}, u32[]{:S(2)}, u32[]{:S(2)}) %collective-permute-start.3) | collective-permute-done | bytes 28704 | tf_op jit(solution)/shard_map/ppermute | solution.py:387
  13.4 5.3 %collective-permute-done.2.c_ref = f32[56,128]{1,0:T(8,128)S(1)} collective-permute-done((f32[56,128]{1,0:T(8,128)S(1)}, f32[56,128]{1,0:T(8,128)S(1)}, u32[]{:S(2)}, u32[]{:S(2)}) %collective-permute-start.2) | collective-permute-done | bytes 28704 | tf_op jit(solution)/shard_map/ppermute | solution.py:387
  18.7 0.3 shard_map.96
  19.0 0.1 collective-permute-start.7
  19.1 2.2 %collective-permute-start.6 = (f32[48,128]{1,0:T(8,128)S(1)}, f32[48,128]{1,0:T(8,128)S(1)}, u32[]{:S(2)}, u32[]{:S(2)}) collective-permute-start(f32[48,128]{1,0:T(8,128)S(1)} %get-tuple-element.40), channel_id=1, source_target_pairs={{0,31},{1,2},{2,1},{3,4},{4,3},{5,6},{6,5},{7,8},{8,7},{9,10},{10,... | collective-permute-start | bytes 73736 | tf_op jit(solution)/shard_map/ppermute | solution.py:387
  21.2 5.3 %collective-permute-done.7.d_ref = f32[48,128]{1,0:T(8,128)S(1)} collective-permute-done((f32[48,128]{1,0:T(8,128)S(1)}, f32[48,128]{1,0:T(8,128)S(1)}, u32[]{:S(2)}, u32[]{:S(2)}) %collective-permute-start.7) | collective-permute-done | bytes 24608 | tf_op jit(solution)/shard_map/ppermute | solution.py:387
  26.5 4.1 %shard_map.97 = (f32[48,256]{1,0:T(8,128)S(1)}, f32[48,128]{1,0:T(8,128)S(1)}, f32[288,128]{1,0:T(8,128)S(1)}, f32[192,128]{1,0:T(8,128)S(1)}, f32[192,128]{1,0:T(8,128)S(1)}) custom-call(f32[8,768]{1,0:T(8,128)S(1)} %get-tuple-element.31.meta_ref.label_ref, bf16[384,768]{1,0:T(8,128)(2,1)S(1)} %get-tuple-element.32.onehot_ref, f32[192,48]{1,0:T(8,128)S(1)} %copy-done, ...), custom_call_target="tpu_custom_call" | custom-call | tf_op jit(solution)/shard_map/pallas_call | solution.py:367
  30.6 2.9 %collective-permute-start.11 = (f32[48,128]{1,0:T(8,128)S(1)}, f32[48,128]{1,0:T(8,128)S(1)}, u32[]{:S(2)}, u32[]{:S(2)}) collective-permute-start(f32[48,128]{1,0:T(8,128)S(1)} %get-tuple-element.42), channel_id=1, source_target_pairs={{0,30},{1,31},{2,0},{3,1},{4,2},{5,3},{6,4},{7,5},{8,6},{9,7},{10,... | collective-permute-start | bytes 73736 | tf_op jit(solution)/shard_map/ppermute | solution.py:387
  33.5 0.3 collective-permute-start.10
  33.9 1.2 %collective-permute-done.11.d_ref = f32[48,128]{1,0:T(8,128)S(1)} collective-permute-done((f32[48,128]{1,0:T(8,128)S(1)}, f32[48,128]{1,0:T(8,128)S(1)}, u32[]{:S(2)}, u32[]{:S(2)}) %collective-permute-start.11) | collective-permute-done | bytes 24608 | tf_op jit(solution)/shard_map/ppermute | solution.py:387
  35.1 5.3 %collective-permute-done.10.c_ref = f32[48,128]{1,0:T(8,128)S(1)} collective-permute-done((f32[48,128]{1,0:T(8,128)S(1)}, f32[48,128]{1,0:T(8,128)S(1)}, u32[]{:S(2)}, u32[]{:S(2)}) %collective-permute-start.10) | collective-permute-done | bytes 24608 | tf_op jit(solution)/shard_map/ppermute | solution.py:387
  40.4 0.3 shard_map.98
  40.7 0.1 collective-permute-start.15
  40.8 2.1 %collective-permute-start.14 = (f32[48,128]{1,0:T(8,128)S(1)}, f32[48,128]{1,0:T(8,128)S(1)}, u32[]{:S(2)}, u32[]{:S(2)}) collective-permute-start(f32[48,128]{1,0:T(8,128)S(1)} %get-tuple-element.44), channel_id=1, source_target_pairs={{0,31},{1,2},{2,1},{3,4},{4,3},{5,6},{6,5},{7,8},{8,7},{9,10},{10,... | collective-permute-start | bytes 73736 | tf_op jit(solution)/shard_map/ppermute | solution.py:387
  42.9 5.3 %collective-permute-done.15.d_ref = f32[48,128]{1,0:T(8,128)S(1)} collective-permute-done((f32[48,128]{1,0:T(8,128)S(1)}, f32[48,128]{1,0:T(8,128)S(1)}, u32[]{:S(2)}, u32[]{:S(2)}) %collective-permute-start.15) | collective-permute-done | bytes 24608 | tf_op jit(solution)/shard_map/ppermute | solution.py:387
  48.2 4.1 %shard_map.99 = (f32[48,256]{1,0:T(8,128)S(1)}, f32[48,128]{1,0:T(8,128)S(1)}, f32[288,128]{1,0:T(8,128)S(1)}, f32[192,128]{1,0:T(8,128)S(1)}, f32[192,128]{1,0:T(8,128)S(1)}) custom-call(f32[8,768]{1,0:T(8,128)S(1)} %get-tuple-element.31.meta_ref.label_ref, bf16[384,768]{1,0:T(8,128)(2,1)S(1)} %get-tuple-element.32.onehot_ref, f32[192,48]{1,0:T(8,128)S(1)} %copy-done, ...), custom_call_target="tpu_custom_call" | custom-call | tf_op jit(solution)/shard_map/pallas_call | solution.py:367
  52.3 2.9 %collective-permute-start.19 = (f32[48,128]{1,0:T(8,128)S(1)}, f32[48,128]{1,0:T(8,128)S(1)}, u32[]{:S(2)}, u32[]{:S(2)}) collective-permute-start(f32[48,128]{1,0:T(8,128)S(1)} %get-tuple-element.46), channel_id=1, source_target_pairs={{0,30},{1,31},{2,0},{3,1},{4,2},{5,3},{6,4},{7,5},{8,6},{9,7},{10,... | collective-permute-start | bytes 73736 | tf_op jit(solution)/shard_map/ppermute | solution.py:387
  55.2 0.3 collective-permute-start.18
  55.5 1.2 %collective-permute-done.19.d_ref = f32[48,128]{1,0:T(8,128)S(1)} collective-permute-done((f32[48,128]{1,0:T(8,128)S(1)}, f32[48,128]{1,0:T(8,128)S(1)}, u32[]{:S(2)}, u32[]{:S(2)}) %collective-permute-start.19) | collective-permute-done | bytes 24608 | tf_op jit(solution)/shard_map/ppermute | solution.py:387
  56.7 5.3 %collective-permute-done.18.c_ref = f32[48,128]{1,0:T(8,128)S(1)} collective-permute-done((f32[48,128]{1,0:T(8,128)S(1)}, f32[48,128]{1,0:T(8,128)S(1)}, u32[]{:S(2)}, u32[]{:S(2)}) %collective-permute-start.18) | collective-permute-done | bytes 24608 | tf_op jit(solution)/shard_map/ppermute | solution.py:387
  62.1 0.3 shard_map.100
  62.4 0.1 collective-permute-start.23
  62.5 2.1 %collective-permute-start.22 = (f32[48,128]{1,0:T(8,128)S(1)}, f32[48,128]{1,0:T(8,128)S(1)}, u32[]{:S(2)}, u32[]{:S(2)}) collective-permute-start(f32[48,128]{1,0:T(8,128)S(1)} %get-tuple-element.48), channel_id=1, source_target_pairs={{0,31},{1,2},{2,1},{3,4},{4,3},{5,6},{6,5},{7,8},{8,7},{9,10},{10,... | collective-permute-start | bytes 73736 | tf_op jit(solution)/shard_map/ppermute | solution.py:387
  64.6 5.3 %collective-permute-done.23.d_ref = f32[48,128]{1,0:T(8,128)S(1)} collective-permute-done((f32[48,128]{1,0:T(8,128)S(1)}, f32[48,128]{1,0:T(8,128)S(1)}, u32[]{:S(2)}, u32[]{:S(2)}) %collective-permute-start.23) | collective-permute-done | bytes 24608 | tf_op jit(solution)/shard_map/ppermute | solution.py:387
  69.9 3.4 %shard_map.101 = (f32[192,128]{1,0:T(8,128)S(1)}, f32[32,1,128]{2,1,0:T(1,128)S(1)}) custom-call(f32[8,768]{1,0:T(8,128)S(1)} %get-tuple-element.31.meta_ref.label_ref, bf16[384,768]{1,0:T(8,128)(2,1)S(1)} %get-tuple-element.32.onehot_ref, f32[192,48]{1,0:T(8,128)S(1)} %copy-done, f32[4096,128]{1,0:T(8,128)S(1)} %get-tuple-element.33.inverse_ref, ...), custom_call_target="tpu_custom_call" | custom-call | tf_op jit(solution)/shard_map/pallas_call | solution.py:367
  73.3 10.2 %all_to_all.5.moment_ref = f32[32,1,128]{2,1,0:T(1,128)S(1)} all-to-all(f32[32,1,128]{2,1,0:T(1,128)S(1)} %get-tuple-element.53), channel_id=1, replica_groups=mesh['dom'=16,'blk'=2] {'dom','blk'}, dimensions={0} | all-to-all | bytes 32768 | tf_op jit(solution)/shard_map/all_to_all | solution.py:466
  83.5 1.8 %shard_map.102 = (f32[48,256]{1,0:T(8,128)}, f32[192,128]{1,0:T(8,128)}) custom-call(f32[32,1,128]{2,1,0:T(1,128)S(1)} %all_to_all.5.moment_ref, f32[48,256]{1,0:T(8,128)S(1)} %get-tuple-element.38.field_ref.k0_ref, f32[48,256]{1,0:T(8,128)S(1)} %get-tuple-element.43.field_ref.k1_ref, f32[48,256]{1,0:T(8,128)S(1)} %get-tuple-element.47.k2_ref, ...), custom_call_target="tpu_custom_call" | custom-call | tf_op jit(solution)/shard_map/pallas_call | solution.py:367
  (29 shorter events, 0.1 us)
Async XLA Ops:
  0.6 25.9 %copy-start = (f32[192,48]{1,0:T(8,128)S(1)}, f32[192,48]{1,0:T(8,128)}, u32[]{:S(2)}) copy-start(f32[192,48]{1,0:T(8,128)} %constant.5.clone.forth_ref) | copy-start | bytes 110596
  0.6 25.9 %copy-start.1 = (f32[192,48]{1,0:T(8,128)S(1)}, f32[192,48]{1,0:T(8,128)}, u32[]{:S(2)}) copy-start(f32[192,48]{1,0:T(8,128)} %constant.4.clone.back_hbm.back_ref) | copy-start | bytes 110596
  4.8 8.5 %collective-permute-start.3 = (f32[56,128]{1,0:T(8,128)S(1)}, f32[56,128]{1,0:T(8,128)S(1)}, u32[]{:S(2)}, u32[]{:S(2)}) collective-permute-start(f32[56,128]{1,0:T(8,128)S(1)} %get-tuple-element.37), channel_id=1, source_target_pairs={{0,30},{1,31},{2,0},{3,1},{4,2},{5,3},{6,4},{7,5},{8,6},{9,7},{10,... | collective-permute-start | bytes 86024 | tf_op jit(solution)/shard_map/ppermute | solution.py:387
  11.8 6.9 %collective-permute-start.2 = (f32[56,128]{1,0:T(8,128)S(1)}, f32[56,128]{1,0:T(8,128)S(1)}, u32[]{:S(2)}, u32[]{:S(2)}) collective-permute-start(f32[56,128]{1,0:T(8,128)S(1)} %get-tuple-element.37), channel_id=1, source_target_pairs={{0,31},{1,2},{2,1},{3,4},{4,3},{5,6},{6,5},{7,8},{8,7},{9,10},{10,... | collective-permute-start | bytes 86024 | tf_op jit(solution)/shard_map/ppermute | solution.py:387
  11.8 6.9 %collective-permute-start.1 = (f32[56,128]{1,0:T(8,128)S(1)}, f32[56,128]{1,0:T(8,128)S(1)}, u32[]{:S(2)}, u32[]{:S(2)}) collective-permute-start(f32[56,128]{1,0:T(8,128)S(1)} %get-tuple-element.37), channel_id=1, source_target_pairs={{0,16},{1,17},{2,18},{3,19},{4,20},{5,21},{6,22},{7,23},{8,24},{9,... | collective-permute-start | bytes 86024 | tf_op jit(solution)/shard_map/ppermute | solution.py:387
  11.8 6.9 %collective-permute-start = (f32[56,128]{1,0:T(8,128)S(1)}, f32[56,128]{1,0:T(8,128)S(1)}, u32[]{:S(2)}, u32[]{:S(2)}) collective-permute-start(f32[56,128]{1,0:T(8,128)S(1)} %get-tuple-element.37), channel_id=1, source_target_pairs={{0,1},{1,0},{2,3},{3,2},{4,5},{5,4},{6,7},{7,6},{8,9},{9,8},{10,11... | collective-permute-start | bytes 86024 | tf_op jit(solution)/shard_map/ppermute | solution.py:387
  19.0 7.5 %collective-permute-start.7 = (f32[48,128]{1,0:T(8,128)S(1)}, f32[48,128]{1,0:T(8,128)S(1)}, u32[]{:S(2)}, u32[]{:S(2)}) collective-permute-start(f32[48,128]{1,0:T(8,128)S(1)} %get-tuple-element.40), channel_id=1, source_target_pairs={{0,2},{1,3},{2,4},{3,5},{4,6},{5,7},{6,8},{7,9},{8,10},{9,11},{10,... | collective-permute-start | bytes 73736 | tf_op jit(solution)/shard_map/ppermute | solution.py:387
  19.1 7.4 %collective-permute-start.6 = (f32[48,128]{1,0:T(8,128)S(1)}, f32[48,128]{1,0:T(8,128)S(1)}, u32[]{:S(2)}, u32[]{:S(2)}) collective-permute-start(f32[48,128]{1,0:T(8,128)S(1)} %get-tuple-element.40), channel_id=1, source_target_pairs={{0,31},{1,2},{2,1},{3,4},{4,3},{5,6},{6,5},{7,8},{8,7},{9,10},{10,... | collective-permute-start | bytes 73736 | tf_op jit(solution)/shard_map/ppermute | solution.py:387
  21.2 5.3 %collective-permute-start.5 = (f32[48,128]{1,0:T(8,128)S(1)}, f32[48,128]{1,0:T(8,128)S(1)}, u32[]{:S(2)}, u32[]{:S(2)}) collective-permute-start(f32[48,128]{1,0:T(8,128)S(1)} %get-tuple-element.40), channel_id=1, source_target_pairs={{0,16},{1,17},{2,18},{3,19},{4,20},{5,21},{6,22},{7,23},{8,24},{9,... | collective-permute-start | bytes 73736 | tf_op jit(solution)/shard_map/ppermute | solution.py:387
  21.2 5.3 %collective-permute-start.4 = (f32[48,128]{1,0:T(8,128)S(1)}, f32[48,128]{1,0:T(8,128)S(1)}, u32[]{:S(2)}, u32[]{:S(2)}) collective-permute-start(f32[48,128]{1,0:T(8,128)S(1)} %get-tuple-element.40), channel_id=1, source_target_pairs={{0,1},{1,0},{2,3},{3,2},{4,5},{5,4},{6,7},{7,6},{8,9},{9,8},{10,11... | collective-permute-start | bytes 73736 | tf_op jit(solution)/shard_map/ppermute | solution.py:387
  30.6 4.4 %collective-permute-start.11 = (f32[48,128]{1,0:T(8,128)S(1)}, f32[48,128]{1,0:T(8,128)S(1)}, u32[]{:S(2)}, u32[]{:S(2)}) collective-permute-start(f32[48,128]{1,0:T(8,128)S(1)} %get-tuple-element.42), channel_id=1, source_target_pairs={{0,30},{1,31},{2,0},{3,1},{4,2},{5,3},{6,4},{7,5},{8,6},{9,7},{10,... | collective-permute-start | bytes 73736 | tf_op jit(solution)/shard_map/ppermute | solution.py:387
  33.5 6.8 %collective-permute-start.10 = (f32[48,128]{1,0:T(8,128)S(1)}, f32[48,128]{1,0:T(8,128)S(1)}, u32[]{:S(2)}, u32[]{:S(2)}) collective-permute-start(f32[48,128]{1,0:T(8,128)S(1)} %get-tuple-element.42), channel_id=1, source_target_pairs={{0,31},{1,2},{2,1},{3,4},{4,3},{5,6},{6,5},{7,8},{8,7},{9,10},{10,... | collective-permute-start | bytes 73736 | tf_op jit(solution)/shard_map/ppermute | solution.py:387
  33.9 6.5 %collective-permute-start.9 = (f32[48,128]{1,0:T(8,128)S(1)}, f32[48,128]{1,0:T(8,128)S(1)}, u32[]{:S(2)}, u32[]{:S(2)}) collective-permute-start(f32[48,128]{1,0:T(8,128)S(1)} %get-tuple-element.42), channel_id=1, source_target_pairs={{0,16},{1,17},{2,18},{3,19},{4,20},{5,21},{6,22},{7,23},{8,24},{9,... | collective-permute-start | bytes 73736 | tf_op jit(solution)/shard_map/ppermute | solution.py:387
  33.9 6.5 %collective-permute-start.8 = (f32[48,128]{1,0:T(8,128)S(1)}, f32[48,128]{1,0:T(8,128)S(1)}, u32[]{:S(2)}, u32[]{:S(2)}) collective-permute-start(f32[48,128]{1,0:T(8,128)S(1)} %get-tuple-element.42), channel_id=1, source_target_pairs={{0,1},{1,0},{2,3},{3,2},{4,5},{5,4},{6,7},{7,6},{8,9},{9,8},{10,11... | collective-permute-start | bytes 73736 | tf_op jit(solution)/shard_map/ppermute | solution.py:387
  40.7 7.5 %collective-permute-start.15 = (f32[48,128]{1,0:T(8,128)S(1)}, f32[48,128]{1,0:T(8,128)S(1)}, u32[]{:S(2)}, u32[]{:S(2)}) collective-permute-start(f32[48,128]{1,0:T(8,128)S(1)} %get-tuple-element.44), channel_id=1, source_target_pairs={{0,2},{1,3},{2,4},{3,5},{4,6},{5,7},{6,8},{7,9},{8,10},{9,11},{10,... | collective-permute-start | bytes 73736 | tf_op jit(solution)/shard_map/ppermute | solution.py:387
  40.8 7.4 %collective-permute-start.14 = (f32[48,128]{1,0:T(8,128)S(1)}, f32[48,128]{1,0:T(8,128)S(1)}, u32[]{:S(2)}, u32[]{:S(2)}) collective-permute-start(f32[48,128]{1,0:T(8,128)S(1)} %get-tuple-element.44), channel_id=1, source_target_pairs={{0,31},{1,2},{2,1},{3,4},{4,3},{5,6},{6,5},{7,8},{8,7},{9,10},{10,... | collective-permute-start | bytes 73736 | tf_op jit(solution)/shard_map/ppermute | solution.py:387
  42.9 5.3 %collective-permute-start.13 = (f32[48,128]{1,0:T(8,128)S(1)}, f32[48,128]{1,0:T(8,128)S(1)}, u32[]{:S(2)}, u32[]{:S(2)}) collective-permute-start(f32[48,128]{1,0:T(8,128)S(1)} %get-tuple-element.44), channel_id=1, source_target_pairs={{0,16},{1,17},{2,18},{3,19},{4,20},{5,21},{6,22},{7,23},{8,24},{9,... | collective-permute-start | bytes 73736 | tf_op jit(solution)/shard_map/ppermute | solution.py:387
  42.9 5.3 %collective-permute-start.12 = (f32[48,128]{1,0:T(8,128)S(1)}, f32[48,128]{1,0:T(8,128)S(1)}, u32[]{:S(2)}, u32[]{:S(2)}) collective-permute-start(f32[48,128]{1,0:T(8,128)S(1)} %get-tuple-element.44), channel_id=1, source_target_pairs={{0,1},{1,0},{2,3},{3,2},{4,5},{5,4},{6,7},{7,6},{8,9},{9,8},{10,11... | collective-permute-start | bytes 73736 | tf_op jit(solution)/shard_map/ppermute | solution.py:387
  52.3 4.4 %collective-permute-start.19 = (f32[48,128]{1,0:T(8,128)S(1)}, f32[48,128]{1,0:T(8,128)S(1)}, u32[]{:S(2)}, u32[]{:S(2)}) collective-permute-start(f32[48,128]{1,0:T(8,128)S(1)} %get-tuple-element.46), channel_id=1, source_target_pairs={{0,30},{1,31},{2,0},{3,1},{4,2},{5,3},{6,4},{7,5},{8,6},{9,7},{10,... | collective-permute-start | bytes 73736 | tf_op jit(solution)/shard_map/ppermute | solution.py:387
  55.2 6.9 %collective-permute-start.18 = (f32[48,128]{1,0:T(8,128)S(1)}, f32[48,128]{1,0:T(8,128)S(1)}, u32[]{:S(2)}, u32[]{:S(2)}) collective-permute-start(f32[48,128]{1,0:T(8,128)S(1)} %get-tuple-element.46), channel_id=1, source_target_pairs={{0,31},{1,2},{2,1},{3,4},{4,3},{5,6},{6,5},{7,8},{8,7},{9,10},{10,... | collective-permute-start | bytes 73736 | tf_op jit(solution)/shard_map/ppermute | solution.py:387
  55.5 6.5 %collective-permute-start.17 = (f32[48,128]{1,0:T(8,128)S(1)}, f32[48,128]{1,0:T(8,128)S(1)}, u32[]{:S(2)}, u32[]{:S(2)}) collective-permute-start(f32[48,128]{1,0:T(8,128)S(1)} %get-tuple-element.46), channel_id=1, source_target_pairs={{0,16},{1,17},{2,18},{3,19},{4,20},{5,21},{6,22},{7,23},{8,24},{9,... | collective-permute-start | bytes 73736 | tf_op jit(solution)/shard_map/ppermute | solution.py:387
  55.5 6.5 %collective-permute-start.16 = (f32[48,128]{1,0:T(8,128)S(1)}, f32[48,128]{1,0:T(8,128)S(1)}, u32[]{:S(2)}, u32[]{:S(2)}) collective-permute-start(f32[48,128]{1,0:T(8,128)S(1)} %get-tuple-element.46), channel_id=1, source_target_pairs={{0,1},{1,0},{2,3},{3,2},{4,5},{5,4},{6,7},{7,6},{8,9},{9,8},{10,11... | collective-permute-start | bytes 73736 | tf_op jit(solution)/shard_map/ppermute | solution.py:387
  62.4 7.5 %collective-permute-start.23 = (f32[48,128]{1,0:T(8,128)S(1)}, f32[48,128]{1,0:T(8,128)S(1)}, u32[]{:S(2)}, u32[]{:S(2)}) collective-permute-start(f32[48,128]{1,0:T(8,128)S(1)} %get-tuple-element.48), channel_id=1, source_target_pairs={{0,2},{1,3},{2,4},{3,5},{4,6},{5,7},{6,8},{7,9},{8,10},{9,11},{10,... | collective-permute-start | bytes 73736 | tf_op jit(solution)/shard_map/ppermute | solution.py:387
  62.5 7.4 %collective-permute-start.22 = (f32[48,128]{1,0:T(8,128)S(1)}, f32[48,128]{1,0:T(8,128)S(1)}, u32[]{:S(2)}, u32[]{:S(2)}) collective-permute-start(f32[48,128]{1,0:T(8,128)S(1)} %get-tuple-element.48), channel_id=1, source_target_pairs={{0,31},{1,2},{2,1},{3,4},{4,3},{5,6},{6,5},{7,8},{8,7},{9,10},{10,... | collective-permute-start | bytes 73736 | tf_op jit(solution)/shard_map/ppermute | solution.py:387
  64.6 5.3 %collective-permute-start.21 = (f32[48,128]{1,0:T(8,128)S(1)}, f32[48,128]{1,0:T(8,128)S(1)}, u32[]{:S(2)}, u32[]{:S(2)}) collective-permute-start(f32[48,128]{1,0:T(8,128)S(1)} %get-tuple-element.48), channel_id=1, source_target_pairs={{0,16},{1,17},{2,18},{3,19},{4,20},{5,21},{6,22},{7,23},{8,24},{9,... | collective-permute-start | bytes 73736 | tf_op jit(solution)/shard_map/ppermute | solution.py:387
  64.6 5.3 %collective-permute-start.20 = (f32[48,128]{1,0:T(8,128)S(1)}, f32[48,128]{1,0:T(8,128)S(1)}, u32[]{:S(2)}, u32[]{:S(2)}) collective-permute-start(f32[48,128]{1,0:T(8,128)S(1)} %get-tuple-element.48), channel_id=1, source_target_pairs={{0,1},{1,0},{2,3},{3,2},{4,5},{5,4},{6,7},{7,6},{8,9},{9,8},{10,11... | collective-permute-start | bytes 73736 | tf_op jit(solution)/shard_map/ppermute | solution.py:387

commit v3 on v2

--- a/solution.py
+++ b/solution.py
@@ -171,7 +171,7 @@
 def start_kernel(
     ranks, inner, trace, owned, cap,
     mortar_hbm, kind_hbm, force_hbm, back_hbm, inverse_hbm, couple_hbm, self_hbm,
-    own_ref, out_ref, onehot_ref, meta_ref, load_ref, inverse_ref, couple_ref, self_ref,
+    own_ref, out_ref, gid_ref, onehot_ref, meta_ref, load_ref, inverse_ref, couple_ref, self_ref,
     mortar_ref, kind_ref, force_ref, back_ref, *sems,
 ):
     copies = [
@@ -211,12 +211,13 @@
         lax.broadcasted_iota(jnp.int32, (slots, slots), 0) == target, 1.0, 0.0
     ).astype(BF16)
     facts = jnp.concatenate(
-        [in_a_row(column), in_a_row(index + 1), in_a_row(kind_ref[...]), jnp.zeros((5, slots), jnp.int32)],
+        [in_a_row(column), in_a_row(mortar + 1), in_a_row(kind_ref[...]), jnp.zeros((5, slots), jnp.int32)],
         axis=0,
     ).astype(F32)
     facts = exact_dot(facts, order)
     meta_ref[...] = facts
     meta_ref[3:4, :] = jnp.broadcast_to(lax.rem(me, 2).astype(F32), (1, slots))
+    meta_ref[4:5, :] = jnp.broadcast_to((me * owned).astype(F32), (1, slots))
     column = facts[0:1, :].astype(jnp.int32)
     onehot_ref[...] = jnp.where(
         lax.broadcasted_iota(jnp.int32, onehot_ref.shape, 0) == column, 1.0, 0.0
@@ -234,6 +235,7 @@
     sums = exact_dot(jnp.concatenate([z, label], axis=0), onehot_ref[...], 1)
     own_ref[...] = sums[: COMP * NODES, :owned]
     out_ref[...] = sums[:, owned:]
+    gid_ref[...] = sums[COMP * NODES :, owned:]
     copies[6].wait()
 
 
@@ -246,29 +248,126 @@
     return jnp.where(lane < cap, fourth, jnp.where(lane < 3 * cap, middle, third))
 
 
-def owner_kernel(owned, cap, initial, meta_ref, label_ref, own_ref, a_ref, b_ref, c_ref, d_ref, *outs):
+def onehot_of(condition):
+    return jnp.where(condition, 1.0, 0.0).astype(BF16)
+
+
+def own_ids(meta_ref, owned, count):
+    base = meta_ref[4:5, :count].astype(jnp.int32)
+    return lax.broadcasted_iota(jnp.int32, (owned, count), 0) + base + 1
+
+
+def wanted_by(label, meta_ref, owned):
+    count = label.shape[1]
+    return onehot_of(own_ids(meta_ref, owned, count) == label.astype(jnp.int32))
+
+
+def owner_kernel(owned, cap, meta_ref, own_ref, a_ref, b_ref, c_ref, d_ref, field_ref, out_ref, label_ref):
     received = merged(meta_ref, a_ref[...], b_ref[...], c_ref[...], d_ref[...], cap, True)
     rows = COMP * NODES
-    if initial:
-        field_ref, out_ref, label_out_ref = outs
-        label = received[rows : rows + 8]
-        label_out_ref[...] = label
-    else:
-        field_ref, out_ref = outs
-        label = label_ref[...]
-    wanted = (
-        lax.broadcasted_iota(jnp.int32, (owned, RUNS * cap), 0)
-        == label[0:1, :].astype(jnp.int32) - 1
-    )
-    wanted = jnp.where(wanted, 1.0, 0.0).astype(BF16)
+    label_ref[...] = received[rows : rows + 8]
+    wanted = wanted_by(received[rows : rows + 1], meta_ref, owned)
     field = own_ref[...] + exact_dot(received[:rows], wanted, 1)
     field_ref[...] = field
     out_ref[...] = exact_dot(field, wanted)
 
 
-def element_values(cap, meta_ref, onehot_ref, forth_ref, field_ref, blocks, spread_ref):
-    received = merged(meta_ref, *[b[...] for b in blocks], cap, False)
-    source = jnp.concatenate([field_ref[...], received], axis=1)
+def share(owned, sums, gid_ref, label_ref, meta_ref, own_ref, shared_ref):
+    rows = COMP * NODES
+    own = sums[:, :owned]
+    own_ref[...] = own
+    shared_ref[:rows, :] = sums[:, owned:]
+    label = label_ref[0:1, :]
+    shared_ref[rows : 2 * rows, :] = exact_dot(own, wanted_by(label, meta_ref, owned))
+    row = lax.broadcasted_iota(jnp.int32, gid_ref.shape, 0)
+    shared_ref[2 * rows :, :] = jnp.where(
+        row == 0, gid_ref[0:1, :], jnp.where(row == 1, label, 0.0)
+    )
+
+
+def ids_down(ids, count):
+    return jnp.broadcast_to(jnp.transpose(jnp.broadcast_to(ids, (8, ids.shape[1])))[:, 0:1], (ids.shape[1], count))
+
+
+def pack_kernel(cap, meta_ref, mine_ref, other_ref, one_ref, two_ref, three_ref, four_ref):
+    rows = COMP * NODES
+    count = RUNS * cap
+    odd = meta_ref[3:4, :count] == 1.0
+    mine, other = mine_ref[...], other_ref[...]
+    even_part = jnp.where(odd, other, mine)
+    odd_part = jnp.where(odd, mine, other)
+    source = jnp.concatenate([even_part[:rows], odd_part[:rows]], axis=1)
+    gids = jnp.concatenate([even_part[2 * rows : 2 * rows + 1], odd_part[2 * rows : 2 * rows + 1]], axis=1)
+    blank = jnp.zeros((8, count), F32)
+    sums = []
+    for part in (even_part, odd_part):
+        label = part[2 * rows + 1 : 2 * rows + 2]
+        match = onehot_of((ids_down(label, 2 * count) == gids) & (gids > 0.0))
+        full = part[rows : 2 * rows] + exact_dot(source, match, 1)
+        sums.append(jnp.concatenate([full, blank], axis=0))
+    outs = [
+        jnp.concatenate([part[:rows], part[2 * rows : 2 * rows + 1], blank[1:]], axis=0)
+        for part in (even_part, odd_part)
+    ]
+    lane = lax.broadcasted_iota(jnp.int32, (1, count), 1)
+
+    def laid(*blocks):
+        result = jnp.zeros((rows + 8, count), F32)
+        for place, block in enumerate(blocks):
+            if block is not None:
+                array, run = block
+                if run != place:
+                    array = pltpu.roll(array, ((place - run) % RUNS) * cap, 1)
+                inside = (lane >= place * cap) & (lane < (place + 1) * cap)
+                result = jnp.where(inside, array, result)
+        return result
+
+    (oe, oo), (ge, go) = outs, sums
+    one_ref[...] = jnp.where(
+        odd, laid((oe, 0), (oe, 1), (ge, 2), (oo, 0)), laid((ge, 0), (go, 1), (oo, 2), (go, 0))
+    )
+    two_ref[...] = jnp.where(odd, laid((oe, 0)), laid(None, None, (oo, 2)))
+    three_ref[...] = jnp.where(
+        odd, laid((oo, 3), None, (oo, 2), (oe, 3)), laid((oe, 0), (oe, 1), (oo, 0), (oe, 3))
+    )
+    four_ref[...] = laid((jnp.where(odd, oo, oe), 3), None, None, (jnp.where(odd, go, ge), 3))
+
+
+def fused_values(owned, cap, meta_ref, own_ref, mine_ref, other_ref, got, passed):
+    rows = COMP * NODES
+    count = RUNS * cap
+    lane = lax.broadcasted_iota(jnp.int32, (1, count), 1)
+    odd = meta_ref[3:4, :count] == 1.0
+    mine, other = mine_ref[...], other_ref[...]
+    blocks = [r[...] for r in (*got, *passed)]
+    source = jnp.concatenate([mine[:rows], other[:rows]] + [x[:rows] for x in blocks], axis=1)
+    gids = jnp.concatenate(
+        [mine[2 * rows : 2 * rows + 1], other[2 * rows : 2 * rows + 1]]
+        + [x[rows : rows + 1] for x in blocks],
+        axis=1,
+    )
+    total_count = gids.shape[1]
+    remote = ids_down(mine[2 * rows : 2 * rows + 1], total_count)
+    own = lax.broadcasted_iota(jnp.int32, (owned, total_count), 0).astype(F32) + (
+        meta_ref[4:5, 0:1] + 1.0
+    )
+    match = onehot_of(jnp.concatenate([own, jnp.where(remote > 0.0, remote, -1.0)], axis=0) == gids)
+    sums = exact_dot(source, match, 1)
+    field = own_ref[...] + sums[:, :owned]
+    near, far = got[0][...][:rows], got[3][...][:rows]
+    across = passed[0][...][:rows]
+    partner = other[rows : 2 * rows]
+    even_form = jnp.where(lane < 2 * cap, across, jnp.where(lane < 3 * cap, partner, far))
+    odd_form = jnp.where(
+        lane < cap,
+        pltpu.roll(near, cap, 1),
+        jnp.where(lane < 2 * cap, partner, jnp.where(lane < 3 * cap, across, far)),
+    )
+    return field, jnp.where(odd, odd_form, even_form) + sums[:, owned:]
+
+
+def element_values(field, received, meta_ref, onehot_ref, forth_ref, spread_ref):
+    source = jnp.concatenate([field, received], axis=1)
     kind = meta_ref[2:3, :]
     faces = by_kind(exact_dot(source, onehot_ref[...]), forth_ref, kind)
     width = spread_ref.shape[1]
@@ -281,23 +380,32 @@
 
 
 def apply_kernel(
-    inner, trace, owned, cap,
-    meta_ref, onehot_ref, forth_ref, back_ref, inverse_ref, couple_ref, self_ref,
-    field_ref, a_ref, b_ref, c_ref, d_ref,
-    own_ref, out_ref, spread_ref, mid_ref, weight_ref, image_ref,
+    inner, trace, owned, cap, fused,
+    meta_ref, onehot_ref, forth_ref, back_ref, gid_ref, label_ref, inverse_ref, couple_ref, self_ref,
+    *refs,
 ):
+    if fused:
+        before_ref, mine_ref, other_ref, *received = refs[:11]
+        refs = refs[11:]
+        field_ref, refs = refs[0], refs[1:]
+        field, received = fused_values(
+            owned, cap, meta_ref, before_ref, mine_ref, other_ref, received[:4], received[4:]
+        )
+        field_ref[...] = field
+    else:
+        field = refs[0][...]
+        received = merged(meta_ref, *[r[...] for r in refs[1:5]], cap, False)
+        refs = refs[5:]
+    own_ref, shared_ref, spread_ref, mid_ref, weight_ref, image_ref = refs
     width = spread_ref.shape[1]
-    kind = element_values(
-        cap, meta_ref, onehot_ref, forth_ref, field_ref, (a_ref, b_ref, c_ref, d_ref), spread_ref
-    )
+    kind = element_values(field, received, meta_ref, onehot_ref, forth_ref, spread_ref)
     rows_times(couple_ref, spread_ref, mid_ref, inner, trace)
     rows_times(inverse_ref, mid_ref, weight_ref, inner, inner)
     rows_times(self_ref, spread_ref, image_ref, trace, trace)
     y = columns_times(tiles_of(image_ref, trace), couple_ref, weight_ref, trace, inner)
     z = by_kind(face_columns(y), back_ref, kind)
     sums = exact_dot(z, onehot_ref[...], 1)
-    own_ref[...] = sums[:, :owned]
-    out_ref[...] = sums[:, owned:]
+    share(owned, sums, gid_ref, label_ref, meta_ref, own_ref, shared_ref)
 
 
 def total(x):
@@ -305,20 +413,23 @@
 
 
 def last_kernel(
-    inner, trace, cap,
+    inner, trace, owned, cap,
     meta_ref, onehot_ref, forth_ref, inverse_ref, couple_ref, self_ref,
-    k0_ref, k1_ref, k2_ref, a_ref, b_ref, c_ref, d_ref, s0_ref, s1_ref, u0_ref, u1_ref,
-    weight_ref, moment_ref, spread_ref, mid_ref, image_ref,
+    k0_ref, k1_ref, s0_ref, s1_ref, u0_ref, u1_ref, before_ref, mine_ref, other_ref, *refs,
 ):
+    received, refs = refs[:8], refs[8:]
+    k2_ref, weight_ref, moment_ref, spread_ref, mid_ref, image_ref = refs
     width = spread_ref.shape[1]
-    element_values(
-        cap, meta_ref, onehot_ref, forth_ref, k2_ref, (a_ref, b_ref, c_ref, d_ref), spread_ref
-    )
+    field, received = fused_values(
+        owned, cap, meta_ref, before_ref, mine_ref, other_ref, received[:4], received[4:]
+    )
+    k2_ref[...] = field
+    element_values(field, received, meta_ref, onehot_ref, forth_ref, spread_ref)
     rows_times(couple_ref, spread_ref, mid_ref, inner, trace)
     rows_times(inverse_ref, mid_ref, weight_ref, inner, inner)
     rows_times(self_ref, spread_ref, image_ref, trace, trace)
     image, weight = image_ref[...], weight_ref[...]
-    ks = (k0_ref[...], k1_ref[...], k2_ref[...])
+    ks = (k0_ref[...], k1_ref[...], field)
     values = [total(ks[i] * ks[j]) for i in range(3) for j in range(i, 3)]
     for s_ref, u_ref in ((s0_ref, u0_ref), (s1_ref, u1_ref), (spread_ref, mid_ref)):
         values.append(total(s_ref[...] * image) + total(u_ref[...] * weight))
@@ -387,6 +498,29 @@
     return [lax.ppermute(block, AXES, pairs[n]) for n in (0, 2, 1, 3)]
 
 
+def fused_exchange(cap, meta, shared, ranks):
+    pair = [(r, r ^ 1) for r in range(ranks)]
+
+    def both_ways(chips):
+        ahead = [(r, (r + 2 * chips + 1) % ranks) for r in range(0, ranks, 2)]
+        return ahead + [(t, r) for r, t in ahead]
+
+    other = lax.ppermute(shared, AXES, pair)
+    shape = (COMP * NODES + 8, RUNS * cap)
+    packed = call(
+        functools.partial(pack_kernel, cap), [(shape, F32)] * 4, meta, shared, other
+    )
+    ways = [
+        both_ways(1),
+        both_ways(2),
+        both_ways(ranks // 4 - 1),
+        [(r, (r + ranks // 2) % ranks) for r in range(ranks)],
+    ]
+    got = [lax.ppermute(block, AXES, way) for block, way in zip(packed, ways)]
+    passed = [lax.ppermute(block, AXES, pair) for block in got]
+    return [shared, other, *got, *passed]
+
+
 def local(self_block, couple, inverse, body_force, face_mortar, face_kind, *, ranks):
     trace, _, elements = self_block.shape
     inner = inverse.shape[0]
@@ -402,11 +536,12 @@
     inverse = inverse.reshape(inner * inner, width)
     force = body_force.reshape(COMP * inner, width)
 
-    own, out, onehot, meta, load, *matrices = call(
+    own, out, gid, onehot, meta, load, *matrices = call(
         functools.partial(start_kernel, ranks, inner, trace, owned, cap),
         [
             ((rows, owned), F32),
             ((rows + 8, RUNS * cap), F32),
+            ((8, RUNS * cap), F32),
             ((owned + RUNS * cap, FACES * width), BF16),
             ((8, FACES * width), F32),
             ((COMP * inner, width), F32),
@@ -422,46 +557,44 @@
     )
     blocks = exchange(out, ranks, True)
     field, out, label = call(
-        functools.partial(owner_kernel, owned, cap, True),
+        functools.partial(owner_kernel, owned, cap),
         [((rows, owned), F32), ((rows, RUNS * cap), F32), ((8, RUNS * cap), F32)],
-        meta, meta, own, *blocks,
-    )
+        meta, own, *blocks,
+    )
+    blocks = exchange(out, ranks, False)
     fields, spreads, mids, weights = [field], [], [], []
-    for _ in range(2):
-        blocks = exchange(out, ranks, False)
-        own, out, spread, mid, weight = call(
-            functools.partial(apply_kernel, inner, trace, owned, cap),
-            [
+    for iteration in range(2):
+        fused = iteration > 0
+        first = [((rows, owned), F32)] if fused else []
+        results = call(
+            functools.partial(apply_kernel, inner, trace, owned, cap, fused),
+            first + [
                 ((rows, owned), F32),
-                ((rows, RUNS * cap), F32),
+                ((2 * rows + 8, RUNS * cap), F32),
                 ((COMP * trace, width), F32),
                 ((COMP * inner, width), F32),
                 ((COMP * inner, width), F32),
             ],
-            meta, onehot, forward, backward, *matrices, field, *blocks,
+            meta, onehot, forward, backward, gid, label, *matrices, own if fused else field, *blocks,
             scratch=[((COMP * trace, width), F32)],
         )
+        fields += results[: len(first)]
+        own, shared, spread, mid, weight = results[len(first) :]
         spreads.append(spread)
         mids.append(mid)
         weights.append(weight)
-        blocks = exchange(out, ranks, True)
-        field, out = call(
-            functools.partial(owner_kernel, owned, cap, False),
-            [((rows, owned), F32), ((rows, RUNS * cap), F32)],
-            meta, label, own, *blocks,
-        )
-        fields.append(field)
-    blocks = exchange(out, ranks, False)
-    weight, moments = call(
-        functools.partial(last_kernel, inner, trace, cap),
-        [((COMP * inner, width), F32), ((ranks, 1, width), F32)],
-        meta, onehot, forward, *matrices, *fields, *blocks, *spreads, *mids,
+        blocks = fused_exchange(cap, meta, shared, ranks)
+    field, weight, moments = call(
+        functools.partial(last_kernel, inner, trace, owned, cap),
+        [((rows, owned), F32), ((COMP * inner, width), F32), ((ranks, 1, width), F32)],
+        meta, onehot, forward, *matrices, *fields, *spreads, *mids, own, *blocks,
         scratch=[
             ((COMP * trace, width), F32),
             ((COMP * inner, width), F32),
             ((COMP * trace, width), F32),
         ],
     )
+    fields.append(field)
     weights.append(weight)
     moments = lax.all_to_all(moments, AXES, split_axis=0, concat_axis=0, tiled=True)
     trace_field, interior = call(

time: 85.5 us -> 78 us (0.912)
  waiting for transfers between devices: 35.9 us -> 16.3 us
  starting transfers between devices: 20.1 us -> 29.4 us
  Pallas kernels: 18.4 us -> 20.2 us
  blocking collectives: 10.2 us -> 11.1 us
    ppermute x24 -> x8, waiting for transfers between devices: 35.9 us -> 12.2 us  [exchange(): return [lax.ppermute(block, AXES, pairs[n]) for n in (0, 2, 1, 3)]]
    ppermute x0 -> x18, starting transfers between devices: none -> 20.2 us  [the longest x8 13.1 us: fused_exchange(): got = [lax.ppermute(block, AXES, way) for block, way in zip(packed, ways)]]
    ppermute x24 -> x8, starting transfers between devices: 20.1 us -> 9.21 us  [exchange(): return [lax.ppermute(block, AXES, pairs[n]) for n in (0, 2, 1, 3)]]
    ppermute x0 -> x18, waiting for transfers between devices: none -> 4.16 us  [the longest x2 2.11 us: fused_exchange(): other = lax.ppermute(shared, AXES, pair)]
    pallas_call x8, Pallas kernels: 18.4 us -> 20.2 us  [call(): pl.pallas_call(kernel, out_shape=[jax.ShapeDtypeStruct(shape, dtype) for...]
    all_to_all x1, blocking collectives: 10.2 us -> 11.1 us  [local(): lax.all_to_all(moments, AXES, split_axis=0, concat_axis=0, tiled=True)]
  transfers between devices with their start and end apart: 24 -> 26, of which waited for: 9 -> 11; matrix products, arithmetic and copies ran while one was open for 0% -> 0% of each run, Pallas kernels for 0% -> 0%
where the time goes in v3:
time: 78 us; the launch traced here: 77.9 us
  starting transfers between devices  29.4 us (38%)
  Pallas kernels  20.2 us (26%)
  waiting for transfers between devices  16.3 us (21%)
  blocking collectives  11.1 us (14%)
  between operations  0.78 us (1%)
    pallas_call x8, Pallas kernels, call(): pl.pallas_call(kernel, out_shape=[jax.ShapeDtypeStruct(shape, dtype) for...  20.2 us
    ppermute x8, starting transfers between devices, fused_exchange(): got = [lax.ppermute(block, AXES, way) for block, way in zip(packed, ways)]  13.1 us
    ppermute x8, waiting for transfers between devices, exchange(): return [lax.ppermute(block, AXES, pairs[n]) for n in (0, 2, 1, 3)]  12.2 us
    all_to_all x1, blocking collectives, local(): lax.all_to_all(moments, AXES, split_axis=0, concat_axis=0, tiled=True)  11.1 us
    ppermute x8, starting transfers between devices, exchange(): return [lax.ppermute(block, AXES, pairs[n]) for n in (0, 2, 1, 3)]  9.21 us
    ppermute x8, starting transfers between devices, fused_exchange(): passed = [lax.ppermute(block, AXES, pair) for block in got]  6.59 us
    ppermute x2, waiting for transfers between devices, fused_exchange(): other = lax.ppermute(shared, AXES, pair)  2.11 us
    ppermute x8, waiting for transfers between devices, fused_exchange(): passed = [lax.ppermute(block, AXES, pair) for block in got]  1.71 us
  transfers between devices with their start and end apart: 26, of which 11 were waited for; matrix products, arithmetic and copies ran while one was open for 0% of the time, Pallas kernels for 0%

profile of v3, /device:TPU:0, one launch (start us, length us, event | category | flops | bytes accessed | tf_op | source)
XLA Modules:
  0.0 77.9 jit_solution(8626408719043332835)
XLA Ops:
  0.7 4.1 %shard_map.95 = (f32[48,256]{1,0:T(8,128)S(1)}, f32[56,128]{1,0:T(8,128)S(1)}, f32[8,128]{1,0:T(8,128)S(1)}, bf16[384,768]{1,0:T(8,128)(2,1)S(1)}, f32[8,768]{1,...) custom-call(s32[6,128]{1,0:T(8,128)} %bitcast.11, ...), custom_call_target="tpu_custom_call" | custom-call | tf_op jit(solution)/shard_map/pallas_call | solution.py:478
  4.8 7.0 %collective-permute-start.3 = (f32[56,128]{1,0:T(8,128)S(1)}, f32[56,128]{1,0:T(8,128)S(1)}, u32[]{:S(2)}, u32[]{:S(2)}) collective-permute-start(f32[56,128]{1,0:T(8,128)S(1)} %get-tuple-element.44), channel_id=1, source_target_pairs={{0,30},{1,31},{2,0},{3,1},{4,2},{5,3},{6,4},{7,5},{8,6},{9,7},{10,... | collective-permute-start | bytes 86024 | tf_op jit(solution)/shard_map/ppermute | solution.py:498
  11.8 1.5 %collective-permute-done.3.d_ref = f32[56,128]{1,0:T(8,128)S(1)} collective-permute-done((f32[56,128]{1,0:T(8,128)S(1)}, f32[56,128]{1,0:T(8,128)S(1)}, u32[]{:S(2)}, u32[]{:S(2)}) %collective-permute-start.3) | collective-permute-done | bytes 28704 | tf_op jit(solution)/shard_map/ppermute | solution.py:498
  13.4 5.3 %collective-permute-done.2.c_ref = f32[56,128]{1,0:T(8,128)S(1)} collective-permute-done((f32[56,128]{1,0:T(8,128)S(1)}, f32[56,128]{1,0:T(8,128)S(1)}, u32[]{:S(2)}, u32[]{:S(2)}) %collective-permute-start.2) | collective-permute-done | bytes 28704 | tf_op jit(solution)/shard_map/ppermute | solution.py:498
  19.1 2.2 %collective-permute-start.6 = (f32[48,128]{1,0:T(8,128)S(1)}, f32[48,128]{1,0:T(8,128)S(1)}, u32[]{:S(2)}, u32[]{:S(2)}) collective-permute-start(f32[48,128]{1,0:T(8,128)S(1)} %get-tuple-element.48), channel_id=1, source_target_pairs={{0,31},{1,2},{2,1},{3,4},{4,3},{5,6},{6,5},{7,8},{8,7},{9,10},{10,... | collective-permute-start | bytes 73736 | tf_op jit(solution)/shard_map/ppermute | solution.py:498
  21.2 5.3 %collective-permute-done.7.refs_4_ = f32[48,128]{1,0:T(8,128)S(1)} collective-permute-done((f32[48,128]{1,0:T(8,128)S(1)}, f32[48,128]{1,0:T(8,128)S(1)}, u32[]{:S(2)}, u32[]{:S(2)}) %collective-permute-start.7) | collective-permute-done | bytes 24608 | tf_op jit(solution)/shard_map/ppermute | solution.py:498
  26.6 4.2 %shard_map.97 = (f32[48,256]{1,0:T(8,128)S(1)}, f32[104,128]{1,0:T(8,128)S(1)}, f32[288,128]{1,0:T(8,128)S(1)}, f32[192,128]{1,0:T(8,128)S(1)}, f32[192,128]{1,0:T(8,128)S(1)}) custom-call(f32[8,768]{1,0:T(8,128)S(1)} %get-tuple-element.38.meta_ref, bf16[384,768]{1,0:T(8,128)(2,1)S(1)} %get-tuple-element.39.onehot_ref, f32[192,48]{1,0:T(8,128)S(1)} %copy-done, ...), custom_call_target="tpu_custom_call" | custom-call | tf_op jit(solution)/shard_map/pallas_call | solution.py:478
  30.9 1.2 %collective-permute-done.8.other_ref.refs_2_ = f32[104,128]{1,0:T(8,128)S(1)} collective-permute-done((f32[104,128]{1,0:T(8,128)S(1)}, f32[104,128]{1,0:T(8,128)S(1)}, u32[]{:S(2)}, u32[]{:S(2)}) %collective-permute-start.8) | collective-permute-done | bytes 53280 | tf_op jit(solution)/shard_map/ppermute | solution.py:508
  32.1 0.4 shard_map.98
  32.7 2.5 %collective-permute-start.11 = (f32[56,128]{1,0:T(8,128)S(1)}, f32[56,128]{1,0:T(8,128)S(1)}, u32[]{:S(2)}, u32[]{:S(2)}) collective-permute-start(f32[56,128]{1,0:T(8,128)S(1)} %get-tuple-element.53), channel_id=1, source_target_pairs={{0,15},{2,17},{4,19},{6,21},{8,23},{10,25},{12,27},{14,29},{16,31}... | collective-permute-start | bytes 86024 | tf_op jit(solution)/shard_map/ppermute | solution.py:519
  35.2 2.6 %collective-permute-start.12 = (f32[56,128]{1,0:T(8,128)S(1)}, f32[56,128]{1,0:T(8,128)S(1)}, u32[]{:S(2)}, u32[]{:S(2)}) collective-permute-start(f32[56,128]{1,0:T(8,128)S(1)} %get-tuple-element.54), channel_id=1, source_target_pairs={{0,16},{1,17},{2,18},{3,19},{4,20},{5,21},{6,22},{7,23},{8,24},{9,... | collective-permute-start | bytes 86024 | tf_op jit(solution)/shard_map/ppermute | solution.py:519
  37.8 2.1 %collective-permute-start.13 = (f32[56,128]{1,0:T(8,128)S(1)}, f32[56,128]{1,0:T(8,128)S(1)}, u32[]{:S(2)}, u32[]{:S(2)}) collective-permute-start(f32[56,128]{1,0:T(8,128)S(1)} %collective-permute-done.9.refs_3_), channel_id=1, source_target_pairs={{0,1},{1,0},{2,3},{3,2},{4,5},{5,4},{6,7},{7,6},{8,9},{9,8},{10,11... | collective-permute-start | bytes 86024 | tf_op jit(solution)/shard_map/ppermute | solution.py:520
  40.0 1.6 %collective-permute-start.14 = (f32[56,128]{1,0:T(8,128)S(1)}, f32[56,128]{1,0:T(8,128)S(1)}, u32[]{:S(2)}, u32[]{:S(2)}) collective-permute-start(f32[56,128]{1,0:T(8,128)S(1)} %collective-permute-done.10.refs_4_), channel_id=1, source_target_pairs={{0,1},{1,0},{2,3},{3,2},{4,5},{5,4},{6,7},{7,6},{8,9},{9,8},{10,11... | collective-permute-start | bytes 86024 | tf_op jit(solution)/shard_map/ppermute | solution.py:520
  41.6 0.5 collective-permute-start.16
  42.1 0.3 collective-permute-done.14.refs_8_
  42.5 0.3 collective-permute-done.15.refs_9_
  43.0 4.8 %shard_map.99 = (f32[48,256]{1,0:T(8,128)S(1)}, f32[48,256]{1,0:T(8,128)S(1)}, f32[104,128]{1,0:T(8,128)S(1)}, f32[288,128]{1,0:T(8,128)S(1)}, f32[192,128]{1,0:T(8,128)S(1)}, /*index=5*/f32[192,128]{1,0:T(8,128)S(1)}) custom-call(f32[8,768]{1,0:T(8,128)S(1)} %get-tuple-element.38.meta_ref, bf16[384,768]{1,0:T(8,128)(2,1)S(1)} %get-tuple-element.39.onehot_ref, ...), custom_call_target="tpu_custom_call" | custom-call | tf_op jit(solution)/shard_map/pallas_call | solution.py:478
  47.8 0.4 collective-permute-start.17
  48.2 0.9 %collective-permute-done.17.other_ref = f32[104,128]{1,0:T(8,128)S(1)} collective-permute-done((f32[104,128]{1,0:T(8,128)S(1)}, f32[104,128]{1,0:T(8,128)S(1)}, u32[]{:S(2)}, u32[]{:S(2)}) %collective-permute-start.17) | collective-permute-done | bytes 53280 | tf_op jit(solution)/shard_map/ppermute | solution.py:508
  49.1 0.4 shard_map.100
  49.6 2.7 %collective-permute-start.18 = (f32[56,128]{1,0:T(8,128)S(1)}, f32[56,128]{1,0:T(8,128)S(1)}, u32[]{:S(2)}, u32[]{:S(2)}) collective-permute-start(f32[56,128]{1,0:T(8,128)S(1)} %get-tuple-element.62), channel_id=1, source_target_pairs={{0,3},{2,5},{4,7},{6,9},{8,11},{10,13},{12,15},{14,17},{16,19},{18... | collective-permute-start | bytes 86024 | tf_op jit(solution)/shard_map/ppermute | solution.py:519
  52.3 1.4 %collective-permute-start.19 = (f32[56,128]{1,0:T(8,128)S(1)}, f32[56,128]{1,0:T(8,128)S(1)}, u32[]{:S(2)}, u32[]{:S(2)}) collective-permute-start(f32[56,128]{1,0:T(8,128)S(1)} %get-tuple-element.63), channel_id=1, source_target_pairs={{0,5},{2,7},{4,9},{6,11},{8,13},{10,15},{12,17},{14,19},{16,21},{1... | collective-permute-start | bytes 86024 | tf_op jit(solution)/shard_map/ppermute | solution.py:519
  53.9 3.5 %collective-permute-start.21 = (f32[56,128]{1,0:T(8,128)S(1)}, f32[56,128]{1,0:T(8,128)S(1)}, u32[]{:S(2)}, u32[]{:S(2)}) collective-permute-start(f32[56,128]{1,0:T(8,128)S(1)} %get-tuple-element.65), channel_id=1, source_target_pairs={{0,16},{1,17},{2,18},{3,19},{4,20},{5,21},{6,22},{7,23},{8,24},{9,... | collective-permute-start | bytes 86024 | tf_op jit(solution)/shard_map/ppermute | solution.py:519
  57.4 1.2 %collective-permute-start.23 = (f32[56,128]{1,0:T(8,128)S(1)}, f32[56,128]{1,0:T(8,128)S(1)}, u32[]{:S(2)}, u32[]{:S(2)}) collective-permute-start(f32[56,128]{1,0:T(8,128)S(1)} %collective-permute-done.19.refs_1_), channel_id=1, source_target_pairs={{0,1},{1,0},{2,3},{3,2},{4,5},{5,4},{6,7},{7,6},{8,9},{9,8},{10,11... | collective-permute-start | bytes 86024 | tf_op jit(solution)/shard_map/ppermute | solution.py:520
  58.7 0.3 collective-permute-done.20.refs_2_
  59.0 0.6 collective-permute-start.24
  59.6 0.5 collective-permute-start.25
  60.1 0.3 collective-permute-done.24.refs_6_
  60.4 0.5 collective-permute-done.25.refs_7_
  60.9 4.0 %shard_map.101 = (f32[48,256]{1,0:T(8,128)S(1)}, f32[192,128]{1,0:T(8,128)S(1)}, f32[32,1,128]{2,1,0:T(1,128)S(1)}) custom-call(f32[8,768]{1,0:T(8,128)S(1)} %get-tuple-element.38.meta_ref, bf16[384,768]{1,0:T(8,128)(2,1)S(1)} %get-tuple-element.39.onehot_ref, f32[192,48]{1,0:T(8,128)S(1)} %copy-done, f32[4096,128]{1,0:T(8,128)S(1)} %get-tuple-element.40.inverse_ref, ...), custom_call_target="tpu_custom_call" | custom-call | tf_op jit(solution)/shard_map/pallas_call | solution.py:478
  64.9 11.1 %all_to_all.5.moment_ref = f32[32,1,128]{2,1,0:T(1,128)S(1)} all-to-all(f32[32,1,128]{2,1,0:T(1,128)S(1)} %get-tuple-element.66), channel_id=1, replica_groups=mesh['dom'=16,'blk'=2] {'dom','blk'}, dimensions={0} | all-to-all | bytes 32768 | tf_op jit(solution)/shard_map/all_to_all | solution.py:599
  76.0 1.8 %shard_map.102 = (f32[48,256]{1,0:T(8,128)}, f32[192,128]{1,0:T(8,128)}) custom-call(f32[32,1,128]{2,1,0:T(1,128)S(1)} %all_to_all.5.moment_ref, f32[48,256]{1,0:T(8,128)S(1)} %get-tuple-element.45.refs_0_.k0_ref, f32[48,256]{1,0:T(8,128)S(1)} %get-tuple-element.55.k1_ref, f32[48,256]{1,0:T(8,128)S(1)} %get-tuple-element.67.k2_ref, ...), custom_call_target="tpu_custom_call" | custom-call | tf_op jit(solution)/shard_map/pallas_call | solution.py:478
  (33 shorter events, 1.0 us)
Async XLA Ops:
  0.6 25.9 %copy-start = (f32[192,48]{1,0:T(8,128)S(1)}, f32[192,48]{1,0:T(8,128)}, u32[]{:S(2)}) copy-start(f32[192,48]{1,0:T(8,128)} %constant.5.clone.forth_ref) | copy-start | bytes 110596
  0.6 25.9 %copy-start.1 = (f32[192,48]{1,0:T(8,128)S(1)}, f32[192,48]{1,0:T(8,128)}, u32[]{:S(2)}) copy-start(f32[192,48]{1,0:T(8,128)} %constant.4.clone.back_hbm.back_ref) | copy-start | bytes 110596
  4.8 8.5 %collective-permute-start.3 = (f32[56,128]{1,0:T(8,128)S(1)}, f32[56,128]{1,0:T(8,128)S(1)}, u32[]{:S(2)}, u32[]{:S(2)}) collective-permute-start(f32[56,128]{1,0:T(8,128)S(1)} %get-tuple-element.44), channel_id=1, source_target_pairs={{0,30},{1,31},{2,0},{3,1},{4,2},{5,3},{6,4},{7,5},{8,6},{9,7},{10,... | collective-permute-start | bytes 86024 | tf_op jit(solution)/shard_map/ppermute | solution.py:498
  11.8 6.9 %collective-permute-start.2 = (f32[56,128]{1,0:T(8,128)S(1)}, f32[56,128]{1,0:T(8,128)S(1)}, u32[]{:S(2)}, u32[]{:S(2)}) collective-permute-start(f32[56,128]{1,0:T(8,128)S(1)} %get-tuple-element.44), channel_id=1, source_target_pairs={{0,31},{1,2},{2,1},{3,4},{4,3},{5,6},{6,5},{7,8},{8,7},{9,10},{10,... | collective-permute-start | bytes 86024 | tf_op jit(solution)/shard_map/ppermute | solution.py:498
  11.8 6.9 %collective-permute-start.1 = (f32[56,128]{1,0:T(8,128)S(1)}, f32[56,128]{1,0:T(8,128)S(1)}, u32[]{:S(2)}, u32[]{:S(2)}) collective-permute-start(f32[56,128]{1,0:T(8,128)S(1)} %get-tuple-element.44), channel_id=1, source_target_pairs={{0,16},{1,17},{2,18},{3,19},{4,20},{5,21},{6,22},{7,23},{8,24},{9,... | collective-permute-start | bytes 86024 | tf_op jit(solution)/shard_map/ppermute | solution.py:498
  11.8 6.9 %collective-permute-start = (f32[56,128]{1,0:T(8,128)S(1)}, f32[56,128]{1,0:T(8,128)S(1)}, u32[]{:S(2)}, u32[]{:S(2)}) collective-permute-start(f32[56,128]{1,0:T(8,128)S(1)} %get-tuple-element.44), channel_id=1, source_target_pairs={{0,1},{1,0},{2,3},{3,2},{4,5},{5,4},{6,7},{7,6},{8,9},{9,8},{10,11... | collective-permute-start | bytes 86024 | tf_op jit(solution)/shard_map/ppermute | solution.py:498
  19.0 7.5 %collective-permute-start.7 = (f32[48,128]{1,0:T(8,128)S(1)}, f32[48,128]{1,0:T(8,128)S(1)}, u32[]{:S(2)}, u32[]{:S(2)}) collective-permute-start(f32[48,128]{1,0:T(8,128)S(1)} %get-tuple-element.48), channel_id=1, source_target_pairs={{0,2},{1,3},{2,4},{3,5},{4,6},{5,7},{6,8},{7,9},{8,10},{9,11},{10,... | collective-permute-start | bytes 73736 | tf_op jit(solution)/shard_map/ppermute | solution.py:498
  19.1 7.4 %collective-permute-start.6 = (f32[48,128]{1,0:T(8,128)S(1)}, f32[48,128]{1,0:T(8,128)S(1)}, u32[]{:S(2)}, u32[]{:S(2)}) collective-permute-start(f32[48,128]{1,0:T(8,128)S(1)} %get-tuple-element.48), channel_id=1, source_target_pairs={{0,31},{1,2},{2,1},{3,4},{4,3},{5,6},{6,5},{7,8},{8,7},{9,10},{10,... | collective-permute-start | bytes 73736 | tf_op jit(solution)/shard_map/ppermute | solution.py:498
  21.2 5.3 %collective-permute-start.5 = (f32[48,128]{1,0:T(8,128)S(1)}, f32[48,128]{1,0:T(8,128)S(1)}, u32[]{:S(2)}, u32[]{:S(2)}) collective-permute-start(f32[48,128]{1,0:T(8,128)S(1)} %get-tuple-element.48), channel_id=1, source_target_pairs={{0,16},{1,17},{2,18},{3,19},{4,20},{5,21},{6,22},{7,23},{8,24},{9,... | collective-permute-start | bytes 73736 | tf_op jit(solution)/shard_map/ppermute | solution.py:498
  21.2 5.3 %collective-permute-start.4 = (f32[48,128]{1,0:T(8,128)S(1)}, f32[48,128]{1,0:T(8,128)S(1)}, u32[]{:S(2)}, u32[]{:S(2)}) collective-permute-start(f32[48,128]{1,0:T(8,128)S(1)} %get-tuple-element.48), channel_id=1, source_target_pairs={{0,1},{1,0},{2,3},{3,2},{4,5},{5,4},{6,7},{7,6},{8,9},{9,8},{10,11... | collective-permute-start | bytes 73736 | tf_op jit(solution)/shard_map/ppermute | solution.py:498
  30.8 1.3 %collective-permute-start.8 = (f32[104,128]{1,0:T(8,128)S(1)}, f32[104,128]{1,0:T(8,128)S(1)}, u32[]{:S(2)}, u32[]{:S(2)}) collective-permute-start(f32[104,128]{1,0:T(8,128)S(1)} %get-tuple-element.50.mine_ref.refs_1_), channel_id=1, source_target_pairs={{0,1},{1,0},{2,3},{3,2},{4,5},{5,4},{6,7},{7,6},{8,9},{9,8},{10,11... | collective-permute-start | bytes 159752 | tf_op jit(solution)/shard_map/ppermute | solution.py:508
  32.6 5.3 %collective-permute-start.9 = (f32[56,128]{1,0:T(8,128)S(1)}, f32[56,128]{1,0:T(8,128)S(1)}, u32[]{:S(2)}, u32[]{:S(2)}) collective-permute-start(f32[56,128]{1,0:T(8,128)S(1)} %get-tuple-element.51), channel_id=1, source_target_pairs={{0,3},{2,5},{4,7},{6,9},{8,11},{10,13},{12,15},{14,17},{16,19},{18... | collective-permute-start | bytes 86024 | tf_op jit(solution)/shard_map/ppermute | solution.py:519
  32.6 7.3 %collective-permute-start.10 = (f32[56,128]{1,0:T(8,128)S(1)}, f32[56,128]{1,0:T(8,128)S(1)}, u32[]{:S(2)}, u32[]{:S(2)}) collective-permute-start(f32[56,128]{1,0:T(8,128)S(1)} %get-tuple-element.52), channel_id=1, source_target_pairs={{0,5},{2,7},{4,9},{6,11},{8,13},{10,15},{12,17},{14,19},{16,21},{1... | collective-permute-start | bytes 86024 | tf_op jit(solution)/shard_map/ppermute | solution.py:519
  32.7 8.9 %collective-permute-start.11 = (f32[56,128]{1,0:T(8,128)S(1)}, f32[56,128]{1,0:T(8,128)S(1)}, u32[]{:S(2)}, u32[]{:S(2)}) collective-permute-start(f32[56,128]{1,0:T(8,128)S(1)} %get-tuple-element.53), channel_id=1, source_target_pairs={{0,15},{2,17},{4,19},{6,21},{8,23},{10,25},{12,27},{14,29},{16,31}... | collective-permute-start | bytes 86024 | tf_op jit(solution)/shard_map/ppermute | solution.py:519
  35.2 6.4 %collective-permute-start.12 = (f32[56,128]{1,0:T(8,128)S(1)}, f32[56,128]{1,0:T(8,128)S(1)}, u32[]{:S(2)}, u32[]{:S(2)}) collective-permute-start(f32[56,128]{1,0:T(8,128)S(1)} %get-tuple-element.54), channel_id=1, source_target_pairs={{0,16},{1,17},{2,18},{3,19},{4,20},{5,21},{6,22},{7,23},{8,24},{9,... | collective-permute-start | bytes 86024 | tf_op jit(solution)/shard_map/ppermute | solution.py:519
  37.8 4.3 %collective-permute-start.13 = (f32[56,128]{1,0:T(8,128)S(1)}, f32[56,128]{1,0:T(8,128)S(1)}, u32[]{:S(2)}, u32[]{:S(2)}) collective-permute-start(f32[56,128]{1,0:T(8,128)S(1)} %collective-permute-done.9.refs_3_), channel_id=1, source_target_pairs={{0,1},{1,0},{2,3},{3,2},{4,5},{5,4},{6,7},{7,6},{8,9},{9,8},{10,11... | collective-permute-start | bytes 86024 | tf_op jit(solution)/shard_map/ppermute | solution.py:520
  40.0 2.5 %collective-permute-start.14 = (f32[56,128]{1,0:T(8,128)S(1)}, f32[56,128]{1,0:T(8,128)S(1)}, u32[]{:S(2)}, u32[]{:S(2)}) collective-permute-start(f32[56,128]{1,0:T(8,128)S(1)} %collective-permute-done.10.refs_4_), channel_id=1, source_target_pairs={{0,1},{1,0},{2,3},{3,2},{4,5},{5,4},{6,7},{7,6},{8,9},{9,8},{10,11... | collective-permute-start | bytes 86024 | tf_op jit(solution)/shard_map/ppermute | solution.py:520
  41.6 1.2 %collective-permute-start.15 = (f32[56,128]{1,0:T(8,128)S(1)}, f32[56,128]{1,0:T(8,128)S(1)}, u32[]{:S(2)}, u32[]{:S(2)}) collective-permute-start(f32[56,128]{1,0:T(8,128)S(1)} %collective-permute-done.11.refs_5_), channel_id=1, source_target_pairs={{0,1},{1,0},{2,3},{3,2},{4,5},{5,4},{6,7},{7,6},{8,9},{9,8},{10,11... | collective-permute-start | bytes 86024 | tf_op jit(solution)/shard_map/ppermute | solution.py:520
  41.6 1.4 %collective-permute-start.16 = (f32[56,128]{1,0:T(8,128)S(1)}, f32[56,128]{1,0:T(8,128)S(1)}, u32[]{:S(2)}, u32[]{:S(2)}) collective-permute-start(f32[56,128]{1,0:T(8,128)S(1)} %collective-permute-done.12.refs_6_), channel_id=1, source_target_pairs={{0,1},{1,0},{2,3},{3,2},{4,5},{5,4},{6,7},{7,6},{8,9},{9,8},{10,11... | collective-permute-start | bytes 86024 | tf_op jit(solution)/shard_map/ppermute | solution.py:520
  47.8 1.3 %collective-permute-start.17 = (f32[104,128]{1,0:T(8,128)S(1)}, f32[104,128]{1,0:T(8,128)S(1)}, u32[]{:S(2)}, u32[]{:S(2)}) collective-permute-start(f32[104,128]{1,0:T(8,128)S(1)} %get-tuple-element.61.mine_ref), channel_id=1, source_target_pairs={{0,1},{1,0},{2,3},{3,2},{4,5},{5,4},{6,7},{7,6},{8,9},{9,8},{10,11... | collective-permute-start | bytes 159752 | tf_op jit(solution)/shard_map/ppermute | solution.py:508
  49.6 7.9 %collective-permute-start.18 = (f32[56,128]{1,0:T(8,128)S(1)}, f32[56,128]{1,0:T(8,128)S(1)}, u32[]{:S(2)}, u32[]{:S(2)}) collective-permute-start(f32[56,128]{1,0:T(8,128)S(1)} %get-tuple-element.62), channel_id=1, source_target_pairs={{0,3},{2,5},{4,7},{6,9},{8,11},{10,13},{12,15},{14,17},{16,19},{18... | collective-permute-start | bytes 86024 | tf_op jit(solution)/shard_map/ppermute | solution.py:519
  52.3 5.1 %collective-permute-start.19 = (f32[56,128]{1,0:T(8,128)S(1)}, f32[56,128]{1,0:T(8,128)S(1)}, u32[]{:S(2)}, u32[]{:S(2)}) collective-permute-start(f32[56,128]{1,0:T(8,128)S(1)} %get-tuple-element.63), channel_id=1, source_target_pairs={{0,5},{2,7},{4,9},{6,11},{8,13},{10,15},{12,17},{14,19},{16,21},{1... | collective-permute-start | bytes 86024 | tf_op jit(solution)/shard_map/ppermute | solution.py:519
  53.7 5.3 %collective-permute-start.20 = (f32[56,128]{1,0:T(8,128)S(1)}, f32[56,128]{1,0:T(8,128)S(1)}, u32[]{:S(2)}, u32[]{:S(2)}) collective-permute-start(f32[56,128]{1,0:T(8,128)S(1)} %get-tuple-element.64), channel_id=1, source_target_pairs={{0,15},{2,17},{4,19},{6,21},{8,23},{10,25},{12,27},{14,29},{16,31}... | collective-permute-start | bytes 86024 | tf_op jit(solution)/shard_map/ppermute | solution.py:519
  53.9 5.6 %collective-permute-start.21 = (f32[56,128]{1,0:T(8,128)S(1)}, f32[56,128]{1,0:T(8,128)S(1)}, u32[]{:S(2)}, u32[]{:S(2)}) collective-permute-start(f32[56,128]{1,0:T(8,128)S(1)} %get-tuple-element.65), channel_id=1, source_target_pairs={{0,16},{1,17},{2,18},{3,19},{4,20},{5,21},{6,22},{7,23},{8,24},{9,... | collective-permute-start | bytes 86024 | tf_op jit(solution)/shard_map/ppermute | solution.py:519
  57.4 2.7 %collective-permute-start.22 = (f32[56,128]{1,0:T(8,128)S(1)}, f32[56,128]{1,0:T(8,128)S(1)}, u32[]{:S(2)}, u32[]{:S(2)}) collective-permute-start(f32[56,128]{1,0:T(8,128)S(1)} %collective-permute-done.18.refs_0_), channel_id=1, source_target_pairs={{0,1},{1,0},{2,3},{3,2},{4,5},{5,4},{6,7},{7,6},{8,9},{9,8},{10,11... | collective-permute-start | bytes 86024 | tf_op jit(solution)/shard_map/ppermute | solution.py:520
  57.4 2.6 %collective-permute-start.23 = (f32[56,128]{1,0:T(8,128)S(1)}, f32[56,128]{1,0:T(8,128)S(1)}, u32[]{:S(2)}, u32[]{:S(2)}) collective-permute-start(f32[56,128]{1,0:T(8,128)S(1)} %collective-permute-done.19.refs_1_), channel_id=1, source_target_pairs={{0,1},{1,0},{2,3},{3,2},{4,5},{5,4},{6,7},{7,6},{8,9},{9,8},{10,11... | collective-permute-start | bytes 86024 | tf_op jit(solution)/shard_map/ppermute | solution.py:520
  59.0 1.4 %collective-permute-start.24 = (f32[56,128]{1,0:T(8,128)S(1)}, f32[56,128]{1,0:T(8,128)S(1)}, u32[]{:S(2)}, u32[]{:S(2)}) collective-permute-start(f32[56,128]{1,0:T(8,128)S(1)} %collective-permute-done.20.refs_2_), channel_id=1, source_target_pairs={{0,1},{1,0},{2,3},{3,2},{4,5},{5,4},{6,7},{7,6},{8,9},{9,8},{10,11... | collective-permute-start | bytes 86024 | tf_op jit(solution)/shard_map/ppermute | solution.py:520
  59.6 1.4 %collective-permute-start.25 = (f32[56,128]{1,0:T(8,128)S(1)}, f32[56,128]{1,0:T(8,128)S(1)}, u32[]{:S(2)}, u32[]{:S(2)}) collective-permute-start(f32[56,128]{1,0:T(8,128)S(1)} %collective-permute-done.21.refs_3_), channel_id=1, source_target_pairs={{0,1},{1,0},{2,3},{3,2},{4,5},{5,4},{6,7},{7,6},{8,9},{9,8},{10,11... | collective-permute-start | bytes 86024 | tf_op jit(solution)/shard_map/ppermute | solution.py:520

commit v4 on v3

--- a/solution.py
+++ b/solution.py
@@ -289,7 +289,7 @@
     return jnp.broadcast_to(jnp.transpose(jnp.broadcast_to(ids, (8, ids.shape[1])))[:, 0:1], (ids.shape[1], count))
 
 
-def pack_kernel(cap, meta_ref, mine_ref, other_ref, one_ref, two_ref, three_ref, four_ref):
+def pack_kernel(cap, meta_ref, mine_ref, other_ref, one_ref, three_ref, four_ref):
     rows = COMP * NODES
     count = RUNS * cap
     odd = meta_ref[3:4, :count] == 1.0
@@ -326,25 +326,23 @@
     one_ref[...] = jnp.where(
         odd, laid((oe, 0), (oe, 1), (ge, 2), (oo, 0)), laid((ge, 0), (go, 1), (oo, 2), (go, 0))
     )
-    two_ref[...] = jnp.where(odd, laid((oe, 0)), laid(None, None, (oo, 2)))
     three_ref[...] = jnp.where(
         odd, laid((oo, 3), None, (oo, 2), (oe, 3)), laid((oe, 0), (oe, 1), (oo, 0), (oe, 3))
     )
-    four_ref[...] = laid((jnp.where(odd, oo, oe), 3), None, None, (jnp.where(odd, go, ge), 3))
-
-
-def fused_values(owned, cap, meta_ref, own_ref, mine_ref, other_ref, got, passed):
+    four_ref[...] = laid((oe, 3), (oo, 3), None, (jnp.where(odd, go, ge), 3))
+
+
+def fused_values(owned, cap, meta_ref, own_ref, offers, blocks):
     rows = COMP * NODES
     count = RUNS * cap
     lane = lax.broadcasted_iota(jnp.int32, (1, count), 1)
     odd = meta_ref[3:4, :count] == 1.0
-    mine, other = mine_ref[...], other_ref[...]
-    blocks = [r[...] for r in (*got, *passed)]
-    source = jnp.concatenate([mine[:rows], other[:rows]] + [x[:rows] for x in blocks], axis=1)
+    offers = [r[...] for r in offers]
+    blocks = [r[...] for r in blocks]
+    mine, other, _ = offers
+    source = jnp.concatenate([x[:rows] for x in offers + blocks], axis=1)
     gids = jnp.concatenate(
-        [mine[2 * rows : 2 * rows + 1], other[2 * rows : 2 * rows + 1]]
-        + [x[rows : rows + 1] for x in blocks],
-        axis=1,
+        [x[2 * rows : 2 * rows + 1] for x in offers] + [x[rows : rows + 1] for x in blocks], axis=1
     )
     total_count = gids.shape[1]
     remote = ids_down(mine[2 * rows : 2 * rows + 1], total_count)
@@ -354,8 +352,7 @@
     match = onehot_of(jnp.concatenate([own, jnp.where(remote > 0.0, remote, -1.0)], axis=0) == gids)
     sums = exact_dot(source, match, 1)
     field = own_ref[...] + sums[:, :owned]
-    near, far = got[0][...][:rows], got[3][...][:rows]
-    across = passed[0][...][:rows]
+    near, _, far, across, _ = (x[:rows] for x in blocks)
     partner = other[rows : 2 * rows]
     even_form = jnp.where(lane < 2 * cap, across, jnp.where(lane < 3 * cap, partner, far))
     odd_form = jnp.where(
@@ -385,11 +382,11 @@
     *refs,
 ):
     if fused:
-        before_ref, mine_ref, other_ref, *received = refs[:11]
-        refs = refs[11:]
+        before_ref, *received = refs[:9]
+        refs = refs[9:]
         field_ref, refs = refs[0], refs[1:]
         field, received = fused_values(
-            owned, cap, meta_ref, before_ref, mine_ref, other_ref, received[:4], received[4:]
+            owned, cap, meta_ref, before_ref, received[:3], received[3:]
         )
         field_ref[...] = field
     else:
@@ -415,13 +412,13 @@
 def last_kernel(
     inner, trace, owned, cap,
     meta_ref, onehot_ref, forth_ref, inverse_ref, couple_ref, self_ref,
-    k0_ref, k1_ref, s0_ref, s1_ref, u0_ref, u1_ref, before_ref, mine_ref, other_ref, *refs,
+    k0_ref, k1_ref, s0_ref, s1_ref, u0_ref, u1_ref, before_ref, *refs,
 ):
     received, refs = refs[:8], refs[8:]
     k2_ref, weight_ref, moment_ref, spread_ref, mid_ref, image_ref = refs
     width = spread_ref.shape[1]
     field, received = fused_values(
-        owned, cap, meta_ref, before_ref, mine_ref, other_ref, received[:4], received[4:]
+        owned, cap, meta_ref, before_ref, received[:3], received[3:]
     )
     k2_ref[...] = field
     element_values(field, received, meta_ref, onehot_ref, forth_ref, spread_ref)
@@ -505,20 +502,20 @@
         ahead = [(r, (r + 2 * chips + 1) % ranks) for r in range(0, ranks, 2)]
         return ahead + [(t, r) for r, t in ahead]
 
+    skip = [(r, (r + (3 if r % 2 else ranks - 3)) % ranks) for r in range(ranks)]
+    far = [(r, (r + ranks // 2) % ranks) for r in range(ranks)]
+    second = lax.ppermute(shared, AXES, skip)
     other = lax.ppermute(shared, AXES, pair)
     shape = (COMP * NODES + 8, RUNS * cap)
     packed = call(
-        functools.partial(pack_kernel, cap), [(shape, F32)] * 4, meta, shared, other
-    )
-    ways = [
-        both_ways(1),
-        both_ways(2),
-        both_ways(ranks // 4 - 1),
-        [(r, (r + ranks // 2) % ranks) for r in range(ranks)],
+        functools.partial(pack_kernel, cap), [(shape, F32)] * 3, meta, shared, other
+    )
+    got = [
+        lax.ppermute(block, AXES, way)
+        for block, way in zip(packed, (both_ways(1), both_ways(ranks // 4 - 1), far))
     ]
-    got = [lax.ppermute(block, AXES, way) for block, way in zip(packed, ways)]
-    passed = [lax.ppermute(block, AXES, pair) for block in got]
-    return [shared, other, *got, *passed]
+    passed = [lax.ppermute(block, AXES, pair) for block in got[:2]]
+    return [shared, other, second, *got, *passed]
 
 
 def local(self_block, couple, inverse, body_force, face_mortar, face_kind, *, ranks):

time: 78 us -> 74.9 us (0.960)
  starting transfers between devices: 29.4 us -> 25.3 us
  waiting for transfers between devices: 16.3 us -> 19.7 us
  blocking collectives: 11.1 us -> 8.84 us
    ppermute x16 -> x12, starting transfers between devices: 19.7 us -> 15.9 us  [the longest x2 7.48 us: fused_exchange(): second = lax.ppermute(shared, AXES, skip)]
    ppermute x16 -> x12, waiting for transfers between devices: 2.05 us -> 5.1 us  [the longest x6 4.05 us: fused_exchange(): lax.ppermute(block, AXES, way)]
    all_to_all x1, blocking collectives: 11.1 us -> 8.84 us  [local(): lax.all_to_all(moments, AXES, split_axis=0, concat_axis=0, tiled=True)]
  transfers between devices with their start and end apart: 26 -> 22, of which waited for: 11 -> 8; matrix products, arithmetic and copies ran while one was open for 0% -> 0% of each run, Pallas kernels for 0% -> 0%
where the time goes in v4:
time: 74.9 us; the launch traced here: 74.7 us
  starting transfers between devices  25.3 us (34%)
  Pallas kernels  20.1 us (27%)
  waiting for transfers between devices  19.7 us (26%)
  blocking collectives  8.84 us (12%)
  between operations  0.78 us (1%)
    pallas_call x8, Pallas kernels, call(): pl.pallas_call(kernel, out_shape=[jax.ShapeDtypeStruct(shape, dtype) for...  20.1 us
    ppermute x8, waiting for transfers between devices, exchange(): return [lax.ppermute(block, AXES, pairs[n]) for n in (0, 2, 1, 3)]  12.2 us
    ppermute x8, starting transfers between devices, exchange(): return [lax.ppermute(block, AXES, pairs[n]) for n in (0, 2, 1, 3)]  9.21 us
    all_to_all x1, blocking collectives, local(): lax.all_to_all(moments, AXES, split_axis=0, concat_axis=0, tiled=True)  8.84 us
    ppermute x2, starting transfers between devices, fused_exchange(): second = lax.ppermute(shared, AXES, skip)  7.48 us
    ppermute x6, starting transfers between devices, fused_exchange(): lax.ppermute(block, AXES, way)  6.9 us
    ppermute x6, waiting for transfers between devices, fused_exchange(): lax.ppermute(block, AXES, way)  4.05 us
    ppermute x2, waiting for transfers between devices, fused_exchange(): other = lax.ppermute(shared, AXES, pair)  2.45 us
  transfers between devices with their start and end apart: 22, of which 8 were waited for; matrix products, arithmetic and copies ran while one was open for 0% of the time, Pallas kernels for 0%

profile of v4, /device:TPU:0, one launch (start us, length us, event | category | flops | bytes accessed | tf_op | source)
XLA Modules:
  0.0 74.7 jit_solution(9304336661604190700)
XLA Ops:
  0.7 4.1 %shard_map.95 = (f32[48,256]{1,0:T(8,128)S(1)}, f32[56,128]{1,0:T(8,128)S(1)}, f32[8,128]{1,0:T(8,128)S(1)}, bf16[384,768]{1,0:T(8,128)(2,1)S(1)}, f32[8,768]{1,...) custom-call(s32[6,128]{1,0:T(8,128)} %bitcast.11, ...), custom_call_target="tpu_custom_call" | custom-call | tf_op jit(solution)/shard_map/pallas_call | solution.py:475
  4.8 7.0 %collective-permute-start.3 = (f32[56,128]{1,0:T(8,128)S(1)}, f32[56,128]{1,0:T(8,128)S(1)}, u32[]{:S(2)}, u32[]{:S(2)}) collective-permute-start(f32[56,128]{1,0:T(8,128)S(1)} %get-tuple-element.42), channel_id=1, source_target_pairs={{0,30},{1,31},{2,0},{3,1},{4,2},{5,3},{6,4},{7,5},{8,6},{9,7},{10,... | collective-permute-start | bytes 86024 | tf_op jit(solution)/shard_map/ppermute | solution.py:495
  11.8 1.5 %collective-permute-done.3.d_ref = f32[56,128]{1,0:T(8,128)S(1)} collective-permute-done((f32[56,128]{1,0:T(8,128)S(1)}, f32[56,128]{1,0:T(8,128)S(1)}, u32[]{:S(2)}, u32[]{:S(2)}) %collective-permute-start.3) | collective-permute-done | bytes 28704 | tf_op jit(solution)/shard_map/ppermute | solution.py:495
  13.4 5.3 %collective-permute-done.2.c_ref = f32[56,128]{1,0:T(8,128)S(1)} collective-permute-done((f32[56,128]{1,0:T(8,128)S(1)}, f32[56,128]{1,0:T(8,128)S(1)}, u32[]{:S(2)}, u32[]{:S(2)}) %collective-permute-start.2) | collective-permute-done | bytes 28704 | tf_op jit(solution)/shard_map/ppermute | solution.py:495
  18.7 0.3 shard_map.96
  19.1 2.2 %collective-permute-start.6 = (f32[48,128]{1,0:T(8,128)S(1)}, f32[48,128]{1,0:T(8,128)S(1)}, u32[]{:S(2)}, u32[]{:S(2)}) collective-permute-start(f32[48,128]{1,0:T(8,128)S(1)} %get-tuple-element.46), channel_id=1, source_target_pairs={{0,31},{1,2},{2,1},{3,4},{4,3},{5,6},{6,5},{7,8},{8,7},{9,10},{10,... | collective-permute-start | bytes 73736 | tf_op jit(solution)/shard_map/ppermute | solution.py:495
  21.2 5.3 %collective-permute-done.7.refs_4_ = f32[48,128]{1,0:T(8,128)S(1)} collective-permute-done((f32[48,128]{1,0:T(8,128)S(1)}, f32[48,128]{1,0:T(8,128)S(1)}, u32[]{:S(2)}, u32[]{:S(2)}) %collective-permute-start.7) | collective-permute-done | bytes 24608 | tf_op jit(solution)/shard_map/ppermute | solution.py:495
  26.6 4.2 %shard_map.97 = (f32[48,256]{1,0:T(8,128)S(1)}, f32[104,128]{1,0:T(8,128)S(1)}, f32[288,128]{1,0:T(8,128)S(1)}, f32[192,128]{1,0:T(8,128)S(1)}, f32[192,128]{1,0:T(8,128)S(1)}) custom-call(f32[8,768]{1,0:T(8,128)S(1)} %get-tuple-element.36.meta_ref, bf16[384,768]{1,0:T(8,128)(2,1)S(1)} %get-tuple-element.37.onehot_ref, f32[192,48]{1,0:T(8,128)S(1)} %copy-done, ...), custom_call_target="tpu_custom_call" | custom-call | tf_op jit(solution)/shard_map/pallas_call | solution.py:475
  30.8 0.1 collective-permute-start.8
  30.9 1.2 %collective-permute-done.8.other_ref.refs_2_ = f32[104,128]{1,0:T(8,128)S(1)} collective-permute-done((f32[104,128]{1,0:T(8,128)S(1)}, f32[104,128]{1,0:T(8,128)S(1)}, u32[]{:S(2)}, u32[]{:S(2)}) %collective-permute-start.8) | collective-permute-done | bytes 53280 | tf_op jit(solution)/shard_map/ppermute | solution.py:508
  32.1 0.4 shard_map.98
  32.6 0.1 collective-permute-start.10
  32.6 1.1 %collective-permute-start.11 = (f32[56,128]{1,0:T(8,128)S(1)}, f32[56,128]{1,0:T(8,128)S(1)}, u32[]{:S(2)}, u32[]{:S(2)}) collective-permute-start(f32[56,128]{1,0:T(8,128)S(1)} %get-tuple-element.50), channel_id=1, source_target_pairs={{0,15},{2,17},{4,19},{6,21},{8,23},{10,25},{12,27},{14,29},{16,31}... | collective-permute-start | bytes 86024 | tf_op jit(solution)/shard_map/ppermute | solution.py:514
  33.8 2.7 %collective-permute-start.9 = (f32[104,128]{1,0:T(8,128)S(1)}, f32[104,128]{1,0:T(8,128)S(1)}, u32[]{:S(2)}, u32[]{:S(2)}) collective-permute-start(f32[104,128]{1,0:T(8,128)S(1)} %get-tuple-element.48.mine_ref.refs_1_), channel_id=1, source_target_pairs={{0,29},{1,4},{2,31},{3,6},{4,1},{5,8},{6,3},{7,10},{8,5},{9,12},{1... | collective-permute-start | bytes 159752 | tf_op jit(solution)/shard_map/ppermute | solution.py:507
  36.5 3.2 %collective-permute-start.12 = (f32[56,128]{1,0:T(8,128)S(1)}, f32[56,128]{1,0:T(8,128)S(1)}, u32[]{:S(2)}, u32[]{:S(2)}) collective-permute-start(f32[56,128]{1,0:T(8,128)S(1)} %get-tuple-element.51), channel_id=1, source_target_pairs={{0,16},{1,17},{2,18},{3,19},{4,20},{5,21},{6,22},{7,23},{8,24},{9,... | collective-permute-start | bytes 86024 | tf_op jit(solution)/shard_map/ppermute | solution.py:514
  39.8 0.2 collective-permute-start.13
  40.0 0.8 %collective-permute-start.14 = (f32[56,128]{1,0:T(8,128)S(1)}, f32[56,128]{1,0:T(8,128)S(1)}, u32[]{:S(2)}, u32[]{:S(2)}) collective-permute-start(f32[56,128]{1,0:T(8,128)S(1)} %collective-permute-done.11.refs_5_), channel_id=1, source_target_pairs={{0,1},{1,0},{2,3},{3,2},{4,5},{5,4},{6,7},{7,6},{8,9},{9,8},{10,11... | collective-permute-start | bytes 86024 | tf_op jit(solution)/shard_map/ppermute | solution.py:517
  40.8 1.4 %collective-permute-done.12.refs_6_ = f32[56,128]{1,0:T(8,128)S(1)} collective-permute-done((f32[56,128]{1,0:T(8,128)S(1)}, f32[56,128]{1,0:T(8,128)S(1)}, u32[]{:S(2)}, u32[]{:S(2)}) %collective-permute-start.12) | collective-permute-done | bytes 28704 | tf_op jit(solution)/shard_map/ppermute | solution.py:514
  42.2 4.7 %shard_map.99 = (f32[48,256]{1,0:T(8,128)S(1)}, f32[48,256]{1,0:T(8,128)S(1)}, f32[104,128]{1,0:T(8,128)S(1)}, f32[288,128]{1,0:T(8,128)S(1)}, f32[192,128]{1,0:T(8,128)S(1)}, /*index=5*/f32[192,128]{1,0:T(8,128)S(1)}) custom-call(f32[8,768]{1,0:T(8,128)S(1)} %get-tuple-element.36.meta_ref, bf16[384,768]{1,0:T(8,128)(2,1)S(1)} %get-tuple-element.37.onehot_ref, ...), custom_call_target="tpu_custom_call" | custom-call | tf_op jit(solution)/shard_map/pallas_call | solution.py:475
  46.9 0.1 collective-permute-start.15
  47.0 1.2 %collective-permute-done.15.other_ref.refs_1_ = f32[104,128]{1,0:T(8,128)S(1)} collective-permute-done((f32[104,128]{1,0:T(8,128)S(1)}, f32[104,128]{1,0:T(8,128)S(1)}, u32[]{:S(2)}, u32[]{:S(2)}) %collective-permute-start.15) | collective-permute-done | bytes 53280 | tf_op jit(solution)/shard_map/ppermute | solution.py:508
  48.2 0.4 shard_map.100
  48.7 0.1 collective-permute-start.17
  48.8 1.8 %collective-permute-start.18 = (f32[56,128]{1,0:T(8,128)S(1)}, f32[56,128]{1,0:T(8,128)S(1)}, u32[]{:S(2)}, u32[]{:S(2)}) collective-permute-start(f32[56,128]{1,0:T(8,128)S(1)} %get-tuple-element.60), channel_id=1, source_target_pairs={{0,15},{2,17},{4,19},{6,21},{8,23},{10,25},{12,27},{14,29},{16,31}... | collective-permute-start | bytes 86024 | tf_op jit(solution)/shard_map/ppermute | solution.py:514
  50.6 4.7 %collective-permute-start.16 = (f32[104,128]{1,0:T(8,128)S(1)}, f32[104,128]{1,0:T(8,128)S(1)}, u32[]{:S(2)}, u32[]{:S(2)}) collective-permute-start(f32[104,128]{1,0:T(8,128)S(1)} %get-tuple-element.58.mine_ref.refs_0_), channel_id=1, source_target_pairs={{0,29},{1,4},{2,31},{3,6},{4,1},{5,8},{6,3},{7,10},{8,5},{9,12},{1... | collective-permute-start | bytes 159752 | tf_op jit(solution)/shard_map/ppermute | solution.py:507
  55.3 0.6 collective-permute-start.19
  56.0 0.4 collective-permute-start.21
  56.4 1.0 %collective-permute-done.16.refs_2_ = f32[104,128]{1,0:T(8,128)S(1)} collective-permute-done((f32[104,128]{1,0:T(8,128)S(1)}, f32[104,128]{1,0:T(8,128)S(1)}, u32[]{:S(2)}, u32[]{:S(2)}) %collective-permute-start.16) | collective-permute-done | bytes 53280 | tf_op jit(solution)/shard_map/ppermute | solution.py:507
  57.4 2.6 %collective-permute-done.19.refs_5_ = f32[56,128]{1,0:T(8,128)S(1)} collective-permute-done((f32[56,128]{1,0:T(8,128)S(1)}, f32[56,128]{1,0:T(8,128)S(1)}, u32[]{:S(2)}, u32[]{:S(2)}) %collective-permute-start.19) | collective-permute-done | bytes 28704 | tf_op jit(solution)/shard_map/ppermute | solution.py:514
  60.1 3.9 %shard_map.101 = (f32[48,256]{1,0:T(8,128)S(1)}, f32[192,128]{1,0:T(8,128)S(1)}, f32[32,1,128]{2,1,0:T(1,128)S(1)}) custom-call(f32[8,768]{1,0:T(8,128)S(1)} %get-tuple-element.36.meta_ref, bf16[384,768]{1,0:T(8,128)(2,1)S(1)} %get-tuple-element.37.onehot_ref, f32[192,48]{1,0:T(8,128)S(1)} %copy-done, f32[4096,128]{1,0:T(8,128)S(1)} %get-tuple-element.38.inverse_ref, ...), custom_call_target="tpu_custom_call" | custom-call | tf_op jit(solution)/shard_map/pallas_call | solution.py:475
  64.0 8.8 %all_to_all.5.moment_ref = f32[32,1,128]{2,1,0:T(1,128)S(1)} all-to-all(f32[32,1,128]{2,1,0:T(1,128)S(1)} %get-tuple-element.62), channel_id=1, replica_groups=mesh['dom'=16,'blk'=2] {'dom','blk'}, dimensions={0} | all-to-all | bytes 32768 | tf_op jit(solution)/shard_map/all_to_all | solution.py:596
  72.9 1.8 %shard_map.102 = (f32[48,256]{1,0:T(8,128)}, f32[192,128]{1,0:T(8,128)}) custom-call(f32[32,1,128]{2,1,0:T(1,128)S(1)} %all_to_all.5.moment_ref, f32[48,256]{1,0:T(8,128)S(1)} %get-tuple-element.43.refs_0_.k0_ref, f32[48,256]{1,0:T(8,128)S(1)} %get-tuple-element.52.k1_ref, f32[48,256]{1,0:T(8,128)S(1)} %get-tuple-element.63.k2_ref, ...), custom_call_target="tpu_custom_call" | custom-call | tf_op jit(solution)/shard_map/pallas_call | solution.py:475
  (25 shorter events, 0.2 us)
Async XLA Ops:
  0.6 25.9 %copy-start = (f32[192,48]{1,0:T(8,128)S(1)}, f32[192,48]{1,0:T(8,128)}, u32[]{:S(2)}) copy-start(f32[192,48]{1,0:T(8,128)} %constant.5.clone.forth_ref) | copy-start | bytes 110596
  0.6 25.9 %copy-start.1 = (f32[192,48]{1,0:T(8,128)S(1)}, f32[192,48]{1,0:T(8,128)}, u32[]{:S(2)}) copy-start(f32[192,48]{1,0:T(8,128)} %constant.4.clone.back_hbm.back_ref) | copy-start | bytes 110596
  4.8 8.5 %collective-permute-start.3 = (f32[56,128]{1,0:T(8,128)S(1)}, f32[56,128]{1,0:T(8,128)S(1)}, u32[]{:S(2)}, u32[]{:S(2)}) collective-permute-start(f32[56,128]{1,0:T(8,128)S(1)} %get-tuple-element.42), channel_id=1, source_target_pairs={{0,30},{1,31},{2,0},{3,1},{4,2},{5,3},{6,4},{7,5},{8,6},{9,7},{10,... | collective-permute-start | bytes 86024 | tf_op jit(solution)/shard_map/ppermute | solution.py:495
  11.8 6.9 %collective-permute-start.2 = (f32[56,128]{1,0:T(8,128)S(1)}, f32[56,128]{1,0:T(8,128)S(1)}, u32[]{:S(2)}, u32[]{:S(2)}) collective-permute-start(f32[56,128]{1,0:T(8,128)S(1)} %get-tuple-element.42), channel_id=1, source_target_pairs={{0,31},{1,2},{2,1},{3,4},{4,3},{5,6},{6,5},{7,8},{8,7},{9,10},{10,... | collective-permute-start | bytes 86024 | tf_op jit(solution)/shard_map/ppermute | solution.py:495
  11.8 6.9 %collective-permute-start.1 = (f32[56,128]{1,0:T(8,128)S(1)}, f32[56,128]{1,0:T(8,128)S(1)}, u32[]{:S(2)}, u32[]{:S(2)}) collective-permute-start(f32[56,128]{1,0:T(8,128)S(1)} %get-tuple-element.42), channel_id=1, source_target_pairs={{0,16},{1,17},{2,18},{3,19},{4,20},{5,21},{6,22},{7,23},{8,24},{9,... | collective-permute-start | bytes 86024 | tf_op jit(solution)/shard_map/ppermute | solution.py:495
  11.8 6.9 %collective-permute-start = (f32[56,128]{1,0:T(8,128)S(1)}, f32[56,128]{1,0:T(8,128)S(1)}, u32[]{:S(2)}, u32[]{:S(2)}) collective-permute-start(f32[56,128]{1,0:T(8,128)S(1)} %get-tuple-element.42), channel_id=1, source_target_pairs={{0,1},{1,0},{2,3},{3,2},{4,5},{5,4},{6,7},{7,6},{8,9},{9,8},{10,11... | collective-permute-start | bytes 86024 | tf_op jit(solution)/shard_map/ppermute | solution.py:495
  19.0 7.5 %collective-permute-start.7 = (f32[48,128]{1,0:T(8,128)S(1)}, f32[48,128]{1,0:T(8,128)S(1)}, u32[]{:S(2)}, u32[]{:S(2)}) collective-permute-start(f32[48,128]{1,0:T(8,128)S(1)} %get-tuple-element.46), channel_id=1, source_target_pairs={{0,2},{1,3},{2,4},{3,5},{4,6},{5,7},{6,8},{7,9},{8,10},{9,11},{10,... | collective-permute-start | bytes 73736 | tf_op jit(solution)/shard_map/ppermute | solution.py:495
  19.1 7.4 %collective-permute-start.6 = (f32[48,128]{1,0:T(8,128)S(1)}, f32[48,128]{1,0:T(8,128)S(1)}, u32[]{:S(2)}, u32[]{:S(2)}) collective-permute-start(f32[48,128]{1,0:T(8,128)S(1)} %get-tuple-element.46), channel_id=1, source_target_pairs={{0,31},{1,2},{2,1},{3,4},{4,3},{5,6},{6,5},{7,8},{8,7},{9,10},{10,... | collective-permute-start | bytes 73736 | tf_op jit(solution)/shard_map/ppermute | solution.py:495
  21.2 5.3 %collective-permute-start.5 = (f32[48,128]{1,0:T(8,128)S(1)}, f32[48,128]{1,0:T(8,128)S(1)}, u32[]{:S(2)}, u32[]{:S(2)}) collective-permute-start(f32[48,128]{1,0:T(8,128)S(1)} %get-tuple-element.46), channel_id=1, source_target_pairs={{0,16},{1,17},{2,18},{3,19},{4,20},{5,21},{6,22},{7,23},{8,24},{9,... | collective-permute-start | bytes 73736 | tf_op jit(solution)/shard_map/ppermute | solution.py:495
  21.2 5.3 %collective-permute-start.4 = (f32[48,128]{1,0:T(8,128)S(1)}, f32[48,128]{1,0:T(8,128)S(1)}, u32[]{:S(2)}, u32[]{:S(2)}) collective-permute-start(f32[48,128]{1,0:T(8,128)S(1)} %get-tuple-element.46), channel_id=1, source_target_pairs={{0,1},{1,0},{2,3},{3,2},{4,5},{5,4},{6,7},{7,6},{8,9},{9,8},{10,11... | collective-permute-start | bytes 73736 | tf_op jit(solution)/shard_map/ppermute | solution.py:495
  30.8 1.3 %collective-permute-start.8 = (f32[104,128]{1,0:T(8,128)S(1)}, f32[104,128]{1,0:T(8,128)S(1)}, u32[]{:S(2)}, u32[]{:S(2)}) collective-permute-start(f32[104,128]{1,0:T(8,128)S(1)} %get-tuple-element.48.mine_ref.refs_1_), channel_id=1, source_target_pairs={{0,1},{1,0},{2,3},{3,2},{4,5},{5,4},{6,7},{7,6},{8,9},{9,8},{10,11... | collective-permute-start | bytes 159752 | tf_op jit(solution)/shard_map/ppermute | solution.py:508
  32.6 7.2 %collective-permute-start.10 = (f32[56,128]{1,0:T(8,128)S(1)}, f32[56,128]{1,0:T(8,128)S(1)}, u32[]{:S(2)}, u32[]{:S(2)}) collective-permute-start(f32[56,128]{1,0:T(8,128)S(1)} %get-tuple-element.49), channel_id=1, source_target_pairs={{0,3},{2,5},{4,7},{6,9},{8,11},{10,13},{12,15},{14,17},{16,19},{18... | collective-permute-start | bytes 86024 | tf_op jit(solution)/shard_map/ppermute | solution.py:514
  32.6 7.4 %collective-permute-start.11 = (f32[56,128]{1,0:T(8,128)S(1)}, f32[56,128]{1,0:T(8,128)S(1)}, u32[]{:S(2)}, u32[]{:S(2)}) collective-permute-start(f32[56,128]{1,0:T(8,128)S(1)} %get-tuple-element.50), channel_id=1, source_target_pairs={{0,15},{2,17},{4,19},{6,21},{8,23},{10,25},{12,27},{14,29},{16,31}... | collective-permute-start | bytes 86024 | tf_op jit(solution)/shard_map/ppermute | solution.py:514
  33.8 7.0 %collective-permute-start.9 = (f32[104,128]{1,0:T(8,128)S(1)}, f32[104,128]{1,0:T(8,128)S(1)}, u32[]{:S(2)}, u32[]{:S(2)}) collective-permute-start(f32[104,128]{1,0:T(8,128)S(1)} %get-tuple-element.48.mine_ref.refs_1_), channel_id=1, source_target_pairs={{0,29},{1,4},{2,31},{3,6},{4,1},{5,8},{6,3},{7,10},{8,5},{9,12},{1... | collective-permute-start | bytes 159752 | tf_op jit(solution)/shard_map/ppermute | solution.py:507
  36.5 5.7 %collective-permute-start.12 = (f32[56,128]{1,0:T(8,128)S(1)}, f32[56,128]{1,0:T(8,128)S(1)}, u32[]{:S(2)}, u32[]{:S(2)}) collective-permute-start(f32[56,128]{1,0:T(8,128)S(1)} %get-tuple-element.51), channel_id=1, source_target_pairs={{0,16},{1,17},{2,18},{3,19},{4,20},{5,21},{6,22},{7,23},{8,24},{9,... | collective-permute-start | bytes 86024 | tf_op jit(solution)/shard_map/ppermute | solution.py:514
  39.8 2.4 %collective-permute-start.13 = (f32[56,128]{1,0:T(8,128)S(1)}, f32[56,128]{1,0:T(8,128)S(1)}, u32[]{:S(2)}, u32[]{:S(2)}) collective-permute-start(f32[56,128]{1,0:T(8,128)S(1)} %collective-permute-done.10.refs_4_), channel_id=1, source_target_pairs={{0,1},{1,0},{2,3},{3,2},{4,5},{5,4},{6,7},{7,6},{8,9},{9,8},{10,11... | collective-permute-start | bytes 86024 | tf_op jit(solution)/shard_map/ppermute | solution.py:517
  40.0 2.2 %collective-permute-start.14 = (f32[56,128]{1,0:T(8,128)S(1)}, f32[56,128]{1,0:T(8,128)S(1)}, u32[]{:S(2)}, u32[]{:S(2)}) collective-permute-start(f32[56,128]{1,0:T(8,128)S(1)} %collective-permute-done.11.refs_5_), channel_id=1, source_target_pairs={{0,1},{1,0},{2,3},{3,2},{4,5},{5,4},{6,7},{7,6},{8,9},{9,8},{10,11... | collective-permute-start | bytes 86024 | tf_op jit(solution)/shard_map/ppermute | solution.py:517
  46.9 1.3 %collective-permute-start.15 = (f32[104,128]{1,0:T(8,128)S(1)}, f32[104,128]{1,0:T(8,128)S(1)}, u32[]{:S(2)}, u32[]{:S(2)}) collective-permute-start(f32[104,128]{1,0:T(8,128)S(1)} %get-tuple-element.58.mine_ref.refs_0_), channel_id=1, source_target_pairs={{0,1},{1,0},{2,3},{3,2},{4,5},{5,4},{6,7},{7,6},{8,9},{9,8},{10,11... | collective-permute-start | bytes 159752 | tf_op jit(solution)/shard_map/ppermute | solution.py:508
  48.7 7.2 %collective-permute-start.17 = (f32[56,128]{1,0:T(8,128)S(1)}, f32[56,128]{1,0:T(8,128)S(1)}, u32[]{:S(2)}, u32[]{:S(2)}) collective-permute-start(f32[56,128]{1,0:T(8,128)S(1)} %get-tuple-element.59), channel_id=1, source_target_pairs={{0,3},{2,5},{4,7},{6,9},{8,11},{10,13},{12,15},{14,17},{16,19},{18... | collective-permute-start | bytes 86024 | tf_op jit(solution)/shard_map/ppermute | solution.py:514
  48.8 7.2 %collective-permute-start.18 = (f32[56,128]{1,0:T(8,128)S(1)}, f32[56,128]{1,0:T(8,128)S(1)}, u32[]{:S(2)}, u32[]{:S(2)}) collective-permute-start(f32[56,128]{1,0:T(8,128)S(1)} %get-tuple-element.60), channel_id=1, source_target_pairs={{0,15},{2,17},{4,19},{6,21},{8,23},{10,25},{12,27},{14,29},{16,31}... | collective-permute-start | bytes 86024 | tf_op jit(solution)/shard_map/ppermute | solution.py:514
  50.6 6.9 %collective-permute-start.16 = (f32[104,128]{1,0:T(8,128)S(1)}, f32[104,128]{1,0:T(8,128)S(1)}, u32[]{:S(2)}, u32[]{:S(2)}) collective-permute-start(f32[104,128]{1,0:T(8,128)S(1)} %get-tuple-element.58.mine_ref.refs_0_), channel_id=1, source_target_pairs={{0,29},{1,4},{2,31},{3,6},{4,1},{5,8},{6,3},{7,10},{8,5},{9,12},{1... | collective-permute-start | bytes 159752 | tf_op jit(solution)/shard_map/ppermute | solution.py:507
  55.3 4.8 %collective-permute-start.19 = (f32[56,128]{1,0:T(8,128)S(1)}, f32[56,128]{1,0:T(8,128)S(1)}, u32[]{:S(2)}, u32[]{:S(2)}) collective-permute-start(f32[56,128]{1,0:T(8,128)S(1)} %get-tuple-element.61), channel_id=1, source_target_pairs={{0,16},{1,17},{2,18},{3,19},{4,20},{5,21},{6,22},{7,23},{8,24},{9,... | collective-permute-start | bytes 86024 | tf_op jit(solution)/shard_map/ppermute | solution.py:514
  55.9 4.2 %collective-permute-start.20 = (f32[56,128]{1,0:T(8,128)S(1)}, f32[56,128]{1,0:T(8,128)S(1)}, u32[]{:S(2)}, u32[]{:S(2)}) collective-permute-start(f32[56,128]{1,0:T(8,128)S(1)} %collective-permute-done.17.refs_3_), channel_id=1, source_target_pairs={{0,1},{1,0},{2,3},{3,2},{4,5},{5,4},{6,7},{7,6},{8,9},{9,8},{10,11... | collective-permute-start | bytes 86024 | tf_op jit(solution)/shard_map/ppermute | solution.py:517
  56.0 4.1 %collective-permute-start.21 = (f32[56,128]{1,0:T(8,128)S(1)}, f32[56,128]{1,0:T(8,128)S(1)}, u32[]{:S(2)}, u32[]{:S(2)}) collective-permute-start(f32[56,128]{1,0:T(8,128)S(1)} %collective-permute-done.18.refs_4_), channel_id=1, source_target_pairs={{0,1},{1,0},{2,3},{3,2},{4,5},{5,4},{6,7},{7,6},{8,9},{9,8},{10,11... | collective-permute-start | bytes 86024 | tf_op jit(solution)/shard_map/ppermute | solution.py:517

commit v5 on v4

--- a/solution.py
+++ b/solution.py
@@ -171,7 +171,7 @@
 def start_kernel(
     ranks, inner, trace, owned, cap,
     mortar_hbm, kind_hbm, force_hbm, back_hbm, inverse_hbm, couple_hbm, self_hbm,
-    own_ref, out_ref, gid_ref, onehot_ref, meta_ref, load_ref, inverse_ref, couple_ref, self_ref,
+    offer_ref, out_ref, onehot_ref, meta_ref, load_ref, inverse_ref, couple_ref, self_ref,
     mortar_ref, kind_ref, force_ref, back_ref, *sems,
 ):
     copies = [
@@ -233,19 +233,14 @@
         lax.broadcasted_iota(jnp.int32, (8, slots), 0) == 0, facts[1:2, :], 0.0
     )
     sums = exact_dot(jnp.concatenate([z, label], axis=0), onehot_ref[...], 1)
-    own_ref[...] = sums[: COMP * NODES, :owned]
+    count = RUNS * cap
+    ids = lax.broadcasted_iota(jnp.int32, (8, owned), 1) + (me * owned + 1)
+    ids = jnp.where(lax.broadcasted_iota(jnp.int32, (8, owned), 0) == 0, ids, 0)
     out_ref[...] = sums[:, owned:]
-    gid_ref[...] = sums[COMP * NODES :, owned:]
+    offer_ref[:, :count] = sums[:, owned:]
+    offer_ref[: COMP * NODES, count:] = sums[: COMP * NODES, :owned]
+    offer_ref[COMP * NODES :, count:] = ids.astype(F32)
     copies[6].wait()
-
-
-def merged(meta_ref, first, third, second, fourth, cap, to_owner):
-    lane = lax.broadcasted_iota(jnp.int32, (1, RUNS * cap), 1)
-    odd = meta_ref[3:4, : RUNS * cap] == 1.0
-    low = lane < 2 * cap
-    take_first = (low != odd) if to_owner else (low == odd)
-    middle = jnp.where(take_first, first, second)
-    return jnp.where(lane < cap, fourth, jnp.where(lane < 3 * cap, middle, third))
 
 
 def onehot_of(condition):
@@ -262,31 +257,61 @@
     return onehot_of(own_ids(meta_ref, owned, count) == label.astype(jnp.int32))
 
 
-def owner_kernel(owned, cap, meta_ref, own_ref, a_ref, b_ref, c_ref, d_ref, field_ref, out_ref, label_ref):
-    received = merged(meta_ref, a_ref[...], b_ref[...], c_ref[...], d_ref[...], cap, True)
-    rows = COMP * NODES
-    label_ref[...] = received[rows : rows + 8]
-    wanted = wanted_by(received[rows : rows + 1], meta_ref, owned)
-    field = own_ref[...] + exact_dot(received[:rows], wanted, 1)
-    field_ref[...] = field
-    out_ref[...] = exact_dot(field, wanted)
-
-
-def share(owned, sums, gid_ref, label_ref, meta_ref, own_ref, shared_ref):
+def share(owned, sums, gid, label, meta_ref, own_ref, shared_ref):
     rows = COMP * NODES
     own = sums[:, :owned]
     own_ref[...] = own
     shared_ref[:rows, :] = sums[:, owned:]
-    label = label_ref[0:1, :]
     shared_ref[rows : 2 * rows, :] = exact_dot(own, wanted_by(label, meta_ref, owned))
-    row = lax.broadcasted_iota(jnp.int32, gid_ref.shape, 0)
-    shared_ref[2 * rows :, :] = jnp.where(
-        row == 0, gid_ref[0:1, :], jnp.where(row == 1, label, 0.0)
-    )
+    row = lax.broadcasted_iota(jnp.int32, (8, gid.shape[1]), 0)
+    shared_ref[2 * rows :, :] = jnp.where(row == 0, gid, jnp.where(row == 1, label, 0.0))
 
 
 def ids_down(ids, count):
     return jnp.broadcast_to(jnp.transpose(jnp.broadcast_to(ids, (8, ids.shape[1])))[:, 0:1], (ids.shape[1], count))
+
+
+def laid_out(cap, *blocks):
+    count = RUNS * cap
+    lane = lax.broadcasted_iota(jnp.int32, (1, count), 1)
+    result = jnp.zeros((COMP * NODES + 8, count), F32)
+    for place, block in enumerate(blocks):
+        if block is not None:
+            array, run = block
+            if run != place:
+                array = pltpu.roll(array, ((place - run) % RUNS) * cap, 1)
+            inside = (lane >= place * cap) & (lane < (place + 1) * cap)
+            result = jnp.where(inside, array, result)
+    return result
+
+
+def first_pack_kernel(owned, cap, meta_ref, mine_ref, other_ref, one_ref, three_ref, four_ref):
+    rows = COMP * NODES
+    count = RUNS * cap
+    laid = functools.partial(laid_out, cap)
+    odd = meta_ref[3:4, :count] == 1.0
+    odd_own = meta_ref[3:4, :owned] == 1.0
+    outs = [mine_ref[:, :count], other_ref[:, :count]]
+    fulls = []
+    for source, target_ref, swap in ((outs[1], mine_ref, False), (outs[0], other_ref, True)):
+        base = meta_ref[4:5, 0:1] + 1.0
+        if swap:
+            base = base + jnp.where(meta_ref[3:4, 0:1] == 1.0, -float(owned), float(owned))
+        ids = lax.broadcasted_iota(jnp.int32, (owned, count), 0).astype(F32) + base
+        match = onehot_of(ids == source[rows : rows + 1])
+        full = target_ref[:rows, count:] + exact_dot(source[:rows], match, 1)
+        fulls.append(jnp.concatenate([full, target_ref[rows:, count:]], axis=0))
+    oe, oo = jnp.where(odd, outs[1], outs[0]), jnp.where(odd, outs[0], outs[1])
+    one_ref[:, :count] = jnp.where(
+        odd, laid((oe, 0), (oe, 1), None, (oo, 0)), laid(None, None, (oo, 2))
+    )
+    one_ref[:, count : count + owned] = jnp.where(odd_own, fulls[1], fulls[0])
+    one_ref[:, count + owned :] = jnp.where(odd_own, fulls[0], fulls[1])
+    three_ref[...] = jnp.where(
+        odd, laid((oo, 3), None, (oo, 2), (oe, 3)), laid((oe, 0), (oe, 1), (oo, 0), (oe, 3))
+    )
+    four_ref[:, :count] = laid((oe, 3), (oo, 3))
+    four_ref[:, count:] = fulls[0]
 
 
 def pack_kernel(cap, meta_ref, mine_ref, other_ref, one_ref, three_ref, four_ref):
@@ -309,19 +334,7 @@
         jnp.concatenate([part[:rows], part[2 * rows : 2 * rows + 1], blank[1:]], axis=0)
         for part in (even_part, odd_part)
     ]
-    lane = lax.broadcasted_iota(jnp.int32, (1, count), 1)
-
-    def laid(*blocks):
-        result = jnp.zeros((rows + 8, count), F32)
-        for place, block in enumerate(blocks):
-            if block is not None:
-                array, run = block
-                if run != place:
-                    array = pltpu.roll(array, ((place - run) % RUNS) * cap, 1)
-                inside = (lane >= place * cap) & (lane < (place + 1) * cap)
-                result = jnp.where(inside, array, result)
-        return result
-
+    laid = functools.partial(laid_out, cap)
     (oe, oo), (ge, go) = outs, sums
     one_ref[...] = jnp.where(
         odd, laid((oe, 0), (oe, 1), (ge, 2), (oo, 0)), laid((ge, 0), (go, 1), (oo, 2), (go, 0))
@@ -330,6 +343,61 @@
         odd, laid((oo, 3), None, (oo, 2), (oe, 3)), laid((oe, 0), (oe, 1), (oo, 0), (oe, 3))
     )
     four_ref[...] = laid((oe, 3), (oo, 3), None, (jnp.where(odd, go, ge), 3))
+
+
+def matched(owned, meta_ref, gid, sources, remote_sources=()):
+    values = jnp.concatenate([v for v, _ in sources], axis=1)
+    ids = jnp.concatenate([i for _, i in sources], axis=1)
+    number = ids.shape[1]
+    own = lax.broadcasted_iota(jnp.int32, (owned, number), 0).astype(F32) + (
+        meta_ref[4:5, 0:1] + 1.0
+    )
+    gid = jnp.where(gid > 0.0, gid, -1.0)
+    match = onehot_of(jnp.concatenate([own, ids_down(gid, number)], axis=0) == ids)
+    sums = exact_dot(values, match, 1)
+    field, remote = sums[:, :owned], sums[:, owned:]
+    if remote_sources:
+        values = jnp.concatenate([v for v, _ in remote_sources], axis=1)
+        ids = jnp.concatenate([i for _, i in remote_sources], axis=1)
+        remote = remote + exact_dot(values, onehot_of(ids_down(gid, ids.shape[1]) == ids), 1)
+    return field, remote
+
+
+def first_values(owned, cap, meta_ref, offers, blocks):
+    rows = COMP * NODES
+    count = RUNS * cap
+    lane = lax.broadcasted_iota(jnp.int32, (1, count), 1)
+    odd = meta_ref[3:4, :count] == 1.0
+    mine_ref, other_ref, _ = offers
+    one_ref, _, far_ref, passed_ref, _ = blocks
+    sources = [(r[:rows, :count], r[rows : rows + 1, :count]) for r in (*offers, *blocks)]
+    owners = [
+        (r[:rows, count:], r[rows : rows + 1, count:])
+        for r in (other_ref, one_ref, far_ref, passed_ref)
+    ]
+    gid = mine_ref[rows : rows + 1, :count]
+    field, remote = matched(owned, meta_ref, gid, sources, owners)
+    label_rows = slice(rows, rows + 8)
+    other = other_ref[label_rows, :count]
+    one = one_ref[label_rows, :count]
+    far = far_ref[label_rows, :count]
+    passed = passed_ref[label_rows, :count]
+    even_form = jnp.where(
+        lane < cap,
+        one,
+        jnp.where(
+            lane < 2 * cap, other, jnp.where(lane < 3 * cap, passed, pltpu.roll(far, 3 * cap, 1))
+        ),
+    )
+    odd_form = jnp.where(
+        lane < cap,
+        pltpu.roll(passed, cap, 1),
+        jnp.where(
+            lane < 2 * cap, passed, jnp.where(lane < 3 * cap, other, pltpu.roll(far, 2 * cap, 1))
+        ),
+    )
+    label = jnp.where(odd, odd_form, even_form)
+    return mine_ref[:rows, count:] + field, remote, gid, label
 
 
 def fused_values(owned, cap, meta_ref, own_ref, offers, blocks):
@@ -337,30 +405,18 @@
     count = RUNS * cap
     lane = lax.broadcasted_iota(jnp.int32, (1, count), 1)
     odd = meta_ref[3:4, :count] == 1.0
-    offers = [r[...] for r in offers]
-    blocks = [r[...] for r in blocks]
-    mine, other, _ = offers
-    source = jnp.concatenate([x[:rows] for x in offers + blocks], axis=1)
-    gids = jnp.concatenate(
-        [x[2 * rows : 2 * rows + 1] for x in offers] + [x[rows : rows + 1] for x in blocks], axis=1
-    )
-    total_count = gids.shape[1]
-    remote = ids_down(mine[2 * rows : 2 * rows + 1], total_count)
-    own = lax.broadcasted_iota(jnp.int32, (owned, total_count), 0).astype(F32) + (
-        meta_ref[4:5, 0:1] + 1.0
-    )
-    match = onehot_of(jnp.concatenate([own, jnp.where(remote > 0.0, remote, -1.0)], axis=0) == gids)
-    sums = exact_dot(source, match, 1)
-    field = own_ref[...] + sums[:, :owned]
-    near, _, far, across, _ = (x[:rows] for x in blocks)
-    partner = other[rows : 2 * rows]
+    sources = [(r[:rows], r[2 * rows : 2 * rows + 1]) for r in offers]
+    sources += [(r[:rows], r[rows : rows + 1]) for r in blocks]
+    field, remote = matched(owned, meta_ref, offers[0][2 * rows : 2 * rows + 1], sources)
+    near, _, far, across, _ = (r[:rows] for r in blocks)
+    partner = offers[1][rows : 2 * rows]
     even_form = jnp.where(lane < 2 * cap, across, jnp.where(lane < 3 * cap, partner, far))
     odd_form = jnp.where(
         lane < cap,
         pltpu.roll(near, cap, 1),
         jnp.where(lane < 2 * cap, partner, jnp.where(lane < 3 * cap, across, far)),
     )
-    return field, jnp.where(odd, odd_form, even_form) + sums[:, owned:]
+    return own_ref[...] + field, jnp.where(odd, odd_form, even_form) + remote
 
 
 def element_values(field, received, meta_ref, onehot_ref, forth_ref, spread_ref):
@@ -378,21 +434,24 @@
 
 def apply_kernel(
     inner, trace, owned, cap, fused,
-    meta_ref, onehot_ref, forth_ref, back_ref, gid_ref, label_ref, inverse_ref, couple_ref, self_ref,
+    meta_ref, onehot_ref, forth_ref, back_ref, inverse_ref, couple_ref, self_ref,
     *refs,
 ):
     if fused:
-        before_ref, *received = refs[:9]
-        refs = refs[9:]
-        field_ref, refs = refs[0], refs[1:]
+        gid_ref, label_ref, before_ref, *received = refs[:11]
+        field_ref, *refs = refs[11:]
+        gid, label = gid_ref[0:1, :], label_ref[0:1, :]
         field, received = fused_values(
             owned, cap, meta_ref, before_ref, received[:3], received[3:]
         )
-        field_ref[...] = field
     else:
-        field = refs[0][...]
-        received = merged(meta_ref, *[r[...] for r in refs[1:5]], cap, False)
-        refs = refs[5:]
+        field_ref, gid_ref, label_ref, *after = refs[8:]
+        field, received, gid, label = first_values(owned, cap, meta_ref, refs[:3], refs[3:8])
+        refs = after
+        gid_ref[...] = jnp.broadcast_to(gid, gid_ref.shape)
+        label_ref[...] = label
+        label = label[0:1, :]
+    field_ref[...] = field
     own_ref, shared_ref, spread_ref, mid_ref, weight_ref, image_ref = refs
     width = spread_ref.shape[1]
     kind = element_values(field, received, meta_ref, onehot_ref, forth_ref, spread_ref)
@@ -402,7 +461,7 @@
     y = columns_times(tiles_of(image_ref, trace), couple_ref, weight_ref, trace, inner)
     z = by_kind(face_columns(y), back_ref, kind)
     sums = exact_dot(z, onehot_ref[...], 1)
-    share(owned, sums, gid_ref, label_ref, meta_ref, own_ref, shared_ref)
+    share(owned, sums, gid, label, meta_ref, own_ref, shared_ref)
 
 
 def total(x):
@@ -484,18 +543,7 @@
     )(*args)
 
 
-def exchange(block, ranks, to_owner):
-    away = ranks - 2 if to_owner else 2
-    pairs = [
-        [(r, r ^ 1) for r in range(ranks)],
-        [(r, (r + (1 if r % 2 else ranks - 1)) % ranks) for r in range(ranks)],
-        [(r, (r + ranks // 2) % ranks) for r in range(ranks)],
-        [(r, (r + away) % ranks) for r in range(ranks)],
-    ]
-    return [lax.ppermute(block, AXES, pairs[n]) for n in (0, 2, 1, 3)]
-
-
-def fused_exchange(cap, meta, shared, ranks):
+def fused_exchange(meta, shared, out, ranks, kernel, widths):
     pair = [(r, r ^ 1) for r in range(ranks)]
 
     def both_ways(chips):
@@ -504,11 +552,10 @@
 
     skip = [(r, (r + (3 if r % 2 else ranks - 3)) % ranks) for r in range(ranks)]
     far = [(r, (r + ranks // 2) % ranks) for r in range(ranks)]
-    second = lax.ppermute(shared, AXES, skip)
+    second = lax.ppermute(out, AXES, skip)
     other = lax.ppermute(shared, AXES, pair)
-    shape = (COMP * NODES + 8, RUNS * cap)
     packed = call(
-        functools.partial(pack_kernel, cap), [(shape, F32)] * 3, meta, shared, other
+        kernel, [((COMP * NODES + 8, width), F32) for width in widths], meta, shared, other
     )
     got = [
         lax.ppermute(block, AXES, way)
@@ -525,6 +572,7 @@
     cap = max(2, elements // 4)
     width = elements
     rows = COMP * NODES
+    count = RUNS * cap
     forward, backward = block_tables()
     mortar = face_mortar.reshape(FACES, width)
     kind = face_kind.reshape(FACES, width)
@@ -533,13 +581,12 @@
     inverse = inverse.reshape(inner * inner, width)
     force = body_force.reshape(COMP * inner, width)
 
-    own, out, gid, onehot, meta, load, *matrices = call(
+    offer, out, onehot, meta, load, *matrices = call(
         functools.partial(start_kernel, ranks, inner, trace, owned, cap),
         [
-            ((rows, owned), F32),
-            ((rows + 8, RUNS * cap), F32),
-            ((8, RUNS * cap), F32),
-            ((owned + RUNS * cap, FACES * width), BF16),
+            ((rows + 8, count + owned), F32),
+            ((rows + 8, count), F32),
+            ((owned + count, FACES * width), BF16),
             ((8, FACES * width), F32),
             ((COMP * inner, width), F32),
             (inverse.shape, F32),
@@ -552,35 +599,36 @@
         ],
         in_hbm=7, vmem=16,
     )
-    blocks = exchange(out, ranks, True)
-    field, out, label = call(
-        functools.partial(owner_kernel, owned, cap),
-        [((rows, owned), F32), ((rows, RUNS * cap), F32), ((8, RUNS * cap), F32)],
-        meta, own, *blocks,
-    )
-    blocks = exchange(out, ranks, False)
-    fields, spreads, mids, weights = [field], [], [], []
+    blocks = fused_exchange(
+        meta, offer, out, ranks,
+        functools.partial(first_pack_kernel, owned, cap),
+        (count + 2 * owned, count, count + owned),
+    )
+    fields, spreads, mids, weights, ids, own = [], [], [], [], [], None
     for iteration in range(2):
         fused = iteration > 0
-        first = [((rows, owned), F32)] if fused else []
+        first = [((rows, owned), F32)] + ([] if fused else [((8, count), F32)] * 2)
         results = call(
             functools.partial(apply_kernel, inner, trace, owned, cap, fused),
             first + [
                 ((rows, owned), F32),
-                ((2 * rows + 8, RUNS * cap), F32),
+                ((2 * rows + 8, count), F32),
                 ((COMP * trace, width), F32),
                 ((COMP * inner, width), F32),
                 ((COMP * inner, width), F32),
             ],
-            meta, onehot, forward, backward, gid, label, *matrices, own if fused else field, *blocks,
+            meta, onehot, forward, backward, *matrices, *([*ids, own] if fused else []), *blocks,
             scratch=[((COMP * trace, width), F32)],
         )
-        fields += results[: len(first)]
+        fields.append(results[0])
+        ids = ids or results[1 : len(first)]
         own, shared, spread, mid, weight = results[len(first) :]
         spreads.append(spread)
         mids.append(mid)
         weights.append(weight)
-        blocks = fused_exchange(cap, meta, shared, ranks)
+        blocks = fused_exchange(
+            meta, shared, shared, ranks, functools.partial(pack_kernel, cap), (count,) * 3
+        )
     field, weight, moments = call(
         functools.partial(last_kernel, inner, trace, owned, cap),
         [((rows, owned), F32), ((COMP * inner, width), F32), ((ranks, 1, width), F32)],

time: 74.9 us -> 76.9 us (1.027)
  starting transfers between devices: 25.3 us -> 31.1 us
  waiting for transfers between devices: 19.7 us -> 15.3 us
    ppermute x10 -> x3, waiting for transfers between devices: 13.2 us -> 4.62 us  [fused_exchange(): second = lax.ppermute(out, AXES, skip)]
    ppermute x6 -> x9, starting transfers between devices: 6.9 us -> 15.3 us  [fused_exchange(): lax.ppermute(block, AXES, way)]
    ppermute x10 -> x3, starting transfers between devices: 16.7 us -> 9.57 us  [fused_exchange(): second = lax.ppermute(out, AXES, skip)]
    ppermute x4 -> x6, starting transfers between devices: 1.52 us -> 5.53 us  [fused_exchange(): passed = [lax.ppermute(block, AXES, pair) for block in got[:2]]]
    ppermute x6 -> x9, waiting for transfers between devices: 4.05 us -> 7.34 us  [fused_exchange(): lax.ppermute(block, AXES, way)]
    ppermute x2 -> x3, waiting for transfers between devices: 2.45 us -> 3.37 us  [fused_exchange(): other = lax.ppermute(shared, AXES, pair)]
  transfers between devices with their start and end apart: 22 -> 21, of which waited for: 8 -> 8; matrix products, arithmetic and copies ran while one was open for 0% -> 0% of each run, Pallas kernels for 0% -> 0%
where the time goes in v5:
time: 76.9 us; the launch traced here: 76.7 us
  starting transfers between devices  31.1 us (40%)
  Pallas kernels  20.6 us (27%)
  waiting for transfers between devices  15.3 us (20%)
  blocking collectives  8.84 us (11%)
  between operations  0.77 us (1%)
    pallas_call x8, Pallas kernels, call(): pl.pallas_call(kernel, out_shape=[jax.ShapeDtypeStruct(shape, dtype) for...  20.6 us
    ppermute x9, starting transfers between devices, fused_exchange(): lax.ppermute(block, AXES, way)  15.3 us
    ppermute x3, starting transfers between devices, fused_exchange(): second = lax.ppermute(out, AXES, skip)  9.57 us
    all_to_all x1, blocking collectives, local(): lax.all_to_all(moments, AXES, split_axis=0, concat_axis=0, tiled=True)  8.84 us
    ppermute x9, waiting for transfers between devices, fused_exchange(): lax.ppermute(block, AXES, way)  7.34 us
    ppermute x6, starting transfers between devices, fused_exchange(): passed = [lax.ppermute(block, AXES, pair) for block in got[:2]]  5.53 us
    ppermute x3, waiting for transfers between devices, fused_exchange(): second = lax.ppermute(out, AXES, skip)  4.62 us
    ppermute x3, waiting for transfers between devices, fused_exchange(): other = lax.ppermute(shared, AXES, pair)  3.37 us
  transfers between devices with their start and end apart: 21, of which 8 were waited for; matrix products, arithmetic and copies ran while one was open for 0% of the time, Pallas kernels for 0%

profile of v5, /device:TPU:0, one launch (start us, length us, event | category | flops | bytes accessed | tf_op | source)
XLA Modules:
  0.0 76.7 jit_solution(10641226646758855393)
XLA Ops:
  0.7 4.1 %shard_map.95 = (f32[56,384]{1,0:T(8,128)S(1)}, f32[56,128]{1,0:T(8,128)S(1)}, bf16[384,768]{1,0:T(8,128)(2,1)S(1)}, f32[8,768]{1,0:T(8,128)S(1)}, f32[192,128]{...) custom-call(s32[6,128]{1,0:T(8,128)} %bitcast.11, s32[6,128]{1,0:T(8,128)} %bitcast.12, ...), custom_call_target="tpu_custom_call" | custom-call | tf_op jit(solution)/shard_map/pallas_call | solution.py:534
  4.8 0.5 collective-permute-start
  5.3 0.9 %collective-permute-done.other_ref.refs_1_ = f32[56,384]{1,0:T(8,128)S(1)} collective-permute-done((f32[56,384]{1,0:T(8,128)S(1)}, f32[56,384]{1,0:T(8,128)S(1)}, u32[]{:S(2)}, u32[]{:S(2)}) %collective-permute-start) | collective-permute-done | bytes 86048 | tf_op jit(solution)/shard_map/ppermute | solution.py:556
  6.3 0.3 shard_map.96
  6.5 2.7 %collective-permute-start.2 = (f32[56,640]{1,0:T(8,128)S(1)}, f32[56,640]{1,0:T(8,128)S(1)}, u32[]{:S(2)}, u32[]{:S(2)}) collective-permute-start(f32[56,640]{1,0:T(8,128)S(1)} %get-tuple-element.45), channel_id=1, source_target_pairs={{0,3},{2,5},{4,7},{6,9},{8,11},{10,13},{12,15},{14,17},{16,19},{18... | collective-permute-start | bytes 430088 | tf_op jit(solution)/shard_map/ppermute | solution.py:561
  9.2 2.8 %collective-permute-done.2.refs_3_ = f32[56,640]{1,0:T(8,128)S(1)} collective-permute-done((f32[56,640]{1,0:T(8,128)S(1)}, f32[56,640]{1,0:T(8,128)S(1)}, u32[]{:S(2)}, u32[]{:S(2)}) %collective-permute-start.2) | collective-permute-done | bytes 143392 | tf_op jit(solution)/shard_map/ppermute | solution.py:561
  12.0 4.3 %collective-permute-start.5 = (f32[56,640]{1,0:T(8,128)S(1)}, f32[56,640]{1,0:T(8,128)S(1)}, u32[]{:S(2)}, u32[]{:S(2)}) collective-permute-start(f32[56,640]{1,0:T(8,128)S(1)} %collective-permute-done.2.refs_3_), channel_id=1, source_target_pairs={{0,1},{1,0},{2,3},{3,2},{4,5},{5,4},{6,7},{7,6},{8,9},{9,8},{10,11... | collective-permute-start | bytes 430088 | tf_op jit(solution)/shard_map/ppermute | solution.py:564
  16.3 0.8 %collective-permute-start.4 = (f32[56,384]{1,0:T(8,128)S(1)}, f32[56,384]{1,0:T(8,128)S(1)}, u32[]{:S(2)}, u32[]{:S(2)}) collective-permute-start(f32[56,384]{1,0:T(8,128)S(1)} %get-tuple-element.47), channel_id=1, source_target_pairs={{0,16},{1,17},{2,18},{3,19},{4,20},{5,21},{6,22},{7,23},{8,24},{9,... | collective-permute-start | bytes 258056 | tf_op jit(solution)/shard_map/ppermute | solution.py:561
  17.1 4.8 %collective-permute-start.3 = (f32[56,128]{1,0:T(8,128)S(1)}, f32[56,128]{1,0:T(8,128)S(1)}, u32[]{:S(2)}, u32[]{:S(2)}) collective-permute-start(f32[56,128]{1,0:T(8,128)S(1)} %get-tuple-element.46), channel_id=1, source_target_pairs={{0,15},{2,17},{4,19},{6,21},{8,23},{10,25},{12,27},{14,29},{16,31}... | collective-permute-start | bytes 86024 | tf_op jit(solution)/shard_map/ppermute | solution.py:561
  21.9 2.2 %collective-permute-start.1 = (f32[56,128]{1,0:T(8,128)S(1)}, f32[56,128]{1,0:T(8,128)S(1)}, u32[]{:S(2)}, u32[]{:S(2)}) collective-permute-start(f32[56,128]{1,0:T(8,128)S(1)} %get-tuple-element.44), channel_id=1, source_target_pairs={{0,29},{1,4},{2,31},{3,6},{4,1},{5,8},{6,3},{7,10},{8,5},{9,12},{1... | collective-permute-start | bytes 86024 | tf_op jit(solution)/shard_map/ppermute | solution.py:555
  24.2 0.2 collective-permute-start.6
  24.4 3.6 %collective-permute-done.1.refs_2_ = f32[56,128]{1,0:T(8,128)S(1)} collective-permute-done((f32[56,128]{1,0:T(8,128)S(1)}, f32[56,128]{1,0:T(8,128)S(1)}, u32[]{:S(2)}, u32[]{:S(2)}) %collective-permute-start.1) | collective-permute-done | bytes 28704 | tf_op jit(solution)/shard_map/ppermute | solution.py:555
  28.0 4.8 %shard_map.97 = (f32[48,256]{1,0:T(8,128)S(1)}, f32[8,128]{1,0:T(8,128)S(1)}, f32[8,128]{1,0:T(8,128)S(1)}, f32[48,256]{1,0:T(8,128)S(1)}, f32[104,128]{1,0:T(8,...) custom-call(f32[8,768]{1,0:T(8,128)S(1)} %get-tuple-element.38.meta_ref, ...), custom_call_target="tpu_custom_call" | custom-call | tf_op jit(solution)/shard_map/pallas_call | solution.py:534
  32.9 1.2 %collective-permute-done.7.other_ref.refs_4_ = f32[104,128]{1,0:T(8,128)S(1)} collective-permute-done((f32[104,128]{1,0:T(8,128)S(1)}, f32[104,128]{1,0:T(8,128)S(1)}, u32[]{:S(2)}, u32[]{:S(2)}) %collective-permute-start.7) | collective-permute-done | bytes 53280 | tf_op jit(solution)/shard_map/ppermute | solution.py:556
  34.1 0.4 shard_map.98
  34.6 0.4 collective-permute-start.10
  35.0 2.9 %collective-permute-start.8 = (f32[104,128]{1,0:T(8,128)S(1)}, f32[104,128]{1,0:T(8,128)S(1)}, u32[]{:S(2)}, u32[]{:S(2)}) collective-permute-start(f32[104,128]{1,0:T(8,128)S(1)} %get-tuple-element.52.mine_ref.refs_3_), channel_id=1, source_target_pairs={{0,29},{1,4},{2,31},{3,6},{4,1},{5,8},{6,3},{7,10},{8,5},{9,12},{1... | collective-permute-start | bytes 159752 | tf_op jit(solution)/shard_map/ppermute | solution.py:555
  37.9 3.9 %collective-permute-start.11 = (f32[56,128]{1,0:T(8,128)S(1)}, f32[56,128]{1,0:T(8,128)S(1)}, u32[]{:S(2)}, u32[]{:S(2)}) collective-permute-start(f32[56,128]{1,0:T(8,128)S(1)} %get-tuple-element.55), channel_id=1, source_target_pairs={{0,16},{1,17},{2,18},{3,19},{4,20},{5,21},{6,22},{7,23},{8,24},{9,... | collective-permute-start | bytes 86024 | tf_op jit(solution)/shard_map/ppermute | solution.py:561
  41.8 0.5 collective-permute-start.13
  42.3 2.2 %collective-permute-done.11.refs_8_ = f32[56,128]{1,0:T(8,128)S(1)} collective-permute-done((f32[56,128]{1,0:T(8,128)S(1)}, f32[56,128]{1,0:T(8,128)S(1)}, u32[]{:S(2)}, u32[]{:S(2)}) %collective-permute-start.11) | collective-permute-done | bytes 28704 | tf_op jit(solution)/shard_map/ppermute | solution.py:561
  44.5 4.8 %shard_map.99 = (f32[48,256]{1,0:T(8,128)S(1)}, f32[48,256]{1,0:T(8,128)S(1)}, f32[104,128]{1,0:T(8,128)S(1)}, f32[288,128]{1,0:T(8,128)S(1)}, f32[192,128]{1,0:T(8,128)S(1)}, /*index=5*/f32[192,128]{1,0:T(8,128)S(1)}) custom-call(f32[8,768]{1,0:T(8,128)S(1)} %get-tuple-element.38.meta_ref, bf16[384,768]{1,0:T(8,128)(2,1)S(1)} %get-tuple-element.39.onehot_ref, ...), custom_call_target="tpu_custom_call" | custom-call | tf_op jit(solution)/shard_map/pallas_call | solution.py:534
  49.3 1.2 %collective-permute-done.14.other_ref.refs_1_ = f32[104,128]{1,0:T(8,128)S(1)} collective-permute-done((f32[104,128]{1,0:T(8,128)S(1)}, f32[104,128]{1,0:T(8,128)S(1)}, u32[]{:S(2)}, u32[]{:S(2)}) %collective-permute-start.14) | collective-permute-done | bytes 53280 | tf_op jit(solution)/shard_map/ppermute | solution.py:556
  50.5 0.4 shard_map.100
  51.1 1.8 %collective-permute-start.17 = (f32[56,128]{1,0:T(8,128)S(1)}, f32[56,128]{1,0:T(8,128)S(1)}, u32[]{:S(2)}, u32[]{:S(2)}) collective-permute-start(f32[56,128]{1,0:T(8,128)S(1)} %get-tuple-element.64), channel_id=1, source_target_pairs={{0,15},{2,17},{4,19},{6,21},{8,23},{10,25},{12,27},{14,29},{16,31}... | collective-permute-start | bytes 86024 | tf_op jit(solution)/shard_map/ppermute | solution.py:561
  52.9 4.4 %collective-permute-start.15 = (f32[104,128]{1,0:T(8,128)S(1)}, f32[104,128]{1,0:T(8,128)S(1)}, u32[]{:S(2)}, u32[]{:S(2)}) collective-permute-start(f32[104,128]{1,0:T(8,128)S(1)} %get-tuple-element.62.mine_ref.refs_0_), channel_id=1, source_target_pairs={{0,29},{1,4},{2,31},{3,6},{4,1},{5,8},{6,3},{7,10},{8,5},{9,12},{1... | collective-permute-start | bytes 159752 | tf_op jit(solution)/shard_map/ppermute | solution.py:555
  57.3 0.9 %collective-permute-start.18 = (f32[56,128]{1,0:T(8,128)S(1)}, f32[56,128]{1,0:T(8,128)S(1)}, u32[]{:S(2)}, u32[]{:S(2)}) collective-permute-start(f32[56,128]{1,0:T(8,128)S(1)} %get-tuple-element.65), channel_id=1, source_target_pairs={{0,16},{1,17},{2,18},{3,19},{4,20},{5,21},{6,22},{7,23},{8,24},{9,... | collective-permute-start | bytes 86024 | tf_op jit(solution)/shard_map/ppermute | solution.py:561
  58.2 0.5 collective-permute-start.20
  58.7 1.0 %collective-permute-done.15.refs_2_ = f32[104,128]{1,0:T(8,128)S(1)} collective-permute-done((f32[104,128]{1,0:T(8,128)S(1)}, f32[104,128]{1,0:T(8,128)S(1)}, u32[]{:S(2)}, u32[]{:S(2)}) %collective-permute-start.15) | collective-permute-done | bytes 53280 | tf_op jit(solution)/shard_map/ppermute | solution.py:555
  59.8 2.3 %collective-permute-done.18.refs_5_ = f32[56,128]{1,0:T(8,128)S(1)} collective-permute-done((f32[56,128]{1,0:T(8,128)S(1)}, f32[56,128]{1,0:T(8,128)S(1)}, u32[]{:S(2)}, u32[]{:S(2)}) %collective-permute-start.18) | collective-permute-done | bytes 28704 | tf_op jit(solution)/shard_map/ppermute | solution.py:561
  62.1 3.9 %shard_map.101 = (f32[48,256]{1,0:T(8,128)S(1)}, f32[192,128]{1,0:T(8,128)S(1)}, f32[32,1,128]{2,1,0:T(1,128)S(1)}) custom-call(f32[8,768]{1,0:T(8,128)S(1)} %get-tuple-element.38.meta_ref, bf16[384,768]{1,0:T(8,128)(2,1)S(1)} %get-tuple-element.39.onehot_ref, f32[192,48]{1,0:T(8,128)S(1)} %copy-done, f32[4096,128]{1,0:T(8,128)S(1)} %get-tuple-element.40.inverse_ref, ...), custom_call_target="tpu_custom_call" | custom-call | tf_op jit(solution)/shard_map/pallas_call | solution.py:534
  66.0 8.8 %all_to_all.5.moment_ref = f32[32,1,128]{2,1,0:T(1,128)S(1)} all-to-all(f32[32,1,128]{2,1,0:T(1,128)S(1)} %get-tuple-element.66), channel_id=1, replica_groups=mesh['dom'=16,'blk'=2] {'dom','blk'}, dimensions={0} | all-to-all | bytes 32768 | tf_op jit(solution)/shard_map/all_to_all | solution.py:644
  74.9 1.8 %shard_map.102 = (f32[48,256]{1,0:T(8,128)}, f32[192,128]{1,0:T(8,128)}) custom-call(f32[32,1,128]{2,1,0:T(1,128)S(1)} %all_to_all.5.moment_ref, f32[48,256]{1,0:T(8,128)S(1)} %get-tuple-element.48.k0_ref, f32[48,256]{1,0:T(8,128)S(1)} %get-tuple-element.56.k1_ref, f32[48,256]{1,0:T(8,128)S(1)} %get-tuple-element.67.k2_ref, ...), custom_call_target="tpu_custom_call" | custom-call | tf_op jit(solution)/shard_map/pallas_call | solution.py:534
  (23 shorter events, 0.4 us)
Async XLA Ops:
  0.6 27.3 %copy-start = (f32[192,48]{1,0:T(8,128)S(1)}, f32[192,48]{1,0:T(8,128)}, u32[]{:S(2)}) copy-start(f32[192,48]{1,0:T(8,128)} %constant.5.clone.forth_ref) | copy-start | bytes 110596
  0.6 27.3 %copy-start.1 = (f32[192,48]{1,0:T(8,128)S(1)}, f32[192,48]{1,0:T(8,128)}, u32[]{:S(2)}) copy-start(f32[192,48]{1,0:T(8,128)} %constant.4.clone.back_hbm.back_ref) | copy-start | bytes 110596
  4.8 1.4 %collective-permute-start = (f32[56,384]{1,0:T(8,128)S(1)}, f32[56,384]{1,0:T(8,128)S(1)}, u32[]{:S(2)}, u32[]{:S(2)}) collective-permute-start(f32[56,384]{1,0:T(8,128)S(1)} %get-tuple-element.43.mine_ref.refs_0_), channel_id=1, source_target_pairs={{0,1},{1,0},{2,3},{3,2},{4,5},{5,4},{6,7},{7,6},{8,9},{9,8},{10,11... | collective-permute-start | bytes 258056 | tf_op jit(solution)/shard_map/ppermute | solution.py:556
  6.5 5.5 %collective-permute-start.2 = (f32[56,640]{1,0:T(8,128)S(1)}, f32[56,640]{1,0:T(8,128)S(1)}, u32[]{:S(2)}, u32[]{:S(2)}) collective-permute-start(f32[56,640]{1,0:T(8,128)S(1)} %get-tuple-element.45), channel_id=1, source_target_pairs={{0,3},{2,5},{4,7},{6,9},{8,11},{10,13},{12,15},{14,17},{16,19},{18... | collective-permute-start | bytes 430088 | tf_op jit(solution)/shard_map/ppermute | solution.py:561
  12.0 16.0 %collective-permute-start.5 = (f32[56,640]{1,0:T(8,128)S(1)}, f32[56,640]{1,0:T(8,128)S(1)}, u32[]{:S(2)}, u32[]{:S(2)}) collective-permute-start(f32[56,640]{1,0:T(8,128)S(1)} %collective-permute-done.2.refs_3_), channel_id=1, source_target_pairs={{0,1},{1,0},{2,3},{3,2},{4,5},{5,4},{6,7},{7,6},{8,9},{9,8},{10,11... | collective-permute-start | bytes 430088 | tf_op jit(solution)/shard_map/ppermute | solution.py:564
  16.3 11.6 %collective-permute-start.4 = (f32[56,384]{1,0:T(8,128)S(1)}, f32[56,384]{1,0:T(8,128)S(1)}, u32[]{:S(2)}, u32[]{:S(2)}) collective-permute-start(f32[56,384]{1,0:T(8,128)S(1)} %get-tuple-element.47), channel_id=1, source_target_pairs={{0,16},{1,17},{2,18},{3,19},{4,20},{5,21},{6,22},{7,23},{8,24},{9,... | collective-permute-start | bytes 258056 | tf_op jit(solution)/shard_map/ppermute | solution.py:561
  17.1 7.1 %collective-permute-start.3 = (f32[56,128]{1,0:T(8,128)S(1)}, f32[56,128]{1,0:T(8,128)S(1)}, u32[]{:S(2)}, u32[]{:S(2)}) collective-permute-start(f32[56,128]{1,0:T(8,128)S(1)} %get-tuple-element.46), channel_id=1, source_target_pairs={{0,15},{2,17},{4,19},{6,21},{8,23},{10,25},{12,27},{14,29},{16,31}... | collective-permute-start | bytes 86024 | tf_op jit(solution)/shard_map/ppermute | solution.py:561
  21.9 6.0 %collective-permute-start.1 = (f32[56,128]{1,0:T(8,128)S(1)}, f32[56,128]{1,0:T(8,128)S(1)}, u32[]{:S(2)}, u32[]{:S(2)}) collective-permute-start(f32[56,128]{1,0:T(8,128)S(1)} %get-tuple-element.44), channel_id=1, source_target_pairs={{0,29},{1,4},{2,31},{3,6},{4,1},{5,8},{6,3},{7,10},{8,5},{9,12},{1... | collective-permute-start | bytes 86024 | tf_op jit(solution)/shard_map/ppermute | solution.py:555
  24.2 3.7 %collective-permute-start.6 = (f32[56,128]{1,0:T(8,128)S(1)}, f32[56,128]{1,0:T(8,128)S(1)}, u32[]{:S(2)}, u32[]{:S(2)}) collective-permute-start(f32[56,128]{1,0:T(8,128)S(1)} %collective-permute-done.3.refs_4_), channel_id=1, source_target_pairs={{0,1},{1,0},{2,3},{3,2},{4,5},{5,4},{6,7},{7,6},{8,9},{9,8},{10,11... | collective-permute-start | bytes 86024 | tf_op jit(solution)/shard_map/ppermute | solution.py:564
  32.8 1.3 %collective-permute-start.7 = (f32[104,128]{1,0:T(8,128)S(1)}, f32[104,128]{1,0:T(8,128)S(1)}, u32[]{:S(2)}, u32[]{:S(2)}) collective-permute-start(f32[104,128]{1,0:T(8,128)S(1)} %get-tuple-element.52.mine_ref.refs_3_), channel_id=1, source_target_pairs={{0,1},{1,0},{2,3},{3,2},{4,5},{5,4},{6,7},{7,6},{8,9},{9,8},{10,11... | collective-permute-start | bytes 159752 | tf_op jit(solution)/shard_map/ppermute | solution.py:556
  34.6 7.2 %collective-permute-start.9 = (f32[56,128]{1,0:T(8,128)S(1)}, f32[56,128]{1,0:T(8,128)S(1)}, u32[]{:S(2)}, u32[]{:S(2)}) collective-permute-start(f32[56,128]{1,0:T(8,128)S(1)} %get-tuple-element.53), channel_id=1, source_target_pairs={{0,3},{2,5},{4,7},{6,9},{8,11},{10,13},{12,15},{14,17},{16,19},{18... | collective-permute-start | bytes 86024 | tf_op jit(solution)/shard_map/ppermute | solution.py:561
  34.6 7.1 %collective-permute-start.10 = (f32[56,128]{1,0:T(8,128)S(1)}, f32[56,128]{1,0:T(8,128)S(1)}, u32[]{:S(2)}, u32[]{:S(2)}) collective-permute-start(f32[56,128]{1,0:T(8,128)S(1)} %get-tuple-element.54), channel_id=1, source_target_pairs={{0,15},{2,17},{4,19},{6,21},{8,23},{10,25},{12,27},{14,29},{16,31}... | collective-permute-start | bytes 86024 | tf_op jit(solution)/shard_map/ppermute | solution.py:561
  35.0 7.3 %collective-permute-start.8 = (f32[104,128]{1,0:T(8,128)S(1)}, f32[104,128]{1,0:T(8,128)S(1)}, u32[]{:S(2)}, u32[]{:S(2)}) collective-permute-start(f32[104,128]{1,0:T(8,128)S(1)} %get-tuple-element.52.mine_ref.refs_3_), channel_id=1, source_target_pairs={{0,29},{1,4},{2,31},{3,6},{4,1},{5,8},{6,3},{7,10},{8,5},{9,12},{1... | collective-permute-start | bytes 159752 | tf_op jit(solution)/shard_map/ppermute | solution.py:555
  37.9 6.6 %collective-permute-start.11 = (f32[56,128]{1,0:T(8,128)S(1)}, f32[56,128]{1,0:T(8,128)S(1)}, u32[]{:S(2)}, u32[]{:S(2)}) collective-permute-start(f32[56,128]{1,0:T(8,128)S(1)} %get-tuple-element.55), channel_id=1, source_target_pairs={{0,16},{1,17},{2,18},{3,19},{4,20},{5,21},{6,22},{7,23},{8,24},{9,... | collective-permute-start | bytes 86024 | tf_op jit(solution)/shard_map/ppermute | solution.py:561
  41.8 2.7 %collective-permute-start.12 = (f32[56,128]{1,0:T(8,128)S(1)}, f32[56,128]{1,0:T(8,128)S(1)}, u32[]{:S(2)}, u32[]{:S(2)}) collective-permute-start(f32[56,128]{1,0:T(8,128)S(1)} %collective-permute-done.9.refs_6_), channel_id=1, source_target_pairs={{0,1},{1,0},{2,3},{3,2},{4,5},{5,4},{6,7},{7,6},{8,9},{9,8},{10,11... | collective-permute-start | bytes 86024 | tf_op jit(solution)/shard_map/ppermute | solution.py:564
  41.8 2.7 %collective-permute-start.13 = (f32[56,128]{1,0:T(8,128)S(1)}, f32[56,128]{1,0:T(8,128)S(1)}, u32[]{:S(2)}, u32[]{:S(2)}) collective-permute-start(f32[56,128]{1,0:T(8,128)S(1)} %collective-permute-done.10.refs_7_), channel_id=1, source_target_pairs={{0,1},{1,0},{2,3},{3,2},{4,5},{5,4},{6,7},{7,6},{8,9},{9,8},{10,11... | collective-permute-start | bytes 86024 | tf_op jit(solution)/shard_map/ppermute | solution.py:564
  49.2 1.3 %collective-permute-start.14 = (f32[104,128]{1,0:T(8,128)S(1)}, f32[104,128]{1,0:T(8,128)S(1)}, u32[]{:S(2)}, u32[]{:S(2)}) collective-permute-start(f32[104,128]{1,0:T(8,128)S(1)} %get-tuple-element.62.mine_ref.refs_0_), channel_id=1, source_target_pairs={{0,1},{1,0},{2,3},{3,2},{4,5},{5,4},{6,7},{7,6},{8,9},{9,8},{10,11... | collective-permute-start | bytes 159752 | tf_op jit(solution)/shard_map/ppermute | solution.py:556
  51.0 7.2 %collective-permute-start.16 = (f32[56,128]{1,0:T(8,128)S(1)}, f32[56,128]{1,0:T(8,128)S(1)}, u32[]{:S(2)}, u32[]{:S(2)}) collective-permute-start(f32[56,128]{1,0:T(8,128)S(1)} %get-tuple-element.63), channel_id=1, source_target_pairs={{0,3},{2,5},{4,7},{6,9},{8,11},{10,13},{12,15},{14,17},{16,19},{18... | collective-permute-start | bytes 86024 | tf_op jit(solution)/shard_map/ppermute | solution.py:561
  51.1 7.1 %collective-permute-start.17 = (f32[56,128]{1,0:T(8,128)S(1)}, f32[56,128]{1,0:T(8,128)S(1)}, u32[]{:S(2)}, u32[]{:S(2)}) collective-permute-start(f32[56,128]{1,0:T(8,128)S(1)} %get-tuple-element.64), channel_id=1, source_target_pairs={{0,15},{2,17},{4,19},{6,21},{8,23},{10,25},{12,27},{14,29},{16,31}... | collective-permute-start | bytes 86024 | tf_op jit(solution)/shard_map/ppermute | solution.py:561
  52.9 6.9 %collective-permute-start.15 = (f32[104,128]{1,0:T(8,128)S(1)}, f32[104,128]{1,0:T(8,128)S(1)}, u32[]{:S(2)}, u32[]{:S(2)}) collective-permute-start(f32[104,128]{1,0:T(8,128)S(1)} %get-tuple-element.62.mine_ref.refs_0_), channel_id=1, source_target_pairs={{0,29},{1,4},{2,31},{3,6},{4,1},{5,8},{6,3},{7,10},{8,5},{9,12},{1... | collective-permute-start | bytes 159752 | tf_op jit(solution)/shard_map/ppermute | solution.py:555
  57.3 4.8 %collective-permute-start.18 = (f32[56,128]{1,0:T(8,128)S(1)}, f32[56,128]{1,0:T(8,128)S(1)}, u32[]{:S(2)}, u32[]{:S(2)}) collective-permute-start(f32[56,128]{1,0:T(8,128)S(1)} %get-tuple-element.65), channel_id=1, source_target_pairs={{0,16},{1,17},{2,18},{3,19},{4,20},{5,21},{6,22},{7,23},{8,24},{9,... | collective-permute-start | bytes 86024 | tf_op jit(solution)/shard_map/ppermute | solution.py:561
  58.2 3.9 %collective-permute-start.19 = (f32[56,128]{1,0:T(8,128)S(1)}, f32[56,128]{1,0:T(8,128)S(1)}, u32[]{:S(2)}, u32[]{:S(2)}) collective-permute-start(f32[56,128]{1,0:T(8,128)S(1)} %collective-permute-done.16.refs_3_), channel_id=1, source_target_pairs={{0,1},{1,0},{2,3},{3,2},{4,5},{5,4},{6,7},{7,6},{8,9},{9,8},{10,11... | collective-permute-start | bytes 86024 | tf_op jit(solution)/shard_map/ppermute | solution.py:564
  58.2 3.9 %collective-permute-start.20 = (f32[56,128]{1,0:T(8,128)S(1)}, f32[56,128]{1,0:T(8,128)S(1)}, u32[]{:S(2)}, u32[]{:S(2)}) collective-permute-start(f32[56,128]{1,0:T(8,128)S(1)} %collective-permute-done.17.refs_4_), channel_id=1, source_target_pairs={{0,1},{1,0},{2,3},{3,2},{4,5},{5,4},{6,7},{7,6},{8,9},{9,8},{10,11... | collective-permute-start | bytes 86024 | tf_op jit(solution)/shard_map/ppermute | solution.py:564

commit v6 on v5

--- a/solution.py
+++ b/solution.py
@@ -561,6 +561,7 @@
         lax.ppermute(block, AXES, way)
         for block, way in zip(packed, (both_ways(1), both_ways(ranks // 4 - 1), far))
     ]
+    second, *got = lax.optimization_barrier((second, *got))
     passed = [lax.ppermute(block, AXES, pair) for block in got[:2]]
     return [shared, other, second, *got, *passed]
 

time: 76.9 us -> 72.4 us (0.941)
  starting transfers between devices: 31.1 us -> 25.8 us
  blocking collectives: 8.84 us -> 10.8 us
  waiting for transfers between devices: 15.3 us -> 14.3 us
    ppermute x6, waiting for transfers between devices: 0.02 us -> 2.99 us  [fused_exchange(): passed = [lax.ppermute(block, AXES, pair) for block in got[:2]]]
    ppermute x3, starting transfers between devices: 9.57 us -> 7 us  [fused_exchange(): second = lax.ppermute(out, AXES, skip)]
    ppermute x3, waiting for transfers between devices: 3.37 us -> 0.93 us  [fused_exchange(): other = lax.ppermute(shared, AXES, pair)]
    all_to_all x1, blocking collectives: 8.84 us -> 10.8 us  [local(): lax.all_to_all(moments, AXES, split_axis=0, concat_axis=0, tiled=True)]
    ppermute x6, starting transfers between devices: 5.53 us -> 3.79 us  [fused_exchange(): passed = [lax.ppermute(block, AXES, pair) for block in got[:2]]]
    ppermute x9, starting transfers between devices: 15.3 us -> 14 us  [fused_exchange(): lax.ppermute(block, AXES, way)]
    ppermute x3, waiting for transfers between devices: 4.62 us -> 3.71 us  [fused_exchange(): second = lax.ppermute(out, AXES, skip)]
  transfers between devices with their start and end apart: 21 -> 21, of which waited for: 8 -> 12; matrix products, arithmetic and copies ran while one was open for 0% -> 0% of each run, Pallas kernels for 0% -> 1%
where the time goes in v6:
time: 72.4 us; the launch traced here: 72.3 us
  starting transfers between devices  25.8 us (36%)
  Pallas kernels  20.6 us (28%)
  waiting for transfers between devices  14.3 us (20%)
  blocking collectives  10.8 us (15%)
    pallas_call x8, Pallas kernels, call(): pl.pallas_call(kernel, out_shape=[jax.ShapeDtypeStruct(shape, dtype) for...  20.6 us
    ppermute x9, starting transfers between devices, fused_exchange(): lax.ppermute(block, AXES, way)  14 us
    all_to_all x1, blocking collectives, local(): lax.all_to_all(moments, AXES, split_axis=0, concat_axis=0, tiled=True)  10.8 us
    ppermute x3, starting transfers between devices, fused_exchange(): second = lax.ppermute(out, AXES, skip)  7 us
    ppermute x9, waiting for transfers between devices, fused_exchange(): lax.ppermute(block, AXES, way)  6.61 us
    ppermute x6, starting transfers between devices, fused_exchange(): passed = [lax.ppermute(block, AXES, pair) for block in got[:2]]  3.79 us
    ppermute x3, waiting for transfers between devices, fused_exchange(): second = lax.ppermute(out, AXES, skip)  3.71 us
    ppermute x6, waiting for transfers between devices, fused_exchange(): passed = [lax.ppermute(block, AXES, pair) for block in got[:2]]  2.99 us
  transfers between devices with their start and end apart: 21, of which 12 were waited for; matrix products, arithmetic and copies ran while one was open for 0% of the time, Pallas kernels for 1%

profile of v6, /device:TPU:0, one launch (start us, length us, event | category | flops | bytes accessed | tf_op | source)
XLA Modules:
  0.0 72.3 jit_solution(6036643746178310843)
XLA Ops:
  0.7 4.1 %shard_map.95 = (f32[56,384]{1,0:T(8,128)S(1)}, f32[56,128]{1,0:T(8,128)S(1)}, bf16[384,768]{1,0:T(8,128)(2,1)S(1)}, f32[8,768]{1,0:T(8,128)S(1)}, f32[192,128]{...) custom-call(s32[6,128]{1,0:T(8,128)} %bitcast.11, s32[6,128]{1,0:T(8,128)} %bitcast.12, ...), custom_call_target="tpu_custom_call" | custom-call | tf_op jit(solution)/shard_map/pallas_call | solution.py:534
  4.8 0.5 collective-permute-start
  5.3 0.9 %collective-permute-done.other_ref.refs_1_ = f32[56,384]{1,0:T(8,128)S(1)} collective-permute-done((f32[56,384]{1,0:T(8,128)S(1)}, f32[56,384]{1,0:T(8,128)S(1)}, u32[]{:S(2)}, u32[]{:S(2)}) %collective-permute-start) | collective-permute-done | bytes 86048 | tf_op jit(solution)/shard_map/ppermute | solution.py:556
  6.5 2.7 %collective-permute-start.2 = (f32[56,640]{1,0:T(8,128)S(1)}, f32[56,640]{1,0:T(8,128)S(1)}, u32[]{:S(2)}, u32[]{:S(2)}) collective-permute-start(f32[56,640]{1,0:T(8,128)S(1)} %get-tuple-element.57), channel_id=1, source_target_pairs={{0,3},{2,5},{4,7},{6,9},{8,11},{10,13},{12,15},{14,17},{16,19},{18... | collective-permute-start | bytes 430088 | tf_op jit(solution)/shard_map/ppermute | solution.py:561
  9.2 2.6 %collective-permute-start.4 = (f32[56,384]{1,0:T(8,128)S(1)}, f32[56,384]{1,0:T(8,128)S(1)}, u32[]{:S(2)}, u32[]{:S(2)}) collective-permute-start(f32[56,384]{1,0:T(8,128)S(1)} %get-tuple-element.59), channel_id=1, source_target_pairs={{0,16},{1,17},{2,18},{3,19},{4,20},{5,21},{6,22},{7,23},{8,24},{9,... | collective-permute-start | bytes 258056 | tf_op jit(solution)/shard_map/ppermute | solution.py:561
  11.8 1.9 %collective-permute-start.1 = (f32[56,128]{1,0:T(8,128)S(1)}, f32[56,128]{1,0:T(8,128)S(1)}, u32[]{:S(2)}, u32[]{:S(2)}) collective-permute-start(f32[56,128]{1,0:T(8,128)S(1)} %get-tuple-element.56), channel_id=1, source_target_pairs={{0,29},{1,4},{2,31},{3,6},{4,1},{5,8},{6,3},{7,10},{8,5},{9,12},{1... | collective-permute-start | bytes 86024 | tf_op jit(solution)/shard_map/ppermute | solution.py:555
  13.7 0.5 collective-permute-start.3
  14.2 3.7 %collective-permute-done.1.refs_2_ = f32[56,128]{1,0:T(8,128)S(1)} collective-permute-done((f32[56,128]{1,0:T(8,128)S(1)}, f32[56,128]{1,0:T(8,128)S(1)}, u32[]{:S(2)}, u32[]{:S(2)}) %collective-permute-start.1) | collective-permute-done | bytes 28704 | tf_op jit(solution)/shard_map/ppermute | solution.py:555
  17.9 1.1 %collective-permute-done.3.refs_4_ = f32[56,128]{1,0:T(8,128)S(1)} collective-permute-done((f32[56,128]{1,0:T(8,128)S(1)}, f32[56,128]{1,0:T(8,128)S(1)}, u32[]{:S(2)}, u32[]{:S(2)}) %collective-permute-start.3) | collective-permute-done | bytes 28704 | tf_op jit(solution)/shard_map/ppermute | solution.py:561
  19.6 0.9 %collective-permute-done.6.refs_7_ = f32[56,128]{1,0:T(8,128)S(1)} collective-permute-done((f32[56,128]{1,0:T(8,128)S(1)}, f32[56,128]{1,0:T(8,128)S(1)}, u32[]{:S(2)}, u32[]{:S(2)}) %collective-permute-start.6) | collective-permute-done | bytes 28704 | tf_op jit(solution)/shard_map/ppermute | solution.py:565
  20.5 4.8 %shard_map.97 = (f32[48,256]{1,0:T(8,128)S(1)}, f32[8,128]{1,0:T(8,128)S(1)}, f32[8,128]{1,0:T(8,128)S(1)}, f32[48,256]{1,0:T(8,128)S(1)}, f32[104,128]{1,0:T(8,...) custom-call(f32[8,768]{1,0:T(8,128)S(1)} %get-tuple-element.50.meta_ref, ...), custom_call_target="tpu_custom_call" | custom-call | tf_op jit(solution)/shard_map/pallas_call | solution.py:534
  25.7 3.4 %collective-permute-start.8 = (f32[104,128]{1,0:T(8,128)S(1)}, f32[104,128]{1,0:T(8,128)S(1)}, u32[]{:S(2)}, u32[]{:S(2)}) collective-permute-start(f32[104,128]{1,0:T(8,128)S(1)} %get-tuple-element.68.mine_ref.refs_3_), channel_id=1, source_target_pairs={{0,29},{1,4},{2,31},{3,6},{4,1},{5,8},{6,3},{7,10},{8,5},{9,12},{1... | collective-permute-start | bytes 159752 | tf_op jit(solution)/shard_map/ppermute | solution.py:555
  29.1 0.4 shard_map.98
  29.9 0.9 %collective-permute-start.10 = (f32[56,128]{1,0:T(8,128)S(1)}, f32[56,128]{1,0:T(8,128)S(1)}, u32[]{:S(2)}, u32[]{:S(2)}) collective-permute-start(f32[56,128]{1,0:T(8,128)S(1)} %get-tuple-element.70), channel_id=1, source_target_pairs={{0,15},{2,17},{4,19},{6,21},{8,23},{10,25},{12,27},{14,29},{16,31}... | collective-permute-start | bytes 86024 | tf_op jit(solution)/shard_map/ppermute | solution.py:561
  30.8 2.3 %collective-permute-start.11 = (f32[56,128]{1,0:T(8,128)S(1)}, f32[56,128]{1,0:T(8,128)S(1)}, u32[]{:S(2)}, u32[]{:S(2)}) collective-permute-start(f32[56,128]{1,0:T(8,128)S(1)} %get-tuple-element.71), channel_id=1, source_target_pairs={{0,16},{1,17},{2,18},{3,19},{4,20},{5,21},{6,22},{7,23},{8,24},{9,... | collective-permute-start | bytes 86024 | tf_op jit(solution)/shard_map/ppermute | solution.py:561
  33.1 1.9 %collective-permute-done.10.refs_7_ = f32[56,128]{1,0:T(8,128)S(1)} collective-permute-done((f32[56,128]{1,0:T(8,128)S(1)}, f32[56,128]{1,0:T(8,128)S(1)}, u32[]{:S(2)}, u32[]{:S(2)}) %collective-permute-start.10) | collective-permute-done | bytes 28704 | tf_op jit(solution)/shard_map/ppermute | solution.py:561
  35.0 0.6 collective-permute-done.11.refs_8_
  35.6 2.8 %collective-permute-start.12 = (f32[56,128]{1,0:T(8,128)S(1)}, f32[56,128]{1,0:T(8,128)S(1)}, u32[]{:S(2)}, u32[]{:S(2)}) collective-permute-start(f32[56,128]{1,0:T(8,128)S(1)} %collective-permute-done.9.refs_6_), channel_id=1, source_target_pairs={{0,1},{1,0},{2,3},{3,2},{4,5},{5,4},{6,7},{7,6},{8,9},{9,8},{10,11... | collective-permute-start | bytes 86024 | tf_op jit(solution)/shard_map/ppermute | solution.py:565
  38.3 0.9 %collective-permute-done.12.refs_9_ = f32[56,128]{1,0:T(8,128)S(1)} collective-permute-done((f32[56,128]{1,0:T(8,128)S(1)}, f32[56,128]{1,0:T(8,128)S(1)}, u32[]{:S(2)}, u32[]{:S(2)}) %collective-permute-start.12) | collective-permute-done | bytes 28704 | tf_op jit(solution)/shard_map/ppermute | solution.py:565
  39.5 4.8 %shard_map.99 = (f32[48,256]{1,0:T(8,128)S(1)}, f32[48,256]{1,0:T(8,128)S(1)}, f32[104,128]{1,0:T(8,128)S(1)}, f32[288,128]{1,0:T(8,128)S(1)}, f32[192,128]{1,0:T(8,128)S(1)}, /*index=5*/f32[192,128]{1,0:T(8,128)S(1)}) custom-call(f32[8,768]{1,0:T(8,128)S(1)} %get-tuple-element.50.meta_ref, bf16[384,768]{1,0:T(8,128)(2,1)S(1)} %get-tuple-element.51.onehot_ref, ...), custom_call_target="tpu_custom_call" | custom-call | tf_op jit(solution)/shard_map/pallas_call | solution.py:534
  44.5 1.7 %collective-permute-start.15 = (f32[104,128]{1,0:T(8,128)S(1)}, f32[104,128]{1,0:T(8,128)S(1)}, u32[]{:S(2)}, u32[]{:S(2)}) collective-permute-start(f32[104,128]{1,0:T(8,128)S(1)} %get-tuple-element.82.mine_ref.refs_0_), channel_id=1, source_target_pairs={{0,29},{1,4},{2,31},{3,6},{4,1},{5,8},{6,3},{7,10},{8,5},{9,12},{1... | collective-permute-start | bytes 159752 | tf_op jit(solution)/shard_map/ppermute | solution.py:555
  46.2 0.4 shard_map.100
  46.7 0.9 %collective-permute-start.16 = (f32[56,128]{1,0:T(8,128)S(1)}, f32[56,128]{1,0:T(8,128)S(1)}, u32[]{:S(2)}, u32[]{:S(2)}) collective-permute-start(f32[56,128]{1,0:T(8,128)S(1)} %get-tuple-element.83), channel_id=1, source_target_pairs={{0,3},{2,5},{4,7},{6,9},{8,11},{10,13},{12,15},{14,17},{16,19},{18... | collective-permute-start | bytes 86024 | tf_op jit(solution)/shard_map/ppermute | solution.py:561
  47.6 2.0 %collective-permute-start.17 = (f32[56,128]{1,0:T(8,128)S(1)}, f32[56,128]{1,0:T(8,128)S(1)}, u32[]{:S(2)}, u32[]{:S(2)}) collective-permute-start(f32[56,128]{1,0:T(8,128)S(1)} %get-tuple-element.84), channel_id=1, source_target_pairs={{0,15},{2,17},{4,19},{6,21},{8,23},{10,25},{12,27},{14,29},{16,31}... | collective-permute-start | bytes 86024 | tf_op jit(solution)/shard_map/ppermute | solution.py:561
  49.5 1.7 %collective-permute-start.18 = (f32[56,128]{1,0:T(8,128)S(1)}, f32[56,128]{1,0:T(8,128)S(1)}, u32[]{:S(2)}, u32[]{:S(2)}) collective-permute-start(f32[56,128]{1,0:T(8,128)S(1)} %get-tuple-element.85), channel_id=1, source_target_pairs={{0,16},{1,17},{2,18},{3,19},{4,20},{5,21},{6,22},{7,23},{8,24},{9,... | collective-permute-start | bytes 86024 | tf_op jit(solution)/shard_map/ppermute | solution.py:561
  51.3 1.4 %collective-permute-done.17.refs_4_ = f32[56,128]{1,0:T(8,128)S(1)} collective-permute-done((f32[56,128]{1,0:T(8,128)S(1)}, f32[56,128]{1,0:T(8,128)S(1)}, u32[]{:S(2)}, u32[]{:S(2)}) %collective-permute-start.17) | collective-permute-done | bytes 28704 | tf_op jit(solution)/shard_map/ppermute | solution.py:561
  52.7 1.6 %collective-permute-done.18.refs_5_ = f32[56,128]{1,0:T(8,128)S(1)} collective-permute-done((f32[56,128]{1,0:T(8,128)S(1)}, f32[56,128]{1,0:T(8,128)S(1)}, u32[]{:S(2)}, u32[]{:S(2)}) %collective-permute-start.18) | collective-permute-done | bytes 28704 | tf_op jit(solution)/shard_map/ppermute | solution.py:561
  54.3 0.5 collective-permute-start.20
  54.8 0.7 collective-permute-done.19.refs_6_
  55.7 3.9 %shard_map.101 = (f32[48,256]{1,0:T(8,128)S(1)}, f32[192,128]{1,0:T(8,128)S(1)}, f32[32,1,128]{2,1,0:T(1,128)S(1)}) custom-call(f32[8,768]{1,0:T(8,128)S(1)} %get-tuple-element.50.meta_ref, bf16[384,768]{1,0:T(8,128)(2,1)S(1)} %get-tuple-element.51.onehot_ref, f32[192,48]{1,0:T(8,128)S(1)} %copy-done, f32[4096,128]{1,0:T(8,128)S(1)} %get-tuple-element.52.inverse_ref, ...), custom_call_target="tpu_custom_call" | custom-call | tf_op jit(solution)/shard_map/pallas_call | solution.py:534
  59.6 10.8 %all_to_all.5.moment_ref = f32[32,1,128]{2,1,0:T(1,128)S(1)} all-to-all(f32[32,1,128]{2,1,0:T(1,128)S(1)} %get-tuple-element.90), channel_id=1, replica_groups=mesh['dom'=16,'blk'=2] {'dom','blk'}, dimensions={0} | all-to-all | bytes 32768 | tf_op jit(solution)/shard_map/all_to_all | solution.py:645
  70.4 1.8 %shard_map.102 = (f32[48,256]{1,0:T(8,128)}, f32[192,128]{1,0:T(8,128)}) custom-call(f32[32,1,128]{2,1,0:T(1,128)S(1)} %all_to_all.5.moment_ref, f32[48,256]{1,0:T(8,128)S(1)} %get-tuple-element.64.k0_ref, f32[48,256]{1,0:T(8,128)S(1)} %get-tuple-element.76.k1_ref, f32[48,256]{1,0:T(8,128)S(1)} %get-tuple-element.91.k2_ref, ...), custom_call_target="tpu_custom_call" | custom-call | tf_op jit(solution)/shard_map/pallas_call | solution.py:534
  (23 shorter events, 2.2 us)
Async XLA Ops:
  0.6 19.9 %copy-start = (f32[192,48]{1,0:T(8,128)S(1)}, f32[192,48]{1,0:T(8,128)}, u32[]{:S(2)}) copy-start(f32[192,48]{1,0:T(8,128)} %constant.5.clone.forth_ref) | copy-start | bytes 110596
  0.6 19.9 %copy-start.1 = (f32[192,48]{1,0:T(8,128)S(1)}, f32[192,48]{1,0:T(8,128)}, u32[]{:S(2)}) copy-start(f32[192,48]{1,0:T(8,128)} %constant.4.clone.back_hbm.back_ref) | copy-start | bytes 110596
  4.8 1.4 %collective-permute-start = (f32[56,384]{1,0:T(8,128)S(1)}, f32[56,384]{1,0:T(8,128)S(1)}, u32[]{:S(2)}, u32[]{:S(2)}) collective-permute-start(f32[56,384]{1,0:T(8,128)S(1)} %get-tuple-element.55.mine_ref.refs_0_), channel_id=1, source_target_pairs={{0,1},{1,0},{2,3},{3,2},{4,5},{5,4},{6,7},{7,6},{8,9},{9,8},{10,11... | collective-permute-start | bytes 258056 | tf_op jit(solution)/shard_map/ppermute | solution.py:556
  6.5 12.5 %collective-permute-start.2 = (f32[56,640]{1,0:T(8,128)S(1)}, f32[56,640]{1,0:T(8,128)S(1)}, u32[]{:S(2)}, u32[]{:S(2)}) collective-permute-start(f32[56,640]{1,0:T(8,128)S(1)} %get-tuple-element.57), channel_id=1, source_target_pairs={{0,3},{2,5},{4,7},{6,9},{8,11},{10,13},{12,15},{14,17},{16,19},{18... | collective-permute-start | bytes 430088 | tf_op jit(solution)/shard_map/ppermute | solution.py:561
  9.2 9.9 %collective-permute-start.4 = (f32[56,384]{1,0:T(8,128)S(1)}, f32[56,384]{1,0:T(8,128)S(1)}, u32[]{:S(2)}, u32[]{:S(2)}) collective-permute-start(f32[56,384]{1,0:T(8,128)S(1)} %get-tuple-element.59), channel_id=1, source_target_pairs={{0,16},{1,17},{2,18},{3,19},{4,20},{5,21},{6,22},{7,23},{8,24},{9,... | collective-permute-start | bytes 258056 | tf_op jit(solution)/shard_map/ppermute | solution.py:561
  11.8 6.2 %collective-permute-start.1 = (f32[56,128]{1,0:T(8,128)S(1)}, f32[56,128]{1,0:T(8,128)S(1)}, u32[]{:S(2)}, u32[]{:S(2)}) collective-permute-start(f32[56,128]{1,0:T(8,128)S(1)} %get-tuple-element.56), channel_id=1, source_target_pairs={{0,29},{1,4},{2,31},{3,6},{4,1},{5,8},{6,3},{7,10},{8,5},{9,12},{1... | collective-permute-start | bytes 86024 | tf_op jit(solution)/shard_map/ppermute | solution.py:555
  13.7 5.4 %collective-permute-start.3 = (f32[56,128]{1,0:T(8,128)S(1)}, f32[56,128]{1,0:T(8,128)S(1)}, u32[]{:S(2)}, u32[]{:S(2)}) collective-permute-start(f32[56,128]{1,0:T(8,128)S(1)} %get-tuple-element.58), channel_id=1, source_target_pairs={{0,15},{2,17},{4,19},{6,21},{8,23},{10,25},{12,27},{14,29},{16,31}... | collective-permute-start | bytes 86024 | tf_op jit(solution)/shard_map/ppermute | solution.py:561
  19.1 1.5 %collective-permute-start.5 = (f32[56,640]{1,0:T(8,128)S(1)}, f32[56,640]{1,0:T(8,128)S(1)}, u32[]{:S(2)}, u32[]{:S(2)}) collective-permute-start(f32[56,640]{1,0:T(8,128)S(1)} %collective-permute-done.2.refs_3_), channel_id=1, source_target_pairs={{0,1},{1,0},{2,3},{3,2},{4,5},{5,4},{6,7},{7,6},{8,9},{9,8},{10,11... | collective-permute-start | bytes 430088 | tf_op jit(solution)/shard_map/ppermute | solution.py:565
  19.3 1.2 %collective-permute-start.6 = (f32[56,128]{1,0:T(8,128)S(1)}, f32[56,128]{1,0:T(8,128)S(1)}, u32[]{:S(2)}, u32[]{:S(2)}) collective-permute-start(f32[56,128]{1,0:T(8,128)S(1)} %collective-permute-done.3.refs_4_), channel_id=1, source_target_pairs={{0,1},{1,0},{2,3},{3,2},{4,5},{5,4},{6,7},{7,6},{8,9},{9,8},{10,11... | collective-permute-start | bytes 86024 | tf_op jit(solution)/shard_map/ppermute | solution.py:565
  25.4 3.7 %collective-permute-start.7 = (f32[104,128]{1,0:T(8,128)S(1)}, f32[104,128]{1,0:T(8,128)S(1)}, u32[]{:S(2)}, u32[]{:S(2)}) collective-permute-start(f32[104,128]{1,0:T(8,128)S(1)} %get-tuple-element.68.mine_ref.refs_3_), channel_id=1, source_target_pairs={{0,1},{1,0},{2,3},{3,2},{4,5},{5,4},{6,7},{7,6},{8,9},{9,8},{10,11... | collective-permute-start | bytes 159752 | tf_op jit(solution)/shard_map/ppermute | solution.py:556
  25.7 7.4 %collective-permute-start.8 = (f32[104,128]{1,0:T(8,128)S(1)}, f32[104,128]{1,0:T(8,128)S(1)}, u32[]{:S(2)}, u32[]{:S(2)}) collective-permute-start(f32[104,128]{1,0:T(8,128)S(1)} %get-tuple-element.68.mine_ref.refs_3_), channel_id=1, source_target_pairs={{0,29},{1,4},{2,31},{3,6},{4,1},{5,8},{6,3},{7,10},{8,5},{9,12},{1... | collective-permute-start | bytes 159752 | tf_op jit(solution)/shard_map/ppermute | solution.py:555
  29.5 3.6 %collective-permute-start.9 = (f32[56,128]{1,0:T(8,128)S(1)}, f32[56,128]{1,0:T(8,128)S(1)}, u32[]{:S(2)}, u32[]{:S(2)}) collective-permute-start(f32[56,128]{1,0:T(8,128)S(1)} %get-tuple-element.69), channel_id=1, source_target_pairs={{0,3},{2,5},{4,7},{6,9},{8,11},{10,13},{12,15},{14,17},{16,19},{18... | collective-permute-start | bytes 86024 | tf_op jit(solution)/shard_map/ppermute | solution.py:561
  29.9 5.1 %collective-permute-start.10 = (f32[56,128]{1,0:T(8,128)S(1)}, f32[56,128]{1,0:T(8,128)S(1)}, u32[]{:S(2)}, u32[]{:S(2)}) collective-permute-start(f32[56,128]{1,0:T(8,128)S(1)} %get-tuple-element.70), channel_id=1, source_target_pairs={{0,15},{2,17},{4,19},{6,21},{8,23},{10,25},{12,27},{14,29},{16,31}... | collective-permute-start | bytes 86024 | tf_op jit(solution)/shard_map/ppermute | solution.py:561
  30.8 4.8 %collective-permute-start.11 = (f32[56,128]{1,0:T(8,128)S(1)}, f32[56,128]{1,0:T(8,128)S(1)}, u32[]{:S(2)}, u32[]{:S(2)}) collective-permute-start(f32[56,128]{1,0:T(8,128)S(1)} %get-tuple-element.71), channel_id=1, source_target_pairs={{0,16},{1,17},{2,18},{3,19},{4,20},{5,21},{6,22},{7,23},{8,24},{9,... | collective-permute-start | bytes 86024 | tf_op jit(solution)/shard_map/ppermute | solution.py:561
  35.6 3.6 %collective-permute-start.12 = (f32[56,128]{1,0:T(8,128)S(1)}, f32[56,128]{1,0:T(8,128)S(1)}, u32[]{:S(2)}, u32[]{:S(2)}) collective-permute-start(f32[56,128]{1,0:T(8,128)S(1)} %collective-permute-done.9.refs_6_), channel_id=1, source_target_pairs={{0,1},{1,0},{2,3},{3,2},{4,5},{5,4},{6,7},{7,6},{8,9},{9,8},{10,11... | collective-permute-start | bytes 86024 | tf_op jit(solution)/shard_map/ppermute | solution.py:565
  38.3 1.2 %collective-permute-start.13 = (f32[56,128]{1,0:T(8,128)S(1)}, f32[56,128]{1,0:T(8,128)S(1)}, u32[]{:S(2)}, u32[]{:S(2)}) collective-permute-start(f32[56,128]{1,0:T(8,128)S(1)} %collective-permute-done.10.refs_7_), channel_id=1, source_target_pairs={{0,1},{1,0},{2,3},{3,2},{4,5},{5,4},{6,7},{7,6},{8,9},{9,8},{10,11... | collective-permute-start | bytes 86024 | tf_op jit(solution)/shard_map/ppermute | solution.py:565
  44.3 1.9 %collective-permute-start.14 = (f32[104,128]{1,0:T(8,128)S(1)}, f32[104,128]{1,0:T(8,128)S(1)}, u32[]{:S(2)}, u32[]{:S(2)}) collective-permute-start(f32[104,128]{1,0:T(8,128)S(1)} %get-tuple-element.82.mine_ref.refs_0_), channel_id=1, source_target_pairs={{0,1},{1,0},{2,3},{3,2},{4,5},{5,4},{6,7},{7,6},{8,9},{9,8},{10,11... | collective-permute-start | bytes 159752 | tf_op jit(solution)/shard_map/ppermute | solution.py:556
  44.5 6.7 %collective-permute-start.15 = (f32[104,128]{1,0:T(8,128)S(1)}, f32[104,128]{1,0:T(8,128)S(1)}, u32[]{:S(2)}, u32[]{:S(2)}) collective-permute-start(f32[104,128]{1,0:T(8,128)S(1)} %get-tuple-element.82.mine_ref.refs_0_), channel_id=1, source_target_pairs={{0,29},{1,4},{2,31},{3,6},{4,1},{5,8},{6,3},{7,10},{8,5},{9,12},{1... | collective-permute-start | bytes 159752 | tf_op jit(solution)/shard_map/ppermute | solution.py:555
  46.7 4.6 %collective-permute-start.16 = (f32[56,128]{1,0:T(8,128)S(1)}, f32[56,128]{1,0:T(8,128)S(1)}, u32[]{:S(2)}, u32[]{:S(2)}) collective-permute-start(f32[56,128]{1,0:T(8,128)S(1)} %get-tuple-element.83), channel_id=1, source_target_pairs={{0,3},{2,5},{4,7},{6,9},{8,11},{10,13},{12,15},{14,17},{16,19},{18... | collective-permute-start | bytes 86024 | tf_op jit(solution)/shard_map/ppermute | solution.py:561
  47.6 5.1 %collective-permute-start.17 = (f32[56,128]{1,0:T(8,128)S(1)}, f32[56,128]{1,0:T(8,128)S(1)}, u32[]{:S(2)}, u32[]{:S(2)}) collective-permute-start(f32[56,128]{1,0:T(8,128)S(1)} %get-tuple-element.84), channel_id=1, source_target_pairs={{0,15},{2,17},{4,19},{6,21},{8,23},{10,25},{12,27},{14,29},{16,31}... | collective-permute-start | bytes 86024 | tf_op jit(solution)/shard_map/ppermute | solution.py:561
  49.5 4.8 %collective-permute-start.18 = (f32[56,128]{1,0:T(8,128)S(1)}, f32[56,128]{1,0:T(8,128)S(1)}, u32[]{:S(2)}, u32[]{:S(2)}) collective-permute-start(f32[56,128]{1,0:T(8,128)S(1)} %get-tuple-element.85), channel_id=1, source_target_pairs={{0,16},{1,17},{2,18},{3,19},{4,20},{5,21},{6,22},{7,23},{8,24},{9,... | collective-permute-start | bytes 86024 | tf_op jit(solution)/shard_map/ppermute | solution.py:561
  54.3 1.2 %collective-permute-start.19 = (f32[56,128]{1,0:T(8,128)S(1)}, f32[56,128]{1,0:T(8,128)S(1)}, u32[]{:S(2)}, u32[]{:S(2)}) collective-permute-start(f32[56,128]{1,0:T(8,128)S(1)} %collective-permute-done.16.refs_3_), channel_id=1, source_target_pairs={{0,1},{1,0},{2,3},{3,2},{4,5},{5,4},{6,7},{7,6},{8,9},{9,8},{10,11... | collective-permute-start | bytes 86024 | tf_op jit(solution)/shard_map/ppermute | solution.py:565
  54.3 1.4 %collective-permute-start.20 = (f32[56,128]{1,0:T(8,128)S(1)}, f32[56,128]{1,0:T(8,128)S(1)}, u32[]{:S(2)}, u32[]{:S(2)}) collective-permute-start(f32[56,128]{1,0:T(8,128)S(1)} %collective-permute-done.17.refs_4_), channel_id=1, source_target_pairs={{0,1},{1,0},{2,3},{3,2},{4,5},{5,4},{6,7},{7,6},{8,9},{9,8},{10,11... | collective-permute-start | bytes 86024 | tf_op jit(solution)/shard_map/ppermute | solution.py:565

commit v7 on v6

--- a/solution.py
+++ b/solution.py
@@ -170,15 +170,15 @@
 
 def start_kernel(
     ranks, inner, trace, owned, cap,
-    mortar_hbm, kind_hbm, force_hbm, back_hbm, inverse_hbm, couple_hbm, self_hbm,
-    offer_ref, out_ref, onehot_ref, meta_ref, load_ref, inverse_ref, couple_ref, self_ref,
+    mortar_hbm, kind_hbm, force_hbm, back_hbm, inverse_hbm, couple_hbm,
+    offer_ref, out_ref, onehot_ref, meta_ref, load_ref, inverse_ref, couple_ref,
     mortar_ref, kind_ref, force_ref, back_ref, *sems,
 ):
     copies = [
         pltpu.make_async_copy(source, target, sem)
         for source, target, sem in zip(
-            (mortar_hbm, kind_hbm, force_hbm, back_hbm, inverse_hbm, couple_hbm, self_hbm),
-            (mortar_ref, kind_ref, force_ref, back_ref, inverse_ref, couple_ref, self_ref),
+            (mortar_hbm, kind_hbm, force_hbm, back_hbm, inverse_hbm, couple_hbm),
+            (mortar_ref, kind_ref, force_ref, back_ref, inverse_ref, couple_ref),
             sems,
         )
     ]
@@ -240,7 +240,6 @@
     offer_ref[:, :count] = sums[:, owned:]
     offer_ref[: COMP * NODES, count:] = sums[: COMP * NODES, :owned]
     offer_ref[COMP * NODES :, count:] = ids.astype(F32)
-    copies[6].wait()
 
 
 def onehot_of(condition):
@@ -345,38 +344,33 @@
     four_ref[...] = laid((oe, 3), (oo, 3), None, (jnp.where(odd, go, ge), 3))
 
 
-def matched(owned, meta_ref, gid, sources, remote_sources=()):
-    values = jnp.concatenate([v for v, _ in sources], axis=1)
-    ids = jnp.concatenate([i for _, i in sources], axis=1)
+def first_match(owned, meta_ref, gid, ids):
     number = ids.shape[1]
     own = lax.broadcasted_iota(jnp.int32, (owned, number), 0).astype(F32) + (
         meta_ref[4:5, 0:1] + 1.0
     )
-    gid = jnp.where(gid > 0.0, gid, -1.0)
-    match = onehot_of(jnp.concatenate([own, ids_down(gid, number)], axis=0) == ids)
-    sums = exact_dot(values, match, 1)
-    field, remote = sums[:, :owned], sums[:, owned:]
-    if remote_sources:
-        values = jnp.concatenate([v for v, _ in remote_sources], axis=1)
-        ids = jnp.concatenate([i for _, i in remote_sources], axis=1)
-        remote = remote + exact_dot(values, onehot_of(ids_down(gid, ids.shape[1]) == ids), 1)
-    return field, remote
-
-
-def first_values(owned, cap, meta_ref, offers, blocks):
+    return onehot_of(jnp.concatenate([own, ids_down(gid, number)], axis=0) == ids)
+
+
+def first_values(owned, cap, meta_ref, offers, blocks, match_ref):
     rows = COMP * NODES
     count = RUNS * cap
     lane = lax.broadcasted_iota(jnp.int32, (1, count), 1)
     odd = meta_ref[3:4, :count] == 1.0
     mine_ref, other_ref, _ = offers
     one_ref, _, far_ref, passed_ref, _ = blocks
-    sources = [(r[:rows, :count], r[rows : rows + 1, :count]) for r in (*offers, *blocks)]
-    owners = [
-        (r[:rows, count:], r[rows : rows + 1, count:])
-        for r in (other_ref, one_ref, far_ref, passed_ref)
-    ]
+    refs = (*offers, *blocks)
+    owners = (other_ref, one_ref, far_ref, passed_ref)
     gid = mine_ref[rows : rows + 1, :count]
-    field, remote = matched(owned, meta_ref, gid, sources, owners)
+    wish = jnp.where(gid > 0.0, gid, -1.0)
+    ids = jnp.concatenate([r[rows : rows + 1, :count] for r in refs], axis=1)
+    match_ref[...] = first_match(owned, meta_ref, wish, ids)
+    source = jnp.concatenate([r[:rows, :count] for r in refs], axis=1)
+    sums = exact_dot(source, match_ref[...], 1)
+    ids = jnp.concatenate([r[rows : rows + 1, count:] for r in owners], axis=1)
+    source = jnp.concatenate([r[:rows, count:] for r in owners], axis=1)
+    field = sums[:, :owned]
+    remote = sums[:, owned:] + exact_dot(source, onehot_of(ids_down(wish, ids.shape[1]) == ids), 1)
     label_rows = slice(rows, rows + 8)
     other = other_ref[label_rows, :count]
     one = one_ref[label_rows, :count]
@@ -400,14 +394,14 @@
     return mine_ref[:rows, count:] + field, remote, gid, label
 
 
-def fused_values(owned, cap, meta_ref, own_ref, offers, blocks):
+def fused_values(owned, cap, meta_ref, own_ref, match_ref, offers, blocks):
     rows = COMP * NODES
     count = RUNS * cap
     lane = lax.broadcasted_iota(jnp.int32, (1, count), 1)
     odd = meta_ref[3:4, :count] == 1.0
-    sources = [(r[:rows], r[2 * rows : 2 * rows + 1]) for r in offers]
-    sources += [(r[:rows], r[rows : rows + 1]) for r in blocks]
-    field, remote = matched(owned, meta_ref, offers[0][2 * rows : 2 * rows + 1], sources)
+    source = jnp.concatenate([r[:rows] for r in (*offers, *blocks)], axis=1)
+    sums = exact_dot(source, match_ref[...], 1)
+    field, remote = sums[:, :owned], sums[:, owned:]
     near, _, far, across, _ = (r[:rows] for r in blocks)
     partner = offers[1][rows : 2 * rows]
     even_form = jnp.where(lane < 2 * cap, across, jnp.where(lane < 3 * cap, partner, far))
@@ -434,19 +428,24 @@
 
 def apply_kernel(
     inner, trace, owned, cap, fused,
-    meta_ref, onehot_ref, forth_ref, back_ref, inverse_ref, couple_ref, self_ref,
+    meta_ref, onehot_ref, forth_ref, back_ref, inverse_ref, couple_ref,
     *refs,
 ):
+    copy = None
     if fused:
-        gid_ref, label_ref, before_ref, *received = refs[:11]
-        field_ref, *refs = refs[11:]
+        self_ref, gid_ref, label_ref, match_ref, before_ref, *received = refs[:13]
+        field_ref, *refs = refs[13:]
         gid, label = gid_ref[0:1, :], label_ref[0:1, :]
         field, received = fused_values(
-            owned, cap, meta_ref, before_ref, received[:3], received[3:]
+            owned, cap, meta_ref, before_ref, match_ref, received[:3], received[3:]
         )
     else:
-        field_ref, gid_ref, label_ref, *after = refs[8:]
-        field, received, gid, label = first_values(owned, cap, meta_ref, refs[:3], refs[3:8])
+        self_hbm, field_ref, self_ref, gid_ref, label_ref, match_ref, *after, sem = refs[8:]
+        copy = pltpu.make_async_copy(self_hbm, self_ref, sem)
+        copy.start()
+        field, received, gid, label = first_values(
+            owned, cap, meta_ref, refs[:3], refs[3:8], match_ref
+        )
         refs = after
         gid_ref[...] = jnp.broadcast_to(gid, gid_ref.shape)
         label_ref[...] = label
@@ -457,6 +456,8 @@
     kind = element_values(field, received, meta_ref, onehot_ref, forth_ref, spread_ref)
     rows_times(couple_ref, spread_ref, mid_ref, inner, trace)
     rows_times(inverse_ref, mid_ref, weight_ref, inner, inner)
+    if copy is not None:
+        copy.wait()
     rows_times(self_ref, spread_ref, image_ref, trace, trace)
     y = columns_times(tiles_of(image_ref, trace), couple_ref, weight_ref, trace, inner)
     z = by_kind(face_columns(y), back_ref, kind)
@@ -471,13 +472,13 @@
 def last_kernel(
     inner, trace, owned, cap,
     meta_ref, onehot_ref, forth_ref, inverse_ref, couple_ref, self_ref,
-    k0_ref, k1_ref, s0_ref, s1_ref, u0_ref, u1_ref, before_ref, *refs,
+    match_ref, k0_ref, k1_ref, s0_ref, s1_ref, u0_ref, u1_ref, before_ref, *refs,
 ):
     received, refs = refs[:8], refs[8:]
     k2_ref, weight_ref, moment_ref, spread_ref, mid_ref, image_ref = refs
     width = spread_ref.shape[1]
     field, received = fused_values(
-        owned, cap, meta_ref, before_ref, received[:3], received[3:]
+        owned, cap, meta_ref, before_ref, match_ref, received[:3], received[3:]
     )
     k2_ref[...] = field
     element_values(field, received, meta_ref, onehot_ref, forth_ref, spread_ref)
@@ -592,23 +593,29 @@
             ((COMP * inner, width), F32),
             (inverse.shape, F32),
             (couple.shape, F32),
-            (self_block.shape, F32),
         ],
-        mortar, kind, force, backward, inverse, couple, self_block,
+        mortar, kind, force, backward, inverse, couple,
         scratch=[
             (mortar.shape, jnp.int32), (kind.shape, jnp.int32), (force.shape, F32), (backward.shape, F32)
         ],
-        in_hbm=7, vmem=16,
+        in_hbm=6, vmem=16,
     )
     blocks = fused_exchange(
         meta, offer, out, ranks,
         functools.partial(first_pack_kernel, owned, cap),
         (count + 2 * owned, count, count + owned),
     )
-    fields, spreads, mids, weights, ids, own = [], [], [], [], [], None
+    fields, spreads, mids, weights, kept, own = [], [], [], [], [], None
     for iteration in range(2):
         fused = iteration > 0
-        first = [((rows, owned), F32)] + ([] if fused else [((8, count), F32)] * 2)
+        first = [((rows, owned), F32)]
+        if not fused:
+            first += [
+                (self_block.shape, F32),
+                ((8, count), F32),
+                ((8, count), F32),
+                ((owned + count, 8 * count), BF16),
+            ]
         results = call(
             functools.partial(apply_kernel, inner, trace, owned, cap, fused),
             first + [
@@ -618,11 +625,12 @@
                 ((COMP * inner, width), F32),
                 ((COMP * inner, width), F32),
             ],
-            meta, onehot, forward, backward, *matrices, *([*ids, own] if fused else []), *blocks,
-            scratch=[((COMP * trace, width), F32)],
+            meta, onehot, forward, backward, *matrices,
+            *([*kept, own, *blocks] if fused else [*blocks, self_block]),
+            scratch=[((COMP * trace, width), F32)], in_hbm=0 if fused else 1,
         )
         fields.append(results[0])
-        ids = ids or results[1 : len(first)]
+        kept = kept or results[1 : len(first)]
         own, shared, spread, mid, weight = results[len(first) :]
         spreads.append(spread)
         mids.append(mid)
@@ -633,7 +641,7 @@
     field, weight, moments = call(
         functools.partial(last_kernel, inner, trace, owned, cap),
         [((rows, owned), F32), ((COMP * inner, width), F32), ((ranks, 1, width), F32)],
-        meta, onehot, forward, *matrices, *fields, *spreads, *mids, own, *blocks,
+        meta, onehot, forward, *matrices, kept[0], kept[3], *fields, *spreads, *mids, own, *blocks,
         scratch=[
             ((COMP * trace, width), F32),
             ((COMP * inner, width), F32),

time: 72.4 us -> 73 us (level)
  no operation moved by 1% of the time
where the time goes in v7:
time: 73 us; the launch traced here: 72.9 us
  starting transfers between devices  25.8 us (35%)
  Pallas kernels  21.2 us (29%)
  waiting for transfers between devices  14.3 us (20%)
  blocking collectives  10.8 us (15%)
    pallas_call x8, Pallas kernels, call(): pl.pallas_call(kernel, out_shape=[jax.ShapeDtypeStruct(shape, dtype) for...  21.2 us
    ppermute x9, starting transfers between devices, fused_exchange(): lax.ppermute(block, AXES, way)  14 us
    all_to_all x1, blocking collectives, local(): lax.all_to_all(moments, AXES, split_axis=0, concat_axis=0, tiled=True)  10.8 us
    ppermute x3, starting transfers between devices, fused_exchange(): second = lax.ppermute(out, AXES, skip)  7 us
    ppermute x9, waiting for transfers between devices, fused_exchange(): lax.ppermute(block, AXES, way)  6.61 us
    ppermute x6, starting transfers between devices, fused_exchange(): passed = [lax.ppermute(block, AXES, pair) for block in got[:2]]  3.79 us
    ppermute x3, waiting for transfers between devices, fused_exchange(): second = lax.ppermute(out, AXES, skip)  3.71 us
    ppermute x6, waiting for transfers between devices, fused_exchange(): passed = [lax.ppermute(block, AXES, pair) for block in got[:2]]  2.99 us
  transfers between devices with their start and end apart: 21, of which 12 were waited for; matrix products, arithmetic and copies ran while one was open for 0% of the time, Pallas kernels for 1%

profile of v7, /device:TPU:0, one launch (start us, length us, event | category | flops | bytes accessed | tf_op | source)
XLA Modules:
  0.0 72.9 jit_solution(8038339678977690976)
XLA Ops:
  0.7 4.0 %shard_map.95 = (f32[56,384]{1,0:T(8,128)S(1)}, f32[56,128]{1,0:T(8,128)S(1)}, bf16[384,768]{1,0:T(8,128)(2,1)S(1)}, f32[8,768]{1,0:T(8,128)S(1)}, f32[192,128]{...) custom-call(s32[6,128]{1,0:T(8,128)} %bitcast.11, s32[6,128]{1,0:T(8,128)} %bitcast.12, ...), custom_call_target="tpu_custom_call" | custom-call | tf_op jit(solution)/shard_map/pallas_call | solution.py:535
  4.7 0.5 collective-permute-start
  5.2 0.9 %collective-permute-done.other_ref.refs_1_ = f32[56,384]{1,0:T(8,128)S(1)} collective-permute-done((f32[56,384]{1,0:T(8,128)S(1)}, f32[56,384]{1,0:T(8,128)S(1)}, u32[]{:S(2)}, u32[]{:S(2)}) %collective-permute-start) | collective-permute-done | bytes 86048 | tf_op jit(solution)/shard_map/ppermute | solution.py:557
  6.4 2.7 %collective-permute-start.2 = (f32[56,640]{1,0:T(8,128)S(1)}, f32[56,640]{1,0:T(8,128)S(1)}, u32[]{:S(2)}, u32[]{:S(2)}) collective-permute-start(f32[56,640]{1,0:T(8,128)S(1)} %get-tuple-element.57), channel_id=1, source_target_pairs={{0,3},{2,5},{4,7},{6,9},{8,11},{10,13},{12,15},{14,17},{16,19},{18... | collective-permute-start | bytes 430088 | tf_op jit(solution)/shard_map/ppermute | solution.py:562
  9.0 2.6 %collective-permute-start.4 = (f32[56,384]{1,0:T(8,128)S(1)}, f32[56,384]{1,0:T(8,128)S(1)}, u32[]{:S(2)}, u32[]{:S(2)}) collective-permute-start(f32[56,384]{1,0:T(8,128)S(1)} %get-tuple-element.59), channel_id=1, source_target_pairs={{0,16},{1,17},{2,18},{3,19},{4,20},{5,21},{6,22},{7,23},{8,24},{9,... | collective-permute-start | bytes 258056 | tf_op jit(solution)/shard_map/ppermute | solution.py:562
  11.6 1.9 %collective-permute-start.1 = (f32[56,128]{1,0:T(8,128)S(1)}, f32[56,128]{1,0:T(8,128)S(1)}, u32[]{:S(2)}, u32[]{:S(2)}) collective-permute-start(f32[56,128]{1,0:T(8,128)S(1)} %get-tuple-element.56), channel_id=1, source_target_pairs={{0,29},{1,4},{2,31},{3,6},{4,1},{5,8},{6,3},{7,10},{8,5},{9,12},{1... | collective-permute-start | bytes 86024 | tf_op jit(solution)/shard_map/ppermute | solution.py:556
  13.5 0.5 collective-permute-start.3
  14.1 3.7 %collective-permute-done.1.refs_2_ = f32[56,128]{1,0:T(8,128)S(1)} collective-permute-done((f32[56,128]{1,0:T(8,128)S(1)}, f32[56,128]{1,0:T(8,128)S(1)}, u32[]{:S(2)}, u32[]{:S(2)}) %collective-permute-start.1) | collective-permute-done | bytes 28704 | tf_op jit(solution)/shard_map/ppermute | solution.py:556
  17.8 1.1 %collective-permute-done.3.refs_4_ = f32[56,128]{1,0:T(8,128)S(1)} collective-permute-done((f32[56,128]{1,0:T(8,128)S(1)}, f32[56,128]{1,0:T(8,128)S(1)}, u32[]{:S(2)}, u32[]{:S(2)}) %collective-permute-start.3) | collective-permute-done | bytes 28704 | tf_op jit(solution)/shard_map/ppermute | solution.py:562
  19.4 0.9 %collective-permute-done.6.refs_7_ = f32[56,128]{1,0:T(8,128)S(1)} collective-permute-done((f32[56,128]{1,0:T(8,128)S(1)}, f32[56,128]{1,0:T(8,128)S(1)}, u32[]{:S(2)}, u32[]{:S(2)}) %collective-permute-start.6) | collective-permute-done | bytes 28704 | tf_op jit(solution)/shard_map/ppermute | solution.py:566
  20.4 5.7 %shard_map.97 = (f32[48,256]{1,0:T(8,128)S(1)}, f32[9216,128]{1,0:T(8,128)S(1)}, f32[8,128]{1,0:T(8,128)S(1)}, f32[8,128]{1,0:T(8,128)S(1)}, bf16[384,1024]{1,0:...) custom-call(f32[8,768]{1,0:T(8,128)S(1)} %get-tuple-element.51.meta_, ...), custom_call_target="tpu_custom_call" | custom-call | tf_op jit(solution)/shard_map/pallas_call | solution.py:535
  26.4 3.4 %collective-permute-start.8 = (f32[104,128]{1,0:T(8,128)S(1)}, f32[104,128]{1,0:T(8,128)S(1)}, u32[]{:S(2)}, u32[]{:S(2)}) collective-permute-start(f32[104,128]{1,0:T(8,128)S(1)} %get-tuple-element.70.mine_ref.refs_5_), channel_id=1, source_target_pairs={{0,29},{1,4},{2,31},{3,6},{4,1},{5,8},{6,3},{7,10},{8,5},{9,12},{1... | collective-permute-start | bytes 159752 | tf_op jit(solution)/shard_map/ppermute | solution.py:556
  29.8 0.4 shard_map.98
  30.6 0.9 %collective-permute-start.10 = (f32[56,128]{1,0:T(8,128)S(1)}, f32[56,128]{1,0:T(8,128)S(1)}, u32[]{:S(2)}, u32[]{:S(2)}) collective-permute-start(f32[56,128]{1,0:T(8,128)S(1)} %get-tuple-element.72), channel_id=1, source_target_pairs={{0,15},{2,17},{4,19},{6,21},{8,23},{10,25},{12,27},{14,29},{16,31}... | collective-permute-start | bytes 86024 | tf_op jit(solution)/shard_map/ppermute | solution.py:562
  31.5 2.3 %collective-permute-start.11 = (f32[56,128]{1,0:T(8,128)S(1)}, f32[56,128]{1,0:T(8,128)S(1)}, u32[]{:S(2)}, u32[]{:S(2)}) collective-permute-start(f32[56,128]{1,0:T(8,128)S(1)} %get-tuple-element.73), channel_id=1, source_target_pairs={{0,16},{1,17},{2,18},{3,19},{4,20},{5,21},{6,22},{7,23},{8,24},{9,... | collective-permute-start | bytes 86024 | tf_op jit(solution)/shard_map/ppermute | solution.py:562
  33.9 1.9 %collective-permute-done.10.refs_9_ = f32[56,128]{1,0:T(8,128)S(1)} collective-permute-done((f32[56,128]{1,0:T(8,128)S(1)}, f32[56,128]{1,0:T(8,128)S(1)}, u32[]{:S(2)}, u32[]{:S(2)}) %collective-permute-start.10) | collective-permute-done | bytes 28704 | tf_op jit(solution)/shard_map/ppermute | solution.py:562
  35.7 0.6 collective-permute-done.11.refs_10_
  36.3 2.8 %collective-permute-start.12 = (f32[56,128]{1,0:T(8,128)S(1)}, f32[56,128]{1,0:T(8,128)S(1)}, u32[]{:S(2)}, u32[]{:S(2)}) collective-permute-start(f32[56,128]{1,0:T(8,128)S(1)} %collective-permute-done.9.refs_8_), channel_id=1, source_target_pairs={{0,1},{1,0},{2,3},{3,2},{4,5},{5,4},{6,7},{7,6},{8,9},{9,8},{10,11... | collective-permute-start | bytes 86024 | tf_op jit(solution)/shard_map/ppermute | solution.py:566
  39.1 0.9 %collective-permute-done.12.refs_11_ = f32[56,128]{1,0:T(8,128)S(1)} collective-permute-done((f32[56,128]{1,0:T(8,128)S(1)}, f32[56,128]{1,0:T(8,128)S(1)}, u32[]{:S(2)}, u32[]{:S(2)}) %collective-permute-start.12) | collective-permute-done | bytes 28704 | tf_op jit(solution)/shard_map/ppermute | solution.py:566
  40.3 4.7 %shard_map.99 = (f32[48,256]{1,0:T(8,128)S(1)}, f32[48,256]{1,0:T(8,128)S(1)}, f32[104,128]{1,0:T(8,128)S(1)}, f32[288,128]{1,0:T(8,128)S(1)}, f32[192,128]{1,0:T(8,128)S(1)}, /*index=5*/f32[192,128]{1,0:T(8,128)S(1)}) custom-call(f32[8,768]{1,0:T(8,128)S(1)} %get-tuple-element.51.meta_ref, bf16[384,768]{1,0:T(8,128)(2,1)S(1)} %get-tuple-element.52.onehot_ref, ...), custom_call_target="tpu_custom_call" | custom-call | tf_op jit(solution)/shard_map/pallas_call | solution.py:535
  45.2 1.7 %collective-permute-start.15 = (f32[104,128]{1,0:T(8,128)S(1)}, f32[104,128]{1,0:T(8,128)S(1)}, u32[]{:S(2)}, u32[]{:S(2)}) collective-permute-start(f32[104,128]{1,0:T(8,128)S(1)} %get-tuple-element.84.mine_ref.refs_0_), channel_id=1, source_target_pairs={{0,29},{1,4},{2,31},{3,6},{4,1},{5,8},{6,3},{7,10},{8,5},{9,12},{1... | collective-permute-start | bytes 159752 | tf_op jit(solution)/shard_map/ppermute | solution.py:556
  46.9 0.4 shard_map.100
  47.4 0.9 %collective-permute-start.16 = (f32[56,128]{1,0:T(8,128)S(1)}, f32[56,128]{1,0:T(8,128)S(1)}, u32[]{:S(2)}, u32[]{:S(2)}) collective-permute-start(f32[56,128]{1,0:T(8,128)S(1)} %get-tuple-element.85), channel_id=1, source_target_pairs={{0,3},{2,5},{4,7},{6,9},{8,11},{10,13},{12,15},{14,17},{16,19},{18... | collective-permute-start | bytes 86024 | tf_op jit(solution)/shard_map/ppermute | solution.py:562
  48.3 2.0 %collective-permute-start.17 = (f32[56,128]{1,0:T(8,128)S(1)}, f32[56,128]{1,0:T(8,128)S(1)}, u32[]{:S(2)}, u32[]{:S(2)}) collective-permute-start(f32[56,128]{1,0:T(8,128)S(1)} %get-tuple-element.86), channel_id=1, source_target_pairs={{0,15},{2,17},{4,19},{6,21},{8,23},{10,25},{12,27},{14,29},{16,31}... | collective-permute-start | bytes 86024 | tf_op jit(solution)/shard_map/ppermute | solution.py:562
  50.2 1.7 %collective-permute-start.18 = (f32[56,128]{1,0:T(8,128)S(1)}, f32[56,128]{1,0:T(8,128)S(1)}, u32[]{:S(2)}, u32[]{:S(2)}) collective-permute-start(f32[56,128]{1,0:T(8,128)S(1)} %get-tuple-element.87), channel_id=1, source_target_pairs={{0,16},{1,17},{2,18},{3,19},{4,20},{5,21},{6,22},{7,23},{8,24},{9,... | collective-permute-start | bytes 86024 | tf_op jit(solution)/shard_map/ppermute | solution.py:562
  51.9 1.4 %collective-permute-done.17.refs_4_ = f32[56,128]{1,0:T(8,128)S(1)} collective-permute-done((f32[56,128]{1,0:T(8,128)S(1)}, f32[56,128]{1,0:T(8,128)S(1)}, u32[]{:S(2)}, u32[]{:S(2)}) %collective-permute-start.17) | collective-permute-done | bytes 28704 | tf_op jit(solution)/shard_map/ppermute | solution.py:562
  53.4 1.6 %collective-permute-done.18.refs_5_ = f32[56,128]{1,0:T(8,128)S(1)} collective-permute-done((f32[56,128]{1,0:T(8,128)S(1)}, f32[56,128]{1,0:T(8,128)S(1)}, u32[]{:S(2)}, u32[]{:S(2)}) %collective-permute-start.18) | collective-permute-done | bytes 28704 | tf_op jit(solution)/shard_map/ppermute | solution.py:562
  55.0 0.5 collective-permute-start.20
  55.5 0.7 collective-permute-done.19.refs_6_
  56.4 3.8 %shard_map.101 = (f32[48,256]{1,0:T(8,128)S(1)}, f32[192,128]{1,0:T(8,128)S(1)}, f32[32,1,128]{2,1,0:T(1,128)S(1)}) custom-call(f32[8,768]{1,0:T(8,128)S(1)} %get-tuple-element.51.meta_ref, bf16[384,768]{1,0:T(8,128)(2,1)S(1)} %get-tuple-element.52.onehot_ref, f32[192,48]{1,0:T(8,128)S(1)} %copy-done, f32[4096,128]{1,0:T(8,128)S(1)} %get-tuple-element.53.inverse_ref, ...), custom_call_target="tpu_custom_call" | custom-call | tf_op jit(solution)/shard_map/pallas_call | solution.py:535
  60.2 10.8 %all_to_all.5.moment_ref = f32[32,1,128]{2,1,0:T(1,128)S(1)} all-to-all(f32[32,1,128]{2,1,0:T(1,128)S(1)} %get-tuple-element.92), channel_id=1, replica_groups=mesh['dom'=16,'blk'=2] {'dom','blk'}, dimensions={0} | all-to-all | bytes 32768 | tf_op jit(solution)/shard_map/all_to_all | solution.py:653
  71.0 1.8 %shard_map.102 = (f32[48,256]{1,0:T(8,128)}, f32[192,128]{1,0:T(8,128)}) custom-call(f32[32,1,128]{2,1,0:T(1,128)S(1)} %all_to_all.5.moment_ref, f32[48,256]{1,0:T(8,128)S(1)} %get-tuple-element.66.k0_ref, f32[48,256]{1,0:T(8,128)S(1)} %get-tuple-element.78.k1_ref, f32[48,256]{1,0:T(8,128)S(1)} %get-tuple-element.93.k2_ref, ...), custom_call_target="tpu_custom_call" | custom-call | tf_op jit(solution)/shard_map/pallas_call | solution.py:535
  (23 shorter events, 2.2 us)
Async XLA Ops:
  0.6 19.7 %copy-start.1 = (f32[192,48]{1,0:T(8,128)S(1)}, f32[192,48]{1,0:T(8,128)}, u32[]{:S(2)}) copy-start(f32[192,48]{1,0:T(8,128)} %constant.4.clone.back_hbm.back_ref) | copy-start | bytes 110596
  0.6 19.7 %copy-start = (f32[192,48]{1,0:T(8,128)S(1)}, f32[192,48]{1,0:T(8,128)}, u32[]{:S(2)}) copy-start(f32[192,48]{1,0:T(8,128)} %constant.5.clone.forth_ref) | copy-start | bytes 110596
  4.7 1.4 %collective-permute-start = (f32[56,384]{1,0:T(8,128)S(1)}, f32[56,384]{1,0:T(8,128)S(1)}, u32[]{:S(2)}, u32[]{:S(2)}) collective-permute-start(f32[56,384]{1,0:T(8,128)S(1)} %get-tuple-element.55.mine_ref.refs_0_), channel_id=1, source_target_pairs={{0,1},{1,0},{2,3},{3,2},{4,5},{5,4},{6,7},{7,6},{8,9},{9,8},{10,11... | collective-permute-start | bytes 258056 | tf_op jit(solution)/shard_map/ppermute | solution.py:557
  6.4 12.5 %collective-permute-start.2 = (f32[56,640]{1,0:T(8,128)S(1)}, f32[56,640]{1,0:T(8,128)S(1)}, u32[]{:S(2)}, u32[]{:S(2)}) collective-permute-start(f32[56,640]{1,0:T(8,128)S(1)} %get-tuple-element.57), channel_id=1, source_target_pairs={{0,3},{2,5},{4,7},{6,9},{8,11},{10,13},{12,15},{14,17},{16,19},{18... | collective-permute-start | bytes 430088 | tf_op jit(solution)/shard_map/ppermute | solution.py:562
  9.0 9.9 %collective-permute-start.4 = (f32[56,384]{1,0:T(8,128)S(1)}, f32[56,384]{1,0:T(8,128)S(1)}, u32[]{:S(2)}, u32[]{:S(2)}) collective-permute-start(f32[56,384]{1,0:T(8,128)S(1)} %get-tuple-element.59), channel_id=1, source_target_pairs={{0,16},{1,17},{2,18},{3,19},{4,20},{5,21},{6,22},{7,23},{8,24},{9,... | collective-permute-start | bytes 258056 | tf_op jit(solution)/shard_map/ppermute | solution.py:562
  11.6 6.2 %collective-permute-start.1 = (f32[56,128]{1,0:T(8,128)S(1)}, f32[56,128]{1,0:T(8,128)S(1)}, u32[]{:S(2)}, u32[]{:S(2)}) collective-permute-start(f32[56,128]{1,0:T(8,128)S(1)} %get-tuple-element.56), channel_id=1, source_target_pairs={{0,29},{1,4},{2,31},{3,6},{4,1},{5,8},{6,3},{7,10},{8,5},{9,12},{1... | collective-permute-start | bytes 86024 | tf_op jit(solution)/shard_map/ppermute | solution.py:556
  13.5 5.4 %collective-permute-start.3 = (f32[56,128]{1,0:T(8,128)S(1)}, f32[56,128]{1,0:T(8,128)S(1)}, u32[]{:S(2)}, u32[]{:S(2)}) collective-permute-start(f32[56,128]{1,0:T(8,128)S(1)} %get-tuple-element.58), channel_id=1, source_target_pairs={{0,15},{2,17},{4,19},{6,21},{8,23},{10,25},{12,27},{14,29},{16,31}... | collective-permute-start | bytes 86024 | tf_op jit(solution)/shard_map/ppermute | solution.py:562
  18.9 1.5 %collective-permute-start.5 = (f32[56,640]{1,0:T(8,128)S(1)}, f32[56,640]{1,0:T(8,128)S(1)}, u32[]{:S(2)}, u32[]{:S(2)}) collective-permute-start(f32[56,640]{1,0:T(8,128)S(1)} %collective-permute-done.2.refs_3_), channel_id=1, source_target_pairs={{0,1},{1,0},{2,3},{3,2},{4,5},{5,4},{6,7},{7,6},{8,9},{9,8},{10,11... | collective-permute-start | bytes 430088 | tf_op jit(solution)/shard_map/ppermute | solution.py:566
  19.2 1.2 %collective-permute-start.6 = (f32[56,128]{1,0:T(8,128)S(1)}, f32[56,128]{1,0:T(8,128)S(1)}, u32[]{:S(2)}, u32[]{:S(2)}) collective-permute-start(f32[56,128]{1,0:T(8,128)S(1)} %collective-permute-done.3.refs_4_), channel_id=1, source_target_pairs={{0,1},{1,0},{2,3},{3,2},{4,5},{5,4},{6,7},{7,6},{8,9},{9,8},{10,11... | collective-permute-start | bytes 86024 | tf_op jit(solution)/shard_map/ppermute | solution.py:566
  26.1 3.7 %collective-permute-start.7 = (f32[104,128]{1,0:T(8,128)S(1)}, f32[104,128]{1,0:T(8,128)S(1)}, u32[]{:S(2)}, u32[]{:S(2)}) collective-permute-start(f32[104,128]{1,0:T(8,128)S(1)} %get-tuple-element.70.mine_ref.refs_5_), channel_id=1, source_target_pairs={{0,1},{1,0},{2,3},{3,2},{4,5},{5,4},{6,7},{7,6},{8,9},{9,8},{10,11... | collective-permute-start | bytes 159752 | tf_op jit(solution)/shard_map/ppermute | solution.py:557
  26.4 7.4 %collective-permute-start.8 = (f32[104,128]{1,0:T(8,128)S(1)}, f32[104,128]{1,0:T(8,128)S(1)}, u32[]{:S(2)}, u32[]{:S(2)}) collective-permute-start(f32[104,128]{1,0:T(8,128)S(1)} %get-tuple-element.70.mine_ref.refs_5_), channel_id=1, source_target_pairs={{0,29},{1,4},{2,31},{3,6},{4,1},{5,8},{6,3},{7,10},{8,5},{9,12},{1... | collective-permute-start | bytes 159752 | tf_op jit(solution)/shard_map/ppermute | solution.py:556
  30.3 3.6 %collective-permute-start.9 = (f32[56,128]{1,0:T(8,128)S(1)}, f32[56,128]{1,0:T(8,128)S(1)}, u32[]{:S(2)}, u32[]{:S(2)}) collective-permute-start(f32[56,128]{1,0:T(8,128)S(1)} %get-tuple-element.71), channel_id=1, source_target_pairs={{0,3},{2,5},{4,7},{6,9},{8,11},{10,13},{12,15},{14,17},{16,19},{18... | collective-permute-start | bytes 86024 | tf_op jit(solution)/shard_map/ppermute | solution.py:562
  30.6 5.1 %collective-permute-start.10 = (f32[56,128]{1,0:T(8,128)S(1)}, f32[56,128]{1,0:T(8,128)S(1)}, u32[]{:S(2)}, u32[]{:S(2)}) collective-permute-start(f32[56,128]{1,0:T(8,128)S(1)} %get-tuple-element.72), channel_id=1, source_target_pairs={{0,15},{2,17},{4,19},{6,21},{8,23},{10,25},{12,27},{14,29},{16,31}... | collective-permute-start | bytes 86024 | tf_op jit(solution)/shard_map/ppermute | solution.py:562
  31.5 4.8 %collective-permute-start.11 = (f32[56,128]{1,0:T(8,128)S(1)}, f32[56,128]{1,0:T(8,128)S(1)}, u32[]{:S(2)}, u32[]{:S(2)}) collective-permute-start(f32[56,128]{1,0:T(8,128)S(1)} %get-tuple-element.73), channel_id=1, source_target_pairs={{0,16},{1,17},{2,18},{3,19},{4,20},{5,21},{6,22},{7,23},{8,24},{9,... | collective-permute-start | bytes 86024 | tf_op jit(solution)/shard_map/ppermute | solution.py:562
  36.3 3.6 %collective-permute-start.12 = (f32[56,128]{1,0:T(8,128)S(1)}, f32[56,128]{1,0:T(8,128)S(1)}, u32[]{:S(2)}, u32[]{:S(2)}) collective-permute-start(f32[56,128]{1,0:T(8,128)S(1)} %collective-permute-done.9.refs_8_), channel_id=1, source_target_pairs={{0,1},{1,0},{2,3},{3,2},{4,5},{5,4},{6,7},{7,6},{8,9},{9,8},{10,11... | collective-permute-start | bytes 86024 | tf_op jit(solution)/shard_map/ppermute | solution.py:566
  39.1 1.2 %collective-permute-start.13 = (f32[56,128]{1,0:T(8,128)S(1)}, f32[56,128]{1,0:T(8,128)S(1)}, u32[]{:S(2)}, u32[]{:S(2)}) collective-permute-start(f32[56,128]{1,0:T(8,128)S(1)} %collective-permute-done.10.refs_9_), channel_id=1, source_target_pairs={{0,1},{1,0},{2,3},{3,2},{4,5},{5,4},{6,7},{7,6},{8,9},{9,8},{10,11... | collective-permute-start | bytes 86024 | tf_op jit(solution)/shard_map/ppermute | solution.py:566
  45.0 1.9 %collective-permute-start.14 = (f32[104,128]{1,0:T(8,128)S(1)}, f32[104,128]{1,0:T(8,128)S(1)}, u32[]{:S(2)}, u32[]{:S(2)}) collective-permute-start(f32[104,128]{1,0:T(8,128)S(1)} %get-tuple-element.84.mine_ref.refs_0_), channel_id=1, source_target_pairs={{0,1},{1,0},{2,3},{3,2},{4,5},{5,4},{6,7},{7,6},{8,9},{9,8},{10,11... | collective-permute-start | bytes 159752 | tf_op jit(solution)/shard_map/ppermute | solution.py:557
  45.2 6.7 %collective-permute-start.15 = (f32[104,128]{1,0:T(8,128)S(1)}, f32[104,128]{1,0:T(8,128)S(1)}, u32[]{:S(2)}, u32[]{:S(2)}) collective-permute-start(f32[104,128]{1,0:T(8,128)S(1)} %get-tuple-element.84.mine_ref.refs_0_), channel_id=1, source_target_pairs={{0,29},{1,4},{2,31},{3,6},{4,1},{5,8},{6,3},{7,10},{8,5},{9,12},{1... | collective-permute-start | bytes 159752 | tf_op jit(solution)/shard_map/ppermute | solution.py:556
  47.4 4.6 %collective-permute-start.16 = (f32[56,128]{1,0:T(8,128)S(1)}, f32[56,128]{1,0:T(8,128)S(1)}, u32[]{:S(2)}, u32[]{:S(2)}) collective-permute-start(f32[56,128]{1,0:T(8,128)S(1)} %get-tuple-element.85), channel_id=1, source_target_pairs={{0,3},{2,5},{4,7},{6,9},{8,11},{10,13},{12,15},{14,17},{16,19},{18... | collective-permute-start | bytes 86024 | tf_op jit(solution)/shard_map/ppermute | solution.py:562
  48.3 5.1 %collective-permute-start.17 = (f32[56,128]{1,0:T(8,128)S(1)}, f32[56,128]{1,0:T(8,128)S(1)}, u32[]{:S(2)}, u32[]{:S(2)}) collective-permute-start(f32[56,128]{1,0:T(8,128)S(1)} %get-tuple-element.86), channel_id=1, source_target_pairs={{0,15},{2,17},{4,19},{6,21},{8,23},{10,25},{12,27},{14,29},{16,31}... | collective-permute-start | bytes 86024 | tf_op jit(solution)/shard_map/ppermute | solution.py:562
  50.2 4.8 %collective-permute-start.18 = (f32[56,128]{1,0:T(8,128)S(1)}, f32[56,128]{1,0:T(8,128)S(1)}, u32[]{:S(2)}, u32[]{:S(2)}) collective-permute-start(f32[56,128]{1,0:T(8,128)S(1)} %get-tuple-element.87), channel_id=1, source_target_pairs={{0,16},{1,17},{2,18},{3,19},{4,20},{5,21},{6,22},{7,23},{8,24},{9,... | collective-permute-start | bytes 86024 | tf_op jit(solution)/shard_map/ppermute | solution.py:562
  55.0 1.2 %collective-permute-start.19 = (f32[56,128]{1,0:T(8,128)S(1)}, f32[56,128]{1,0:T(8,128)S(1)}, u32[]{:S(2)}, u32[]{:S(2)}) collective-permute-start(f32[56,128]{1,0:T(8,128)S(1)} %collective-permute-done.16.refs_3_), channel_id=1, source_target_pairs={{0,1},{1,0},{2,3},{3,2},{4,5},{5,4},{6,7},{7,6},{8,9},{9,8},{10,11... | collective-permute-start | bytes 86024 | tf_op jit(solution)/shard_map/ppermute | solution.py:566
  55.0 1.4 %collective-permute-start.20 = (f32[56,128]{1,0:T(8,128)S(1)}, f32[56,128]{1,0:T(8,128)S(1)}, u32[]{:S(2)}, u32[]{:S(2)}) collective-permute-start(f32[56,128]{1,0:T(8,128)S(1)} %collective-permute-done.17.refs_4_), channel_id=1, source_target_pairs={{0,1},{1,0},{2,3},{3,2},{4,5},{5,4},{6,7},{7,6},{8,9},{9,8},{10,11... | collective-permute-start | bytes 86024 | tf_op jit(solution)/shard_map/ppermute | solution.py:566

commit v8 on v5

--- a/solution.py
+++ b/solution.py
@@ -184,10 +184,15 @@
     ]
     for copy in copies:
         copy.start()
+    width = mortar_ref.shape[1]
+    slots = FACES * width
+    target = lax.broadcasted_iota(jnp.int32, (1, slots), 1)
+    target = lax.rem(target, width) * FACES + lax.div(target, width)
+    order = jnp.where(
+        lax.broadcasted_iota(jnp.int32, (slots, slots), 0) == target, 1.0, 0.0
+    ).astype(BF16)
     copies[0].wait()
     copies[1].wait()
-    width = mortar_ref.shape[1]
-    slots = FACES * width
     mortar = mortar_ref[...]
     owner = lax.div(mortar, owned)
     index = lax.rem(mortar, owned)
@@ -205,11 +210,6 @@
             run = number - (number > 2)
             column = jnp.where(inside, owned + run * cap + slot - begin, column)
         begin = begin + count
-    target = lax.broadcasted_iota(jnp.int32, (1, slots), 1)
-    target = lax.rem(target, width) * FACES + lax.div(target, width)
-    order = jnp.where(
-        lax.broadcasted_iota(jnp.int32, (slots, slots), 0) == target, 1.0, 0.0
-    ).astype(BF16)
     facts = jnp.concatenate(
         [in_a_row(column), in_a_row(mortar + 1), in_a_row(kind_ref[...]), jnp.zeros((5, slots), jnp.int32)],
         axis=0,
@@ -561,6 +561,8 @@
         lax.ppermute(block, AXES, way)
         for block, way in zip(packed, (both_ways(1), both_ways(ranks // 4 - 1), far))
     ]
+    if out is not shared:
+        second, *got = lax.optimization_barrier((second, *got))
     passed = [lax.ppermute(block, AXES, pair) for block in got[:2]]
     return [shared, other, second, *got, *passed]
 

time: 76.9 us -> 70.7 us (0.919)
  starting transfers between devices: 31.1 us -> 26.7 us
  waiting for transfers between devices: 15.3 us -> 12.8 us
  blocking collectives: 8.84 us -> 9.72 us
    ppermute x9, waiting for transfers between devices: 7.34 us -> 4.4 us  [fused_exchange(): lax.ppermute(block, AXES, way)]
    ppermute x6, starting transfers between devices: 5.53 us -> 3.58 us  [fused_exchange(): passed = [lax.ppermute(block, AXES, pair) for block in got[:2]]]
    ppermute x3, starting transfers between devices: 9.57 us -> 8.17 us  [fused_exchange(): second = lax.ppermute(out, AXES, skip)]
    ppermute x9, starting transfers between devices: 15.3 us -> 14 us  [fused_exchange(): lax.ppermute(block, AXES, way)]
    ppermute x6, waiting for transfers between devices: 0.02 us -> 0.95 us  [fused_exchange(): passed = [lax.ppermute(block, AXES, pair) for block in got[:2]]]
    all_to_all x1, blocking collectives: 8.84 us -> 9.72 us  [local(): lax.all_to_all(moments, AXES, split_axis=0, concat_axis=0, tiled=True)]
  transfers between devices with their start and end apart: 21 -> 21, of which waited for: 8 -> 10; matrix products, arithmetic and copies ran while one was open for 0% -> 0% of each run, Pallas kernels for 0% -> 0%
where the time goes in v8:
time: 70.7 us; the launch traced here: 70.6 us
  starting transfers between devices  26.7 us (38%)
  Pallas kernels  20.6 us (29%)
  waiting for transfers between devices  12.8 us (18%)
  blocking collectives  9.72 us (14%)
  between operations  0.73 us (1%)
    pallas_call x8, Pallas kernels, call(): pl.pallas_call(kernel, out_shape=[jax.ShapeDtypeStruct(shape, dtype) for...  20.6 us
    ppermute x9, starting transfers between devices, fused_exchange(): lax.ppermute(block, AXES, way)  14 us
    all_to_all x1, blocking collectives, local(): lax.all_to_all(moments, AXES, split_axis=0, concat_axis=0, tiled=True)  9.72 us
    ppermute x3, starting transfers between devices, fused_exchange(): second = lax.ppermute(out, AXES, skip)  8.17 us
    ppermute x9, waiting for transfers between devices, fused_exchange(): lax.ppermute(block, AXES, way)  4.4 us
    ppermute x3, waiting for transfers between devices, fused_exchange(): second = lax.ppermute(out, AXES, skip)  4.32 us
    ppermute x6, starting transfers between devices, fused_exchange(): passed = [lax.ppermute(block, AXES, pair) for block in got[:2]]  3.58 us
    ppermute x3, waiting for transfers between devices, fused_exchange(): other = lax.ppermute(shared, AXES, pair)  3.12 us
  transfers between devices with their start and end apart: 21, of which 10 were waited for; matrix products, arithmetic and copies ran while one was open for 0% of the time, Pallas kernels for 0%

profile of v8, /device:TPU:0, one launch (start us, length us, event | category | flops | bytes accessed | tf_op | source)
XLA Modules:
  0.0 70.6 jit_solution(1616662040057104482)
XLA Ops:
  0.7 4.1 %shard_map.95 = (f32[56,384]{1,0:T(8,128)S(1)}, f32[56,128]{1,0:T(8,128)S(1)}, bf16[384,768]{1,0:T(8,128)(2,1)S(1)}, f32[8,768]{1,0:T(8,128)S(1)}, f32[192,128]{...) custom-call(s32[6,128]{1,0:T(8,128)} %bitcast.11, s32[6,128]{1,0:T(8,128)} %bitcast.12, ...), custom_call_target="tpu_custom_call" | custom-call | tf_op jit(solution)/shard_map/pallas_call | solution.py:534
  4.8 0.5 collective-permute-start
  5.3 0.9 %collective-permute-done.other_ref.refs_1_ = f32[56,384]{1,0:T(8,128)S(1)} collective-permute-done((f32[56,384]{1,0:T(8,128)S(1)}, f32[56,384]{1,0:T(8,128)S(1)}, u32[]{:S(2)}, u32[]{:S(2)}) %collective-permute-start) | collective-permute-done | bytes 86048 | tf_op jit(solution)/shard_map/ppermute | solution.py:556
  6.5 2.7 %collective-permute-start.2 = (f32[56,640]{1,0:T(8,128)S(1)}, f32[56,640]{1,0:T(8,128)S(1)}, u32[]{:S(2)}, u32[]{:S(2)}) collective-permute-start(f32[56,640]{1,0:T(8,128)S(1)} %get-tuple-element.49), channel_id=1, source_target_pairs={{0,3},{2,5},{4,7},{6,9},{8,11},{10,13},{12,15},{14,17},{16,19},{18... | collective-permute-start | bytes 430088 | tf_op jit(solution)/shard_map/ppermute | solution.py:561
  9.2 2.6 %collective-permute-start.4 = (f32[56,384]{1,0:T(8,128)S(1)}, f32[56,384]{1,0:T(8,128)S(1)}, u32[]{:S(2)}, u32[]{:S(2)}) collective-permute-start(f32[56,384]{1,0:T(8,128)S(1)} %get-tuple-element.51), channel_id=1, source_target_pairs={{0,16},{1,17},{2,18},{3,19},{4,20},{5,21},{6,22},{7,23},{8,24},{9,... | collective-permute-start | bytes 258056 | tf_op jit(solution)/shard_map/ppermute | solution.py:561
  11.8 1.9 %collective-permute-start.1 = (f32[56,128]{1,0:T(8,128)S(1)}, f32[56,128]{1,0:T(8,128)S(1)}, u32[]{:S(2)}, u32[]{:S(2)}) collective-permute-start(f32[56,128]{1,0:T(8,128)S(1)} %get-tuple-element.48), channel_id=1, source_target_pairs={{0,29},{1,4},{2,31},{3,6},{4,1},{5,8},{6,3},{7,10},{8,5},{9,12},{1... | collective-permute-start | bytes 86024 | tf_op jit(solution)/shard_map/ppermute | solution.py:555
  13.7 0.5 collective-permute-start.3
  14.2 3.7 %collective-permute-done.1.refs_2_ = f32[56,128]{1,0:T(8,128)S(1)} collective-permute-done((f32[56,128]{1,0:T(8,128)S(1)}, f32[56,128]{1,0:T(8,128)S(1)}, u32[]{:S(2)}, u32[]{:S(2)}) %collective-permute-start.1) | collective-permute-done | bytes 28704 | tf_op jit(solution)/shard_map/ppermute | solution.py:555
  17.9 1.1 %collective-permute-done.3.refs_4_ = f32[56,128]{1,0:T(8,128)S(1)} collective-permute-done((f32[56,128]{1,0:T(8,128)S(1)}, f32[56,128]{1,0:T(8,128)S(1)}, u32[]{:S(2)}, u32[]{:S(2)}) %collective-permute-start.3) | collective-permute-done | bytes 28704 | tf_op jit(solution)/shard_map/ppermute | solution.py:561
  19.6 0.9 %collective-permute-done.6.refs_7_ = f32[56,128]{1,0:T(8,128)S(1)} collective-permute-done((f32[56,128]{1,0:T(8,128)S(1)}, f32[56,128]{1,0:T(8,128)S(1)}, u32[]{:S(2)}, u32[]{:S(2)}) %collective-permute-start.6) | collective-permute-done | bytes 28704 | tf_op jit(solution)/shard_map/ppermute | solution.py:566
  20.5 4.8 %shard_map.97 = (f32[48,256]{1,0:T(8,128)S(1)}, f32[8,128]{1,0:T(8,128)S(1)}, f32[8,128]{1,0:T(8,128)S(1)}, f32[48,256]{1,0:T(8,128)S(1)}, f32[104,128]{1,0:T(8,...) custom-call(f32[8,768]{1,0:T(8,128)S(1)} %get-tuple-element.42.meta_ref, ...), custom_call_target="tpu_custom_call" | custom-call | tf_op jit(solution)/shard_map/pallas_call | solution.py:534
  25.4 0.3 collective-permute-start.7
  25.7 1.0 %collective-permute-done.7.other_ref.refs_4_ = f32[104,128]{1,0:T(8,128)S(1)} collective-permute-done((f32[104,128]{1,0:T(8,128)S(1)}, f32[104,128]{1,0:T(8,128)S(1)}, u32[]{:S(2)}, u32[]{:S(2)}) %collective-permute-start.7) | collective-permute-done | bytes 53280 | tf_op jit(solution)/shard_map/ppermute | solution.py:556
  26.7 0.4 shard_map.98
  27.1 2.1 %collective-permute-start.9 = (f32[56,128]{1,0:T(8,128)S(1)}, f32[56,128]{1,0:T(8,128)S(1)}, u32[]{:S(2)}, u32[]{:S(2)}) collective-permute-start(f32[56,128]{1,0:T(8,128)S(1)} %get-tuple-element.61), channel_id=1, source_target_pairs={{0,3},{2,5},{4,7},{6,9},{8,11},{10,13},{12,15},{14,17},{16,19},{18... | collective-permute-start | bytes 86024 | tf_op jit(solution)/shard_map/ppermute | solution.py:561
  29.2 1.6 %collective-permute-start.10 = (f32[56,128]{1,0:T(8,128)S(1)}, f32[56,128]{1,0:T(8,128)S(1)}, u32[]{:S(2)}, u32[]{:S(2)}) collective-permute-start(f32[56,128]{1,0:T(8,128)S(1)} %get-tuple-element.62), channel_id=1, source_target_pairs={{0,15},{2,17},{4,19},{6,21},{8,23},{10,25},{12,27},{14,29},{16,31}... | collective-permute-start | bytes 86024 | tf_op jit(solution)/shard_map/ppermute | solution.py:561
  30.8 3.1 %collective-permute-start.8 = (f32[104,128]{1,0:T(8,128)S(1)}, f32[104,128]{1,0:T(8,128)S(1)}, u32[]{:S(2)}, u32[]{:S(2)}) collective-permute-start(f32[104,128]{1,0:T(8,128)S(1)} %get-tuple-element.60.mine_ref.refs_3_), channel_id=1, source_target_pairs={{0,29},{1,4},{2,31},{3,6},{4,1},{5,8},{6,3},{7,10},{8,5},{9,12},{1... | collective-permute-start | bytes 159752 | tf_op jit(solution)/shard_map/ppermute | solution.py:555
  33.9 0.5 collective-permute-start.11
  34.6 2.5 %collective-permute-start.13 = (f32[56,128]{1,0:T(8,128)S(1)}, f32[56,128]{1,0:T(8,128)S(1)}, u32[]{:S(2)}, u32[]{:S(2)}) collective-permute-start(f32[56,128]{1,0:T(8,128)S(1)} %collective-permute-done.10.refs_7_), channel_id=1, source_target_pairs={{0,1},{1,0},{2,3},{3,2},{4,5},{5,4},{6,7},{7,6},{8,9},{9,8},{10,11... | collective-permute-start | bytes 86024 | tf_op jit(solution)/shard_map/ppermute | solution.py:566
  37.2 1.5 %collective-permute-done.11.refs_8_ = f32[56,128]{1,0:T(8,128)S(1)} collective-permute-done((f32[56,128]{1,0:T(8,128)S(1)}, f32[56,128]{1,0:T(8,128)S(1)}, u32[]{:S(2)}, u32[]{:S(2)}) %collective-permute-start.11) | collective-permute-done | bytes 28704 | tf_op jit(solution)/shard_map/ppermute | solution.py:561
  38.7 4.8 %shard_map.99 = (f32[48,256]{1,0:T(8,128)S(1)}, f32[48,256]{1,0:T(8,128)S(1)}, f32[104,128]{1,0:T(8,128)S(1)}, f32[288,128]{1,0:T(8,128)S(1)}, f32[192,128]{1,0:T(8,128)S(1)}, /*index=5*/f32[192,128]{1,0:T(8,128)S(1)}) custom-call(f32[8,768]{1,0:T(8,128)S(1)} %get-tuple-element.42.meta_ref, bf16[384,768]{1,0:T(8,128)(2,1)S(1)} %get-tuple-element.43.onehot_ref, ...), custom_call_target="tpu_custom_call" | custom-call | tf_op jit(solution)/shard_map/pallas_call | solution.py:534
  43.5 1.2 %collective-permute-done.14.other_ref.refs_1_ = f32[104,128]{1,0:T(8,128)S(1)} collective-permute-done((f32[104,128]{1,0:T(8,128)S(1)}, f32[104,128]{1,0:T(8,128)S(1)}, u32[]{:S(2)}, u32[]{:S(2)}) %collective-permute-start.14) | collective-permute-done | bytes 53280 | tf_op jit(solution)/shard_map/ppermute | solution.py:556
  44.7 0.4 shard_map.100
  45.3 1.6 %collective-permute-start.17 = (f32[56,128]{1,0:T(8,128)S(1)}, f32[56,128]{1,0:T(8,128)S(1)}, u32[]{:S(2)}, u32[]{:S(2)}) collective-permute-start(f32[56,128]{1,0:T(8,128)S(1)} %get-tuple-element.72), channel_id=1, source_target_pairs={{0,15},{2,17},{4,19},{6,21},{8,23},{10,25},{12,27},{14,29},{16,31}... | collective-permute-start | bytes 86024 | tf_op jit(solution)/shard_map/ppermute | solution.py:561
  47.0 3.2 %collective-permute-start.15 = (f32[104,128]{1,0:T(8,128)S(1)}, f32[104,128]{1,0:T(8,128)S(1)}, u32[]{:S(2)}, u32[]{:S(2)}) collective-permute-start(f32[104,128]{1,0:T(8,128)S(1)} %get-tuple-element.70.mine_ref.refs_0_), channel_id=1, source_target_pairs={{0,29},{1,4},{2,31},{3,6},{4,1},{5,8},{6,3},{7,10},{8,5},{9,12},{1... | collective-permute-start | bytes 159752 | tf_op jit(solution)/shard_map/ppermute | solution.py:555
  50.1 2.3 %collective-permute-start.18 = (f32[56,128]{1,0:T(8,128)S(1)}, f32[56,128]{1,0:T(8,128)S(1)}, u32[]{:S(2)}, u32[]{:S(2)}) collective-permute-start(f32[56,128]{1,0:T(8,128)S(1)} %get-tuple-element.73), channel_id=1, source_target_pairs={{0,16},{1,17},{2,18},{3,19},{4,20},{5,21},{6,22},{7,23},{8,24},{9,... | collective-permute-start | bytes 86024 | tf_op jit(solution)/shard_map/ppermute | solution.py:561
  52.4 0.5 collective-permute-start.20
  52.9 0.6 collective-permute-done.15.refs_2_
  53.5 1.6 %collective-permute-done.18.refs_5_ = f32[56,128]{1,0:T(8,128)S(1)} collective-permute-done((f32[56,128]{1,0:T(8,128)S(1)}, f32[56,128]{1,0:T(8,128)S(1)}, u32[]{:S(2)}, u32[]{:S(2)}) %collective-permute-start.18) | collective-permute-done | bytes 28704 | tf_op jit(solution)/shard_map/ppermute | solution.py:561
  55.1 3.9 %shard_map.101 = (f32[48,256]{1,0:T(8,128)S(1)}, f32[192,128]{1,0:T(8,128)S(1)}, f32[32,1,128]{2,1,0:T(1,128)S(1)}) custom-call(f32[8,768]{1,0:T(8,128)S(1)} %get-tuple-element.42.meta_ref, bf16[384,768]{1,0:T(8,128)(2,1)S(1)} %get-tuple-element.43.onehot_ref, f32[192,48]{1,0:T(8,128)S(1)} %copy-done, f32[4096,128]{1,0:T(8,128)S(1)} %get-tuple-element.44.inverse_ref, ...), custom_call_target="tpu_custom_call" | custom-call | tf_op jit(solution)/shard_map/pallas_call | solution.py:534
  59.0 9.7 %all_to_all.5.moment_ref = f32[32,1,128]{2,1,0:T(1,128)S(1)} all-to-all(f32[32,1,128]{2,1,0:T(1,128)S(1)} %get-tuple-element.74), channel_id=1, replica_groups=mesh['dom'=16,'blk'=2] {'dom','blk'}, dimensions={0} | all-to-all | bytes 32768 | tf_op jit(solution)/shard_map/all_to_all | solution.py:646
  68.7 1.8 %shard_map.102 = (f32[48,256]{1,0:T(8,128)}, f32[192,128]{1,0:T(8,128)}) custom-call(f32[32,1,128]{2,1,0:T(1,128)S(1)} %all_to_all.5.moment_ref, f32[48,256]{1,0:T(8,128)S(1)} %get-tuple-element.56.k0_ref, f32[48,256]{1,0:T(8,128)S(1)} %get-tuple-element.64.k1_ref, f32[48,256]{1,0:T(8,128)S(1)} %get-tuple-element.75.k2_ref, ...), custom_call_target="tpu_custom_call" | custom-call | tf_op jit(solution)/shard_map/pallas_call | solution.py:534
  (23 shorter events, 1.3 us)
Async XLA Ops:
  0.6 19.9 %copy-start = (f32[192,48]{1,0:T(8,128)S(1)}, f32[192,48]{1,0:T(8,128)}, u32[]{:S(2)}) copy-start(f32[192,48]{1,0:T(8,128)} %constant.5.clone.forth_ref) | copy-start | bytes 110596
  0.6 19.9 %copy-start.1 = (f32[192,48]{1,0:T(8,128)S(1)}, f32[192,48]{1,0:T(8,128)}, u32[]{:S(2)}) copy-start(f32[192,48]{1,0:T(8,128)} %constant.4.clone.back_hbm.back_ref) | copy-start | bytes 110596
  4.8 1.4 %collective-permute-start = (f32[56,384]{1,0:T(8,128)S(1)}, f32[56,384]{1,0:T(8,128)S(1)}, u32[]{:S(2)}, u32[]{:S(2)}) collective-permute-start(f32[56,384]{1,0:T(8,128)S(1)} %get-tuple-element.47.mine_ref.refs_0_), channel_id=1, source_target_pairs={{0,1},{1,0},{2,3},{3,2},{4,5},{5,4},{6,7},{7,6},{8,9},{9,8},{10,11... | collective-permute-start | bytes 258056 | tf_op jit(solution)/shard_map/ppermute | solution.py:556
  6.5 12.5 %collective-permute-start.2 = (f32[56,640]{1,0:T(8,128)S(1)}, f32[56,640]{1,0:T(8,128)S(1)}, u32[]{:S(2)}, u32[]{:S(2)}) collective-permute-start(f32[56,640]{1,0:T(8,128)S(1)} %get-tuple-element.49), channel_id=1, source_target_pairs={{0,3},{2,5},{4,7},{6,9},{8,11},{10,13},{12,15},{14,17},{16,19},{18... | collective-permute-start | bytes 430088 | tf_op jit(solution)/shard_map/ppermute | solution.py:561
  9.2 9.9 %collective-permute-start.4 = (f32[56,384]{1,0:T(8,128)S(1)}, f32[56,384]{1,0:T(8,128)S(1)}, u32[]{:S(2)}, u32[]{:S(2)}) collective-permute-start(f32[56,384]{1,0:T(8,128)S(1)} %get-tuple-element.51), channel_id=1, source_target_pairs={{0,16},{1,17},{2,18},{3,19},{4,20},{5,21},{6,22},{7,23},{8,24},{9,... | collective-permute-start | bytes 258056 | tf_op jit(solution)/shard_map/ppermute | solution.py:561
  11.8 6.2 %collective-permute-start.1 = (f32[56,128]{1,0:T(8,128)S(1)}, f32[56,128]{1,0:T(8,128)S(1)}, u32[]{:S(2)}, u32[]{:S(2)}) collective-permute-start(f32[56,128]{1,0:T(8,128)S(1)} %get-tuple-element.48), channel_id=1, source_target_pairs={{0,29},{1,4},{2,31},{3,6},{4,1},{5,8},{6,3},{7,10},{8,5},{9,12},{1... | collective-permute-start | bytes 86024 | tf_op jit(solution)/shard_map/ppermute | solution.py:555
  13.7 5.4 %collective-permute-start.3 = (f32[56,128]{1,0:T(8,128)S(1)}, f32[56,128]{1,0:T(8,128)S(1)}, u32[]{:S(2)}, u32[]{:S(2)}) collective-permute-start(f32[56,128]{1,0:T(8,128)S(1)} %get-tuple-element.50), channel_id=1, source_target_pairs={{0,15},{2,17},{4,19},{6,21},{8,23},{10,25},{12,27},{14,29},{16,31}... | collective-permute-start | bytes 86024 | tf_op jit(solution)/shard_map/ppermute | solution.py:561
  19.1 1.5 %collective-permute-start.5 = (f32[56,640]{1,0:T(8,128)S(1)}, f32[56,640]{1,0:T(8,128)S(1)}, u32[]{:S(2)}, u32[]{:S(2)}) collective-permute-start(f32[56,640]{1,0:T(8,128)S(1)} %collective-permute-done.2.refs_3_), channel_id=1, source_target_pairs={{0,1},{1,0},{2,3},{3,2},{4,5},{5,4},{6,7},{7,6},{8,9},{9,8},{10,11... | collective-permute-start | bytes 430088 | tf_op jit(solution)/shard_map/ppermute | solution.py:566
  19.3 1.2 %collective-permute-start.6 = (f32[56,128]{1,0:T(8,128)S(1)}, f32[56,128]{1,0:T(8,128)S(1)}, u32[]{:S(2)}, u32[]{:S(2)}) collective-permute-start(f32[56,128]{1,0:T(8,128)S(1)} %collective-permute-done.3.refs_4_), channel_id=1, source_target_pairs={{0,1},{1,0},{2,3},{3,2},{4,5},{5,4},{6,7},{7,6},{8,9},{9,8},{10,11... | collective-permute-start | bytes 86024 | tf_op jit(solution)/shard_map/ppermute | solution.py:566
  25.4 1.3 %collective-permute-start.7 = (f32[104,128]{1,0:T(8,128)S(1)}, f32[104,128]{1,0:T(8,128)S(1)}, u32[]{:S(2)}, u32[]{:S(2)}) collective-permute-start(f32[104,128]{1,0:T(8,128)S(1)} %get-tuple-element.60.mine_ref.refs_3_), channel_id=1, source_target_pairs={{0,1},{1,0},{2,3},{3,2},{4,5},{5,4},{6,7},{7,6},{8,9},{9,8},{10,11... | collective-permute-start | bytes 159752 | tf_op jit(solution)/shard_map/ppermute | solution.py:556
  27.1 7.3 %collective-permute-start.9 = (f32[56,128]{1,0:T(8,128)S(1)}, f32[56,128]{1,0:T(8,128)S(1)}, u32[]{:S(2)}, u32[]{:S(2)}) collective-permute-start(f32[56,128]{1,0:T(8,128)S(1)} %get-tuple-element.61), channel_id=1, source_target_pairs={{0,3},{2,5},{4,7},{6,9},{8,11},{10,13},{12,15},{14,17},{16,19},{18... | collective-permute-start | bytes 86024 | tf_op jit(solution)/shard_map/ppermute | solution.py:561
  29.2 5.4 %collective-permute-start.10 = (f32[56,128]{1,0:T(8,128)S(1)}, f32[56,128]{1,0:T(8,128)S(1)}, u32[]{:S(2)}, u32[]{:S(2)}) collective-permute-start(f32[56,128]{1,0:T(8,128)S(1)} %get-tuple-element.62), channel_id=1, source_target_pairs={{0,15},{2,17},{4,19},{6,21},{8,23},{10,25},{12,27},{14,29},{16,31}... | collective-permute-start | bytes 86024 | tf_op jit(solution)/shard_map/ppermute | solution.py:561
  30.8 6.4 %collective-permute-start.8 = (f32[104,128]{1,0:T(8,128)S(1)}, f32[104,128]{1,0:T(8,128)S(1)}, u32[]{:S(2)}, u32[]{:S(2)}) collective-permute-start(f32[104,128]{1,0:T(8,128)S(1)} %get-tuple-element.60.mine_ref.refs_3_), channel_id=1, source_target_pairs={{0,29},{1,4},{2,31},{3,6},{4,1},{5,8},{6,3},{7,10},{8,5},{9,12},{1... | collective-permute-start | bytes 159752 | tf_op jit(solution)/shard_map/ppermute | solution.py:555
  33.9 4.8 %collective-permute-start.11 = (f32[56,128]{1,0:T(8,128)S(1)}, f32[56,128]{1,0:T(8,128)S(1)}, u32[]{:S(2)}, u32[]{:S(2)}) collective-permute-start(f32[56,128]{1,0:T(8,128)S(1)} %get-tuple-element.63), channel_id=1, source_target_pairs={{0,16},{1,17},{2,18},{3,19},{4,20},{5,21},{6,22},{7,23},{8,24},{9,... | collective-permute-start | bytes 86024 | tf_op jit(solution)/shard_map/ppermute | solution.py:561
  34.4 4.2 %collective-permute-start.12 = (f32[56,128]{1,0:T(8,128)S(1)}, f32[56,128]{1,0:T(8,128)S(1)}, u32[]{:S(2)}, u32[]{:S(2)}) collective-permute-start(f32[56,128]{1,0:T(8,128)S(1)} %collective-permute-done.9.refs_6_), channel_id=1, source_target_pairs={{0,1},{1,0},{2,3},{3,2},{4,5},{5,4},{6,7},{7,6},{8,9},{9,8},{10,11... | collective-permute-start | bytes 86024 | tf_op jit(solution)/shard_map/ppermute | solution.py:566
  34.6 4.0 %collective-permute-start.13 = (f32[56,128]{1,0:T(8,128)S(1)}, f32[56,128]{1,0:T(8,128)S(1)}, u32[]{:S(2)}, u32[]{:S(2)}) collective-permute-start(f32[56,128]{1,0:T(8,128)S(1)} %collective-permute-done.10.refs_7_), channel_id=1, source_target_pairs={{0,1},{1,0},{2,3},{3,2},{4,5},{5,4},{6,7},{7,6},{8,9},{9,8},{10,11... | collective-permute-start | bytes 86024 | tf_op jit(solution)/shard_map/ppermute | solution.py:566
  43.4 1.3 %collective-permute-start.14 = (f32[104,128]{1,0:T(8,128)S(1)}, f32[104,128]{1,0:T(8,128)S(1)}, u32[]{:S(2)}, u32[]{:S(2)}) collective-permute-start(f32[104,128]{1,0:T(8,128)S(1)} %get-tuple-element.70.mine_ref.refs_0_), channel_id=1, source_target_pairs={{0,1},{1,0},{2,3},{3,2},{4,5},{5,4},{6,7},{7,6},{8,9},{9,8},{10,11... | collective-permute-start | bytes 159752 | tf_op jit(solution)/shard_map/ppermute | solution.py:556
  45.2 7.2 %collective-permute-start.16 = (f32[56,128]{1,0:T(8,128)S(1)}, f32[56,128]{1,0:T(8,128)S(1)}, u32[]{:S(2)}, u32[]{:S(2)}) collective-permute-start(f32[56,128]{1,0:T(8,128)S(1)} %get-tuple-element.71), channel_id=1, source_target_pairs={{0,3},{2,5},{4,7},{6,9},{8,11},{10,13},{12,15},{14,17},{16,19},{18... | collective-permute-start | bytes 86024 | tf_op jit(solution)/shard_map/ppermute | solution.py:561
  45.3 7.0 %collective-permute-start.17 = (f32[56,128]{1,0:T(8,128)S(1)}, f32[56,128]{1,0:T(8,128)S(1)}, u32[]{:S(2)}, u32[]{:S(2)}) collective-permute-start(f32[56,128]{1,0:T(8,128)S(1)} %get-tuple-element.72), channel_id=1, source_target_pairs={{0,15},{2,17},{4,19},{6,21},{8,23},{10,25},{12,27},{14,29},{16,31}... | collective-permute-start | bytes 86024 | tf_op jit(solution)/shard_map/ppermute | solution.py:561
  47.0 6.5 %collective-permute-start.15 = (f32[104,128]{1,0:T(8,128)S(1)}, f32[104,128]{1,0:T(8,128)S(1)}, u32[]{:S(2)}, u32[]{:S(2)}) collective-permute-start(f32[104,128]{1,0:T(8,128)S(1)} %get-tuple-element.70.mine_ref.refs_0_), channel_id=1, source_target_pairs={{0,29},{1,4},{2,31},{3,6},{4,1},{5,8},{6,3},{7,10},{8,5},{9,12},{1... | collective-permute-start | bytes 159752 | tf_op jit(solution)/shard_map/ppermute | solution.py:555
  50.1 5.0 %collective-permute-start.18 = (f32[56,128]{1,0:T(8,128)S(1)}, f32[56,128]{1,0:T(8,128)S(1)}, u32[]{:S(2)}, u32[]{:S(2)}) collective-permute-start(f32[56,128]{1,0:T(8,128)S(1)} %get-tuple-element.73), channel_id=1, source_target_pairs={{0,16},{1,17},{2,18},{3,19},{4,20},{5,21},{6,22},{7,23},{8,24},{9,... | collective-permute-start | bytes 86024 | tf_op jit(solution)/shard_map/ppermute | solution.py:561
  52.4 2.7 %collective-permute-start.19 = (f32[56,128]{1,0:T(8,128)S(1)}, f32[56,128]{1,0:T(8,128)S(1)}, u32[]{:S(2)}, u32[]{:S(2)}) collective-permute-start(f32[56,128]{1,0:T(8,128)S(1)} %collective-permute-done.16.refs_3_), channel_id=1, source_target_pairs={{0,1},{1,0},{2,3},{3,2},{4,5},{5,4},{6,7},{7,6},{8,9},{9,8},{10,11... | collective-permute-start | bytes 86024 | tf_op jit(solution)/shard_map/ppermute | solution.py:566
  52.4 2.7 %collective-permute-start.20 = (f32[56,128]{1,0:T(8,128)S(1)}, f32[56,128]{1,0:T(8,128)S(1)}, u32[]{:S(2)}, u32[]{:S(2)}) collective-permute-start(f32[56,128]{1,0:T(8,128)S(1)} %collective-permute-done.17.refs_4_), channel_id=1, source_target_pairs={{0,1},{1,0},{2,3},{3,2},{4,5},{5,4},{6,7},{7,6},{8,9},{9,8},{10,11... | collective-permute-start | bytes 86024 | tf_op jit(solution)/shard_map/ppermute | solution.py:566

commit v9 on v8

--- a/solution.py
+++ b/solution.py
@@ -102,8 +102,9 @@
     return tiles[0]
 
 
-def rows_times(mat_ref, vec_ref, out_ref, outs, terms, group=32):
+def rows_times(mat_ref, vec_ref, out_ref, outs, terms):
     width = vec_ref.shape[1]
+    group = outs // 2
     sublane = lax.broadcasted_iota(jnp.int32, (8, width), 0)
     vecs = [
         [vec_ref[c * terms + t : c * terms + t + 8, :] for t in range(0, terms, 8)]
@@ -131,7 +132,7 @@
     lax.fori_loop(0, outs // group, body, 0)
 
 
-def columns_times(acc, mat_ref, vec_ref, outs, terms, unroll=16):
+def columns_times(acc, mat_ref, vec_ref, outs, terms, unroll=32):
     def body(t, acc):
         acc = [list(a) for a in acc]
         vecs = [

time: 70.7 us -> 70.7 us (level)
  no operation moved by 1% of the time
where the time goes in v9:
time: 70.7 us; the launch traced here: 70.5 us
  starting transfers between devices  26.7 us (38%)
  Pallas kernels  20.5 us (29%)
  waiting for transfers between devices  12.8 us (18%)
  blocking collectives  9.72 us (14%)
  between operations  0.73 us (1%)
    pallas_call x8, Pallas kernels, call(): pl.pallas_call(kernel, out_shape=[jax.ShapeDtypeStruct(shape, dtype) for...  20.5 us
    ppermute x9, starting transfers between devices, fused_exchange(): lax.ppermute(block, AXES, way)  14 us
    all_to_all x1, blocking collectives, local(): lax.all_to_all(moments, AXES, split_axis=0, concat_axis=0, tiled=True)  9.72 us
    ppermute x3, starting transfers between devices, fused_exchange(): second = lax.ppermute(out, AXES, skip)  8.16 us
    ppermute x9, waiting for transfers between devices, fused_exchange(): lax.ppermute(block, AXES, way)  4.39 us
    ppermute x3, waiting for transfers between devices, fused_exchange(): second = lax.ppermute(out, AXES, skip)  4.31 us
    ppermute x6, starting transfers between devices, fused_exchange(): passed = [lax.ppermute(block, AXES, pair) for block in got[:2]]  3.59 us
    ppermute x3, waiting for transfers between devices, fused_exchange(): other = lax.ppermute(shared, AXES, pair)  3.13 us
  transfers between devices with their start and end apart: 21, of which 10 were waited for; matrix products, arithmetic and copies ran while one was open for 0% of the time, Pallas kernels for 0%

profile of v9, /device:TPU:0, one launch (start us, length us, event | category | flops | bytes accessed | tf_op | source)
XLA Modules:
  0.0 70.5 jit_solution(4874050660899523934)
XLA Ops:
  0.7 4.1 %shard_map.95 = (f32[56,384]{1,0:T(8,128)S(1)}, f32[56,128]{1,0:T(8,128)S(1)}, bf16[384,768]{1,0:T(8,128)(2,1)S(1)}, f32[8,768]{1,0:T(8,128)S(1)}, f32[192,128]{...) custom-call(s32[6,128]{1,0:T(8,128)} %bitcast.11, s32[6,128]{1,0:T(8,128)} %bitcast.12, ...), custom_call_target="tpu_custom_call" | custom-call | tf_op jit(solution)/shard_map/pallas_call | solution.py:535
  4.8 0.5 collective-permute-start
  5.3 0.9 %collective-permute-done.other_ref.refs_1_ = f32[56,384]{1,0:T(8,128)S(1)} collective-permute-done((f32[56,384]{1,0:T(8,128)S(1)}, f32[56,384]{1,0:T(8,128)S(1)}, u32[]{:S(2)}, u32[]{:S(2)}) %collective-permute-start) | collective-permute-done | bytes 86048 | tf_op jit(solution)/shard_map/ppermute | solution.py:557
  6.5 2.7 %collective-permute-start.2 = (f32[56,640]{1,0:T(8,128)S(1)}, f32[56,640]{1,0:T(8,128)S(1)}, u32[]{:S(2)}, u32[]{:S(2)}) collective-permute-start(f32[56,640]{1,0:T(8,128)S(1)} %get-tuple-element.49), channel_id=1, source_target_pairs={{0,3},{2,5},{4,7},{6,9},{8,11},{10,13},{12,15},{14,17},{16,19},{18... | collective-permute-start | bytes 430088 | tf_op jit(solution)/shard_map/ppermute | solution.py:562
  9.2 2.6 %collective-permute-start.4 = (f32[56,384]{1,0:T(8,128)S(1)}, f32[56,384]{1,0:T(8,128)S(1)}, u32[]{:S(2)}, u32[]{:S(2)}) collective-permute-start(f32[56,384]{1,0:T(8,128)S(1)} %get-tuple-element.51), channel_id=1, source_target_pairs={{0,16},{1,17},{2,18},{3,19},{4,20},{5,21},{6,22},{7,23},{8,24},{9,... | collective-permute-start | bytes 258056 | tf_op jit(solution)/shard_map/ppermute | solution.py:562
  11.8 1.9 %collective-permute-start.1 = (f32[56,128]{1,0:T(8,128)S(1)}, f32[56,128]{1,0:T(8,128)S(1)}, u32[]{:S(2)}, u32[]{:S(2)}) collective-permute-start(f32[56,128]{1,0:T(8,128)S(1)} %get-tuple-element.48), channel_id=1, source_target_pairs={{0,29},{1,4},{2,31},{3,6},{4,1},{5,8},{6,3},{7,10},{8,5},{9,12},{1... | collective-permute-start | bytes 86024 | tf_op jit(solution)/shard_map/ppermute | solution.py:556
  13.7 0.5 collective-permute-start.3
  14.2 3.7 %collective-permute-done.1.refs_2_ = f32[56,128]{1,0:T(8,128)S(1)} collective-permute-done((f32[56,128]{1,0:T(8,128)S(1)}, f32[56,128]{1,0:T(8,128)S(1)}, u32[]{:S(2)}, u32[]{:S(2)}) %collective-permute-start.1) | collective-permute-done | bytes 28704 | tf_op jit(solution)/shard_map/ppermute | solution.py:556
  17.9 1.1 %collective-permute-done.3.refs_4_ = f32[56,128]{1,0:T(8,128)S(1)} collective-permute-done((f32[56,128]{1,0:T(8,128)S(1)}, f32[56,128]{1,0:T(8,128)S(1)}, u32[]{:S(2)}, u32[]{:S(2)}) %collective-permute-start.3) | collective-permute-done | bytes 28704 | tf_op jit(solution)/shard_map/ppermute | solution.py:562
  19.6 0.9 %collective-permute-done.6.refs_7_ = f32[56,128]{1,0:T(8,128)S(1)} collective-permute-done((f32[56,128]{1,0:T(8,128)S(1)}, f32[56,128]{1,0:T(8,128)S(1)}, u32[]{:S(2)}, u32[]{:S(2)}) %collective-permute-start.6) | collective-permute-done | bytes 28704 | tf_op jit(solution)/shard_map/ppermute | solution.py:567
  20.5 4.8 %shard_map.97 = (f32[48,256]{1,0:T(8,128)S(1)}, f32[8,128]{1,0:T(8,128)S(1)}, f32[8,128]{1,0:T(8,128)S(1)}, f32[48,256]{1,0:T(8,128)S(1)}, f32[104,128]{1,0:T(8,...) custom-call(f32[8,768]{1,0:T(8,128)S(1)} %get-tuple-element.42.meta_ref, ...), custom_call_target="tpu_custom_call" | custom-call | tf_op jit(solution)/shard_map/pallas_call | solution.py:535
  25.3 0.3 collective-permute-start.7
  25.6 1.0 %collective-permute-done.7.other_ref.refs_4_ = f32[104,128]{1,0:T(8,128)S(1)} collective-permute-done((f32[104,128]{1,0:T(8,128)S(1)}, f32[104,128]{1,0:T(8,128)S(1)}, u32[]{:S(2)}, u32[]{:S(2)}) %collective-permute-start.7) | collective-permute-done | bytes 53280 | tf_op jit(solution)/shard_map/ppermute | solution.py:557
  26.6 0.4 shard_map.98
  27.1 2.1 %collective-permute-start.9 = (f32[56,128]{1,0:T(8,128)S(1)}, f32[56,128]{1,0:T(8,128)S(1)}, u32[]{:S(2)}, u32[]{:S(2)}) collective-permute-start(f32[56,128]{1,0:T(8,128)S(1)} %get-tuple-element.61), channel_id=1, source_target_pairs={{0,3},{2,5},{4,7},{6,9},{8,11},{10,13},{12,15},{14,17},{16,19},{18... | collective-permute-start | bytes 86024 | tf_op jit(solution)/shard_map/ppermute | solution.py:562
  29.2 1.5 %collective-permute-start.10 = (f32[56,128]{1,0:T(8,128)S(1)}, f32[56,128]{1,0:T(8,128)S(1)}, u32[]{:S(2)}, u32[]{:S(2)}) collective-permute-start(f32[56,128]{1,0:T(8,128)S(1)} %get-tuple-element.62), channel_id=1, source_target_pairs={{0,15},{2,17},{4,19},{6,21},{8,23},{10,25},{12,27},{14,29},{16,31}... | collective-permute-start | bytes 86024 | tf_op jit(solution)/shard_map/ppermute | solution.py:562
  30.8 3.1 %collective-permute-start.8 = (f32[104,128]{1,0:T(8,128)S(1)}, f32[104,128]{1,0:T(8,128)S(1)}, u32[]{:S(2)}, u32[]{:S(2)}) collective-permute-start(f32[104,128]{1,0:T(8,128)S(1)} %get-tuple-element.60.mine_ref.refs_3_), channel_id=1, source_target_pairs={{0,29},{1,4},{2,31},{3,6},{4,1},{5,8},{6,3},{7,10},{8,5},{9,12},{1... | collective-permute-start | bytes 159752 | tf_op jit(solution)/shard_map/ppermute | solution.py:556
  33.8 0.5 collective-permute-start.11
  34.6 2.5 %collective-permute-start.13 = (f32[56,128]{1,0:T(8,128)S(1)}, f32[56,128]{1,0:T(8,128)S(1)}, u32[]{:S(2)}, u32[]{:S(2)}) collective-permute-start(f32[56,128]{1,0:T(8,128)S(1)} %collective-permute-done.10.refs_7_), channel_id=1, source_target_pairs={{0,1},{1,0},{2,3},{3,2},{4,5},{5,4},{6,7},{7,6},{8,9},{9,8},{10,11... | collective-permute-start | bytes 86024 | tf_op jit(solution)/shard_map/ppermute | solution.py:567
  37.1 1.5 %collective-permute-done.11.refs_8_ = f32[56,128]{1,0:T(8,128)S(1)} collective-permute-done((f32[56,128]{1,0:T(8,128)S(1)}, f32[56,128]{1,0:T(8,128)S(1)}, u32[]{:S(2)}, u32[]{:S(2)}) %collective-permute-start.11) | collective-permute-done | bytes 28704 | tf_op jit(solution)/shard_map/ppermute | solution.py:562
  38.6 4.7 %shard_map.99 = (f32[48,256]{1,0:T(8,128)S(1)}, f32[48,256]{1,0:T(8,128)S(1)}, f32[104,128]{1,0:T(8,128)S(1)}, f32[288,128]{1,0:T(8,128)S(1)}, f32[192,128]{1,0:T(8,128)S(1)}, /*index=5*/f32[192,128]{1,0:T(8,128)S(1)}) custom-call(f32[8,768]{1,0:T(8,128)S(1)} %get-tuple-element.42.meta_ref, bf16[384,768]{1,0:T(8,128)(2,1)S(1)} %get-tuple-element.43.onehot_ref, ...), custom_call_target="tpu_custom_call" | custom-call | tf_op jit(solution)/shard_map/pallas_call | solution.py:535
  43.4 1.2 %collective-permute-done.14.other_ref.refs_1_ = f32[104,128]{1,0:T(8,128)S(1)} collective-permute-done((f32[104,128]{1,0:T(8,128)S(1)}, f32[104,128]{1,0:T(8,128)S(1)}, u32[]{:S(2)}, u32[]{:S(2)}) %collective-permute-start.14) | collective-permute-done | bytes 53280 | tf_op jit(solution)/shard_map/ppermute | solution.py:557
  44.7 0.4 shard_map.100
  45.3 1.6 %collective-permute-start.17 = (f32[56,128]{1,0:T(8,128)S(1)}, f32[56,128]{1,0:T(8,128)S(1)}, u32[]{:S(2)}, u32[]{:S(2)}) collective-permute-start(f32[56,128]{1,0:T(8,128)S(1)} %get-tuple-element.72), channel_id=1, source_target_pairs={{0,15},{2,17},{4,19},{6,21},{8,23},{10,25},{12,27},{14,29},{16,31}... | collective-permute-start | bytes 86024 | tf_op jit(solution)/shard_map/ppermute | solution.py:562
  46.9 3.1 %collective-permute-start.15 = (f32[104,128]{1,0:T(8,128)S(1)}, f32[104,128]{1,0:T(8,128)S(1)}, u32[]{:S(2)}, u32[]{:S(2)}) collective-permute-start(f32[104,128]{1,0:T(8,128)S(1)} %get-tuple-element.70.mine_ref.refs_0_), channel_id=1, source_target_pairs={{0,29},{1,4},{2,31},{3,6},{4,1},{5,8},{6,3},{7,10},{8,5},{9,12},{1... | collective-permute-start | bytes 159752 | tf_op jit(solution)/shard_map/ppermute | solution.py:556
  50.1 2.3 %collective-permute-start.18 = (f32[56,128]{1,0:T(8,128)S(1)}, f32[56,128]{1,0:T(8,128)S(1)}, u32[]{:S(2)}, u32[]{:S(2)}) collective-permute-start(f32[56,128]{1,0:T(8,128)S(1)} %get-tuple-element.73), channel_id=1, source_target_pairs={{0,16},{1,17},{2,18},{3,19},{4,20},{5,21},{6,22},{7,23},{8,24},{9,... | collective-permute-start | bytes 86024 | tf_op jit(solution)/shard_map/ppermute | solution.py:562
  52.3 0.5 collective-permute-start.20
  52.8 0.6 collective-permute-done.15.refs_2_
  53.4 1.6 %collective-permute-done.18.refs_5_ = f32[56,128]{1,0:T(8,128)S(1)} collective-permute-done((f32[56,128]{1,0:T(8,128)S(1)}, f32[56,128]{1,0:T(8,128)S(1)}, u32[]{:S(2)}, u32[]{:S(2)}) %collective-permute-start.18) | collective-permute-done | bytes 28704 | tf_op jit(solution)/shard_map/ppermute | solution.py:562
  55.0 3.9 %shard_map.101 = (f32[48,256]{1,0:T(8,128)S(1)}, f32[192,128]{1,0:T(8,128)S(1)}, f32[32,1,128]{2,1,0:T(1,128)S(1)}) custom-call(f32[8,768]{1,0:T(8,128)S(1)} %get-tuple-element.42.meta_ref, bf16[384,768]{1,0:T(8,128)(2,1)S(1)} %get-tuple-element.43.onehot_ref, f32[192,48]{1,0:T(8,128)S(1)} %copy-done, f32[4096,128]{1,0:T(8,128)S(1)} %get-tuple-element.44.inverse_ref, ...), custom_call_target="tpu_custom_call" | custom-call | tf_op jit(solution)/shard_map/pallas_call | solution.py:535
  58.9 9.7 %all_to_all.5.moment_ref = f32[32,1,128]{2,1,0:T(1,128)S(1)} all-to-all(f32[32,1,128]{2,1,0:T(1,128)S(1)} %get-tuple-element.74), channel_id=1, replica_groups=mesh['dom'=16,'blk'=2] {'dom','blk'}, dimensions={0} | all-to-all | bytes 32768 | tf_op jit(solution)/shard_map/all_to_all | solution.py:647
  68.7 1.8 %shard_map.102 = (f32[48,256]{1,0:T(8,128)}, f32[192,128]{1,0:T(8,128)}) custom-call(f32[32,1,128]{2,1,0:T(1,128)S(1)} %all_to_all.5.moment_ref, f32[48,256]{1,0:T(8,128)S(1)} %get-tuple-element.56.k0_ref, f32[48,256]{1,0:T(8,128)S(1)} %get-tuple-element.64.k1_ref, f32[48,256]{1,0:T(8,128)S(1)} %get-tuple-element.75.k2_ref, ...), custom_call_target="tpu_custom_call" | custom-call | tf_op jit(solution)/shard_map/pallas_call | solution.py:535
  (23 shorter events, 1.3 us)
Async XLA Ops:
  0.6 19.9 %copy-start = (f32[192,48]{1,0:T(8,128)S(1)}, f32[192,48]{1,0:T(8,128)}, u32[]{:S(2)}) copy-start(f32[192,48]{1,0:T(8,128)} %constant.5.clone.forth_ref) | copy-start | bytes 110596
  0.6 19.9 %copy-start.1 = (f32[192,48]{1,0:T(8,128)S(1)}, f32[192,48]{1,0:T(8,128)}, u32[]{:S(2)}) copy-start(f32[192,48]{1,0:T(8,128)} %constant.4.clone.back_hbm.back_ref) | copy-start | bytes 110596
  4.8 1.4 %collective-permute-start = (f32[56,384]{1,0:T(8,128)S(1)}, f32[56,384]{1,0:T(8,128)S(1)}, u32[]{:S(2)}, u32[]{:S(2)}) collective-permute-start(f32[56,384]{1,0:T(8,128)S(1)} %get-tuple-element.47.mine_ref.refs_0_), channel_id=1, source_target_pairs={{0,1},{1,0},{2,3},{3,2},{4,5},{5,4},{6,7},{7,6},{8,9},{9,8},{10,11... | collective-permute-start | bytes 258056 | tf_op jit(solution)/shard_map/ppermute | solution.py:557
  6.5 12.5 %collective-permute-start.2 = (f32[56,640]{1,0:T(8,128)S(1)}, f32[56,640]{1,0:T(8,128)S(1)}, u32[]{:S(2)}, u32[]{:S(2)}) collective-permute-start(f32[56,640]{1,0:T(8,128)S(1)} %get-tuple-element.49), channel_id=1, source_target_pairs={{0,3},{2,5},{4,7},{6,9},{8,11},{10,13},{12,15},{14,17},{16,19},{18... | collective-permute-start | bytes 430088 | tf_op jit(solution)/shard_map/ppermute | solution.py:562
  9.2 9.9 %collective-permute-start.4 = (f32[56,384]{1,0:T(8,128)S(1)}, f32[56,384]{1,0:T(8,128)S(1)}, u32[]{:S(2)}, u32[]{:S(2)}) collective-permute-start(f32[56,384]{1,0:T(8,128)S(1)} %get-tuple-element.51), channel_id=1, source_target_pairs={{0,16},{1,17},{2,18},{3,19},{4,20},{5,21},{6,22},{7,23},{8,24},{9,... | collective-permute-start | bytes 258056 | tf_op jit(solution)/shard_map/ppermute | solution.py:562
  11.8 6.2 %collective-permute-start.1 = (f32[56,128]{1,0:T(8,128)S(1)}, f32[56,128]{1,0:T(8,128)S(1)}, u32[]{:S(2)}, u32[]{:S(2)}) collective-permute-start(f32[56,128]{1,0:T(8,128)S(1)} %get-tuple-element.48), channel_id=1, source_target_pairs={{0,29},{1,4},{2,31},{3,6},{4,1},{5,8},{6,3},{7,10},{8,5},{9,12},{1... | collective-permute-start | bytes 86024 | tf_op jit(solution)/shard_map/ppermute | solution.py:556
  13.7 5.4 %collective-permute-start.3 = (f32[56,128]{1,0:T(8,128)S(1)}, f32[56,128]{1,0:T(8,128)S(1)}, u32[]{:S(2)}, u32[]{:S(2)}) collective-permute-start(f32[56,128]{1,0:T(8,128)S(1)} %get-tuple-element.50), channel_id=1, source_target_pairs={{0,15},{2,17},{4,19},{6,21},{8,23},{10,25},{12,27},{14,29},{16,31}... | collective-permute-start | bytes 86024 | tf_op jit(solution)/shard_map/ppermute | solution.py:562
  19.1 1.5 %collective-permute-start.5 = (f32[56,640]{1,0:T(8,128)S(1)}, f32[56,640]{1,0:T(8,128)S(1)}, u32[]{:S(2)}, u32[]{:S(2)}) collective-permute-start(f32[56,640]{1,0:T(8,128)S(1)} %collective-permute-done.2.refs_3_), channel_id=1, source_target_pairs={{0,1},{1,0},{2,3},{3,2},{4,5},{5,4},{6,7},{7,6},{8,9},{9,8},{10,11... | collective-permute-start | bytes 430088 | tf_op jit(solution)/shard_map/ppermute | solution.py:567
  19.3 1.2 %collective-permute-start.6 = (f32[56,128]{1,0:T(8,128)S(1)}, f32[56,128]{1,0:T(8,128)S(1)}, u32[]{:S(2)}, u32[]{:S(2)}) collective-permute-start(f32[56,128]{1,0:T(8,128)S(1)} %collective-permute-done.3.refs_4_), channel_id=1, source_target_pairs={{0,1},{1,0},{2,3},{3,2},{4,5},{5,4},{6,7},{7,6},{8,9},{9,8},{10,11... | collective-permute-start | bytes 86024 | tf_op jit(solution)/shard_map/ppermute | solution.py:567
  25.3 1.3 %collective-permute-start.7 = (f32[104,128]{1,0:T(8,128)S(1)}, f32[104,128]{1,0:T(8,128)S(1)}, u32[]{:S(2)}, u32[]{:S(2)}) collective-permute-start(f32[104,128]{1,0:T(8,128)S(1)} %get-tuple-element.60.mine_ref.refs_3_), channel_id=1, source_target_pairs={{0,1},{1,0},{2,3},{3,2},{4,5},{5,4},{6,7},{7,6},{8,9},{9,8},{10,11... | collective-permute-start | bytes 159752 | tf_op jit(solution)/shard_map/ppermute | solution.py:557
  27.1 7.3 %collective-permute-start.9 = (f32[56,128]{1,0:T(8,128)S(1)}, f32[56,128]{1,0:T(8,128)S(1)}, u32[]{:S(2)}, u32[]{:S(2)}) collective-permute-start(f32[56,128]{1,0:T(8,128)S(1)} %get-tuple-element.61), channel_id=1, source_target_pairs={{0,3},{2,5},{4,7},{6,9},{8,11},{10,13},{12,15},{14,17},{16,19},{18... | collective-permute-start | bytes 86024 | tf_op jit(solution)/shard_map/ppermute | solution.py:562
  29.2 5.4 %collective-permute-start.10 = (f32[56,128]{1,0:T(8,128)S(1)}, f32[56,128]{1,0:T(8,128)S(1)}, u32[]{:S(2)}, u32[]{:S(2)}) collective-permute-start(f32[56,128]{1,0:T(8,128)S(1)} %get-tuple-element.62), channel_id=1, source_target_pairs={{0,15},{2,17},{4,19},{6,21},{8,23},{10,25},{12,27},{14,29},{16,31}... | collective-permute-start | bytes 86024 | tf_op jit(solution)/shard_map/ppermute | solution.py:562
  30.8 6.4 %collective-permute-start.8 = (f32[104,128]{1,0:T(8,128)S(1)}, f32[104,128]{1,0:T(8,128)S(1)}, u32[]{:S(2)}, u32[]{:S(2)}) collective-permute-start(f32[104,128]{1,0:T(8,128)S(1)} %get-tuple-element.60.mine_ref.refs_3_), channel_id=1, source_target_pairs={{0,29},{1,4},{2,31},{3,6},{4,1},{5,8},{6,3},{7,10},{8,5},{9,12},{1... | collective-permute-start | bytes 159752 | tf_op jit(solution)/shard_map/ppermute | solution.py:556
  33.8 4.8 %collective-permute-start.11 = (f32[56,128]{1,0:T(8,128)S(1)}, f32[56,128]{1,0:T(8,128)S(1)}, u32[]{:S(2)}, u32[]{:S(2)}) collective-permute-start(f32[56,128]{1,0:T(8,128)S(1)} %get-tuple-element.63), channel_id=1, source_target_pairs={{0,16},{1,17},{2,18},{3,19},{4,20},{5,21},{6,22},{7,23},{8,24},{9,... | collective-permute-start | bytes 86024 | tf_op jit(solution)/shard_map/ppermute | solution.py:562
  34.4 4.2 %collective-permute-start.12 = (f32[56,128]{1,0:T(8,128)S(1)}, f32[56,128]{1,0:T(8,128)S(1)}, u32[]{:S(2)}, u32[]{:S(2)}) collective-permute-start(f32[56,128]{1,0:T(8,128)S(1)} %collective-permute-done.9.refs_6_), channel_id=1, source_target_pairs={{0,1},{1,0},{2,3},{3,2},{4,5},{5,4},{6,7},{7,6},{8,9},{9,8},{10,11... | collective-permute-start | bytes 86024 | tf_op jit(solution)/shard_map/ppermute | solution.py:567
  34.6 4.0 %collective-permute-start.13 = (f32[56,128]{1,0:T(8,128)S(1)}, f32[56,128]{1,0:T(8,128)S(1)}, u32[]{:S(2)}, u32[]{:S(2)}) collective-permute-start(f32[56,128]{1,0:T(8,128)S(1)} %collective-permute-done.10.refs_7_), channel_id=1, source_target_pairs={{0,1},{1,0},{2,3},{3,2},{4,5},{5,4},{6,7},{7,6},{8,9},{9,8},{10,11... | collective-permute-start | bytes 86024 | tf_op jit(solution)/shard_map/ppermute | solution.py:567
  43.4 1.3 %collective-permute-start.14 = (f32[104,128]{1,0:T(8,128)S(1)}, f32[104,128]{1,0:T(8,128)S(1)}, u32[]{:S(2)}, u32[]{:S(2)}) collective-permute-start(f32[104,128]{1,0:T(8,128)S(1)} %get-tuple-element.70.mine_ref.refs_0_), channel_id=1, source_target_pairs={{0,1},{1,0},{2,3},{3,2},{4,5},{5,4},{6,7},{7,6},{8,9},{9,8},{10,11... | collective-permute-start | bytes 159752 | tf_op jit(solution)/shard_map/ppermute | solution.py:557
  45.1 7.2 %collective-permute-start.16 = (f32[56,128]{1,0:T(8,128)S(1)}, f32[56,128]{1,0:T(8,128)S(1)}, u32[]{:S(2)}, u32[]{:S(2)}) collective-permute-start(f32[56,128]{1,0:T(8,128)S(1)} %get-tuple-element.71), channel_id=1, source_target_pairs={{0,3},{2,5},{4,7},{6,9},{8,11},{10,13},{12,15},{14,17},{16,19},{18... | collective-permute-start | bytes 86024 | tf_op jit(solution)/shard_map/ppermute | solution.py:562
  45.3 7.0 %collective-permute-start.17 = (f32[56,128]{1,0:T(8,128)S(1)}, f32[56,128]{1,0:T(8,128)S(1)}, u32[]{:S(2)}, u32[]{:S(2)}) collective-permute-start(f32[56,128]{1,0:T(8,128)S(1)} %get-tuple-element.72), channel_id=1, source_target_pairs={{0,15},{2,17},{4,19},{6,21},{8,23},{10,25},{12,27},{14,29},{16,31}... | collective-permute-start | bytes 86024 | tf_op jit(solution)/shard_map/ppermute | solution.py:562
  46.9 6.5 %collective-permute-start.15 = (f32[104,128]{1,0:T(8,128)S(1)}, f32[104,128]{1,0:T(8,128)S(1)}, u32[]{:S(2)}, u32[]{:S(2)}) collective-permute-start(f32[104,128]{1,0:T(8,128)S(1)} %get-tuple-element.70.mine_ref.refs_0_), channel_id=1, source_target_pairs={{0,29},{1,4},{2,31},{3,6},{4,1},{5,8},{6,3},{7,10},{8,5},{9,12},{1... | collective-permute-start | bytes 159752 | tf_op jit(solution)/shard_map/ppermute | solution.py:556
  50.1 5.0 %collective-permute-start.18 = (f32[56,128]{1,0:T(8,128)S(1)}, f32[56,128]{1,0:T(8,128)S(1)}, u32[]{:S(2)}, u32[]{:S(2)}) collective-permute-start(f32[56,128]{1,0:T(8,128)S(1)} %get-tuple-element.73), channel_id=1, source_target_pairs={{0,16},{1,17},{2,18},{3,19},{4,20},{5,21},{6,22},{7,23},{8,24},{9,... | collective-permute-start | bytes 86024 | tf_op jit(solution)/shard_map/ppermute | solution.py:562
  52.3 2.7 %collective-permute-start.19 = (f32[56,128]{1,0:T(8,128)S(1)}, f32[56,128]{1,0:T(8,128)S(1)}, u32[]{:S(2)}, u32[]{:S(2)}) collective-permute-start(f32[56,128]{1,0:T(8,128)S(1)} %collective-permute-done.16.refs_3_), channel_id=1, source_target_pairs={{0,1},{1,0},{2,3},{3,2},{4,5},{5,4},{6,7},{7,6},{8,9},{9,8},{10,11... | collective-permute-start | bytes 86024 | tf_op jit(solution)/shard_map/ppermute | solution.py:567
  52.3 2.7 %collective-permute-start.20 = (f32[56,128]{1,0:T(8,128)S(1)}, f32[56,128]{1,0:T(8,128)S(1)}, u32[]{:S(2)}, u32[]{:S(2)}) collective-permute-start(f32[56,128]{1,0:T(8,128)S(1)} %collective-permute-done.17.refs_4_), channel_id=1, source_target_pairs={{0,1},{1,0},{2,3},{3,2},{4,5},{5,4},{6,7},{7,6},{8,9},{9,8},{10,11... | collective-permute-start | bytes 86024 | tf_op jit(solution)/shard_map/ppermute | solution.py:567

commit v10 on v8

--- a/solution.py
+++ b/solution.py
@@ -562,7 +562,7 @@
         for block, way in zip(packed, (both_ways(1), both_ways(ranks // 4 - 1), far))
     ]
     if out is not shared:
-        second, *got = lax.optimization_barrier((second, *got))
+        got = [*lax.optimization_barrier(tuple(got[:2])), got[2]]
     passed = [lax.ppermute(block, AXES, pair) for block in got[:2]]
     return [shared, other, second, *got, *passed]
 

time: 70.7 us -> 74.2 us (1.050)
  waiting for transfers between devices: 12.8 us -> 15.5 us
  starting transfers between devices: 26.7 us -> 28.1 us
    ppermute x9, waiting for transfers between devices: 4.4 us -> 7.28 us  [fused_exchange(): lax.ppermute(block, AXES, way)]
    ppermute x9, starting transfers between devices: 14 us -> 11.4 us  [fused_exchange(): lax.ppermute(block, AXES, way)]
    ppermute x6, starting transfers between devices: 3.58 us -> 6 us  [fused_exchange(): passed = [lax.ppermute(block, AXES, pair) for block in got[:2]]]
    ppermute x3, starting transfers between devices: 8.17 us -> 9.99 us  [fused_exchange(): second = lax.ppermute(out, AXES, skip)]
    ppermute x6, waiting for transfers between devices: 0.95 us -> 0.02 us  [fused_exchange(): passed = [lax.ppermute(block, AXES, pair) for block in got[:2]]]
where the time goes in v10:
time: 74.2 us; the launch traced here: 74 us
  starting transfers between devices  28.1 us (38%)
  Pallas kernels  20.6 us (28%)
  waiting for transfers between devices  15.5 us (21%)
  blocking collectives  9 us (12%)
    pallas_call x8, Pallas kernels, call(): pl.pallas_call(kernel, out_shape=[jax.ShapeDtypeStruct(shape, dtype) for...  20.6 us
    ppermute x9, starting transfers between devices, fused_exchange(): lax.ppermute(block, AXES, way)  11.4 us
    ppermute x3, starting transfers between devices, fused_exchange(): second = lax.ppermute(out, AXES, skip)  9.99 us
    all_to_all x1, blocking collectives, local(): lax.all_to_all(moments, AXES, split_axis=0, concat_axis=0, tiled=True)  9 us
    ppermute x9, waiting for transfers between devices, fused_exchange(): lax.ppermute(block, AXES, way)  7.28 us
    ppermute x6, starting transfers between devices, fused_exchange(): passed = [lax.ppermute(block, AXES, pair) for block in got[:2]]  6 us
    ppermute x3, waiting for transfers between devices, fused_exchange(): second = lax.ppermute(out, AXES, skip)  4.84 us
    ppermute x3, waiting for transfers between devices, fused_exchange(): other = lax.ppermute(shared, AXES, pair)  3.36 us
  transfers between devices with their start and end apart: 21, of which 10 were waited for; matrix products, arithmetic and copies ran while one was open for 0% of the time, Pallas kernels for 0%

profile of v10, /device:TPU:0, one launch (start us, length us, event | category | flops | bytes accessed | tf_op | source)
XLA Modules:
  0.0 74.0 jit_solution(686751830502085875)
XLA Ops:
  0.7 4.1 %shard_map.95 = (f32[56,384]{1,0:T(8,128)S(1)}, f32[56,128]{1,0:T(8,128)S(1)}, bf16[384,768]{1,0:T(8,128)(2,1)S(1)}, f32[8,768]{1,0:T(8,128)S(1)}, f32[192,128]{...) custom-call(s32[6,128]{1,0:T(8,128)} %bitcast.11, s32[6,128]{1,0:T(8,128)} %bitcast.12, ...), custom_call_target="tpu_custom_call" | custom-call | tf_op jit(solution)/shard_map/pallas_call | solution.py:534
  4.8 0.5 collective-permute-start
  5.3 0.9 %collective-permute-done.other_ref.refs_1_ = f32[56,384]{1,0:T(8,128)S(1)} collective-permute-done((f32[56,384]{1,0:T(8,128)S(1)}, f32[56,384]{1,0:T(8,128)S(1)}, u32[]{:S(2)}, u32[]{:S(2)}) %collective-permute-start) | collective-permute-done | bytes 86048 | tf_op jit(solution)/shard_map/ppermute | solution.py:556
  6.3 0.3 shard_map.96
  6.5 2.7 %collective-permute-start.2 = (f32[56,640]{1,0:T(8,128)S(1)}, f32[56,640]{1,0:T(8,128)S(1)}, u32[]{:S(2)}, u32[]{:S(2)}) collective-permute-start(f32[56,640]{1,0:T(8,128)S(1)} %get-tuple-element.47), channel_id=1, source_target_pairs={{0,3},{2,5},{4,7},{6,9},{8,11},{10,13},{12,15},{14,17},{16,19},{18... | collective-permute-start | bytes 430088 | tf_op jit(solution)/shard_map/ppermute | solution.py:561
  9.2 2.5 %collective-permute-start.3 = (f32[56,128]{1,0:T(8,128)S(1)}, f32[56,128]{1,0:T(8,128)S(1)}, u32[]{:S(2)}, u32[]{:S(2)}) collective-permute-start(f32[56,128]{1,0:T(8,128)S(1)} %get-tuple-element.48), channel_id=1, source_target_pairs={{0,15},{2,17},{4,19},{6,21},{8,23},{10,25},{12,27},{14,29},{16,31}... | collective-permute-start | bytes 86024 | tf_op jit(solution)/shard_map/ppermute | solution.py:561
  11.6 2.6 %collective-permute-done.3.refs_4_ = f32[56,128]{1,0:T(8,128)S(1)} collective-permute-done((f32[56,128]{1,0:T(8,128)S(1)}, f32[56,128]{1,0:T(8,128)S(1)}, u32[]{:S(2)}, u32[]{:S(2)}) %collective-permute-start.3) | collective-permute-done | bytes 28704 | tf_op jit(solution)/shard_map/ppermute | solution.py:561
  14.3 4.4 %collective-permute-start.5 = (f32[56,640]{1,0:T(8,128)S(1)}, f32[56,640]{1,0:T(8,128)S(1)}, u32[]{:S(2)}, u32[]{:S(2)}) collective-permute-start(f32[56,640]{1,0:T(8,128)S(1)} %collective-permute-done.2.refs_3_), channel_id=1, source_target_pairs={{0,1},{1,0},{2,3},{3,2},{4,5},{5,4},{6,7},{7,6},{8,9},{9,8},{10,11... | collective-permute-start | bytes 430088 | tf_op jit(solution)/shard_map/ppermute | solution.py:566
  18.6 1.9 %collective-permute-start.1 = (f32[56,128]{1,0:T(8,128)S(1)}, f32[56,128]{1,0:T(8,128)S(1)}, u32[]{:S(2)}, u32[]{:S(2)}) collective-permute-start(f32[56,128]{1,0:T(8,128)S(1)} %get-tuple-element.46), channel_id=1, source_target_pairs={{0,29},{1,4},{2,31},{3,6},{4,1},{5,8},{6,3},{7,10},{8,5},{9,12},{1... | collective-permute-start | bytes 86024 | tf_op jit(solution)/shard_map/ppermute | solution.py:555
  20.6 4.2 %collective-permute-done.1.refs_2_ = f32[56,128]{1,0:T(8,128)S(1)} collective-permute-done((f32[56,128]{1,0:T(8,128)S(1)}, f32[56,128]{1,0:T(8,128)S(1)}, u32[]{:S(2)}, u32[]{:S(2)}) %collective-permute-start.1) | collective-permute-done | bytes 28704 | tf_op jit(solution)/shard_map/ppermute | solution.py:555
  24.7 0.3 collective-permute-done.4.refs_5_
  25.1 4.8 %shard_map.97 = (f32[48,256]{1,0:T(8,128)S(1)}, f32[8,128]{1,0:T(8,128)S(1)}, f32[8,128]{1,0:T(8,128)S(1)}, f32[48,256]{1,0:T(8,128)S(1)}, f32[104,128]{1,0:T(8,...) custom-call(f32[8,768]{1,0:T(8,128)S(1)} %get-tuple-element.40.meta_ref, ...), custom_call_target="tpu_custom_call" | custom-call | tf_op jit(solution)/shard_map/pallas_call | solution.py:534
  30.0 1.2 %collective-permute-done.7.other_ref.refs_4_ = f32[104,128]{1,0:T(8,128)S(1)} collective-permute-done((f32[104,128]{1,0:T(8,128)S(1)}, f32[104,128]{1,0:T(8,128)S(1)}, u32[]{:S(2)}, u32[]{:S(2)}) %collective-permute-start.7) | collective-permute-done | bytes 53280 | tf_op jit(solution)/shard_map/ppermute | solution.py:556
  31.2 0.4 shard_map.98
  31.7 1.4 %collective-permute-start.9 = (f32[56,128]{1,0:T(8,128)S(1)}, f32[56,128]{1,0:T(8,128)S(1)}, u32[]{:S(2)}, u32[]{:S(2)}) collective-permute-start(f32[56,128]{1,0:T(8,128)S(1)} %get-tuple-element.57), channel_id=1, source_target_pairs={{0,3},{2,5},{4,7},{6,9},{8,11},{10,13},{12,15},{14,17},{16,19},{18... | collective-permute-start | bytes 86024 | tf_op jit(solution)/shard_map/ppermute | solution.py:561
  33.1 1.1 %collective-permute-start.10 = (f32[56,128]{1,0:T(8,128)S(1)}, f32[56,128]{1,0:T(8,128)S(1)}, u32[]{:S(2)}, u32[]{:S(2)}) collective-permute-start(f32[56,128]{1,0:T(8,128)S(1)} %get-tuple-element.58), channel_id=1, source_target_pairs={{0,15},{2,17},{4,19},{6,21},{8,23},{10,25},{12,27},{14,29},{16,31}... | collective-permute-start | bytes 86024 | tf_op jit(solution)/shard_map/ppermute | solution.py:561
  34.2 3.5 %collective-permute-start.8 = (f32[104,128]{1,0:T(8,128)S(1)}, f32[104,128]{1,0:T(8,128)S(1)}, u32[]{:S(2)}, u32[]{:S(2)}) collective-permute-start(f32[104,128]{1,0:T(8,128)S(1)} %get-tuple-element.56.mine_ref.refs_3_), channel_id=1, source_target_pairs={{0,29},{1,4},{2,31},{3,6},{4,1},{5,8},{6,3},{7,10},{8,5},{9,12},{1... | collective-permute-start | bytes 159752 | tf_op jit(solution)/shard_map/ppermute | solution.py:555
  37.6 1.2 %collective-permute-start.11 = (f32[56,128]{1,0:T(8,128)S(1)}, f32[56,128]{1,0:T(8,128)S(1)}, u32[]{:S(2)}, u32[]{:S(2)}) collective-permute-start(f32[56,128]{1,0:T(8,128)S(1)} %get-tuple-element.59), channel_id=1, source_target_pairs={{0,16},{1,17},{2,18},{3,19},{4,20},{5,21},{6,22},{7,23},{8,24},{9,... | collective-permute-start | bytes 86024 | tf_op jit(solution)/shard_map/ppermute | solution.py:561
  38.9 1.1 %collective-permute-start.13 = (f32[56,128]{1,0:T(8,128)S(1)}, f32[56,128]{1,0:T(8,128)S(1)}, u32[]{:S(2)}, u32[]{:S(2)}) collective-permute-start(f32[56,128]{1,0:T(8,128)S(1)} %collective-permute-done.10.refs_7_), channel_id=1, source_target_pairs={{0,1},{1,0},{2,3},{3,2},{4,5},{5,4},{6,7},{7,6},{8,9},{9,8},{10,11... | collective-permute-start | bytes 86024 | tf_op jit(solution)/shard_map/ppermute | solution.py:566
  40.0 0.5 collective-permute-done.8.refs_5_
  40.5 1.9 %collective-permute-done.11.refs_8_ = f32[56,128]{1,0:T(8,128)S(1)} collective-permute-done((f32[56,128]{1,0:T(8,128)S(1)}, f32[56,128]{1,0:T(8,128)S(1)}, u32[]{:S(2)}, u32[]{:S(2)}) %collective-permute-start.11) | collective-permute-done | bytes 28704 | tf_op jit(solution)/shard_map/ppermute | solution.py:561
  42.4 4.8 %shard_map.99 = (f32[48,256]{1,0:T(8,128)S(1)}, f32[48,256]{1,0:T(8,128)S(1)}, f32[104,128]{1,0:T(8,128)S(1)}, f32[288,128]{1,0:T(8,128)S(1)}, f32[192,128]{1,0:T(8,128)S(1)}, /*index=5*/f32[192,128]{1,0:T(8,128)S(1)}) custom-call(f32[8,768]{1,0:T(8,128)S(1)} %get-tuple-element.40.meta_ref, bf16[384,768]{1,0:T(8,128)(2,1)S(1)} %get-tuple-element.41.onehot_ref, ...), custom_call_target="tpu_custom_call" | custom-call | tf_op jit(solution)/shard_map/pallas_call | solution.py:534
  47.3 1.2 %collective-permute-done.14.other_ref.refs_1_ = f32[104,128]{1,0:T(8,128)S(1)} collective-permute-done((f32[104,128]{1,0:T(8,128)S(1)}, f32[104,128]{1,0:T(8,128)S(1)}, u32[]{:S(2)}, u32[]{:S(2)}) %collective-permute-start.14) | collective-permute-done | bytes 53280 | tf_op jit(solution)/shard_map/ppermute | solution.py:556
  48.5 0.4 shard_map.100
  49.0 0.8 %collective-permute-start.17 = (f32[56,128]{1,0:T(8,128)S(1)}, f32[56,128]{1,0:T(8,128)S(1)}, u32[]{:S(2)}, u32[]{:S(2)}) collective-permute-start(f32[56,128]{1,0:T(8,128)S(1)} %get-tuple-element.68), channel_id=1, source_target_pairs={{0,15},{2,17},{4,19},{6,21},{8,23},{10,25},{12,27},{14,29},{16,31}... | collective-permute-start | bytes 86024 | tf_op jit(solution)/shard_map/ppermute | solution.py:561
  49.8 4.6 %collective-permute-start.15 = (f32[104,128]{1,0:T(8,128)S(1)}, f32[104,128]{1,0:T(8,128)S(1)}, u32[]{:S(2)}, u32[]{:S(2)}) collective-permute-start(f32[104,128]{1,0:T(8,128)S(1)} %get-tuple-element.66.mine_ref.refs_0_), channel_id=1, source_target_pairs={{0,29},{1,4},{2,31},{3,6},{4,1},{5,8},{6,3},{7,10},{8,5},{9,12},{1... | collective-permute-start | bytes 159752 | tf_op jit(solution)/shard_map/ppermute | solution.py:555
  54.5 1.7 %collective-permute-start.18 = (f32[56,128]{1,0:T(8,128)S(1)}, f32[56,128]{1,0:T(8,128)S(1)}, u32[]{:S(2)}, u32[]{:S(2)}) collective-permute-start(f32[56,128]{1,0:T(8,128)S(1)} %get-tuple-element.69), channel_id=1, source_target_pairs={{0,16},{1,17},{2,18},{3,19},{4,20},{5,21},{6,22},{7,23},{8,24},{9,... | collective-permute-start | bytes 86024 | tf_op jit(solution)/shard_map/ppermute | solution.py:561
  56.2 0.4 collective-permute-start.20
  56.8 2.4 %collective-permute-done.18.refs_5_ = f32[56,128]{1,0:T(8,128)S(1)} collective-permute-done((f32[56,128]{1,0:T(8,128)S(1)}, f32[56,128]{1,0:T(8,128)S(1)}, u32[]{:S(2)}, u32[]{:S(2)}) %collective-permute-start.18) | collective-permute-done | bytes 28704 | tf_op jit(solution)/shard_map/ppermute | solution.py:561
  59.2 3.9 %shard_map.101 = (f32[48,256]{1,0:T(8,128)S(1)}, f32[192,128]{1,0:T(8,128)S(1)}, f32[32,1,128]{2,1,0:T(1,128)S(1)}) custom-call(f32[8,768]{1,0:T(8,128)S(1)} %get-tuple-element.40.meta_ref, bf16[384,768]{1,0:T(8,128)(2,1)S(1)} %get-tuple-element.41.onehot_ref, f32[192,48]{1,0:T(8,128)S(1)} %copy-done, f32[4096,128]{1,0:T(8,128)S(1)} %get-tuple-element.42.inverse_ref, ...), custom_call_target="tpu_custom_call" | custom-call | tf_op jit(solution)/shard_map/pallas_call | solution.py:534
  63.2 9.0 %all_to_all.5.moment_ref = f32[32,1,128]{2,1,0:T(1,128)S(1)} all-to-all(f32[32,1,128]{2,1,0:T(1,128)S(1)} %get-tuple-element.70), channel_id=1, replica_groups=mesh['dom'=16,'blk'=2] {'dom','blk'}, dimensions={0} | all-to-all | bytes 32768 | tf_op jit(solution)/shard_map/all_to_all | solution.py:646
  72.2 1.8 %shard_map.102 = (f32[48,256]{1,0:T(8,128)}, f32[192,128]{1,0:T(8,128)}) custom-call(f32[32,1,128]{2,1,0:T(1,128)S(1)} %all_to_all.5.moment_ref, f32[48,256]{1,0:T(8,128)S(1)} %get-tuple-element.52.k0_ref, f32[48,256]{1,0:T(8,128)S(1)} %get-tuple-element.60.k1_ref, f32[48,256]{1,0:T(8,128)S(1)} %get-tuple-element.71.k2_ref, ...), custom_call_target="tpu_custom_call" | custom-call | tf_op jit(solution)/shard_map/pallas_call | solution.py:534
  (23 shorter events, 0.5 us)
Async XLA Ops:
  0.6 24.5 %copy-start = (f32[192,48]{1,0:T(8,128)S(1)}, f32[192,48]{1,0:T(8,128)}, u32[]{:S(2)}) copy-start(f32[192,48]{1,0:T(8,128)} %constant.5.clone.forth_ref) | copy-start | bytes 110596
  0.6 24.4 %copy-start.1 = (f32[192,48]{1,0:T(8,128)S(1)}, f32[192,48]{1,0:T(8,128)}, u32[]{:S(2)}) copy-start(f32[192,48]{1,0:T(8,128)} %constant.4.clone.back_hbm.back_ref) | copy-start | bytes 110596
  4.8 1.4 %collective-permute-start = (f32[56,384]{1,0:T(8,128)S(1)}, f32[56,384]{1,0:T(8,128)S(1)}, u32[]{:S(2)}, u32[]{:S(2)}) collective-permute-start(f32[56,384]{1,0:T(8,128)S(1)} %get-tuple-element.45.mine_ref.refs_0_), channel_id=1, source_target_pairs={{0,1},{1,0},{2,3},{3,2},{4,5},{5,4},{6,7},{7,6},{8,9},{9,8},{10,11... | collective-permute-start | bytes 258056 | tf_op jit(solution)/shard_map/ppermute | solution.py:556
  6.5 7.8 %collective-permute-start.2 = (f32[56,640]{1,0:T(8,128)S(1)}, f32[56,640]{1,0:T(8,128)S(1)}, u32[]{:S(2)}, u32[]{:S(2)}) collective-permute-start(f32[56,640]{1,0:T(8,128)S(1)} %get-tuple-element.47), channel_id=1, source_target_pairs={{0,3},{2,5},{4,7},{6,9},{8,11},{10,13},{12,15},{14,17},{16,19},{18... | collective-permute-start | bytes 430088 | tf_op jit(solution)/shard_map/ppermute | solution.py:561
  9.2 5.1 %collective-permute-start.3 = (f32[56,128]{1,0:T(8,128)S(1)}, f32[56,128]{1,0:T(8,128)S(1)}, u32[]{:S(2)}, u32[]{:S(2)}) collective-permute-start(f32[56,128]{1,0:T(8,128)S(1)} %get-tuple-element.48), channel_id=1, source_target_pairs={{0,15},{2,17},{4,19},{6,21},{8,23},{10,25},{12,27},{14,29},{16,31}... | collective-permute-start | bytes 86024 | tf_op jit(solution)/shard_map/ppermute | solution.py:561
  14.3 10.8 %collective-permute-start.5 = (f32[56,640]{1,0:T(8,128)S(1)}, f32[56,640]{1,0:T(8,128)S(1)}, u32[]{:S(2)}, u32[]{:S(2)}) collective-permute-start(f32[56,640]{1,0:T(8,128)S(1)} %collective-permute-done.2.refs_3_), channel_id=1, source_target_pairs={{0,1},{1,0},{2,3},{3,2},{4,5},{5,4},{6,7},{7,6},{8,9},{9,8},{10,11... | collective-permute-start | bytes 430088 | tf_op jit(solution)/shard_map/ppermute | solution.py:566
  18.6 6.4 %collective-permute-start.4 = (f32[56,384]{1,0:T(8,128)S(1)}, f32[56,384]{1,0:T(8,128)S(1)}, u32[]{:S(2)}, u32[]{:S(2)}) collective-permute-start(f32[56,384]{1,0:T(8,128)S(1)} %get-tuple-element.51), channel_id=1, source_target_pairs={{0,16},{1,17},{2,18},{3,19},{4,20},{5,21},{6,22},{7,23},{8,24},{9,... | collective-permute-start | bytes 258056 | tf_op jit(solution)/shard_map/ppermute | solution.py:561
  18.6 6.1 %collective-permute-start.1 = (f32[56,128]{1,0:T(8,128)S(1)}, f32[56,128]{1,0:T(8,128)S(1)}, u32[]{:S(2)}, u32[]{:S(2)}) collective-permute-start(f32[56,128]{1,0:T(8,128)S(1)} %get-tuple-element.46), channel_id=1, source_target_pairs={{0,29},{1,4},{2,31},{3,6},{4,1},{5,8},{6,3},{7,10},{8,5},{9,12},{1... | collective-permute-start | bytes 86024 | tf_op jit(solution)/shard_map/ppermute | solution.py:555
  20.6 4.5 %collective-permute-start.6 = (f32[56,128]{1,0:T(8,128)S(1)}, f32[56,128]{1,0:T(8,128)S(1)}, u32[]{:S(2)}, u32[]{:S(2)}) collective-permute-start(f32[56,128]{1,0:T(8,128)S(1)} %collective-permute-done.3.refs_4_), channel_id=1, source_target_pairs={{0,1},{1,0},{2,3},{3,2},{4,5},{5,4},{6,7},{7,6},{8,9},{9,8},{10,11... | collective-permute-start | bytes 86024 | tf_op jit(solution)/shard_map/ppermute | solution.py:566
  29.9 1.3 %collective-permute-start.7 = (f32[104,128]{1,0:T(8,128)S(1)}, f32[104,128]{1,0:T(8,128)S(1)}, u32[]{:S(2)}, u32[]{:S(2)}) collective-permute-start(f32[104,128]{1,0:T(8,128)S(1)} %get-tuple-element.56.mine_ref.refs_3_), channel_id=1, source_target_pairs={{0,1},{1,0},{2,3},{3,2},{4,5},{5,4},{6,7},{7,6},{8,9},{9,8},{10,11... | collective-permute-start | bytes 159752 | tf_op jit(solution)/shard_map/ppermute | solution.py:556
  31.7 7.2 %collective-permute-start.9 = (f32[56,128]{1,0:T(8,128)S(1)}, f32[56,128]{1,0:T(8,128)S(1)}, u32[]{:S(2)}, u32[]{:S(2)}) collective-permute-start(f32[56,128]{1,0:T(8,128)S(1)} %get-tuple-element.57), channel_id=1, source_target_pairs={{0,3},{2,5},{4,7},{6,9},{8,11},{10,13},{12,15},{14,17},{16,19},{18... | collective-permute-start | bytes 86024 | tf_op jit(solution)/shard_map/ppermute | solution.py:561
  33.1 5.8 %collective-permute-start.10 = (f32[56,128]{1,0:T(8,128)S(1)}, f32[56,128]{1,0:T(8,128)S(1)}, u32[]{:S(2)}, u32[]{:S(2)}) collective-permute-start(f32[56,128]{1,0:T(8,128)S(1)} %get-tuple-element.58), channel_id=1, source_target_pairs={{0,15},{2,17},{4,19},{6,21},{8,23},{10,25},{12,27},{14,29},{16,31}... | collective-permute-start | bytes 86024 | tf_op jit(solution)/shard_map/ppermute | solution.py:561
  34.2 6.4 %collective-permute-start.8 = (f32[104,128]{1,0:T(8,128)S(1)}, f32[104,128]{1,0:T(8,128)S(1)}, u32[]{:S(2)}, u32[]{:S(2)}) collective-permute-start(f32[104,128]{1,0:T(8,128)S(1)} %get-tuple-element.56.mine_ref.refs_3_), channel_id=1, source_target_pairs={{0,29},{1,4},{2,31},{3,6},{4,1},{5,8},{6,3},{7,10},{8,5},{9,12},{1... | collective-permute-start | bytes 159752 | tf_op jit(solution)/shard_map/ppermute | solution.py:555
  37.6 4.8 %collective-permute-start.11 = (f32[56,128]{1,0:T(8,128)S(1)}, f32[56,128]{1,0:T(8,128)S(1)}, u32[]{:S(2)}, u32[]{:S(2)}) collective-permute-start(f32[56,128]{1,0:T(8,128)S(1)} %get-tuple-element.59), channel_id=1, source_target_pairs={{0,16},{1,17},{2,18},{3,19},{4,20},{5,21},{6,22},{7,23},{8,24},{9,... | collective-permute-start | bytes 86024 | tf_op jit(solution)/shard_map/ppermute | solution.py:561
  38.9 3.5 %collective-permute-start.12 = (f32[56,128]{1,0:T(8,128)S(1)}, f32[56,128]{1,0:T(8,128)S(1)}, u32[]{:S(2)}, u32[]{:S(2)}) collective-permute-start(f32[56,128]{1,0:T(8,128)S(1)} %collective-permute-done.9.refs_6_), channel_id=1, source_target_pairs={{0,1},{1,0},{2,3},{3,2},{4,5},{5,4},{6,7},{7,6},{8,9},{9,8},{10,11... | collective-permute-start | bytes 86024 | tf_op jit(solution)/shard_map/ppermute | solution.py:566
  38.9 3.5 %collective-permute-start.13 = (f32[56,128]{1,0:T(8,128)S(1)}, f32[56,128]{1,0:T(8,128)S(1)}, u32[]{:S(2)}, u32[]{:S(2)}) collective-permute-start(f32[56,128]{1,0:T(8,128)S(1)} %collective-permute-done.10.refs_7_), channel_id=1, source_target_pairs={{0,1},{1,0},{2,3},{3,2},{4,5},{5,4},{6,7},{7,6},{8,9},{9,8},{10,11... | collective-permute-start | bytes 86024 | tf_op jit(solution)/shard_map/ppermute | solution.py:566
  47.2 1.3 %collective-permute-start.14 = (f32[104,128]{1,0:T(8,128)S(1)}, f32[104,128]{1,0:T(8,128)S(1)}, u32[]{:S(2)}, u32[]{:S(2)}) collective-permute-start(f32[104,128]{1,0:T(8,128)S(1)} %get-tuple-element.66.mine_ref.refs_0_), channel_id=1, source_target_pairs={{0,1},{1,0},{2,3},{3,2},{4,5},{5,4},{6,7},{7,6},{8,9},{9,8},{10,11... | collective-permute-start | bytes 159752 | tf_op jit(solution)/shard_map/ppermute | solution.py:556
  48.9 7.2 %collective-permute-start.16 = (f32[56,128]{1,0:T(8,128)S(1)}, f32[56,128]{1,0:T(8,128)S(1)}, u32[]{:S(2)}, u32[]{:S(2)}) collective-permute-start(f32[56,128]{1,0:T(8,128)S(1)} %get-tuple-element.67), channel_id=1, source_target_pairs={{0,3},{2,5},{4,7},{6,9},{8,11},{10,13},{12,15},{14,17},{16,19},{18... | collective-permute-start | bytes 86024 | tf_op jit(solution)/shard_map/ppermute | solution.py:561
  49.0 7.2 %collective-permute-start.17 = (f32[56,128]{1,0:T(8,128)S(1)}, f32[56,128]{1,0:T(8,128)S(1)}, u32[]{:S(2)}, u32[]{:S(2)}) collective-permute-start(f32[56,128]{1,0:T(8,128)S(1)} %get-tuple-element.68), channel_id=1, source_target_pairs={{0,15},{2,17},{4,19},{6,21},{8,23},{10,25},{12,27},{14,29},{16,31}... | collective-permute-start | bytes 86024 | tf_op jit(solution)/shard_map/ppermute | solution.py:561
  49.8 7.0 %collective-permute-start.15 = (f32[104,128]{1,0:T(8,128)S(1)}, f32[104,128]{1,0:T(8,128)S(1)}, u32[]{:S(2)}, u32[]{:S(2)}) collective-permute-start(f32[104,128]{1,0:T(8,128)S(1)} %get-tuple-element.66.mine_ref.refs_0_), channel_id=1, source_target_pairs={{0,29},{1,4},{2,31},{3,6},{4,1},{5,8},{6,3},{7,10},{8,5},{9,12},{1... | collective-permute-start | bytes 159752 | tf_op jit(solution)/shard_map/ppermute | solution.py:555
  54.5 4.8 %collective-permute-start.18 = (f32[56,128]{1,0:T(8,128)S(1)}, f32[56,128]{1,0:T(8,128)S(1)}, u32[]{:S(2)}, u32[]{:S(2)}) collective-permute-start(f32[56,128]{1,0:T(8,128)S(1)} %get-tuple-element.69), channel_id=1, source_target_pairs={{0,16},{1,17},{2,18},{3,19},{4,20},{5,21},{6,22},{7,23},{8,24},{9,... | collective-permute-start | bytes 86024 | tf_op jit(solution)/shard_map/ppermute | solution.py:561
  56.1 3.1 %collective-permute-start.19 = (f32[56,128]{1,0:T(8,128)S(1)}, f32[56,128]{1,0:T(8,128)S(1)}, u32[]{:S(2)}, u32[]{:S(2)}) collective-permute-start(f32[56,128]{1,0:T(8,128)S(1)} %collective-permute-done.16.refs_3_), channel_id=1, source_target_pairs={{0,1},{1,0},{2,3},{3,2},{4,5},{5,4},{6,7},{7,6},{8,9},{9,8},{10,11... | collective-permute-start | bytes 86024 | tf_op jit(solution)/shard_map/ppermute | solution.py:566
  56.2 3.0 %collective-permute-start.20 = (f32[56,128]{1,0:T(8,128)S(1)}, f32[56,128]{1,0:T(8,128)S(1)}, u32[]{:S(2)}, u32[]{:S(2)}) collective-permute-start(f32[56,128]{1,0:T(8,128)S(1)} %collective-permute-done.17.refs_4_), channel_id=1, source_target_pairs={{0,1},{1,0},{2,3},{3,2},{4,5},{5,4},{6,7},{7,6},{8,9},{9,8},{10,11... | collective-permute-start | bytes 86024 | tf_op jit(solution)/shard_map/ppermute | solution.py:566
